TPU v7x, 32 devices: a whole 2x2x4 slice. The times are simulated.
32 devices in a mesh: rep: 4 (over y, core), fsdp: 8 (over z, x).
Axes of the slice: x: 2, y: 2, z: 4, core: 2. Of those that a mesh axis runs over, the one named last changes fastest.
Arguments:
- layer_input: bfloat16 [64, 512, 768], P(('rep', 'fsdp')), may hold values from -6 to 6
- masked: int32 [64, 512], P(('rep', 'fsdp')), may hold values 0 or 1
- replaced: int32 [64, 512], P(('rep', 'fsdp')), may hold values 0 or 1
- lengths: int32 [64], P(('rep', 'fsdp')), may hold values from 256 to 512
- w_qkv: bfloat16 [768, 2304], P('fsdp'), may hold values from -0.21875 to 0.21875
- b_q: bfloat16 [768], P('fsdp'), may hold values from -3 to 3
- b_v: bfloat16 [768], P('fsdp'), may hold values from -3 to 3
- w_out: bfloat16 [768, 768], P('fsdp'), may hold values from -0.875 to 0.875
- b_out: bfloat16 [768], P('fsdp'), may hold values from -3 to 3
- gain1: bfloat16 [768], P('fsdp'), may hold values from 0.25 to 1.75
- shift1: bfloat16 [768], P('fsdp'), may hold values from -3 to 3
- mask_vec: bfloat16 [768], P('fsdp'), may hold values from -4 to 4
- repl_vec: bfloat16 [768], P('fsdp'), may hold values from -4 to 4
- w_in: bfloat16 [768, 3072], P('fsdp'), may hold values from -0.21875 to 0.21875
- b_in: bfloat16 [3072], P('fsdp'), may hold values from -3 to 3
- w_down: bfloat16 [3072, 768], P('fsdp'), may hold values from -0.109375 to 0.109375
- b_down: bfloat16 [768], P('fsdp'), may hold values from -3 to 3
- gain2: bfloat16 [768], P('fsdp'), may hold values from 0.25 to 1.75
- shift2: bfloat16 [768], P('fsdp'), may hold values from -3 to 3
- cotangent: bfloat16 [64, 512, 768], P(('rep', 'fsdp')), may hold values from -6 to 6
Outputs:
- layer_output: bfloat16 [64, 512, 768], P(('rep', 'fsdp'))
- grad_input: bfloat16 [64, 512, 768], P(('rep', 'fsdp'))
- grad_w_qkv: float32 [768, 2304], P('fsdp')
- grad_b_q: float32 [768], P('fsdp')
- grad_b_v: float32 [768], P('fsdp')
- grad_w_out: float32 [768, 768], P('fsdp')
- grad_b_out: float32 [768], P('fsdp')
- grad_gain1: float32 [768], P('fsdp')
- grad_shift1: float32 [768], P('fsdp')
- grad_mask_vec: float32 [768], P('fsdp')
- grad_repl_vec: float32 [768], P('fsdp')
- grad_w_in: float32 [768, 3072], P('fsdp')
- grad_b_in: float32 [3072], P('fsdp')
- grad_w_down: float32 [3072, 768], P('fsdp')
- grad_b_down: float32 [768], P('fsdp')
- grad_gain2: float32 [768], P('fsdp')
- grad_shift2: float32 [768], P('fsdp')
All inputs are finite; a program needn't handle non-finite values. No bound on the sum of `masked` or of `replaced` on one device may be relied on, other than what follows from the above.
Results may differ from a plain program's by a relative error of at most 0.018.
Values may be sent and summed in bfloat16 or wider, within the bound.
No kernel may reach another device: no remote copies, remote signals or barrier semaphores. Data moves between devices by JAX's collectives and lax.ppermute only.
A program may use at most 192 MiB of HBM per device.

v0:
```python
import jax
import jax.numpy as jnp
from jax import lax
from jax.sharding import PartitionSpec as P

HEADS = 12


epsilon = 1e-05


def norm_forward(resid, gain, shift):
    center = resid - jnp.mean(resid, axis=-1, keepdims=True)
    inv_std = lax.rsqrt(jnp.mean(center * center, axis=-1, keepdims=True) + epsilon)
    normal = center * inv_std
    return (normal * gain + shift, normal, inv_std)


def norm_backward(grad_out, normal, inv_std, gain):
    scaled = grad_out * gain
    grad_in = inv_std * (
        scaled
        - jnp.mean(scaled, axis=-1, keepdims=True)
        - normal * jnp.mean(scaled * normal, axis=-1, keepdims=True)
    )
    return (grad_in, jnp.sum(grad_out * normal, axis=0), jnp.sum(grad_out, axis=0))


def cross_rows(left, right):
    return lax.dot_general(
        left, right, (((0,), (0,)), ((), ())), preferred_element_type=jnp.float32
    )


def cross_cols(left, right):
    return lax.dot_general(
        left, right, (((1,), (1,)), ((), ())), preferred_element_type=jnp.float32
    )


def attend(operands):
    query, keys, values, length = operands
    scale = query.shape[-1] ** (-0.5)
    scores = jnp.einsum("qhd,khd->hqk", query, keys, preferred_element_type=jnp.float32) * scale
    allowed = lax.broadcasted_iota(jnp.int32, (1, 1, scores.shape[-1]), 2) < length
    limited = jnp.where(allowed, scores, -1e30)
    row_max = jnp.max(limited, axis=-1, keepdims=True)
    expo = jnp.exp(limited - row_max)
    row_total = jnp.sum(expo, axis=-1, keepdims=True)
    probs_low = (expo / row_total).astype(jnp.bfloat16)
    context = jnp.einsum("hqk,khd->qhd", probs_low, values, preferred_element_type=jnp.float32)
    return (context.astype(jnp.bfloat16), row_max + jnp.log(row_total))


def attend_back(operands):
    query, keys, values, length, log_total, dcontext = operands
    scale = query.shape[-1] ** (-0.5)
    scores = jnp.einsum("qhd,khd->hqk", query, keys, preferred_element_type=jnp.float32) * scale
    allowed = lax.broadcasted_iota(jnp.int32, (1, 1, scores.shape[-1]), 2) < length
    probs = jnp.exp(jnp.where(allowed, scores, -1e30) - log_total)
    probs_low = probs.astype(jnp.bfloat16)
    dvalues = jnp.einsum("hqk,qhd->khd", probs_low, dcontext, preferred_element_type=jnp.float32)
    dprobs = jnp.einsum("qhd,khd->hqk", dcontext, values, preferred_element_type=jnp.float32)
    dscores = (probs * (dprobs - jnp.sum(probs * dprobs, axis=-1, keepdims=True))).astype(
        jnp.bfloat16
    )
    dquery = jnp.einsum("hqk,khd->qhd", dscores, keys, preferred_element_type=jnp.float32) * scale
    dkeys = jnp.einsum("hqk,qhd->khd", dscores, query, preferred_element_type=jnp.float32) * scale
    return (dquery.astype(jnp.bfloat16), dkeys.astype(jnp.bfloat16), dvalues.astype(jnp.bfloat16))


def body(
    layer_input,
    masked,
    replaced,
    lengths,
    w_qkv,
    b_q,
    b_v,
    w_out,
    b_out,
    gain1,
    shift1,
    mask_vec,
    repl_vec,
    w_in,
    b_in,
    w_down,
    b_down,
    gain2,
    shift2,
    cotangent,
):
    doc_count, seq_len, width = layer_input.shape
    tok_count = doc_count * seq_len
    head_size = width // HEADS
    wide_type = jnp.float32
    attn_full = (
        lax.all_gather(w_qkv, "fsdp", axis=0, tiled=True),
        lax.all_gather(b_q, "fsdp", axis=0, tiled=True),
        lax.all_gather(b_v, "fsdp", axis=0, tiled=True),
        lax.all_gather(w_out, "fsdp", axis=0, tiled=True),
        lax.all_gather(b_out, "fsdp", axis=0, tiled=True),
        lax.all_gather(gain1, "fsdp", axis=0, tiled=True),
        lax.all_gather(shift1, "fsdp", axis=0, tiled=True),
        lax.all_gather(mask_vec, "fsdp", axis=0, tiled=True),
        lax.all_gather(repl_vec, "fsdp", axis=0, tiled=True),
    )
    ffn_full = (
        lax.all_gather(w_in, "fsdp", axis=0, tiled=True),
        lax.all_gather(b_in, "fsdp", axis=0, tiled=True),
        lax.all_gather(w_down, "fsdp", axis=0, tiled=True),
        lax.all_gather(b_down, "fsdp", axis=0, tiled=True),
        lax.all_gather(gain2, "fsdp", axis=0, tiled=True),
        lax.all_gather(shift2, "fsdp", axis=0, tiled=True),
    )
    mask_flag = masked.astype(wide_type).reshape(tok_count, 1)
    repl_flag = replaced.astype(wide_type).reshape(tok_count, 1)
    embed = (
        layer_input.astype(wide_type).reshape(tok_count, width)
        + mask_flag * attn_full[7].astype(wide_type)
        + repl_flag * attn_full[8].astype(wide_type)
    )
    embed_low = embed.astype(jnp.bfloat16)
    qkv_bias = jnp.concatenate(
        [
            attn_full[1].astype(wide_type),
            jnp.zeros((width,), wide_type),
            attn_full[2].astype(wide_type),
        ]
    )
    qkv_low = (
        jnp.dot(embed_low, attn_full[0], preferred_element_type=wide_type) + qkv_bias
    ).astype(jnp.bfloat16)
    split_shape = (doc_count, seq_len, HEADS, head_size)
    query = qkv_low[:, :width].reshape(split_shape)
    keys = qkv_low[:, width : 2 * width].reshape(split_shape)
    values = qkv_low[:, 2 * width :].reshape(split_shape)
    context, log_total = lax.map(attend, (query, keys, values, lengths))
    context_low = context.reshape(tok_count, width)
    resid1 = (
        embed
        + jnp.dot(context_low, attn_full[3], preferred_element_type=wide_type)
        + attn_full[4].astype(wide_type)
    )
    normed, normal1, inv_one = norm_forward(
        resid1, attn_full[5].astype(wide_type), attn_full[6].astype(wide_type)
    )
    normed_low = normed.astype(jnp.bfloat16)
    hidden = jnp.dot(normed_low, ffn_full[0], preferred_element_type=wide_type) + ffn_full[
        1
    ].astype(wide_type)
    activated = jax.nn.gelu(hidden, approximate=False).astype(jnp.bfloat16)
    resid2 = (
        normed
        + jnp.dot(activated, ffn_full[2], preferred_element_type=wide_type)
        + ffn_full[3].astype(wide_type)
    )
    result, normal2, inv_two = norm_forward(
        resid2, ffn_full[4].astype(wide_type), ffn_full[5].astype(wide_type)
    )
    layer_output = result.astype(jnp.bfloat16).reshape(doc_count, seq_len, width)
    attn_back = (
        lax.all_gather(w_qkv, "fsdp", axis=0, tiled=True),
        lax.all_gather(b_q, "fsdp", axis=0, tiled=True),
        lax.all_gather(b_v, "fsdp", axis=0, tiled=True),
        lax.all_gather(w_out, "fsdp", axis=0, tiled=True),
        lax.all_gather(b_out, "fsdp", axis=0, tiled=True),
        lax.all_gather(gain1, "fsdp", axis=0, tiled=True),
        lax.all_gather(shift1, "fsdp", axis=0, tiled=True),
        lax.all_gather(mask_vec, "fsdp", axis=0, tiled=True),
        lax.all_gather(repl_vec, "fsdp", axis=0, tiled=True),
    )
    ffn_back = (
        lax.all_gather(w_in, "fsdp", axis=0, tiled=True),
        lax.all_gather(b_in, "fsdp", axis=0, tiled=True),
        lax.all_gather(w_down, "fsdp", axis=0, tiled=True),
        lax.all_gather(b_down, "fsdp", axis=0, tiled=True),
        lax.all_gather(gain2, "fsdp", axis=0, tiled=True),
        lax.all_gather(shift2, "fsdp", axis=0, tiled=True),
    )
    grad_out = cotangent.astype(wide_type).reshape(tok_count, width)
    dresid2, grad_gain2, grad_shift2 = norm_backward(
        grad_out, normal2, inv_two, ffn_back[4].astype(wide_type)
    )
    dbranch = dresid2.astype(jnp.bfloat16)
    grad_b_down = jnp.sum(dbranch.astype(wide_type), axis=0)
    dactive = cross_cols(dbranch, ffn_back[2])
    gelu_pull = jax.vjp(lambda inner: jax.nn.gelu(inner, approximate=False), hidden)[1]
    dhidden = gelu_pull(dactive)[0].astype(jnp.bfloat16)
    grad_b_in = jnp.sum(dhidden.astype(wide_type), axis=0)
    dnormed = dresid2 + cross_cols(dhidden, ffn_back[0])
    ffn_owned = (
        lax.psum_scatter(cross_rows(normed_low, dhidden), "fsdp", scatter_dimension=0, tiled=True),
        lax.psum_scatter(grad_b_in, "fsdp", scatter_dimension=0, tiled=True),
        lax.psum_scatter(cross_rows(activated, dbranch), "fsdp", scatter_dimension=0, tiled=True),
        lax.psum_scatter(grad_b_down, "fsdp", scatter_dimension=0, tiled=True),
        lax.psum_scatter(grad_gain2, "fsdp", scatter_dimension=0, tiled=True),
        lax.psum_scatter(grad_shift2, "fsdp", scatter_dimension=0, tiled=True),
    )
    dresid1, grad_gain1, grad_shift1 = norm_backward(
        dnormed, normal1, inv_one, attn_back[5].astype(wide_type)
    )
    dattn = dresid1.astype(jnp.bfloat16)
    grad_b_out = jnp.sum(dattn.astype(wide_type), axis=0)
    dcontext = cross_cols(dattn, attn_back[3]).astype(jnp.bfloat16).reshape(split_shape)
    dquery, dkeys, dvalues = lax.map(
        attend_back, (query, keys, values, lengths, log_total, dcontext)
    )
    dqkv = jnp.concatenate(
        [
            dquery.reshape(tok_count, width),
            dkeys.reshape(tok_count, width),
            dvalues.reshape(tok_count, width),
        ],
        axis=1,
    )
    grad_b_q = jnp.sum(dquery.astype(wide_type).reshape(tok_count, width), axis=0)
    grad_b_v = jnp.sum(dvalues.astype(wide_type).reshape(tok_count, width), axis=0)
    dembed = dresid1 + cross_cols(dqkv, attn_back[0])
    grad_mask_vec = jnp.sum(mask_flag * dembed, axis=0)
    grad_repl_vec = jnp.sum(repl_flag * dembed, axis=0)
    grad_input = dembed.astype(jnp.bfloat16).reshape(doc_count, seq_len, width)
    attn_owned = (
        lax.psum_scatter(cross_rows(embed_low, dqkv), "fsdp", scatter_dimension=0, tiled=True),
        lax.psum_scatter(grad_b_q, "fsdp", scatter_dimension=0, tiled=True),
        lax.psum_scatter(grad_b_v, "fsdp", scatter_dimension=0, tiled=True),
        lax.psum_scatter(cross_rows(context_low, dattn), "fsdp", scatter_dimension=0, tiled=True),
        lax.psum_scatter(grad_b_out, "fsdp", scatter_dimension=0, tiled=True),
        lax.psum_scatter(grad_gain1, "fsdp", scatter_dimension=0, tiled=True),
        lax.psum_scatter(grad_shift1, "fsdp", scatter_dimension=0, tiled=True),
        lax.psum_scatter(grad_mask_vec, "fsdp", scatter_dimension=0, tiled=True),
        lax.psum_scatter(grad_repl_vec, "fsdp", scatter_dimension=0, tiled=True),
    )
    summed = (
        lax.psum(attn_owned[0].astype(jnp.bfloat16), "rep").astype(jnp.float32),
        lax.psum(attn_owned[1].astype(jnp.bfloat16), "rep").astype(jnp.float32),
        lax.psum(attn_owned[2].astype(jnp.bfloat16), "rep").astype(jnp.float32),
        lax.psum(attn_owned[3].astype(jnp.bfloat16), "rep").astype(jnp.float32),
        lax.psum(attn_owned[4].astype(jnp.bfloat16), "rep").astype(jnp.float32),
        lax.psum(attn_owned[5].astype(jnp.bfloat16), "rep").astype(jnp.float32),
        lax.psum(attn_owned[6].astype(jnp.bfloat16), "rep").astype(jnp.float32),
        lax.psum(attn_owned[7].astype(jnp.bfloat16), "rep").astype(jnp.float32),
        lax.psum(attn_owned[8].astype(jnp.bfloat16), "rep").astype(jnp.float32),
        lax.psum(ffn_owned[0].astype(jnp.bfloat16), "rep").astype(jnp.float32),
        lax.psum(ffn_owned[1].astype(jnp.bfloat16), "rep").astype(jnp.float32),
        lax.psum(ffn_owned[2].astype(jnp.bfloat16), "rep").astype(jnp.float32),
        lax.psum(ffn_owned[3].astype(jnp.bfloat16), "rep").astype(jnp.float32),
        lax.psum(ffn_owned[4].astype(jnp.bfloat16), "rep").astype(jnp.float32),
        lax.psum(ffn_owned[5].astype(jnp.bfloat16), "rep").astype(jnp.float32),
    )
    return (
        layer_output,
        grad_input,
        summed[0],
        summed[1],
        summed[2],
        summed[3],
        summed[4],
        summed[5],
        summed[6],
        summed[7],
        summed[8],
        summed[9],
        summed[10],
        summed[11],
        summed[12],
        summed[13],
        summed[14],
    )


def solution(mesh):
    return jax.shard_map(
        body,
        mesh=mesh,
        in_specs=(
            P(("rep", "fsdp"), None, None),
            P(("rep", "fsdp"), None),
            P(("rep", "fsdp"), None),
            P(("rep", "fsdp")),
            P("fsdp", None),
            P("fsdp"),
            P("fsdp"),
            P("fsdp", None),
            P("fsdp"),
            P("fsdp"),
            P("fsdp"),
            P("fsdp"),
            P("fsdp"),
            P("fsdp", None),
            P("fsdp"),
            P("fsdp", None),
            P("fsdp"),
            P("fsdp"),
            P("fsdp"),
            P(("rep", "fsdp"), None, None),
        ),
        out_specs=(
            P(("rep", "fsdp"), None, None),
            P(("rep", "fsdp"), None, None),
            P("fsdp", None),
            P("fsdp"),
            P("fsdp"),
            P("fsdp", None),
            P("fsdp"),
            P("fsdp"),
            P("fsdp"),
            P("fsdp"),
            P("fsdp"),
            P("fsdp", None),
            P("fsdp"),
            P("fsdp", None),
            P("fsdp"),
            P("fsdp"),
            P("fsdp"),
        ),
        check_vma=False,
    )
```

profile of v0, /device:TPU:0, one launch (start us, length us, event | category | flops | bytes accessed | tf_op | source)
XLA Modules:
  0.0 946.1 jit_solution(17632911012862228820)
XLA Ops:
  20.4 39.5 %all-reduce.22 = (bf16[768]{0:T(1024)(128)(2,1)S(1)}, bf16[768]{0:T(1024)(128)(2,1)S(1)}, bf16[768]{0:T(1024)(128)(2,1)S(1)}, bf16[768]{0:T(1024)(128)(2,1)S(1)}...) all-reduce(bf16[768]{0:T(1024)(128)(2,1)S(1)} %dynamic-update-slice, ...), channel_id=1, replica_groups=mesh['rep'=4,'fsdp'=8] {'fsdp'}, use_global_device_ids=true, to_apply=%add.1 | all-reduce | flops 7680 | bytes 30720
  62.1 25.9 %all-gather = bf16[8,1,384]{2,1,0:T(2,128)(2,1)S(1)} all-gather(bf16[1,1,384]{2,1,0:T(2,128)(2,1)S(1)} %reshape.220), channel_id=1, replica_groups=mesh['rep'=4,'fsdp'=8] {'fsdp'}, dimensions={0}, use_global_device_ids=true | all-gather | bytes 6912 | tf_op jit(solution)/shard_map/all_gather | solution.py:111
  88.7 2.7 convert_reduce_fusion.1
  94.4 6.0 add_convert_fusion.1
  101.9 2.6 copy.71
  104.5 3.8 reshape.177
  108.3 2.9 copy.74
  112.8 3.8 reshape.178
  120.0 3.8 reshape.179
  126.9 22.6 %while.26 = (s32[]{:T(128)}, bf16[2,512,12,64]{1,3,2,0:T(8,128)(2,1)}, f32[2,12,512,1]{2,1,3,0:T(8,128)S(1)}, bf16[2,512,12,64]{1,3,2,0:T(8,128)(2,1)}, s32[2]{0...) while((s32[]{:T(128)}, ...), condition=%wide.region_3.4_spmd, body=%wide.region_0.3_spmd.sunk | while | flops 843442688 | bytes 47427716 | solution.py:139
  128.3 3.1 fusion.127
  131.4 2.6 fusion.128
  134.1 4.2 fusion.129
  139.5 3.1 fusion.127
  142.6 2.6 fusion.128
  145.2 4.2 fusion.129
  149.6 4.2 copy.77
  155.4 4.2 fusion.87
  160.1 41.6 %all-gather.10.cloned.1.call-done = bf16[768,3072]{1,0:T(8,128)(2,1)} async-done(((bf16[96,3072]{1,0:T(8,128)(2,1)}), bf16[768,3072]{1,0:T(8,128)(2,1)}) %all-gather.10.cloned.1.call-update) | async-done | bytes 4718608 | tf_op jit(solution)/shard_map/all_gather | solution.py:110
  201.7 35.7 %multiply_convert_fusion.3 = (bf16[1024,3072]{1,0:T(8,128)(2,1)}, f32[1024,3072]{1,0:T(8,128)}, f32[1024,3072]{1,0:T(8,128)}) fusion(f32[3072]{0:T(1024)S(1)} %bitcast.204, bf16[768,3072]{1,0:T(8,128)(2,1)} %all-gather.10.cloned.1.call-done, f32[1024,768]{1,0:T(8,128)S(1)} %get-tuple-element.263, f32[768]{0:T(1024)S(1)} %convert_element_type.223, ...), kind=kOutput, calls=%fused_computation.66 | convolution fusion | flops 5043388416 | bytes 39348224 | tf_op jit(solution)/shard_map/dot_general | solution.py:150
  237.5 44.4 %all-gather.12.cloned.1.call-done = bf16[3072,768]{1,0:T(8,128)(2,1)} async-done(((bf16[384,768]{1,0:T(8,128)(2,1)}), bf16[3072,768]{1,0:T(8,128)(2,1)}) %all-gather.12.cloned.1.call-update) | async-done | bytes 4718608 | tf_op jit(solution)/shard_map/all_gather | solution.py:112
  281.8 9.2 fusion.88
  294.3 3.5 convert_reduce_fusion.2
  297.8 19.4 %convert_reduce_fusion = (f32[3072]{0:T(1024)}, bf16[1024,3072]{1,0:T(8,128)(2,1)}) fusion(f32[1024,3072]{1,0:T(8,128)} %get-tuple-element.250, bf16[3072,768]{1,0:T(8,128)(2,1)} %all-gather.12.cloned.1.call-done, f32[1024,768]{1,0:T(8,128)} %get-tuple-element.246, f32[1024,3072]{1,0:T(8,128)} %get-tuple-element.264, f32[3072]{0:T(1024)S(1)} %bitcast.205), kind=kOutput, calls=%fused_computation.64 | convolution fusion | flops 4886098944 | bytes 39346176 | tf_op jit(solution)/shard_map/dot_general | solution.py:36
  317.1 10.6 %multiply_reduce_fusion.3 = (f32[768]{0:T(1024)}, f32[1024]{0:T(1024)S(1)}, f32[1024]{0:T(1024)S(1)}, f32[768]{0:T(1024)}, f32[1024,768]{1,0:T(8,128)S(1)}) fusion(f32[1024,768]{1,0:T(8,128)S(1)} %get-tuple-element.263, f32[1024]{0:T(1024)S(1)} %add_rsqrt_fusion.1, f32[1024]{0:T(1024)S(1)} %broadcast_multiply_fusion.4, f32[768]{0:T(1024)S(1)} %convert_element_type.222, ...), kind=kOutput, calls=%fused_computation.97 | convolution fusion | flops 4839698432 | bytes 20472832 | tf_op jit(solution)/shard_map/dot_general | solution.py:36
  331.1 2.9 fusion.73
  334.0 3.3 convolution_convert_fusion
  345.0 52.1 %while.27 = (s32[]{:T(128)}, bf16[2,512,12,64]{1,3,2,0:T(8,128)(2,1)}, bf16[2,512,12,64]{1,3,2,0:T(8,128)(2,1)}, bf16[2,512,12,64]{1,3,2,0:T(8,128)(2,1)}, bf16[...) while((s32[]{:T(128)}, ...), condition=%wide.region_14.15_spmd, body=%wide.region_12.14_spmd.sunk | while | flops 2062412288 | bytes 140180784 | solution.py:207
  348.1 7.3 multiply_reduce_fusion.9
  355.4 7.4 multiply_convert_fusion.5
  367.2 3.8 fusion.141
  374.1 7.3 multiply_reduce_fusion.9
  381.4 7.3 multiply_convert_fusion.5
  393.1 3.8 fusion.141
  397.1 3.1 copy.83
  407.3 6.0 fusion.89
  415.2 10.2 %fusion.76 = f32[3072,768]{1,0:T(8,128)} fusion(bf16[1024,3072]{1,0:T(8,128)(2,1)} %get-tuple-element.249, f32[1024,768]{1,0:T(8,128)S(1)} %copy-done.18), kind=kOutput, calls=%fused_computation.145 | convolution fusion | flops 4832624640 | bytes 18874368 | tf_op jit(solution)/shard_map/dot_general | solution.py:30
  427.4 10.9 %fusion.79 = f32[768,3072]{1,0:T(8,128)} fusion(bf16[1024,3072]{1,0:T(8,128)(2,1)} %get-tuple-element.270, f32[1024,768]{1,0:T(8,128)S(1)} %copy-done.5, f32[768]{0:T(1024)S(1)} %copy-done.39, f32[768]{0:T(1024)S(1)} %copy-done.35, f32[1024]{0:T(1024)S(1)} %copy-done.32, f32[1024]{0:T(1024)S(1)} %copy-done.30), kind=kOutput, calls=%fused_computation.148 | convolution fusion | flops 4835770368 | bytes 18888704 | tf_op jit(solution)/shard_map/dot_general | solution.py:30
  442.2 98.5 %reduce-scatter.5.cloned.1.call-done = f32[96,2304]{1,0:T(8,128)} async-done(((f32[768,2304]{1,0:T(8,128)}), f32[96,2304]{1,0:T(8,128)}) %reduce-scatter.5.cloned.1.call-update) | async-done | bytes 884752 | tf_op jit(solution)/shard_map/reduce_scatter | solution.py:225
  542.7 164.6 %reduce-scatter.11.cloned.1.call-done = f32[384,768]{1,0:T(8,128)} async-done(((f32[3072,768]{1,0:T(8,128)}), f32[384,768]{1,0:T(8,128)}) %reduce-scatter.11.cloned.1.call-update) | async-done | bytes 1179664 | tf_op jit(solution)/shard_map/reduce_scatter | solution.py:196
  707.3 2.1 convert_element_type.263
  709.4 164.5 %reduce-scatter.9.cloned.1.call-done = f32[96,3072]{1,0:T(8,128)} async-done(((f32[768,3072]{1,0:T(8,128)}), f32[96,3072]{1,0:T(8,128)}) %reduce-scatter.9.cloned.1.call-update) | async-done | bytes 1179664 | tf_op jit(solution)/shard_map/reduce_scatter | solution.py:194
  873.9 2.2 convert_element_type.258
  876.2 8.8 multiply_reduce_fusion.1
  885.0 35.7 %all-reduce.21 = (bf16[768]{0:T(1024)(128)(2,1)S(1)}, bf16[768]{0:T(1024)(128)(2,1)S(1)}, bf16[768]{0:T(1024)(128)(2,1)S(1)}, bf16[768]{0:T(1024)(128)(2,1)S(1)}...) all-reduce(f32[768]{0:T(1024)S(1)} %reduce_sum.202, ...), channel_id=3, replica_groups=mesh['rep'=4,'fsdp'=8] {'fsdp'}, use_global_device_ids=true, to_apply=%region_18.19.clone | all-reduce | flops 10752 | bytes 64512
  921.5 5.7 all-reduce.23
  933.0 2.2 convert_element_type.259
  935.2 2.2 convert_element_type.264
  (272 shorter events, 84.5 us)
Async XLA Ops:
  7.2 85.4 %copy-start.21 = (bf16[2,512,768]{2,1,0:T(8,128)(2,1)S(1)}, bf16[2,512,768]{2,1,0:T(8,128)(2,1)}, u32[]{:S(2)}) copy-start(bf16[2,512,768]{2,1,0:T(8,128)(2,1)} %param.24) | copy-start | bytes 4718596
  7.2 86.1 %all-gather.6.cloned.1.call-start = ((), (), s32[]{:S(2)}) async-start(), calls=%async_computation.4 | async-start | bytes 3981312 | tf_op jit(solution)/shard_map/all_gather | solution.py:99
  7.9 147.4 %all-gather.8.cloned.1.call-start = ((), (), s32[]{:S(2)}) async-start(), calls=%async_computation.5 | async-start | bytes 1327104 | tf_op jit(solution)/shard_map/all_gather | solution.py:102
  8.7 193.1 %all-gather.10.cloned.1.call-start = ((), (), s32[]{:S(2)}) async-start(), calls=%async_computation.6 | async-start | bytes 5308416 | tf_op jit(solution)/shard_map/all_gather | solution.py:110
  9.4 272.4 %all-gather.12.cloned.1.call-start = ((), (), s32[]{:S(2)}) async-start(), calls=%async_computation.7 | async-start | bytes 5308416 | tf_op jit(solution)/shard_map/all_gather | solution.py:112
  10.0 430.6 %reduce-scatter.7.cloned.1.call-start = ((), (), s32[]{:S(2)}) async-start(), calls=%async_computation.9 | async-start | bytes 2654208 | tf_op jit(solution)/shard_map/reduce_scatter | solution.py:228
  60.7 94.7 %copy-start.43 = (f32[1,4,2,128]{3,1,2,0:T(4,128)}, f32[1,4,2,128]{3,1,2,0:T(4,128)S(1)}, u32[]{:S(2)}) copy-start(f32[1,4,2,128]{3,1,2,0:T(4,128)S(1)} %copy.90) | copy-start | bytes 12292
  61.4 94.0 %copy-start.45 = (f32[1,4,2,128]{3,1,2,0:T(4,128)}, f32[1,4,2,128]{3,1,2,0:T(4,128)S(1)}, u32[]{:S(2)}) copy-start(f32[1,4,2,128]{3,1,2,0:T(4,128)S(1)} %copy.91) | copy-start | bytes 12292
  61.4 266.3 %copy-start.34 = (f32[768]{0:T(1024)}, f32[768]{0:T(1024)S(1)}, u32[]{:S(2)}) copy-start(f32[768]{0:T(1024)S(1)} %convert_element_type.222) | copy-start | bytes 9220
  61.4 220.4 %copy-start.38 = (f32[768]{0:T(1024)}, f32[768]{0:T(1024)S(1)}, u32[]{:S(2)}) copy-start(f32[768]{0:T(1024)S(1)} %convert_element_type.223) | copy-start | bytes 9220
  88.7 3.9 copy-start.36
  123.9 3.1 copy-start.55
  149.6 5.8 copy-start
  149.6 5.8 copy-start.2
  149.6 5.8 copy-start.27
  159.6 168.1 %copy-start.4 = (f32[1024,768]{1,0:T(8,128)}, f32[1024,768]{1,0:T(8,128)S(1)}, u32[]{:S(2)}) copy-start(f32[1024,768]{1,0:T(8,128)S(1)} %get-tuple-element.263) | copy-start | bytes 9437188
  159.6 168.1 %copy-start.29 = (f32[1024]{0:T(1024)}, f32[1024]{0:T(1024)S(1)}, u32[]{:S(2)}) copy-start(f32[1024]{0:T(1024)S(1)} %broadcast_multiply_fusion.4) | copy-start | bytes 12292
  160.1 167.6 %copy-start.31 = (f32[1024]{0:T(1024)}, f32[1024]{0:T(1024)S(1)}, u32[]{:S(2)}) copy-start(f32[1024]{0:T(1024)S(1)} %add_rsqrt_fusion.1) | copy-start | bytes 12292
  201.7 80.1 %copy-start.51 = (f32[768]{0:T(1024)S(1)}, f32[768]{0:T(1024)}, u32[]{:S(2)}) copy-start(f32[768]{0:T(1024)} %convert_element_type.227) | copy-start | bytes 9220
  327.7 3.4 copy-start.24
  331.1 2.9 copy-start.54
  340.9 4.0 copy-start.1
  340.9 4.0 copy-start.3
  341.0 4.0 copy-start.28
  341.0 4.0 copy-start.56
  341.0 199.7 %reduce-scatter.5.cloned.1.call-start = ((), (), s32[]{:S(2)}) async-start(), calls=%async_computation.8 | async-start | bytes 7962624 | tf_op jit(solution)/shard_map/reduce_scatter | solution.py:225
  345.0 3.1 copy-start.7
  345.0 3.1 copy-start.8
  355.4 7.4 copy-start.15
  371.0 3.1 copy-start.7
  371.0 3.1 copy-start.8
  381.4 7.3 copy-start.15
  397.1 3.6 copy-start.17
  413.3 294.0 %reduce-scatter.11.cloned.1.call-start = ((), (), s32[]{:S(2)}) async-start(), calls=%async_computation.11 | async-start | bytes 10616832 | tf_op jit(solution)/shard_map/reduce_scatter | solution.py:196
  425.5 448.4 %reduce-scatter.9.cloned.1.call-start = ((), (), s32[]{:S(2)}) async-start(), calls=%async_computation.10 | async-start | bytes 10616832 | tf_op jit(solution)/shard_map/reduce_scatter | solution.py:194
  438.3 494.7 %all-reduce.27.cloned.1.call-start = ((), (), s32[]{:S(2)}) async-start(), calls=%async_computation.12 | async-start | bytes 3538944 | tf_op jit(solution)/shard_map/psum | solution.py:236
  442.2 433.8 %copy-start.20 = (f32[1024,768]{1,0:T(8,128)S(1)}, f32[1024,768]{1,0:T(8,128)}, u32[]{:S(2)}) copy-start(f32[1024,768]{1,0:T(8,128)} %copy-done.19) | copy-start | bytes 9437188
  442.2 433.8 %copy-start.44 = (f32[1,4,2,128]{3,1,2,0:T(4,128)S(1)}, f32[1,4,2,128]{3,1,2,0:T(4,128)}, u32[]{:S(2)}) copy-start(f32[1,4,2,128]{3,1,2,0:T(4,128)} %copy-done.43) | copy-start | bytes 12292
  442.2 433.9 %copy-start.46 = (f32[1,4,2,128]{3,1,2,0:T(4,128)S(1)}, f32[1,4,2,128]{3,1,2,0:T(4,128)}, u32[]{:S(2)}) copy-start(f32[1,4,2,128]{3,1,2,0:T(4,128)} %copy-done.45) | copy-start | bytes 12292
  876.1 8.9 copy-start.42
  876.1 8.9 copy-start.47
  876.1 8.9 copy-start.48
  876.1 8.8 copy-start.49
  876.1 8.8 copy-start.50
  876.2 8.8 copy-start.52
  876.2 8.8 copy-start.53
  933.0 4.4 copy-start.26
  933.0 5.4 copy-start.33
  (25 other events, 46.5 us)
Sparse Core Ops, SparseCore 0:
  10.2 68.4 all-gather.5
  80.9 39.8 all-gather.7
  123.0 78.7 all-gather.9
  203.8 78.0 all-gather.11
  341.1 67.1 reduce-scatter.6
  413.5 127.2 reduce-scatter.4
  544.7 162.5 reduce-scatter.10
  711.3 162.5 reduce-scatter.8
  877.9 45.7 all-reduce.26
where the time goes:
time: 954 us; the launch traced here: 946 us
  waiting for transfers between devices  516 us (54%)
  matrix products  174 us (18%)
  blocking collectives  107 us (11%)
  local copies, waits for them, and re-layouts  73.9 us (8%)
  other arithmetic  56.8 us (6%)
  between operations  17.3 us (2%)
    reduce_scatter x1, waiting for transfers between devices, body(): lax.psum_scatter(cross_rows(activated, dbranch), 'fsdp', scatter_dimensio...  165 us
    reduce_scatter x1, waiting for transfers between devices, body(): lax.psum_scatter(cross_rows(normed_low, dhidden), 'fsdp', scatter_dimensi...  164 us
    reduce_scatter x1, waiting for transfers between devices, body(): lax.psum_scatter(cross_rows(embed_low, dqkv), 'fsdp', scatter_dimension=0...  98.5 us
    unnamed x2, blocking collectives  75.2 us
    all_gather x1, waiting for transfers between devices, body(): lax.all_gather(w_down, 'fsdp', axis=0, tiled=True)  44.4 us
    dot_general x4, matrix products, cross_cols(): lax.dot_general(left, right, (((1,), (1,)), ((), ())), preferred_element_...  42.1 us
    all_gather x1, waiting for transfers between devices, body(): lax.all_gather(w_in, 'fsdp', axis=0, tiled=True)  41.6 us
    dot_general x1, matrix products, body(): jnp.dot(normed_low, ffn_full[0], preferred_element_type=wide_type)  35.7 us
  transfers between devices with their start and end apart: 9, of which 5 were waited for; matrix products, arithmetic and copies ran while one was open for 24% of the time, Pallas kernels for 0%

commit v1 on v0

v1 whole, which is shorter than its diff:
```python
import functools

import jax
import jax.numpy as jnp
from jax import lax
from jax.experimental import pallas as pl
from jax.experimental.pallas import tpu as pltpu
from jax.sharding import PartitionSpec as P

HEADS = 12
AXES = ("rep", "fsdp")
EPSILON = 1e-05
TILE = 256
VMEM_BYTES = 60 * 1024 * 1024
STEEP = 0.28
TAIL = (0.11652066258099363, 0.06749752053058514, 0.2689081593014359, -0.23699088133158833, 0.38987234732742354, -0.10580781763400933)


def wiring(n_fsdp):
    n_z = n_fsdp // 2

    def pairs(move):
        out = []
        for i in range(4 * n_fsdp):
            y, c, z, x = i // (2 * n_fsdp), i // n_fsdp % 2, i % n_fsdp // 2, i % 2
            y2, c2, z2, x2 = move(y, c, z, x)
            out.append((i, ((y2 * 2 + c2) * n_z + z2) * 2 + x2))
        return out

    return {
        "core": pairs(lambda y, c, z, x: (y, 1 - c, z, x)),
        "first": pairs(lambda y, c, z, x: (1 - y, c, z, x) if c == 0 else (y, c, z, 1 - x)),
        "second": pairs(lambda y, c, z, x: (y, c, z, 1 - x) if c == 0 else (1 - y, c, z, x)),
        "z": [pairs(lambda y, c, z, x, m=m: (y, c, z ^ m, x)) for m in range(1, n_z)],
        "rep": [pairs(lambda y, c, z, x, m=m: (y ^ (m // 2), c ^ (m % 2), z, x)) for m in (1, 2, 3)],
        "fsdp_bits": [
            [(i, i ^ (1 << b)) for i in range(4 * n_fsdp)] for b in range(n_fsdp.bit_length() - 1)
        ],
        "rep_bits": [[(i, i ^ (n_fsdp << b)) for i in range(4 * n_fsdp)] for b in (0, 1)],
    }


def send(value, pairs):
    return lax.ppermute(value, AXES, pairs)


def tie(*values):
    return lax.optimization_barrier(values)


def pick(value, axis, index):
    return lax.dynamic_index_in_dim(value, index, axis, keepdims=False)


def add_low(left, right):
    return (left.astype(jnp.float32) + right.astype(jnp.float32)).astype(jnp.bfloat16)


def flip_by(value, axis, mask):
    for bit in range(value.shape[axis].bit_length() - 1):
        shape = value.shape
        cut = value.reshape(shape[:axis] + (-1, 2, 1 << bit) + shape[axis + 1 :])
        value = jnp.where(mask >> bit & 1 == 1, jnp.flip(cut, axis + 1), cut).reshape(shape)
    return value


def gather_z(piece, wires):
    return jnp.concatenate([piece] + [send(piece, pairs) for pairs in wires["z"]])


def grow(value, got):
    return jnp.concatenate([value, got])


def sides_of(half, other, at, n_z):
    rows = half.shape[0] // (4 * n_z)
    if in_blocks(rows):
        return half, other
    y, z, x = at[0], at[2], at[3]
    out = []
    for side, source in ((0, half), (1, other)):
        blocks = source.reshape(2, 2, n_z, rows, -1)
        blocks = jnp.where(at[1] ^ side == 0, blocks, blocks.swapaxes(0, 1))
        blocks = flip_by(flip_by(flip_by(blocks, 0, x), 1, y), 2, z)
        out.append(blocks.transpose(2, 0, 1, 3, 4).reshape(half.shape))
    return tuple(out)


def in_blocks(rows):
    return rows % 16 == 0


def arrival_of(slot, at, side, n_z):
    y, c, z, x = at[0], at[1] ^ side, at[2], at[3]
    by_y, by_x, by_z = slot % 2 ^ y, slot // 2 % 2 ^ x, slot // 4 ^ z
    return jnp.where(c == 0, by_x * 2 + by_y, by_y * 2 + by_x) * n_z + by_z


def sum_core(keep, got, at, n_z):
    y, c, x = at[0], at[1], at[3]
    summed = add_low(keep, got).reshape(n_z, 2, 2, -1, keep.shape[1])
    away = jnp.where(c == 0, pick(summed, 1, 1 - x), pick(summed, 2, 1 - y))
    return jnp.where(c == 0, pick(summed, 1, x), pick(summed, 2, y)), away


def sum_second(keep, got, at):
    spot = jnp.where(at[1] == 0, at[0], at[3])
    summed = add_low(keep, got)
    return pick(summed, 1, spot), pick(summed, 1, 1 - spot)


def sum_first(keep, got, at):
    summed = add_low(keep, got)
    return pick(summed, 0, at[2]), [pick(summed, 0, at[2] ^ m) for m in range(1, summed.shape[0])]


def sum_z(keep, gots):
    total = keep.astype(jnp.float32)
    for got in gots:
        total = total + got.astype(jnp.float32)
    return total.astype(jnp.bfloat16)


def blocks_of(owned, gots, at):
    quarters = jnp.stack([owned] + list(gots))
    return [
        [pick(quarters, 0, (at[0] ^ row) * 2 + (at[1] ^ col)).astype(jnp.float32) for col in (0, 1)] for row in (0, 1)
    ]


def send_all(values, wires):
    return [send(value, pairs) for value, pairs in zip(values, wires, strict=True)]


def dot(left, right):
    return lax.dot_general(left, right, (((1,), (0,)), ((), ())), preferred_element_type=jnp.float32)


def dot_cols(left, right):
    return lax.dot_general(left, right, (((1,), (1,)), ((), ())), preferred_element_type=jnp.float32)


def dot_rows(left, right):
    return lax.dot_general(left, right, (((0,), (0,)), ((), ())), preferred_element_type=jnp.float32)


def call(kernel, grid, in_specs, out_specs, out_shape, scratch=(), flops=0, prefetch=0, aliases=None, name=None):
    sizes = [s.size * s.dtype.itemsize for s in jax.tree.leaves(out_shape)]
    return pl.pallas_call(
        kernel,
        grid_spec=pltpu.PrefetchScalarGridSpec(
            num_scalar_prefetch=prefetch, grid=grid, in_specs=in_specs, out_specs=out_specs, scratch_shapes=scratch
        ),
        out_shape=out_shape,
        compiler_params=pltpu.CompilerParams(
            dimension_semantics=("arbitrary",) * len(grid), vmem_limit_bytes=VMEM_BYTES
        ),
        cost_estimate=pl.CostEstimate(flops=flops, bytes_accessed=2 * sum(sizes), transcendentals=0),
        input_output_aliases=aliases or {},
        name=name,
    )


def whole(shape):
    return pl.BlockSpec(shape, lambda i, *_: (0,) * len(shape))


def tiles(width):
    return pl.BlockSpec((TILE, width), lambda i, *_: (i, 0))


ANY = pl.BlockSpec(memory_space=pl.ANY)


def load(at_ref, sides, n_z, targets, relative=False):
    for side, ref in enumerate(sides):
        half = side if relative else jnp.bitwise_xor(at_ref[1], side)
        rows = ref.shape[0] // (4 * n_z)
        for first, cols, into, sem in targets:
            lanes = pl.ds(pl.multiple_of(half * cols, 128), cols)
            if not in_blocks(rows):
                pltpu.make_async_copy(ref.at[:, pl.ds(first, cols)], into.at[:, lanes], sem).start()
                continue
            for slot in range(4 * n_z):
                block = arrival_of(slot, at_ref, side, n_z)
                pltpu.make_async_copy(
                    ref.at[pl.ds(pl.multiple_of(block * rows, rows), rows), pl.ds(first, cols)],
                    into.at[pl.ds(slot * rows, rows), lanes],
                    sem,
                ).start()


def loaded(array, sem):
    pltpu.make_async_copy(array, array, sem).wait()


def qkv_kernel(n_z, at_ref, flag_ref, x_ref, row_ref, bias_ref, scale_ref, own_ref, other_ref, qkv_ref, low_ref, w_ref, sem):
    @pl.when(pl.program_id(0) == 0)
    def _():
        load(at_ref, (own_ref, other_ref), n_z, [(0, own_ref.shape[1], w_ref, sem)])
        loaded(w_ref, sem)

    embed_low = (x_ref[...].astype(jnp.float32) + dot_rows(flag_ref[...], row_ref[...])).astype(jnp.bfloat16)
    low_ref[...] = embed_low
    out = ((dot(embed_low, w_ref[...]) + bias_ref[...]) * scale_ref[...]).astype(jnp.bfloat16)
    cols = out.shape[1] // 2
    qkv_ref[0] = out[:, :cols]
    qkv_ref[1] = out[:, cols:]


def project(at, flags, x, rows, bias, scale, sides, n_z):
    count, width = x.shape
    cols = sides[0].shape[1]
    return call(
        functools.partial(qkv_kernel, n_z),
        (count // TILE,),
        [
            pl.BlockSpec((16, TILE), lambda i, *_: (0, i)),
            tiles(width),
            whole((16, width)),
            whole((1, 2 * cols)),
            whole((1, 2 * cols)),
            ANY,
            ANY,
        ],
        [pl.BlockSpec((2, TILE, cols), lambda i, *_: (0, i, 0)), tiles(width)],
        [jax.ShapeDtypeStruct((2, count, cols), jnp.bfloat16), jax.ShapeDtypeStruct((count, width), jnp.bfloat16)],
        [pltpu.VMEM((width, 2 * cols), jnp.bfloat16), pltpu.SemaphoreType.DMA],
        4 * count * width * cols,
        1,
        name="project",
    )(at, flags, x, rows, bias, scale, *sides)


def attend_kernel(n_pair, len_ref, q_ref, k_ref, v_ref, *refs):
    ctx_ref, inv_ref, p_ref = refs[-3:]
    length = len_ref[pl.program_id(0) // n_pair]
    query, keys, values = q_ref[...], k_ref[...], v_ref[...]
    lane = lax.broadcasted_iota(jnp.int32, query.shape, 1)
    row = lax.broadcasted_iota(jnp.int32, query.shape, 0)
    unused = jnp.where(row >= length, -1e30, 0.0).astype(jnp.bfloat16)
    zero, one = jnp.zeros_like(query), jnp.ones_like(query)
    low = lane < 64
    parts = []
    for head in (0, 1):
        mine = low if head == 0 else ~low
        spare = lane == 64 - 64 * head
        scores = dot_cols(
            jnp.where(mine, query, jnp.where(spare, one, zero)), jnp.where(mine, keys, jnp.where(spare, unused, zero))
        )
        expo = jnp.exp(scores - jnp.max(scores, axis=1, keepdims=True)).astype(jnp.bfloat16)
        p_ref[head] = expo
        parts.append(dot(expo, jnp.where(mine, values, one)))
    inv = 1.0 / pltpu.roll(jnp.where(low, parts[1], parts[0]), 64, axis=1)
    inv_ref[...] = inv
    ctx_ref[...] = (jnp.where(low, parts[0], parts[1]) * inv).astype(jnp.bfloat16)


def attend(half, lengths, qkv, before):
    docs = lengths.shape[0]
    count, cols = qkv.shape[1:]
    seq, n_pair = count // docs, cols // 384

    def part(which):
        return pl.BlockSpec((None, seq, 128), lambda i, *_: (half, i // n_pair, which * n_pair + i % n_pair))

    def out():
        return pl.BlockSpec((seq, 128), lambda i, *_: (i // n_pair, half * n_pair + i % n_pair))

    return call(
        functools.partial(attend_kernel, n_pair),
        (docs * n_pair,),
        [part(0), part(1), part(2)] + [ANY] * len(before),
        [out(), out(), pl.BlockSpec((None, None, 2, seq, seq), lambda i, *_: (half, i, 0, 0, 0))],
        [
            jax.ShapeDtypeStruct((count, 2 * cols // 3), jnp.bfloat16),
            jax.ShapeDtypeStruct((count, 2 * cols // 3), jnp.float32),
            jax.ShapeDtypeStruct((2, docs * n_pair, 2, seq, seq), jnp.bfloat16),
        ],
        flops=docs * n_pair * 2 * seq * seq * 256 * 4,
        prefetch=1,
        aliases={4 + i: i for i in range(len(before))},
        name="attend",
    )(lengths, qkv, qkv, qkv, *before)


def norm(resid):
    center = resid - jnp.mean(resid, axis=1, keepdims=True)
    inv = lax.rsqrt(jnp.mean(center * center, axis=1, keepdims=True) + EPSILON)
    return center * inv, inv


def norm_back(grad, normal, inv, gain):
    scaled = grad * gain
    return inv * (
        scaled
        - jnp.mean(scaled, axis=1, keepdims=True)
        - normal * jnp.mean(scaled * normal, axis=1, keepdims=True)
    )


def gelu_parts(u):
    expo = jnp.exp(u * u * -0.5)
    t = 1.0 / (1.0 + STEEP * jnp.abs(u))
    poly = TAIL[5]
    for coef in TAIL[4::-1]:
        poly = poly * t + coef
    tail = expo * (t * poly)
    phi = jnp.where(u >= 0, 1.0 - tail, tail)
    return phi, phi + u * (expo * 0.3989422804014327)


def sum_rows(value):
    return jnp.sum(value, axis=0, keepdims=True)


def ffn_kernel(
    n_z,
    at_ref,
    flag_ref,
    x_ref,
    ctx_ref,
    cot_ref,
    row_ref,
    b_in_ref,
    mid_own,
    mid_other,
    down_own,
    down_other,
    out_ref,
    low_ref,
    act_ref,
    dbranch_ref,
    dhidden_ref,
    dattn_ref,
    dresid_ref,
    dctx_ref,
    sums_ref,
    in_sums_ref,
    wo_ref,
    wi_ref,
    wd_ref,
    slope_ref,
    sems,
):
    first = pl.program_id(0) == 0
    width = x_ref.shape[1]
    chunks = range(0, wi_ref.shape[1], width)

    @pl.when(first)
    def _():
        sums_ref[...] = jnp.zeros_like(sums_ref)
        in_sums_ref[...] = jnp.zeros_like(in_sums_ref)
        mid = (mid_own, mid_other)
        load(at_ref, mid, n_z, [(0, width // 2, wo_ref, sems.at[0])])
        load(at_ref, mid, n_z, [(width // 2, mid_own.shape[1] - width // 2, wi_ref, sems.at[1])])
        load(at_ref, (down_own, down_other), n_z, [(0, width // 2, wd_ref, sems.at[2])])
        loaded(wo_ref, sems.at[0])
        loaded(wi_ref, sems.at[1])
        loaded(wd_ref, sems.at[2])

    rows = row_ref[...].astype(jnp.float32)
    b_out, gain1, shift1, b_down, gain2, shift2 = (rows[i : i + 1] for i in range(2, 8))
    embed = x_ref[...].astype(jnp.float32) + dot_rows(flag_ref[...], row_ref[...])
    normal1, inv1 = norm(embed + dot(ctx_ref[...], wo_ref[...]) + b_out)
    normed = normal1 * gain1 + shift1
    normed_low = normed.astype(jnp.bfloat16)
    low_ref[...] = normed_low
    branch = normed + b_down
    for at in chunks:
        cols = slice(at, at + width)
        hidden = dot(normed_low, wi_ref[:, cols]) + b_in_ref[:, cols]
        phi, slope = gelu_parts(hidden)
        slope_ref[:, cols] = slope
        activated = (hidden * phi).astype(jnp.bfloat16)
        act_ref[:, cols] = activated
        branch = branch + dot(activated, wd_ref[cols, :])
    normal2, inv2 = norm(branch)
    out_ref[...] = (normal2 * gain2 + shift2).astype(jnp.bfloat16)
    grad = cot_ref[...].astype(jnp.float32)
    dresid2 = norm_back(grad, normal2, inv2, gain2)
    dbranch = dresid2.astype(jnp.bfloat16)
    dbranch_ref[...] = dbranch
    sums_ref[0:1] += sum_rows(grad * normal2)
    sums_ref[1:2] += sum_rows(grad)
    sums_ref[2:3] += sum_rows(dbranch.astype(jnp.float32))
    dnormed = dresid2
    for at in chunks:
        cols = slice(at, at + width)
        dhidden = (dot_cols(dbranch, wd_ref[cols, :]) * slope_ref[:, cols]).astype(jnp.bfloat16)
        dhidden_ref[:, cols] = dhidden
        in_sums_ref[0:1, cols] += sum_rows(dhidden.astype(jnp.float32))
        dnormed = dnormed + dot_cols(dhidden, wi_ref[:, cols])
    dresid1 = norm_back(dnormed, normal1, inv1, gain1)
    dattn = dresid1.astype(jnp.bfloat16)
    dresid_ref[...] = dresid1
    dattn_ref[...] = dattn
    sums_ref[3:4] += sum_rows(dnormed * normal1)
    sums_ref[4:5] += sum_rows(dnormed)
    sums_ref[5:6] += sum_rows(dattn.astype(jnp.float32))
    dctx_ref[...] = dot_cols(dattn, wo_ref[...]).astype(jnp.bfloat16)


def ffn(at, flags, x, ctx, cot, rows, b_in, mid, down, n_z):
    count, width = x.shape
    ff_width = b_in.shape[1]
    low = jax.ShapeDtypeStruct((count, width), jnp.bfloat16)
    wide = jax.ShapeDtypeStruct((count, ff_width), jnp.bfloat16)
    return call(
        functools.partial(ffn_kernel, n_z),
        (count // TILE,),
        [pl.BlockSpec((16, TILE), lambda i, *_: (0, i))]
        + [tiles(width)] * 3
        + [whole((16, width)), whole((1, ff_width))]
        + [ANY] * 4,
        [tiles(width)] * 2
        + [tiles(ff_width), tiles(width), tiles(ff_width)]
        + [tiles(width)] * 3
        + [whole((8, width)), whole((8, ff_width))],
        [low, low, wide, low, wide, low, jax.ShapeDtypeStruct((count, width), jnp.float32), low]
        + [jax.ShapeDtypeStruct((8, width), jnp.float32), jax.ShapeDtypeStruct((8, ff_width), jnp.float32)],
        [
            pltpu.VMEM((width, width), jnp.bfloat16),
            pltpu.VMEM((width, ff_width), jnp.bfloat16),
            pltpu.VMEM((ff_width, width), jnp.bfloat16),
            pltpu.VMEM((TILE, ff_width), jnp.float32),
            pltpu.SemaphoreType.DMA((3,)),
        ],
        4 * count * width * (width + 2 * ff_width),
        1,
        name="ffn",
    )(at, flags, x, ctx, cot, rows, b_in, *mid, *down)


def down_grad_kernel(at_ref, a_ref, b_ref, keep_ref, give_ref):
    cols = b_ref.shape[1] // 2
    mine, theirs = at_ref[1], 1 - at_ref[1]
    right = jnp.concatenate(
        [b_ref[:, pl.ds(pl.multiple_of(half * cols, 128), cols)] for half in (mine, theirs)], axis=1
    )
    grad = dot_rows(a_ref[...], right).astype(jnp.bfloat16)
    keep_ref[...] = grad[:, :cols]
    give_ref[...] = grad[:, cols:]


def down_grad(at, left, right):
    count, width = right.shape
    rows = left.shape[1]
    return call(
        down_grad_kernel,
        (rows // width,),
        [pl.BlockSpec((count, width), lambda i, *_: (0, i)), whole((count, width))],
        [pl.BlockSpec((width, width // 2), lambda i, *_: (i, 0))] * 2,
        [jax.ShapeDtypeStruct((rows, width // 2), jnp.bfloat16)] * 2,
        flops=2 * count * width * rows,
        prefetch=1,
        name="down_grad",
    )(at, left, right)


def in_grad_kernel(at_ref, a_ref, b_ref, give_ref, keep_ref):
    grad = dot_rows(a_ref[...], b_ref[...]).astype(jnp.bfloat16)

    @pl.when(pl.program_id(0) < 2)
    def _():
        give_ref[...] = grad

    @pl.when(pl.program_id(0) >= 2)
    def _():
        keep_ref[...] = grad


def in_grad(at, left, right):
    count, width = left.shape
    cols = right.shape[1] // 4
    return call(
        in_grad_kernel,
        (4,),
        [
            whole((count, width)),
            pl.BlockSpec((count, cols), lambda i, at_ref: (0, jnp.where(i < 2, 1 - at_ref[1], at_ref[1]) * 2 + i % 2)),
        ],
        [
            pl.BlockSpec((width, cols), lambda i, at_ref: (0, jnp.minimum(i, 1))),
            pl.BlockSpec((width, cols), lambda i, at_ref: (0, jnp.maximum(i - 2, 0))),
        ],
        [jax.ShapeDtypeStruct((width, 2 * cols), jnp.bfloat16)] * 2,
        flops=8 * count * width * cols,
        prefetch=1,
        name="in_grad",
    )(at, left, right)


def attend_back_kernel(n_pair, half_ref, q_ref, k_ref, v_ref, ctx_ref, inv_ref, p_ref, dctx_ref, out_ref):
    pair = pl.program_id(0) % n_pair
    query, keys, values = q_ref[...], k_ref[...], v_ref[...]
    lane = lax.broadcasted_iota(jnp.int32, query.shape, 1)
    low = lane < 64
    zero, one = jnp.zeros_like(query), jnp.ones_like(query)
    dctx = (dctx_ref[...].astype(jnp.float32) * inv_ref[...]).astype(jnp.bfloat16)
    product = dctx.astype(jnp.float32) * ctx_ref[...].astype(jnp.float32)
    grads = []
    for head in (0, 1):
        mine = low if head == 0 else ~low
        spare = lane == 64 - 64 * head
        fine = lane == 65 - 64 * head
        delta = jnp.sum(jnp.where(mine, product, 0.0), axis=1, keepdims=True)
        coarse = delta.astype(jnp.bfloat16)
        rest = (delta - coarse.astype(jnp.float32)).astype(jnp.bfloat16)
        left = jnp.where(mine, dctx, jnp.where(spare, -coarse, jnp.where(fine, -rest, zero)))
        expo = p_ref[head]
        dprobs = dot_cols(left, jnp.where(mine, values, jnp.where(spare | fine, one, zero)))
        dscores = (expo.astype(jnp.float32) * dprobs).astype(jnp.bfloat16)
        grads.append((dot(dscores, keys) * 0.125, dot_rows(dscores, query), dot_rows(expo, dctx)))
    third = out_ref.shape[1] // 3
    for which in range(3):
        grad = jnp.where(low, grads[0][which], grads[1][which]).astype(jnp.bfloat16)
        out_ref[:, pl.ds(pl.multiple_of(which * third + pair * 128, 128), 128)] = grad


def attend_back(half, docs, qkv, ctx, inv, expo, dctx):
    count, cols = qkv.shape[1:]
    seq, n_pair = count // docs, cols // 384

    def part(which):
        return pl.BlockSpec((None, seq, 128), lambda i, h: (h[0], i // n_pair, which * n_pair + i % n_pair))

    one = pl.BlockSpec((seq, 128), lambda i, h: (i // n_pair, h[0] * n_pair + i % n_pair))
    return call(
        functools.partial(attend_back_kernel, n_pair),
        (docs * n_pair,),
        [part(0), part(1), part(2), one, one]
        + [pl.BlockSpec((None, None, 2, seq, seq), lambda i, h: (h[0], i, 0, 0, 0)), one],
        pl.BlockSpec((seq, cols), lambda i, h: (i // n_pair, 0)),
        jax.ShapeDtypeStruct((count, cols), jnp.bfloat16),
        flops=docs * n_pair * 2 * seq * seq * 256 * 10,
        prefetch=1,
        name="attend_back",
    )(half, qkv, qkv, qkv, ctx, inv, expo, dctx)


def attn_grad_kernel(half_ref, ctx_ref, dattn_ref, low_ref, dqkv_ref, out_ref):
    cols = dattn_ref.shape[1]
    out_ref[:, :cols] = dot_rows(ctx_ref[...], dattn_ref[...]).astype(jnp.bfloat16)
    out_ref[:, cols:] = dot_rows(low_ref[...], dqkv_ref[...]).astype(jnp.bfloat16)


def attn_grad(half, ctx, dattn, low, dqkv):
    count, width = ctx.shape
    cols = width // 2 + dqkv.shape[1]
    return call(
        attn_grad_kernel,
        (1,),
        [
            whole((count, width)),
            pl.BlockSpec((count, width // 2), lambda i, h: (0, h[0])),
            whole((count, width)),
            whole(dqkv.shape),
        ],
        whole((width, cols)),
        jax.ShapeDtypeStruct((width, cols), jnp.bfloat16),
        flops=2 * count * width * cols,
        prefetch=1,
        name="attn_grad",
    )(half, ctx, dattn, low, dqkv)


def embed_grad_kernel(n_z, at_ref, flag_ref, dresid_ref, mine_ref, theirs_ref, own_ref, other_ref, grad_ref, sums_ref, bias_ref, w_ref, sem):
    cols = own_ref.shape[1]

    @pl.when(pl.program_id(0) == 0)
    def _():
        sums_ref[...] = jnp.zeros_like(sums_ref)
        bias_ref[...] = jnp.zeros_like(bias_ref)
        load(at_ref, (own_ref, other_ref), n_z, [(0, cols, w_ref, sem)], relative=True)
        loaded(w_ref, sem)

    mine, theirs = mine_ref[...], theirs_ref[...]
    dembed = dresid_ref[...] + dot_cols(mine, w_ref[:, :cols]) + dot_cols(theirs, w_ref[:, cols:])
    coarse = dembed.astype(jnp.bfloat16)
    grad_ref[...] = coarse
    rest = (dembed - coarse.astype(jnp.float32)).astype(jnp.bfloat16)
    sums_ref[...] += dot(flag_ref[...], coarse) + dot(flag_ref[...], rest)
    bias_ref[0:1] += sum_rows(mine.astype(jnp.float32))
    bias_ref[1:2] += sum_rows(theirs.astype(jnp.float32))


def embed_grad(at, flags, dresid, mine, theirs, sides, n_z):
    count, width = dresid.shape
    cols = mine.shape[1]
    return call(
        functools.partial(embed_grad_kernel, n_z),
        (count // TILE,),
        [pl.BlockSpec((16, TILE), lambda i, *_: (0, i)), tiles(width), tiles(cols), tiles(cols), ANY, ANY],
        [tiles(width), whole((16, width)), whole((8, cols))],
        [
            jax.ShapeDtypeStruct((count, width), jnp.bfloat16),
            jax.ShapeDtypeStruct((16, width), jnp.float32),
            jax.ShapeDtypeStruct((8, cols), jnp.float32),
        ],
        [pltpu.VMEM((width, 2 * cols), jnp.bfloat16), pltpu.SemaphoreType.DMA],
        4 * count * width * cols,
        1,
        name="embed_grad",
    )(at, flags, dresid, mine, theirs, *sides)


def body(
    layer_input,
    masked,
    replaced,
    lengths,
    w_qkv,
    b_q,
    b_v,
    w_out,
    b_out,
    gain1,
    shift1,
    mask_vec,
    repl_vec,
    w_in,
    b_in,
    w_down,
    b_down,
    gain2,
    shift2,
    cotangent,
):
    doc_count, seq_len, width = layer_input.shape
    tok_count = doc_count * seq_len
    n_fsdp = lax.axis_size("fsdp")
    n_z = n_fsdp // 2
    wires = wiring(n_fsdp)
    rep, own = lax.axis_index("rep"), lax.axis_index("fsdp")
    at = jnp.stack([rep // 2, rep % 2, own // 2, own % 2]).astype(jnp.int32)
    y, c = at[0], at[1]
    ff_width = w_in.shape[1]
    split = width // 2
    step = width // n_fsdp

    def quarter(weight):
        rows, cols = weight.shape[0] // 2, weight.shape[1] // 2
        return lax.dynamic_slice(weight, (y * rows, c * cols), (rows, cols))

    vectors = (mask_vec, repl_vec, b_out, gain1, shift1, b_down, gain2, shift2, b_q, b_v, b_in)
    packed = jnp.concatenate(vectors)[None]
    for pairs in wires["fsdp_bits"]:
        packed = jnp.concatenate([packed, send(packed, pairs)])
    packed = flip_by(packed, 0, own)
    rows = packed[:, : 10 * step].reshape(n_fsdp, 10, step).transpose(1, 0, 2).reshape(10, width)
    b_in = packed[:, 10 * step :].reshape(1, ff_width).astype(jnp.float32)
    b_qv = rows[8:].astype(jnp.float32)
    bias = jnp.concatenate(
        [piece for h in (0, split) for piece in (b_qv[0, h : h + split], jnp.zeros((split,)), b_qv[1, h : h + split])]
    )[None]
    scale = jnp.where(jnp.arange(6 * split) // split % 3 == 0, (width // HEADS) ** -0.5, 1.0).astype(jnp.float32)[None]
    rows = jnp.concatenate([rows, jnp.zeros((6, width), rows.dtype)])
    first_attn = jnp.concatenate([quarter(w_qkv[:, i * width : (i + 1) * width]) for i in range(3)], axis=1)
    first_mid = jnp.concatenate([quarter(w_out), quarter(w_in)], axis=1)
    first_down = quarter(w_down)

    flags = jnp.stack([masked.reshape(tok_count), replaced.reshape(tok_count)]).astype(jnp.bfloat16)
    flags = jnp.concatenate([flags, jnp.zeros((14, tok_count), jnp.bfloat16)])
    x = layer_input.reshape(tok_count, width)
    cot = cotangent.reshape(tok_count, width)
    attn = gather_z(first_attn, wires)
    first_mid, attn = tie(first_mid, attn)
    attn = grow(attn, send(attn, wires["first"]))
    mid = gather_z(first_mid, wires)
    first_down, mid = tie(first_down, mid)
    got_mid = send(mid, wires["first"])
    got_down = send_all([first_down] * (n_z - 1), wires["z"])
    attn = grow(attn, send(attn, wires["second"]))
    w_attn = sides_of(attn, send(attn, wires["core"]), at, n_z)

    qkv, embed_low = project(at, flags, x, rows, bias, scale, w_attn, n_z)
    qkv, got_mid, got_down = tie(qkv, got_mid, got_down)
    mid = grow(mid, got_mid)
    down = jnp.concatenate([first_down] + got_down)
    qkv, mid, down = tie(qkv, mid, down)
    got_mid = send(mid, wires["second"])
    got_down = send(down, wires["first"])
    part = attend(0, lengths, qkv, ())
    part, got_mid, got_down = tie(part, got_mid, got_down)
    mid = grow(mid, got_mid)
    down = grow(down, got_down)
    part, mid, down = tie(part, mid, down)
    got_mid = send(mid, wires["core"])
    got_down = send(down, wires["second"])
    ctx, inv, expo = attend(1, lengths, qkv, part)
    ctx, got_down = tie(ctx, got_down)
    down = grow(down, got_down)
    w_mid = sides_of(mid, got_mid, at, n_z)
    w_back = sides_of(down, send(down, wires["core"]), at, n_z)
    out, normed_low, activated, dbranch, dhidden, dattn, dresid1, dctx, sums, in_sums = ffn(
        at, flags, x, ctx, cot, rows, b_in, w_mid, w_back, n_z
    )

    mine, theirs = c[None], 1 - c[None]
    keep_d, give_d = down_grad(at, activated, dbranch)
    dhidden, give_d = tie(dhidden, give_d)
    got_d = send(give_d, wires["core"])
    give_i, keep_i = in_grad(at, normed_low, dhidden)
    got_d, give_i = tie(got_d, give_i)
    keep_d, give_d = sum_core(keep_d, got_d, at, n_z)
    dctx, give_d, give_i = tie(dctx, give_d, give_i)
    got_d = send(give_d, wires["second"])
    got_i = send(give_i, wires["core"])
    dqkv_theirs = attend_back(theirs, doc_count, qkv, ctx, inv, expo, dctx)
    got_d, got_i, dqkv_theirs = tie(got_d, got_i, dqkv_theirs)
    keep_d, give_d = sum_second(keep_d, got_d, at)
    keep_i, give_i = sum_core(keep_i, got_i, at, n_z)
    dqkv_theirs, give_d, give_i = tie(dqkv_theirs, give_d, give_i)
    got_d = send(give_d, wires["first"])
    got_i = send(give_i, wires["second"])
    give_a = attn_grad(theirs, ctx, dattn, embed_low, dqkv_theirs)
    dctx, give_a = tie(dctx, give_a)
    got_a = send(give_a, wires["core"])
    dqkv_mine = attend_back(mine, doc_count, qkv, ctx, inv, expo, dctx)
    got_d, got_i, dqkv_mine = tie(got_d, got_i, dqkv_mine)
    keep_d, give_d = sum_first(keep_d, got_d, at)
    keep_i, give_i = sum_second(keep_i, got_i, at)
    dqkv_mine, give_d, give_i = tie(dqkv_mine, give_d, give_i)
    got_d = send_all(give_d, wires["z"])
    got_i = send(give_i, wires["first"])
    keep_a = attn_grad(mine, ctx, dattn, embed_low, dqkv_mine)
    got_a, keep_a = tie(got_a, keep_a)
    keep_a, give_a = sum_core(keep_a, got_a, at, n_z)
    dqkv_mine, give_a = tie(dqkv_mine, give_a)
    got_a = send(give_a, wires["second"])
    grad_input, flag_sums, bias_sums = embed_grad(at, flags, dresid1, dqkv_mine, dqkv_theirs, w_attn, n_z)
    got_d, got_i, got_a, flag_sums = tie(got_d, got_i, got_a, flag_sums)
    keep_i, give_i = sum_first(keep_i, got_i, at)
    keep_a, give_a = sum_second(keep_a, got_a, at)
    got_a = send(give_a, wires["first"])
    got_i = send_all(give_i, wires["z"])
    owned_d = sum_z(keep_d, got_d)
    got_d = send_all([owned_d] * 3, wires["rep"])
    keep_a, give_a = sum_first(keep_a, got_a, at)
    got_a = send_all(give_a, wires["z"])
    owned_i = sum_z(keep_i, got_i)
    got_i = send_all([owned_i] * 3, wires["rep"])
    owned_a = sum_z(keep_a, got_a)
    got_a = send_all([owned_a] * 3, wires["rep"])
    o_down, o_in, o_attn = blocks_of(owned_d, got_d, at), blocks_of(owned_i, got_i, at), blocks_of(owned_a, got_a, at)

    halves = [jnp.where(c == h, bias_sums[0], bias_sums[1]) for h in (0, 1)]
    grad_b_q = jnp.concatenate([half[:split] for half in halves])
    grad_b_v = jnp.concatenate([half[2 * split :] for half in halves])
    small = (grad_b_q, grad_b_v, sums[5], sums[3], sums[4], flag_sums[0], flag_sums[1], sums[2], sums[0], sums[1], in_sums[0])
    packed = jnp.concatenate([value.reshape(n_fsdp, -1) for value in small], axis=1)
    for pairs in wires["rep_bits"] + wires["fsdp_bits"]:
        packed = packed + send(packed, pairs)
    packed = pick(packed, 0, own)
    o_small = [packed[i * step : (i + 1) * step] for i in range(10)]

    def join(blocks, cut=slice(None)):
        return jnp.concatenate([jnp.concatenate([block[:, cut] for block in row], axis=1) for row in blocks])

    o_qkv = jnp.concatenate([join(o_attn, slice(i * split, (i + 1) * split)) for i in (1, 2, 3)], axis=1)
    return (
        out.reshape(layer_input.shape),
        grad_input.reshape(layer_input.shape),
        o_qkv,
        o_small[0],
        o_small[1],
        join(o_attn, slice(0, split)),
        o_small[2],
        o_small[3],
        o_small[4],
        o_small[5],
        o_small[6],
        join(o_in),
        packed[10 * step :],
        join(o_down),
        o_small[7],
        o_small[8],
        o_small[9],
    )


def solution(mesh):
    return jax.shard_map(
        body,
        mesh=mesh,
        in_specs=(
            P(("rep", "fsdp"), None, None),
            P(("rep", "fsdp"), None),
            P(("rep", "fsdp"), None),
            P(("rep", "fsdp")),
            P("fsdp", None),
            P("fsdp"),
            P("fsdp"),
            P("fsdp", None),
            P("fsdp"),
            P("fsdp"),
            P("fsdp"),
            P("fsdp"),
            P("fsdp"),
            P("fsdp", None),
            P("fsdp"),
            P("fsdp", None),
            P("fsdp"),
            P("fsdp"),
            P("fsdp"),
            P(("rep", "fsdp"), None, None),
        ),
        out_specs=(
            P(("rep", "fsdp"), None, None),
            P(("rep", "fsdp"), None, None),
            P("fsdp", None),
            P("fsdp"),
            P("fsdp"),
            P("fsdp", None),
            P("fsdp"),
            P("fsdp"),
            P("fsdp"),
            P("fsdp"),
            P("fsdp"),
            P("fsdp", None),
            P("fsdp"),
            P("fsdp", None),
            P("fsdp"),
            P("fsdp"),
            P("fsdp"),
        ),
        check_vma=False,
    )
```

time: 954 us -> 372 us (0.39)
  waiting for transfers between devices: 516 us -> 74.5 us
  matrix products: 174 us -> 0 us
  Pallas kernels: 0 us -> 148 us
  blocking collectives: 107 us -> 0 us
  starting transfers between devices: 0.36 us -> 59.1 us
  local copies, waits for them, and re-layouts: 73.9 us -> 44.4 us
  other arithmetic: 56.8 us -> 36.3 us
  between operations: 17.3 us -> 1.84 us
    reduce_scatter x4 -> x0, waiting for transfers between devices: 428 us -> none  [the longest x1 165 us: body(): lax.psum_scatter(cross_rows(activated, dbranch), 'fsdp', scatter_dimensio...]
    dot_general x26 -> x0, matrix products: 174 us -> none  [the longest x4 42.1 us: cross_cols(): lax.dot_general(left, right, (((1,), (1,)), ((), ())), preferred_element_...]
    pallas_call x0 -> x11, Pallas kernels: none -> 148 us  [the longest x1 45.4 us: ffn(): call(functools.partial(ffn_kernel, n_z), (count // TILE,), [pl.BlockSpec(...]
    all_gather x4 -> x0, waiting for transfers between devices: 86 us -> none  [the longest x1 44.4 us: body(): lax.all_gather(w_down, 'fsdp', axis=0, tiled=True)]
    unnamed x2 -> x0, blocking collectives: 75.2 us -> none
    ppermute x0 -> x53, waiting for transfers between devices: none -> 74.5 us  [send(): return lax.ppermute(value, AXES, pairs)]
    ppermute x0 -> x53, starting transfers between devices: none -> 59.1 us  [send(): return lax.ppermute(value, AXES, pairs)]
    all_gather x1 -> x0, blocking collectives: 25.9 us -> none  [body(): lax.all_gather(b_in, 'fsdp', axis=0, tiled=True)]
  transfers between devices with their start and end apart: 9 -> 53, of which waited for: 5 -> 23; matrix products, arithmetic and copies ran while one was open for 24% -> 13% of each run, Pallas kernels for 0% -> 26%
where the time goes in v1:
time: 372 us; the launch traced here: 365 us
  Pallas kernels  148 us (40%)
  waiting for transfers between devices  74.5 us (20%)
  starting transfers between devices  59.1 us (16%)
  local copies, waits for them, and re-layouts  44.4 us (12%)
  other arithmetic  36.3 us (10%)
    ppermute x53, waiting for transfers between devices, send(): return lax.ppermute(value, AXES, pairs)  74.5 us
    ppermute x53, starting transfers between devices, send(): return lax.ppermute(value, AXES, pairs)  59.1 us
    pallas_call x1, Pallas kernels, ffn(): call(functools.partial(ffn_kernel, n_z), (count // TILE,), [pl.BlockSpec(...  45.4 us
    pallas_call x2, Pallas kernels, attend_back(): call(functools.partial(attend_back_kernel, n_pair), (docs * n_pair,), [pa...  24.9 us
    pallas_call x2, Pallas kernels, attend(): call(functools.partial(attend_kernel, n_pair), (docs * n_pair,), [part(0)...  21.5 us
    convert_element_type x9, other arithmetic, add_low(): (left.astype(jnp.float32) + right.astype(jnp.float32)).astype(jnp.bfloat16)  15.5 us
    pallas_call x2, Pallas kernels, attn_grad(): call(attn_grad_kernel, (1,), [whole((count, width)), pl.BlockSpec((count,...  14.6 us
    pallas_call x1, Pallas kernels, embed_grad(): call(functools.partial(embed_grad_kernel, n_z), (count // TILE,), [pl.Blo...  11.3 us
  transfers between devices with their start and end apart: 53, of which 23 were waited for; matrix products, arithmetic and copies ran while one was open for 13% of the time, Pallas kernels for 26%

profile of v1, /device:TPU:0, one launch (start us, length us, event | category | flops | bytes accessed | tf_op | source)
XLA Modules:
  0.0 364.6 jit_solution(628024749466935454)
XLA Ops:
  1.9 3.1 collective-permute-start.3
  5.0 2.6 collective-permute-start.4
  7.6 7.4 %concatenate.136 = bf16[1344]{0:T(1024)(128)(2,1)S(1)} concatenate(bf16[96]{0:T(256)(128)(2,1)} %param.31, bf16[96]{0:T(256)(128)(2,1)} %param.32, bf16[96]{0:T(256)(128)(2,1)} %param.28, bf16[96]{0:T(256)(128)(2,1)} %param.29, bf16[96]{0:T(256)(128)(2,1)} %param.30, bf16[96]{0:T(256)(128)(2,1)} %param.36, bf16[96]{0:T(256)(128)(2,1)} %param.37, bf16[96]{0:T(256)(128)(2,1)} %param.38, ...), dimensions={0} | concatenate | bytes 5376 | tf_op jit(solution)/shard_map/concatenate | solution.py:647
  15.0 1.8 collective-permute-start
  23.6 2.3 collective-permute-start.2
  31.4 10.8 %collective-permute-done.7 = bf16[384,1152]{1,0:T(8,128)(2,1)S(1)} collective-permute-done((bf16[384,1152]{1,0:T(8,128)(2,1)S(1)}, bf16[384,1152]{1,0:T(8,128)(2,1)S(1)}, u32[]{:S(2)}, u32[]{:S(2)}) %collective-permute-start.7) | collective-permute-done | bytes 884768 | tf_op jit(solution)/shard_map/ppermute | solution.py:44
  43.7 3.6 collective-permute-start.10
  47.9 12.6 %collective-permute-done.10 = bf16[48,1920]{1,0:T(8,128)(2,1)S(1)} collective-permute-done((bf16[48,1920]{1,0:T(8,128)(2,1)S(1)}, bf16[48,1920]{1,0:T(8,128)(2,1)S(1)}, u32[]{:S(2)}, u32[]{:S(2)}) %collective-permute-start.10) | collective-permute-done | bytes 184352 | tf_op jit(solution)/shard_map/ppermute | solution.py:44
  64.8 3.1 collective-permute-start.13
  70.4 10.1 %project.1 = (bf16[2,1024,1152]{2,1,0:T(8,128)(2,1)}, bf16[1024,768]{1,0:T(8,128)(2,1)}) custom-call(s32[4]{0:T(128)} %pad_add_fusion.at_ref, bf16[16,1024]{1,0:T(8,128)(2,1)} %fusion.14.flag_ref, bf16[1024,768]{1,0:T(8,128)(2,1)} %bitcast.194, bf16[16,768]{1,0:T(8,128)(2,1)} %concatenate.140.row_ref, f32[1,2304]{1,0:T(1,128)} %broadcast_in_dim.18.bias_ref, ...), custom_call_target="tpu_custom_call" | custom-call | flops 3623878656 | bytes 12582912 | tf_op jit(solution)/shard_map/project/pallas_call | solution.py:214
  83.1 10.7 %attend.2 = (bf16[1024,768]{1,0:T(8,128)(2,1)}, f32[1024,768]{1,0:T(8,128)}, bf16[2,6,2,512,512]{4,3,2,1,0:T(8,128)(2,1)}) custom-call(s32[2]{0:T(128)} %len_ref.3, bf16[2,1024,1152]{2,1,0:T(8,128)(2,1)} %get-tuple-element.109.q_ref.k_ref.v_ref, bf16[2,1024,1152]{2,1,0:T(8,128)(2,1)} %get-tuple-element.109.q_ref.k_ref.v_ref, ...), custom_call_target="tpu_custom_call" | custom-call | flops 3221225472 | bytes 34603008 | tf_op jit(solution)/shard_map/attend/pallas_call | solution.py:270
  93.8 5.0 %collective-permute-done.17 = bf16[768,384]{1,0:T(8,128)(2,1)} collective-permute-done((bf16[768,384]{1,0:T(8,128)(2,1)S(1)}, bf16[768,384]{1,0:T(8,128)(2,1)}, u32[]{:S(2)}, u32[]{:S(2)}) %collective-permute-start.17) | collective-permute-done | bytes 589856 | tf_op jit(solution)/shard_map/ppermute | solution.py:44
  98.8 6.3 %collective-permute-done.16 = bf16[384,1920]{1,0:T(8,128)(2,1)S(1)} collective-permute-done((bf16[384,1920]{1,0:T(8,128)(2,1)S(1)}, bf16[384,1920]{1,0:T(8,128)(2,1)S(1)}, u32[]{:S(2)}, u32[]{:S(2)}) %collective-permute-start.16) | collective-permute-done | bytes 1474592 | tf_op jit(solution)/shard_map/ppermute | solution.py:44
  107.8 1.8 pad_maximum_fusion.mid_own
  109.6 1.7 collective-permute-start.18
  112.5 10.8 %attend.3 = (bf16[1024,768]{1,0:T(8,128)(2,1)}, f32[1024,768]{1,0:T(8,128)}, bf16[2,6,2,512,512]{4,3,2,1,0:T(8,128)(2,1)}) custom-call(s32[2]{0:T(128)} %len_ref.3, bf16[2,1024,1152]{2,1,0:T(8,128)(2,1)} %get-tuple-element.109.q_ref.k_ref.v_ref, ...), custom_call_target="tpu_custom_call", output_to_operand_aliasing={{0}: (4, {}), {1}: (5, {}), {2}: (6, {})} | custom-call | flops 3221225472 | bytes 34603008 | tf_op jit(solution)/shard_map/attend/pallas_call | solution.py:270
  123.3 2.6 collective-permute-done.18
  127.6 4.0 %collective-permute-done.20.down_other = bf16[3072,384]{1,0:T(8,128)(2,1)S(1)} collective-permute-done((bf16[3072,384]{1,0:T(8,128)(2,1)}, bf16[3072,384]{1,0:T(8,128)(2,1)S(1)}, u32[]{:S(2)}, u32[]{:S(2)}) %collective-permute-start.20) | collective-permute-done | bytes 2359328 | tf_op jit(solution)/shard_map/ppermute | solution.py:44
  133.1 45.4 %ffn.1 = (bf16[1024,768]{1,0:T(8,128)(2,1)}, bf16[1024,768]{1,0:T(8,128)(2,1)}, bf16[1024,3072]{1,0:T(8,128)(2,1)}, bf16[1024,768]{1,0:T(8,128)(2,1)}, bf16[1024...) custom-call(s32[4]{0:T(128)} %pad_add_fusion.at_ref, ...), custom_call_target="tpu_custom_call" | custom-call | flops 21743271936 | bytes 47431680 | tf_op jit(solution)/shard_map/ffn/pallas_call | solution.py:409
  178.5 9.9 %down_grad.1 = (bf16[3072,384]{1,0:T(8,128)(2,1)}, bf16[3072,384]{1,0:T(8,128)(2,1)}) custom-call(s32[4]{0:T(128)} %pad_add_fusion.at_ref, bf16[1024,3072]{1,0:T(8,128)(2,1)} %get-tuple-element.131.a_ref, bf16[1024,768]{1,0:T(8,128)(2,1)} %get-tuple-element.132.b_ref), custom_call_target="tpu_custom_call" | custom-call | flops 4831838208 | bytes 9437184 | tf_op jit(solution)/shard_map/down_grad/pallas_call | solution.py:449
  188.5 10.8 %in_grad.1 = (bf16[768,1536]{1,0:T(8,128)(2,1)}, bf16[768,1536]{1,0:T(8,128)(2,1)}) custom-call(s32[4]{0:T(128)} %pad_add_fusion.at_ref, bf16[1024,768]{1,0:T(8,128)(2,1)} %get-tuple-element.137.a_ref, bf16[1024,3072]{1,0:T(8,128)(2,1)} %get-tuple-element.138.b_ref), custom_call_target="tpu_custom_call" | custom-call | flops 4831838208 | bytes 9437184 | tf_op jit(solution)/shard_map/in_grad/pallas_call | solution.py:476
  200.8 3.0 add_convert_fusion.2
  205.3 1.8 collective-permute-start.22
  207.0 12.3 %attend_back.2.dqkv_ref.theirs_ref = bf16[1024,1152]{1,0:T(8,128)(2,1)} custom-call(s32[1]{0:T(128)S(6)} %sub.36.half_ref, bf16[2,1024,1152]{2,1,0:T(8,128)(2,1)} %get-tuple-element.109.q_ref.k_ref.v_ref, bf16[2,1024,1152]{2,1,0:T(8,128)(2,1)} %get-tuple-element.109.q_ref.k_ref.v_ref, bf16[2,1024,1152]{2,1,0:T(8,128)(2,1)} %get-tuple-element.109.q_ref.k_ref.v_ref, ...), custom_call_target="tpu_custom_call" | custom-call | flops 8053063680 | bytes 4718592 | tf_op jit(solution)/shard_map/attend_back/pallas_call | solution.py:529
  219.3 2.4 collective-permute-done.22
  221.7 3.4 add_convert_fusion.1
  229.7 1.8 collective-permute-start.25
  231.4 7.3 %attn_grad.2 = bf16[768,1536]{1,0:T(8,128)(2,1)} custom-call(s32[1]{0:T(128)S(6)} %sub.36.half_ref, bf16[1024,768]{1,0:T(8,128)(2,1)} %get-tuple-element.125.ctx_ref, bf16[1024,768]{1,0:T(8,128)(2,1)} %get-tuple-element.153.dattn_ref, bf16[1024,768]{1,0:T(8,128)(2,1)} %get-tuple-element.154.low_ref, bf16[1024,1152]{1,0:T(8,128)(2,1)} %attend_back.2.dqkv_ref.theirs_ref), custom_call_target="tpu_custom_call" | custom-call | flops 2415919104 | bytes 4718592 | tf_op jit(solution)/shard_map/attn_grad/pallas_call | solution.py:551
  239.8 12.5 %attend_back.3.dqkv_ref.mine_ref = bf16[1024,1152]{1,0:T(8,128)(2,1)} custom-call(s32[1]{0:T(128)} %bitcast.1.half_ref, bf16[2,1024,1152]{2,1,0:T(8,128)(2,1)} %get-tuple-element.109.q_ref.k_ref.v_ref, bf16[2,1024,1152]{2,1,0:T(8,128)(2,1)} %get-tuple-element.109.q_ref.k_ref.v_ref, bf16[2,1024,1152]{2,1,0:T(8,128)(2,1)} %get-tuple-element.109.q_ref.k_ref.v_ref, ...), custom_call_target="tpu_custom_call" | custom-call | flops 8053063680 | bytes 4718592 | tf_op jit(solution)/shard_map/attend_back/pallas_call | solution.py:529
  257.0 7.3 %attn_grad.3 = bf16[768,1536]{1,0:T(8,128)(2,1)} custom-call(s32[1]{0:T(128)} %bitcast.1.half_ref, bf16[1024,768]{1,0:T(8,128)(2,1)} %get-tuple-element.125.ctx_ref, bf16[1024,768]{1,0:T(8,128)(2,1)} %get-tuple-element.153.dattn_ref, bf16[1024,768]{1,0:T(8,128)(2,1)} %get-tuple-element.154.low_ref, bf16[1024,1152]{1,0:T(8,128)(2,1)} %attend_back.3.dqkv_ref.mine_ref), custom_call_target="tpu_custom_call" | custom-call | flops 2415919104 | bytes 4718592 | tf_op jit(solution)/shard_map/attn_grad/pallas_call | solution.py:551
  264.3 3.0 add_convert_fusion
  275.2 3.7 %collective-permute-start.27 = (bf16[192,384]{1,0:T(8,128)(2,1)}, bf16[192,384]{1,0:T(8,128)(2,1)}, u32[]{:S(2)}, u32[]{:S(2)}) collective-permute-start(bf16[192,384]{1,0:T(8,128)(2,1)} %get-tuple-element.166), channel_id=1, source_target_pairs={{0,2},{1,3},{2,0},{3,1},{4,6},{5,7},{6,4},{7,5},{8,10},{9,11},{10,... | collective-permute-start | bytes 442376 | tf_op jit(solution)/shard_map/ppermute | solution.py:44
  279.2 2.1 collective-permute-start.29
  281.3 11.3 %embed_grad.1 = (bf16[1024,768]{1,0:T(8,128)(2,1)}, f32[16,768]{1,0:T(8,128)}, f32[8,1152]{1,0:T(8,128)}) custom-call(s32[4]{0:T(128)} %pad_add_fusion.at_ref, bf16[16,1024]{1,0:T(8,128)(2,1)} %fusion.14.flag_ref, f32[1024,768]{1,0:T(8,128)} %get-tuple-element.129.dresid_ref, bf16[1024,1152]{1,0:T(8,128)(2,1)} %attend_back.3.dqkv_ref.mine_ref, ...), custom_call_target="tpu_custom_call" | custom-call | flops 3623878656 | bytes 3317760 | tf_op jit(solution)/shard_map/embed_grad/pallas_call | solution.py:591
  302.0 1.9 fusion.5
  303.9 2.0 fusion
  311.7 2.1 collective-permute-start.46
  314.7 1.7 add_convert_fusion.3
  318.0 1.8 collective-permute-start.41
  319.8 2.3 collective-permute-done.41
  325.3 1.7 collective-permute-start.42
  332.5 4.3 %collective-permute-done.43 = f32[8,1344]{1,0:T(8,128)S(1)} collective-permute-done((f32[8,1344]{1,0:T(8,128)S(1)}, f32[8,1344]{1,0:T(8,128)S(1)}, u32[]{:S(2)}, u32[]{:S(2)}) %collective-permute-start.43) | collective-permute-done | bytes 43040 | tf_op jit(solution)/shard_map/ppermute | solution.py:44
  336.8 1.7 collective-permute-done.32
  339.0 2.0 collective-permute-start.34
  341.0 2.1 collective-permute-start.35
  345.0 6.9 %collective-permute-done.34 = bf16[48,1536]{1,0:T(8,128)(2,1)S(1)} collective-permute-done((bf16[48,1536]{1,0:T(8,128)(2,1)S(1)}, bf16[48,1536]{1,0:T(8,128)(2,1)S(1)}, u32[]{:S(2)}, u32[]{:S(2)}) %collective-permute-start.34) | collective-permute-done | bytes 147488 | tf_op jit(solution)/shard_map/ppermute | solution.py:44
  354.0 4.8 %collective-permute-done.37 = bf16[48,1536]{1,0:T(8,128)(2,1)S(1)} collective-permute-done((bf16[48,1536]{1,0:T(8,128)(2,1)S(1)}, bf16[48,1536]{1,0:T(8,128)(2,1)S(1)}, u32[]{:S(2)}, u32[]{:S(2)}) %collective-permute-start.37) | collective-permute-done | bytes 147488 | tf_op jit(solution)/shard_map/ppermute | solution.py:44
  358.8 2.3 collective-permute-done.38
  (229 shorter events, 87.1 us)
Async XLA Ops:
  1.9 18.8 %collective-permute-start.3 = (bf16[48,1152]{1,0:T(8,128)(2,1)S(1)}, bf16[48,1152]{1,0:T(8,128)(2,1)S(1)}, u32[]{:S(2)}, u32[]{:S(2)}) collective-permute-start(bf16[48,1152]{1,0:T(8,128)(2,1)S(1)} %pad_maximum_fusion.11), channel_id=1, source_target_pairs={{0,2},{1,3},{2,0},{3,1},{4,6},{5,7},{6,4},{7,5},{8,10},{9,11},{10,... | collective-permute-start | bytes 331784 | tf_op jit(solution)/shard_map/ppermute | solution.py:44
  5.0 15.7 %collective-permute-start.4 = (bf16[48,1152]{1,0:T(8,128)(2,1)S(1)}, bf16[48,1152]{1,0:T(8,128)(2,1)S(1)}, u32[]{:S(2)}, u32[]{:S(2)}) collective-permute-start(bf16[48,1152]{1,0:T(8,128)(2,1)S(1)} %pad_maximum_fusion.11), channel_id=1, source_target_pairs={{0,4},{1,5},{2,6},{3,7},{4,0},{5,1},{6,2},{7,3},{8,12},{9,13},{10,... | collective-permute-start | bytes 331784 | tf_op jit(solution)/shard_map/ppermute | solution.py:44
  7.6 13.1 %collective-permute-start.5 = (bf16[48,1152]{1,0:T(8,128)(2,1)S(1)}, bf16[48,1152]{1,0:T(8,128)(2,1)S(1)}, u32[]{:S(2)}, u32[]{:S(2)}) collective-permute-start(bf16[48,1152]{1,0:T(8,128)(2,1)S(1)} %pad_maximum_fusion.11), channel_id=1, source_target_pairs={{0,6},{1,7},{2,4},{3,5},{4,2},{5,3},{6,0},{7,1},{8,14},{9,15},{10,... | collective-permute-start | bytes 331784 | tf_op jit(solution)/shard_map/ppermute | solution.py:44
  15.0 4.9 %collective-permute-start = (bf16[1,1344]{1,0:T(2,128)(2,1)S(1)}, bf16[1,1344]{1,0:T(2,128)(2,1)S(1)}, u32[]{:S(2)}, u32[]{:S(2)}) collective-permute-start(bf16[1,1344]{1,0:T(2,128)(2,1)S(1)} %broadcast_in_dim.17), channel_id=1, source_target_pairs={{0,1},{1,0},{2,3},{3,2},{4,5},{5,4},{6,7},{7,6},{8,9},{9,8},{10,11... | collective-permute-start | bytes 8072 | tf_op jit(solution)/shard_map/ppermute | solution.py:44
  20.7 8.4 %collective-permute-start.6 = (bf16[192,1152]{1,0:T(8,128)(2,1)S(1)}, bf16[192,1152]{1,0:T(8,128)(2,1)S(1)}, u32[]{:S(2)}, u32[]{:S(2)}) collective-permute-start(bf16[192,1152]{1,0:T(8,128)(2,1)S(1)} %pad_maximum_fusion.9), channel_id=1, source_target_pairs={{0,16},{1,17},{2,18},{3,19},{4,20},{5,21},{6,22},{7,23},{8,9},{9,8... | collective-permute-start | bytes 1327112 | tf_op jit(solution)/shard_map/ppermute | solution.py:44
  29.2 13.1 %collective-permute-start.7 = (bf16[384,1152]{1,0:T(8,128)(2,1)S(1)}, bf16[384,1152]{1,0:T(8,128)(2,1)S(1)}, u32[]{:S(2)}, u32[]{:S(2)}) collective-permute-start(bf16[384,1152]{1,0:T(8,128)(2,1)S(1)} %pad_maximum_fusion.3), channel_id=1, source_target_pairs={{0,1},{1,0},{2,3},{3,2},{4,5},{5,4},{6,7},{7,6},{8,24},{9,25},{10,... | collective-permute-start | bytes 2654216 | tf_op jit(solution)/shard_map/ppermute | solution.py:44
  43.3 27.1 %collective-permute-start.8 = (bf16[768,1152]{1,0:T(8,128)(2,1)}, bf16[768,1152]{1,0:T(8,128)(2,1)}, u32[]{:S(2)}, u32[]{:S(2)}) collective-permute-start(bf16[768,1152]{1,0:T(8,128)(2,1)} %constant_dynamic-update-slice_fusion.1.own_ref), channel_id=1, source_target_pairs={{0,8},{1,9},{2,10},{3,11},{4,12},{5,13},{6,14},{7,15},{8,0},{9,1},... | collective-permute-start | bytes 5308424 | tf_op jit(solution)/shard_map/ppermute | solution.py:44
  43.7 16.8 %collective-permute-start.10 = (bf16[48,1920]{1,0:T(8,128)(2,1)S(1)}, bf16[48,1920]{1,0:T(8,128)(2,1)S(1)}, u32[]{:S(2)}, u32[]{:S(2)}) collective-permute-start(bf16[48,1920]{1,0:T(8,128)(2,1)S(1)} %pad_maximum_fusion.10), channel_id=1, source_target_pairs={{0,4},{1,5},{2,6},{3,7},{4,0},{5,1},{6,2},{7,3},{8,12},{9,13},{10,... | collective-permute-start | bytes 552968 | tf_op jit(solution)/shard_map/ppermute | solution.py:44
  47.3 13.3 %collective-permute-start.11 = (bf16[48,1920]{1,0:T(8,128)(2,1)S(1)}, bf16[48,1920]{1,0:T(8,128)(2,1)S(1)}, u32[]{:S(2)}, u32[]{:S(2)}) collective-permute-start(bf16[48,1920]{1,0:T(8,128)(2,1)S(1)} %pad_maximum_fusion.10), channel_id=1, source_target_pairs={{0,6},{1,7},{2,4},{3,5},{4,2},{5,3},{6,0},{7,1},{8,14},{9,15},{10,... | collective-permute-start | bytes 552968 | tf_op jit(solution)/shard_map/ppermute | solution.py:44
  47.5 14.4 %collective-permute-start.9 = (bf16[48,1920]{1,0:T(8,128)(2,1)S(1)}, bf16[48,1920]{1,0:T(8,128)(2,1)S(1)}, u32[]{:S(2)}, u32[]{:S(2)}) collective-permute-start(bf16[48,1920]{1,0:T(8,128)(2,1)S(1)} %pad_maximum_fusion.10), channel_id=1, source_target_pairs={{0,2},{1,3},{2,0},{3,1},{4,6},{5,7},{6,4},{7,5},{8,10},{9,11},{10,... | collective-permute-start | bytes 552968 | tf_op jit(solution)/shard_map/ppermute | solution.py:44
  61.9 18.8 %collective-permute-start.12 = (bf16[192,1920]{1,0:T(8,128)(2,1)S(1)}, bf16[192,1920]{1,0:T(8,128)(2,1)S(1)}, u32[]{:S(2)}, u32[]{:S(2)}) collective-permute-start(bf16[192,1920]{1,0:T(8,128)(2,1)S(1)} %pad_maximum_fusion.4), channel_id=1, source_target_pairs={{0,16},{1,17},{2,18},{3,19},{4,20},{5,21},{6,22},{7,23},{8,9},{9,8... | collective-permute-start | bytes 2211848 | tf_op jit(solution)/shard_map/ppermute | solution.py:44
  64.8 15.7 %collective-permute-start.13 = (bf16[192,384]{1,0:T(8,128)(2,1)S(1)}, bf16[192,384]{1,0:T(8,128)(2,1)S(1)}, u32[]{:S(2)}, u32[]{:S(2)}) collective-permute-start(bf16[192,384]{1,0:T(8,128)(2,1)S(1)} %dynamic_slice.161), channel_id=1, source_target_pairs={{0,2},{1,3},{2,0},{3,1},{4,6},{5,7},{6,4},{7,5},{8,10},{9,11},{10,... | collective-permute-start | bytes 442376 | tf_op jit(solution)/shard_map/ppermute | solution.py:44
  67.9 12.8 %collective-permute-start.14 = (bf16[192,384]{1,0:T(8,128)(2,1)S(1)}, bf16[192,384]{1,0:T(8,128)(2,1)S(1)}, u32[]{:S(2)}, u32[]{:S(2)}) collective-permute-start(bf16[192,384]{1,0:T(8,128)(2,1)S(1)} %dynamic_slice.161), channel_id=1, source_target_pairs={{0,4},{1,5},{2,6},{3,7},{4,0},{5,1},{6,2},{7,3},{8,12},{9,13},{10,... | collective-permute-start | bytes 442376 | tf_op jit(solution)/shard_map/ppermute | solution.py:44
  68.9 11.8 %collective-permute-start.15 = (bf16[192,384]{1,0:T(8,128)(2,1)S(1)}, bf16[192,384]{1,0:T(8,128)(2,1)S(1)}, u32[]{:S(2)}, u32[]{:S(2)}) collective-permute-start(bf16[192,384]{1,0:T(8,128)(2,1)S(1)} %dynamic_slice.161), channel_id=1, source_target_pairs={{0,6},{1,7},{2,4},{3,5},{4,2},{5,3},{6,0},{7,1},{8,14},{9,15},{10,... | collective-permute-start | bytes 442376 | tf_op jit(solution)/shard_map/ppermute | solution.py:44
  80.9 24.2 %collective-permute-start.16 = (bf16[384,1920]{1,0:T(8,128)(2,1)S(1)}, bf16[384,1920]{1,0:T(8,128)(2,1)S(1)}, u32[]{:S(2)}, u32[]{:S(2)}) collective-permute-start(bf16[384,1920]{1,0:T(8,128)(2,1)S(1)} %pad_maximum_fusion.1), channel_id=1, source_target_pairs={{0,1},{1,0},{2,3},{3,2},{4,5},{5,4},{6,7},{7,6},{8,24},{9,25},{10,... | collective-permute-start | bytes 4423688 | tf_op jit(solution)/shard_map/ppermute | solution.py:44
  82.5 16.4 %collective-permute-start.17 = (bf16[768,384]{1,0:T(8,128)(2,1)S(1)}, bf16[768,384]{1,0:T(8,128)(2,1)}, u32[]{:S(2)}, u32[]{:S(2)}) collective-permute-start(bf16[768,384]{1,0:T(8,128)(2,1)S(1)} %pad_maximum_fusion.5), channel_id=1, source_target_pairs={{0,16},{1,17},{2,18},{3,19},{4,20},{5,21},{6,22},{7,23},{8,9},{9,8... | collective-permute-start | bytes 1769480 | tf_op jit(solution)/shard_map/ppermute | solution.py:44
  109.6 16.2 %collective-permute-start.18 = (bf16[1536,384]{1,0:T(8,128)(2,1)S(1)}, bf16[1536,384]{1,0:T(8,128)(2,1)S(1)}, u32[]{:S(2)}, u32[]{:S(2)}) collective-permute-start(bf16[1536,384]{1,0:T(8,128)(2,1)S(1)} %pad_maximum_fusion.2), channel_id=1, source_target_pairs={{0,1},{1,0},{2,3},{3,2},{4,5},{5,4},{6,7},{7,6},{8,24},{9,25},{10,... | collective-permute-start | bytes 3538952 | tf_op jit(solution)/shard_map/ppermute | solution.py:44
  111.3 16.3 %collective-permute-start.19 = (bf16[768,1920]{1,0:T(8,128)(2,1)}, bf16[768,1920]{1,0:T(8,128)(2,1)}, u32[]{:S(2)}, u32[]{:S(2)}) collective-permute-start(bf16[768,1920]{1,0:T(8,128)(2,1)} %pad_maximum_fusion.mid_own), channel_id=1, source_target_pairs={{0,8},{1,9},{2,10},{3,11},{4,12},{5,13},{6,14},{7,15},{8,0},{9,1},... | collective-permute-start | bytes 8847368 | tf_op jit(solution)/shard_map/ppermute | solution.py:44
  127.0 4.7 %collective-permute-start.20 = (bf16[3072,384]{1,0:T(8,128)(2,1)}, bf16[3072,384]{1,0:T(8,128)(2,1)S(1)}, u32[]{:S(2)}, u32[]{:S(2)}) collective-permute-start(bf16[3072,384]{1,0:T(8,128)(2,1)} %constant_dynamic-update-slice_fusion.4.down_own), channel_id=1, source_target_pairs={{0,8},{1,9},{2,10},{3,11},{4,12},{5,13},{6,14},{7,15},{8,0},{9,1},... | collective-permute-start | bytes 7077896 | tf_op jit(solution)/shard_map/ppermute | solution.py:44
  188.4 11.0 %collective-permute-start.21 = (bf16[3072,384]{1,0:T(8,128)(2,1)}, bf16[3072,384]{1,0:T(8,128)(2,1)S(1)}, u32[]{:S(2)}, u32[]{:S(2)}) collective-permute-start(bf16[3072,384]{1,0:T(8,128)(2,1)} %get-tuple-element.136), channel_id=1, source_target_pairs={{0,8},{1,9},{2,10},{3,11},{4,12},{5,13},{6,14},{7,15},{8,0},{9,1},... | collective-permute-start | bytes 7077896 | tf_op jit(solution)/shard_map/ppermute | solution.py:44
  204.9 16.8 %collective-permute-start.23 = (bf16[768,1536]{1,0:T(8,128)(2,1)}, bf16[768,1536]{1,0:T(8,128)(2,1)}, u32[]{:S(2)}, u32[]{:S(2)}) collective-permute-start(bf16[768,1536]{1,0:T(8,128)(2,1)} %get-tuple-element.143), channel_id=1, source_target_pairs={{0,8},{1,9},{2,10},{3,11},{4,12},{5,13},{6,14},{7,15},{8,0},{9,1},... | collective-permute-start | bytes 7077896 | tf_op jit(solution)/shard_map/ppermute | solution.py:44
  205.3 16.4 %collective-permute-start.22 = (bf16[4,2,192,384]{3,2,1,0:T(8,128)(2,1)}, bf16[4,2,192,384]{3,2,1,0:T(8,128)(2,1)S(1)}, u32[]{:S(2)}, u32[]{:S(2)}) collective-permute-start(bf16[4,2,192,384]{3,2,1,0:T(8,128)(2,1)} %bitcast_select_fusion.1), channel_id=1, source_target_pairs={{0,1},{1,0},{2,3},{3,2},{4,5},{5,4},{6,7},{7,6},{8,24},{9,25},{10,... | collective-permute-start | bytes 3538952 | tf_op jit(solution)/shard_map/ppermute | solution.py:44
  229.7 22.7 %collective-permute-start.25 = (bf16[4,2,48,1536]{3,2,0,1:T(8,128)(2,1)}, bf16[4,2,48,1536]{3,2,0,1:T(8,128)(2,1)S(1)}, u32[]{:S(2)}, u32[]{:S(2)}) collective-permute-start(bf16[4,2,48,1536]{3,2,0,1:T(8,128)(2,1)} %bitcast_select_fusion.5), channel_id=1, source_target_pairs={{0,1},{1,0},{2,3},{3,2},{4,5},{5,4},{6,7},{7,6},{8,24},{9,25},{10,... | collective-permute-start | bytes 3538952 | tf_op jit(solution)/shard_map/ppermute | solution.py:44
  238.8 25.6 %collective-permute-start.26 = (bf16[768,1536]{1,0:T(8,128)(2,1)}, bf16[768,1536]{1,0:T(8,128)(2,1)}, u32[]{:S(2)}, u32[]{:S(2)}) collective-permute-start(bf16[768,1536]{1,0:T(8,128)(2,1)} %attn_grad.2), channel_id=1, source_target_pairs={{0,8},{1,9},{2,10},{3,11},{4,12},{5,13},{6,14},{7,15},{8,0},{9,1},... | collective-permute-start | bytes 7077896 | tf_op jit(solution)/shard_map/ppermute | solution.py:44
  239.4 12.9 %collective-permute-start.24 = (bf16[4,192,384]{2,1,0:T(8,128)(2,1)}, bf16[4,192,384]{2,1,0:T(8,128)(2,1)}, u32[]{:S(2)}, u32[]{:S(2)}) collective-permute-start(bf16[4,192,384]{2,1,0:T(8,128)(2,1)} %dynamic-slice_bitcast_fusion.2), channel_id=1, source_target_pairs={{0,16},{1,17},{2,18},{3,19},{4,20},{5,21},{6,22},{7,23},{8,9},{9,8... | collective-permute-start | bytes 1769480 | tf_op jit(solution)/shard_map/ppermute | solution.py:44
  268.9 33.1 %collective-permute-start.31 = (bf16[4,2,48,1536]{3,2,0,1:T(8,128)(2,1)}, bf16[4,2,48,1536]{3,2,0,1:T(8,128)(2,1)}, u32[]{:S(2)}, u32[]{:S(2)}) collective-permute-start(bf16[4,2,48,1536]{3,2,0,1:T(8,128)(2,1)} %bitcast_select_fusion.3), channel_id=1, source_target_pairs={{0,1},{1,0},{2,3},{3,2},{4,5},{5,4},{6,7},{7,6},{8,24},{9,25},{10,... | collective-permute-start | bytes 3538952 | tf_op jit(solution)/shard_map/ppermute | solution.py:44
  274.0 28.1 %collective-permute-start.30 = (bf16[4,48,1536]{2,1,0:T(8,128)(2,1)}, bf16[4,48,1536]{2,1,0:T(8,128)(2,1)}, u32[]{:S(2)}, u32[]{:S(2)}) collective-permute-start(bf16[4,48,1536]{2,1,0:T(8,128)(2,1)} %dynamic-slice_bitcast_fusion.1), channel_id=1, source_target_pairs={{0,16},{1,17},{2,18},{3,19},{4,20},{5,21},{6,22},{7,23},{8,9},{9,8... | collective-permute-start | bytes 1769480 | tf_op jit(solution)/shard_map/ppermute | solution.py:44
  275.2 26.8 %collective-permute-start.27 = (bf16[192,384]{1,0:T(8,128)(2,1)}, bf16[192,384]{1,0:T(8,128)(2,1)}, u32[]{:S(2)}, u32[]{:S(2)}) collective-permute-start(bf16[192,384]{1,0:T(8,128)(2,1)} %get-tuple-element.166), channel_id=1, source_target_pairs={{0,2},{1,3},{2,0},{3,1},{4,6},{5,7},{6,4},{7,5},{8,10},{9,11},{10,... | collective-permute-start | bytes 442376 | tf_op jit(solution)/shard_map/ppermute | solution.py:44
  278.9 23.1 %collective-permute-start.28 = (bf16[192,384]{1,0:T(8,128)(2,1)}, bf16[192,384]{1,0:T(8,128)(2,1)}, u32[]{:S(2)}, u32[]{:S(2)}) collective-permute-start(bf16[192,384]{1,0:T(8,128)(2,1)} %get-tuple-element.167), channel_id=1, source_target_pairs={{0,4},{1,5},{2,6},{3,7},{4,0},{5,1},{6,2},{7,3},{8,12},{9,13},{10,... | collective-permute-start | bytes 442376 | tf_op jit(solution)/shard_map/ppermute | solution.py:44
  279.2 22.8 %collective-permute-start.29 = (bf16[192,384]{1,0:T(8,128)(2,1)}, bf16[192,384]{1,0:T(8,128)(2,1)}, u32[]{:S(2)}, u32[]{:S(2)}) collective-permute-start(bf16[192,384]{1,0:T(8,128)(2,1)} %get-tuple-element.168), channel_id=1, source_target_pairs={{0,6},{1,7},{2,4},{3,5},{4,2},{5,3},{6,0},{7,1},{8,14},{9,15},{10,... | collective-permute-start | bytes 442376 | tf_op jit(solution)/shard_map/ppermute | solution.py:44
  303.9 24.1 %collective-permute-start.50 = (bf16[192,384]{1,0:T(8,128)(2,1)}, bf16[192,384]{1,0:T(8,128)(2,1)}, u32[]{:S(2)}, u32[]{:S(2)}) collective-permute-start(bf16[192,384]{1,0:T(8,128)(2,1)} %fusion.5), channel_id=1, source_target_pairs={{0,8},{1,9},{2,10},{3,11},{4,12},{5,13},{6,14},{7,15},{8,0},{9,1},... | collective-permute-start | bytes 442376 | tf_op jit(solution)/shard_map/ppermute | solution.py:44
  307.7 6.1 %collective-permute-start.39 = (f32[8,1344]{1,0:T(8,128)S(1)}, f32[8,1344]{1,0:T(8,128)S(1)}, u32[]{:S(2)}, u32[]{:S(2)}) collective-permute-start(f32[8,1344]{1,0:T(8,128)S(1)} %concatenate.165), channel_id=1, source_target_pairs={{0,8},{1,9},{2,10},{3,11},{4,12},{5,13},{6,14},{7,15},{8,0},{9,1},... | collective-permute-start | bytes 129032 | tf_op jit(solution)/shard_map/ppermute | solution.py:44
  309.4 13.5 %collective-permute-start.44 = (bf16[48,1536]{1,0:T(8,128)(2,1)S(1)}, bf16[48,1536]{1,0:T(8,128)(2,1)S(1)}, u32[]{:S(2)}, u32[]{:S(2)}) collective-permute-start(bf16[48,1536]{1,0:T(8,128)(2,1)S(1)} %get-tuple-element.213), channel_id=1, source_target_pairs={{0,2},{1,3},{2,0},{3,1},{4,6},{5,7},{6,4},{7,5},{8,10},{9,11},{10,... | collective-permute-start | bytes 442376 | tf_op jit(solution)/shard_map/ppermute | solution.py:44
  310.6 14.0 %collective-permute-start.45 = (bf16[48,1536]{1,0:T(8,128)(2,1)S(1)}, bf16[48,1536]{1,0:T(8,128)(2,1)S(1)}, u32[]{:S(2)}, u32[]{:S(2)}) collective-permute-start(bf16[48,1536]{1,0:T(8,128)(2,1)S(1)} %get-tuple-element.215), channel_id=1, source_target_pairs={{0,4},{1,5},{2,6},{3,7},{4,0},{5,1},{6,2},{7,3},{8,12},{9,13},{10,... | collective-permute-start | bytes 442376 | tf_op jit(solution)/shard_map/ppermute | solution.py:44
  311.7 13.6 %collective-permute-start.46 = (bf16[48,1536]{1,0:T(8,128)(2,1)S(1)}, bf16[48,1536]{1,0:T(8,128)(2,1)S(1)}, u32[]{:S(2)}, u32[]{:S(2)}) collective-permute-start(bf16[48,1536]{1,0:T(8,128)(2,1)S(1)} %get-tuple-element.214), channel_id=1, source_target_pairs={{0,6},{1,7},{2,4},{3,5},{4,2},{5,3},{6,0},{7,1},{8,14},{9,15},{10,... | collective-permute-start | bytes 442376 | tf_op jit(solution)/shard_map/ppermute | solution.py:44
  322.1 6.6 %collective-permute-start.51 = (bf16[192,384]{1,0:T(8,128)(2,1)}, bf16[192,384]{1,0:T(8,128)(2,1)S(1)}, u32[]{:S(2)}, u32[]{:S(2)}) collective-permute-start(bf16[192,384]{1,0:T(8,128)(2,1)} %fusion.5), channel_id=1, source_target_pairs={{0,16},{1,17},{2,18},{3,19},{4,20},{5,21},{6,22},{7,23},{8,24},{9,... | collective-permute-start | bytes 442376 | tf_op jit(solution)/shard_map/ppermute | solution.py:44
  322.9 6.4 %collective-permute-start.52 = (bf16[192,384]{1,0:T(8,128)(2,1)}, bf16[192,384]{1,0:T(8,128)(2,1)S(1)}, u32[]{:S(2)}, u32[]{:S(2)}) collective-permute-start(bf16[192,384]{1,0:T(8,128)(2,1)} %fusion.5), channel_id=1, source_target_pairs={{0,24},{1,25},{2,26},{3,27},{4,28},{5,29},{6,30},{7,31},{8,16},{9,... | collective-permute-start | bytes 442376 | tf_op jit(solution)/shard_map/ppermute | solution.py:44
  324.5 13.9 %collective-permute-start.32 = (bf16[4,48,1536]{2,1,0:T(8,128)(2,1)S(1)}, bf16[4,48,1536]{2,1,0:T(8,128)(2,1)S(1)}, u32[]{:S(2)}, u32[]{:S(2)}) collective-permute-start(bf16[4,48,1536]{2,1,0:T(8,128)(2,1)S(1)} %dynamic-slice_bitcast_fusion), channel_id=1, source_target_pairs={{0,16},{1,17},{2,18},{3,19},{4,20},{5,21},{6,22},{7,23},{8,9},{9,8... | collective-permute-start | bytes 1769480 | tf_op jit(solution)/shard_map/ppermute | solution.py:44
  325.3 5.1 %collective-permute-start.42 = (f32[8,1344]{1,0:T(8,128)S(1)}, f32[8,1344]{1,0:T(8,128)S(1)}, u32[]{:S(2)}, u32[]{:S(2)}) collective-permute-start(f32[8,1344]{1,0:T(8,128)S(1)} %add.266), channel_id=1, source_target_pairs={{0,2},{1,3},{2,0},{3,1},{4,6},{5,7},{6,4},{7,5},{8,10},{9,11},{10,... | collective-permute-start | bytes 129032 | tf_op jit(solution)/shard_map/ppermute | solution.py:44
  328.1 25.0 %collective-permute-start.47 = (bf16[48,1536]{1,0:T(8,128)(2,1)S(1)}, bf16[48,1536]{1,0:T(8,128)(2,1)S(1)}, u32[]{:S(2)}, u32[]{:S(2)}) collective-permute-start(bf16[48,1536]{1,0:T(8,128)(2,1)S(1)} %fusion.8), channel_id=1, source_target_pairs={{0,8},{1,9},{2,10},{3,11},{4,12},{5,13},{6,14},{7,15},{8,0},{9,1},... | collective-permute-start | bytes 442376 | tf_op jit(solution)/shard_map/ppermute | solution.py:44
  328.7 25.2 %collective-permute-start.48 = (bf16[48,1536]{1,0:T(8,128)(2,1)S(1)}, bf16[48,1536]{1,0:T(8,128)(2,1)S(1)}, u32[]{:S(2)}, u32[]{:S(2)}) collective-permute-start(bf16[48,1536]{1,0:T(8,128)(2,1)S(1)} %fusion.8), channel_id=1, source_target_pairs={{0,16},{1,17},{2,18},{3,19},{4,20},{5,21},{6,22},{7,23},{8,24},{9,... | collective-permute-start | bytes 442376 | tf_op jit(solution)/shard_map/ppermute | solution.py:44
  330.5 6.3 %collective-permute-start.43 = (f32[8,1344]{1,0:T(8,128)S(1)}, f32[8,1344]{1,0:T(8,128)S(1)}, u32[]{:S(2)}, u32[]{:S(2)}) collective-permute-start(f32[8,1344]{1,0:T(8,128)S(1)} %add.267), channel_id=1, source_target_pairs={{0,4},{1,5},{2,6},{3,7},{4,0},{5,1},{6,2},{7,3},{8,12},{9,13},{10,... | collective-permute-start | bytes 129032 | tf_op jit(solution)/shard_map/ppermute | solution.py:44
  338.7 6.3 %collective-permute-start.33 = (bf16[48,1536]{1,0:T(8,128)(2,1)S(1)}, bf16[48,1536]{1,0:T(8,128)(2,1)S(1)}, u32[]{:S(2)}, u32[]{:S(2)}) collective-permute-start(bf16[48,1536]{1,0:T(8,128)(2,1)S(1)} %get-tuple-element.220), channel_id=1, source_target_pairs={{0,2},{1,3},{2,0},{3,1},{4,6},{5,7},{6,4},{7,5},{8,10},{9,11},{10,... | collective-permute-start | bytes 442376 | tf_op jit(solution)/shard_map/ppermute | solution.py:44
  339.0 12.9 %collective-permute-start.34 = (bf16[48,1536]{1,0:T(8,128)(2,1)S(1)}, bf16[48,1536]{1,0:T(8,128)(2,1)S(1)}, u32[]{:S(2)}, u32[]{:S(2)}) collective-permute-start(bf16[48,1536]{1,0:T(8,128)(2,1)S(1)} %get-tuple-element.222), channel_id=1, source_target_pairs={{0,4},{1,5},{2,6},{3,7},{4,0},{5,1},{6,2},{7,3},{8,12},{9,13},{10,... | collective-permute-start | bytes 442376 | tf_op jit(solution)/shard_map/ppermute | solution.py:44
  341.0 10.9 %collective-permute-start.35 = (bf16[48,1536]{1,0:T(8,128)(2,1)S(1)}, bf16[48,1536]{1,0:T(8,128)(2,1)S(1)}, u32[]{:S(2)}, u32[]{:S(2)}) collective-permute-start(bf16[48,1536]{1,0:T(8,128)(2,1)S(1)} %get-tuple-element.221), channel_id=1, source_target_pairs={{0,6},{1,7},{2,4},{3,5},{4,2},{5,3},{6,0},{7,1},{8,14},{9,15},{10,... | collective-permute-start | bytes 442376 | tf_op jit(solution)/shard_map/ppermute | solution.py:44
  345.0 8.9 %collective-permute-start.49 = (bf16[48,1536]{1,0:T(8,128)(2,1)S(1)}, bf16[48,1536]{1,0:T(8,128)(2,1)S(1)}, u32[]{:S(2)}, u32[]{:S(2)}) collective-permute-start(bf16[48,1536]{1,0:T(8,128)(2,1)S(1)} %fusion.8), channel_id=1, source_target_pairs={{0,24},{1,25},{2,26},{3,27},{4,28},{5,29},{6,30},{7,31},{8,16},{9,... | collective-permute-start | bytes 442376 | tf_op jit(solution)/shard_map/ppermute | solution.py:44
  352.1 6.7 %collective-permute-start.37 = (bf16[48,1536]{1,0:T(8,128)(2,1)S(1)}, bf16[48,1536]{1,0:T(8,128)(2,1)S(1)}, u32[]{:S(2)}, u32[]{:S(2)}) collective-permute-start(bf16[48,1536]{1,0:T(8,128)(2,1)S(1)} %fusion.11), channel_id=1, source_target_pairs={{0,16},{1,17},{2,18},{3,19},{4,20},{5,21},{6,22},{7,23},{8,24},{9,... | collective-permute-start | bytes 442376 | tf_op jit(solution)/shard_map/ppermute | solution.py:44
  353.1 7.9 %collective-permute-start.38 = (bf16[48,1536]{1,0:T(8,128)(2,1)S(1)}, bf16[48,1536]{1,0:T(8,128)(2,1)S(1)}, u32[]{:S(2)}, u32[]{:S(2)}) collective-permute-start(bf16[48,1536]{1,0:T(8,128)(2,1)S(1)} %fusion.11), channel_id=1, source_target_pairs={{0,24},{1,25},{2,26},{3,27},{4,28},{5,29},{6,30},{7,31},{8,16},{9,... | collective-permute-start | bytes 442376 | tf_op jit(solution)/shard_map/ppermute | solution.py:44
  (23 other events, 122.0 us)

commit v2 on v1

--- a/solution.py
+++ b/solution.py
@@ -33,10 +33,7 @@
         "second": pairs(lambda y, c, z, x: (y, c, z, 1 - x) if c == 0 else (1 - y, c, z, x)),
         "z": [pairs(lambda y, c, z, x, m=m: (y, c, z ^ m, x)) for m in range(1, n_z)],
         "rep": [pairs(lambda y, c, z, x, m=m: (y ^ (m // 2), c ^ (m % 2), z, x)) for m in (1, 2, 3)],
-        "fsdp_bits": [
-            [(i, i ^ (1 << b)) for i in range(4 * n_fsdp)] for b in range(n_fsdp.bit_length() - 1)
-        ],
-        "rep_bits": [[(i, i ^ (n_fsdp << b)) for i in range(4 * n_fsdp)] for b in (0, 1)],
+        "x": pairs(lambda y, c, z, x: (y, c, z, 1 - x)),
     }
 
 
@@ -72,28 +69,22 @@
     return jnp.concatenate([value, got])
 
 
-def sides_of(half, other, at, n_z):
-    rows = half.shape[0] // (4 * n_z)
+def pieces_of(eight, got, other_eight, other_got, at, n_z):
+    rows = eight.shape[0] // (2 * n_z)
     if in_blocks(rows):
-        return half, other
+        return (eight, got), (other_eight, other_got)
     y, z, x = at[0], at[2], at[3]
     out = []
-    for side, source in ((0, half), (1, other)):
+    for side, source in ((0, grow(eight, got)), (1, grow(other_eight, other_got))):
         blocks = source.reshape(2, 2, n_z, rows, -1)
         blocks = jnp.where(at[1] ^ side == 0, blocks, blocks.swapaxes(0, 1))
         blocks = flip_by(flip_by(flip_by(blocks, 0, x), 1, y), 2, z)
-        out.append(blocks.transpose(2, 0, 1, 3, 4).reshape(half.shape))
+        out.append((blocks.transpose(2, 0, 1, 3, 4).reshape(source.shape),))
     return tuple(out)
 
 
 def in_blocks(rows):
     return rows % 16 == 0
-
-
-def arrival_of(slot, at, side, n_z):
-    y, c, z, x = at[0], at[1] ^ side, at[2], at[3]
-    by_y, by_x, by_z = slot % 2 ^ y, slot // 2 % 2 ^ x, slot // 4 ^ z
-    return jnp.where(c == 0, by_x * 2 + by_y, by_y * 2 + by_x) * n_z + by_z
 
 
 def sum_core(keep, got, at, n_z):
@@ -105,13 +96,13 @@
 
 def sum_second(keep, got, at):
     spot = jnp.where(at[1] == 0, at[0], at[3])
-    summed = add_low(keep, got)
-    return pick(summed, 1, spot), pick(summed, 1, 1 - spot)
+    return tuple(add_low(pick(keep, 1, which), pick(got, 1, which)) for which in (spot, 1 - spot))
 
 
 def sum_first(keep, got, at):
-    summed = add_low(keep, got)
-    return pick(summed, 0, at[2]), [pick(summed, 0, at[2] ^ m) for m in range(1, summed.shape[0])]
+    z = at[2]
+    sums = [add_low(pick(keep, 0, z ^ m), pick(got, 0, z ^ m)) for m in range(keep.shape[0])]
+    return sums[0], sums[1:]
 
 
 def sum_z(keep, gots):
@@ -125,6 +116,13 @@
     quarters = jnp.stack([owned] + list(gots))
     return [
         [pick(quarters, 0, (at[0] ^ row) * 2 + (at[1] ^ col)).astype(jnp.float32) for col in (0, 1)] for row in (0, 1)
+    ]
+
+
+def blocks_of_pairs(pair, got, at):
+    halves = jnp.stack([pair, got])
+    return [
+        [pick(pick(halves, 0, at[1] ^ col), 0, at[0] ^ row).astype(jnp.float32) for col in (0, 1)] for row in (0, 1)
     ]
 
 
@@ -172,64 +170,107 @@
 ANY = pl.BlockSpec(memory_space=pl.ANY)
 
 
-def load(at_ref, sides, n_z, targets, relative=False):
-    for side, ref in enumerate(sides):
-        half = side if relative else jnp.bitwise_xor(at_ref[1], side)
-        rows = ref.shape[0] // (4 * n_z)
+def load(at_ref, refs, n_z, targets, relative=False):
+    y, c, z, x = at_ref[0], at_ref[1], at_ref[2], at_ref[3]
+    per_side = len(refs) // 2
+    for side in (0, 1):
+        core = jnp.bitwise_xor(c, side)
+        half = side if relative else core
+        pieces = refs[side * per_side : (side + 1) * per_side]
+        rows = pieces[0].shape[0] // (2 * n_z)
         for first, cols, into, sem in targets:
             lanes = pl.ds(pl.multiple_of(half * cols, 128), cols)
-            if not in_blocks(rows):
-                pltpu.make_async_copy(ref.at[:, pl.ds(first, cols)], into.at[:, lanes], sem).start()
+            if per_side == 1:
+                pltpu.make_async_copy(pieces[0].at[:, pl.ds(first, cols)], into.at[:, lanes], sem).start()
                 continue
-            for slot in range(4 * n_z):
-                block = arrival_of(slot, at_ref, side, n_z)
-                pltpu.make_async_copy(
-                    ref.at[pl.ds(pl.multiple_of(block * rows, rows), rows), pl.ds(first, cols)],
-                    into.at[pl.ds(slot * rows, rows), lanes],
-                    sem,
-                ).start()
+            for late, ref in enumerate(pieces):
+                for b in (0, 1):
+                    by_x = jnp.bitwise_xor(x, jnp.where(core == 0, late, b))
+                    by_y = jnp.bitwise_xor(y, jnp.where(core == 0, b, late))
+                    for m in range(n_z):
+                        slot = (jnp.bitwise_xor(z, m) * 2 + by_x) * 2 + by_y
+                        pltpu.make_async_copy(
+                            ref.at[pl.ds((b * n_z + m) * rows, rows), pl.ds(first, cols)],
+                            into.at[pl.ds(pl.multiple_of(slot * rows, rows), rows), lanes],
+                            sem,
+                        ).start()
 
 
 def loaded(array, sem):
     pltpu.make_async_copy(array, array, sem).wait()
 
 
-def qkv_kernel(n_z, at_ref, flag_ref, x_ref, row_ref, bias_ref, scale_ref, own_ref, other_ref, qkv_ref, low_ref, w_ref, sem):
+def qkv_kernel(n_z, at_ref, flag_ref, x_ref, row_ref, bias_ref, *refs):
+    pieces, (qkv_ref, low_ref, w_ref, sem) = refs[:-4], refs[-4:]
+
     @pl.when(pl.program_id(0) == 0)
     def _():
-        load(at_ref, (own_ref, other_ref), n_z, [(0, own_ref.shape[1], w_ref, sem)])
+        load(at_ref, pieces, n_z, [(0, w_ref.shape[1] // 2, w_ref, sem)])
         loaded(w_ref, sem)
 
     embed_low = (x_ref[...].astype(jnp.float32) + dot_rows(flag_ref[...], row_ref[...])).astype(jnp.bfloat16)
     low_ref[...] = embed_low
-    out = ((dot(embed_low, w_ref[...]) + bias_ref[...]) * scale_ref[...]).astype(jnp.bfloat16)
-    cols = out.shape[1] // 2
-    qkv_ref[0] = out[:, :cols]
-    qkv_ref[1] = out[:, cols:]
-
-
-def project(at, flags, x, rows, bias, scale, sides, n_z):
+    out = dot(embed_low, w_ref[...]) + bias_ref[...]
+    third = out.shape[1] // 6
+    for half in (0, 1):
+        at = half * 3 * third
+        qkv_ref[half, :, :third] = (out[:, at : at + third] * 0.125).astype(jnp.bfloat16)
+        qkv_ref[half, :, third:] = out[:, at + third : at + 3 * third].astype(jnp.bfloat16)
+
+
+FLAGS = pl.BlockSpec((16, TILE), lambda i, *_: (0, i))
+
+
+def project(at, flags, x, rows, bias, pieces, n_z):
     count, width = x.shape
-    cols = sides[0].shape[1]
+    cols = bias.shape[1] // 2
     return call(
         functools.partial(qkv_kernel, n_z),
         (count // TILE,),
-        [
-            pl.BlockSpec((16, TILE), lambda i, *_: (0, i)),
-            tiles(width),
-            whole((16, width)),
-            whole((1, 2 * cols)),
-            whole((1, 2 * cols)),
-            ANY,
-            ANY,
-        ],
+        [FLAGS, tiles(width), whole((16, width)), whole((1, 2 * cols))] + [ANY] * len(pieces),
         [pl.BlockSpec((2, TILE, cols), lambda i, *_: (0, i, 0)), tiles(width)],
         [jax.ShapeDtypeStruct((2, count, cols), jnp.bfloat16), jax.ShapeDtypeStruct((count, width), jnp.bfloat16)],
         [pltpu.VMEM((width, 2 * cols), jnp.bfloat16), pltpu.SemaphoreType.DMA],
         4 * count * width * cols,
         1,
         name="project",
-    )(at, flags, x, rows, bias, scale, *sides)
+    )(at, flags, x, rows, bias, *pieces)
+
+
+def unpack_kernel(at_ref, packed_ref, rows_ref, bias_ref, b_in_ref):
+    n_fsdp = packed_ref.shape[0]
+    own = at_ref[2] * 2 + at_ref[3]
+    shards = [packed_ref[jnp.bitwise_xor(own, f)] for f in range(n_fsdp)]
+    rows = jnp.concatenate([shard[:16] for shard in shards], axis=1)
+    rows_ref[...] = rows.astype(jnp.bfloat16)
+    split = rows.shape[1] // 2
+    zero = jnp.zeros((1, split), jnp.float32)
+    cut = [rows[i : i + 1, at : at + split] for at in (0, split) for i in (8, 9)]
+    bias_ref[...] = jnp.concatenate([cut[0], zero, cut[1], cut[2], zero, cut[3]], axis=1)
+    b_in_ref[...] = jnp.concatenate([shard[i : i + 1] for shard in shards for i in range(10, 14)], axis=1)
+
+
+def unpack(at, packed, own):
+    n_fsdp, _, step = packed.shape
+    width = n_fsdp * step
+    if step % 32:
+        packed = flip_by(packed, 0, own)
+        rows = packed.transpose(1, 0, 2).reshape(16, width)
+        split = width // 2
+        zero = jnp.zeros((split,))
+        bias = [p for h in (0, split) for p in (rows[8, h : h + split], zero, rows[9, h : h + split])]
+        return rows.astype(jnp.bfloat16), jnp.concatenate(bias)[None], packed[:, 10:14].reshape(1, 4 * width)
+    return pl.pallas_call(
+        unpack_kernel,
+        in_specs=[pl.BlockSpec(memory_space=pltpu.SMEM), pl.BlockSpec(memory_space=pltpu.VMEM)],
+        out_specs=[pl.BlockSpec(memory_space=pltpu.VMEM)] * 3,
+        out_shape=[
+            jax.ShapeDtypeStruct((16, width), jnp.bfloat16),
+            jax.ShapeDtypeStruct((1, 3 * width), jnp.float32),
+            jax.ShapeDtypeStruct((1, 4 * width), jnp.float32),
+        ],
+        name="unpack",
+    )(at, packed)
 
 
 def attend_kernel(n_pair, len_ref, q_ref, k_ref, v_ref, *refs):
@@ -314,8 +355,21 @@
     return jnp.sum(value, axis=0, keepdims=True)
 
 
+def start_sums(*refs):
+    @pl.when(pl.program_id(0) == 0)
+    def _():
+        for ref in refs:
+            ref[...] = jnp.zeros_like(ref)
+
+
+def wide_of(rows, *indices):
+    rows = rows.astype(jnp.float32)
+    return [rows[i : i + 1] for i in indices]
+
+
 def ffn_kernel(
     n_z,
+    n_mid,
     at_ref,
     flag_ref,
     x_ref,
@@ -323,44 +377,28 @@
     cot_ref,
     row_ref,
     b_in_ref,
-    mid_own,
-    mid_other,
-    down_own,
-    down_other,
-    out_ref,
-    low_ref,
-    act_ref,
-    dbranch_ref,
-    dhidden_ref,
-    dattn_ref,
-    dresid_ref,
-    dctx_ref,
-    sums_ref,
-    in_sums_ref,
-    wo_ref,
-    wi_ref,
-    wd_ref,
-    slope_ref,
-    sems,
+    *refs,
 ):
+    mid, down = refs[:n_mid], refs[n_mid:-15]
+    out_ref, low_ref, act_ref, dbranch_ref, dhidden_ref, dattn_ref, dresid_ref, dctx_ref = refs[-15:-7]
+    sums_ref, in_sums_ref, wo_ref, wi_ref, wd_ref, slope_ref, sems = refs[-7:]
     first = pl.program_id(0) == 0
     width = x_ref.shape[1]
     chunks = range(0, wi_ref.shape[1], width)
 
+    start_sums(sums_ref, in_sums_ref)
+
     @pl.when(first)
     def _():
-        sums_ref[...] = jnp.zeros_like(sums_ref)
-        in_sums_ref[...] = jnp.zeros_like(in_sums_ref)
-        mid = (mid_own, mid_other)
-        load(at_ref, mid, n_z, [(0, width // 2, wo_ref, sems.at[0])])
-        load(at_ref, mid, n_z, [(width // 2, mid_own.shape[1] - width // 2, wi_ref, sems.at[1])])
-        load(at_ref, (down_own, down_other), n_z, [(0, width // 2, wd_ref, sems.at[2])])
+        half = wi_ref.shape[1] // 2
+        load(at_ref, mid, n_z, [(half, width // 2, wo_ref, sems.at[0])])
+        load(at_ref, mid, n_z, [(0, half, wi_ref, sems.at[1])])
+        load(at_ref, down, n_z, [(0, width // 2, wd_ref, sems.at[2])])
         loaded(wo_ref, sems.at[0])
         loaded(wi_ref, sems.at[1])
         loaded(wd_ref, sems.at[2])
 
-    rows = row_ref[...].astype(jnp.float32)
-    b_out, gain1, shift1, b_down, gain2, shift2 = (rows[i : i + 1] for i in range(2, 8))
+    b_out, gain1, shift1, b_down, gain2, shift2 = wide_of(row_ref[...], 2, 3, 4, 5, 6, 7)
     embed = x_ref[...].astype(jnp.float32) + dot_rows(flag_ref[...], row_ref[...])
     normal1, inv1 = norm(embed + dot(ctx_ref[...], wo_ref[...]) + b_out)
     normed = normal1 * gain1 + shift1
@@ -407,12 +445,12 @@
     low = jax.ShapeDtypeStruct((count, width), jnp.bfloat16)
     wide = jax.ShapeDtypeStruct((count, ff_width), jnp.bfloat16)
     return call(
-        functools.partial(ffn_kernel, n_z),
+        functools.partial(ffn_kernel, n_z, len(mid)),
         (count // TILE,),
-        [pl.BlockSpec((16, TILE), lambda i, *_: (0, i))]
+        [FLAGS]
         + [tiles(width)] * 3
         + [whole((16, width)), whole((1, ff_width))]
-        + [ANY] * 4,
+        + [ANY] * (len(mid) + len(down)),
         [tiles(width)] * 2
         + [tiles(ff_width), tiles(width), tiles(ff_width)]
         + [tiles(width)] * 3
@@ -432,63 +470,84 @@
     )(at, flags, x, ctx, cot, rows, b_in, *mid, *down)
 
 
-def down_grad_kernel(at_ref, a_ref, b_ref, keep_ref, give_ref):
-    cols = b_ref.shape[1] // 2
-    mine, theirs = at_ref[1], 1 - at_ref[1]
-    right = jnp.concatenate(
-        [b_ref[:, pl.ds(pl.multiple_of(half * cols, 128), cols)] for half in (mine, theirs)], axis=1
+def grad_kernel(n_first, first_z, by_z, at_ref, *refs):
+    *lefts, got_ref, away_ref, stay_ref, sum_ref = refs if first_z else (*refs[:-1], None, None, refs[-1], None)
+    step = pl.program_id(0)
+
+    def put(left_ref, right_ref):
+        grad = dot_rows(left_ref[...], right_ref[...])
+        lanes = slice(0, grad.shape[1])
+        if not first_z:
+            stay_ref[:, lanes] = grad.astype(jnp.bfloat16)
+            return
+        sum_ref[:, lanes] = (grad + got_ref[:, lanes].astype(jnp.float32)).astype(jnp.bfloat16)
+        y, c, x = at_ref[0], at_ref[1], at_ref[3]
+        rows = away_ref.shape[2]
+        for z in range(by_z):
+            for b in (0, 1):
+                for ref, this_x, this_y in ((away_ref, 1 - x, 1 - y), (stay_ref, x, y)):
+                    block = jnp.where(c == 0, this_x * 2 + b, b * 2 + this_y) + z * 4
+                    ref[z, b, :, lanes] = sum_ref[pl.ds(pl.multiple_of(block * rows, rows), rows), lanes]
+
+    if len(lefts) == 2:
+        put(*lefts)
+        return
+    pl.when(step < n_first)(lambda: put(lefts[0], lefts[1]))
+    pl.when(step >= n_first)(lambda: put(lefts[2], lefts[3]))
+
+
+def grads(at, half, parts, got, n_z, tile, name):
+    count, rows = parts[0][0].shape
+    width = sum(cols for _, _, cols in parts)
+    tall = rows > 2 * width
+    n_first = (rows if tall else parts[0][2]) // tile
+    steps = n_first + len(parts) - 1
+    specs, arrays = [], []
+    for left, right, cols in parts:
+        if tall:
+            specs += [pl.BlockSpec((count, tile), lambda i, *_: (0, i))]
+            specs += [pl.BlockSpec((count, cols), lambda i, at_ref: (0, at_ref[4]))]
+        else:
+            n_tile = max(cols // tile, 1)
+            start = n_tile if right.shape[1] > cols else 0
+            specs += [
+                whole((count, rows)),
+                pl.BlockSpec(
+                    (count, min(tile, cols)),
+                    lambda i, at_ref, n=n_tile, start=start: (0, at_ref[4] * start + jnp.minimum(i, n - 1)),
+                ),
+            ]
+        arrays += [left, right]
+    at = jnp.concatenate([at, half])
+    block = rows // (4 * n_z)
+    shape = (tile, width) if tall else (rows, tile)
+    spec = pl.BlockSpec(shape, (lambda i, *_: (i, 0)) if tall else (lambda i, *_: (0, i)))
+    flops = 2 * count * rows * width
+    plain = functools.partial(grad_kernel, n_first, False, 0)
+    fused = got is not None and block % 16 == 0
+    if not fused:
+        grad = call(
+            plain, (steps,), specs, spec, jax.ShapeDtypeStruct((rows, width), jnp.bfloat16), flops=flops, prefetch=1, name=name
+        )(at, *arrays)
+        if got is None:
+            return grad
+        stay, away = sum_core(grad, got, at, n_z)
+        return away, stay
+    by_z = shape[0] // (4 * block)
+    split = pl.BlockSpec(
+        (by_z, 2, block, shape[1]), (lambda i, *_: (i, 0, 0, 0)) if tall else (lambda i, *_: (0, 0, 0, i))
     )
-    grad = dot_rows(a_ref[...], right).astype(jnp.bfloat16)
-    keep_ref[...] = grad[:, :cols]
-    give_ref[...] = grad[:, cols:]
-
-
-def down_grad(at, left, right):
-    count, width = right.shape
-    rows = left.shape[1]
     return call(
-        down_grad_kernel,
-        (rows // width,),
-        [pl.BlockSpec((count, width), lambda i, *_: (0, i)), whole((count, width))],
-        [pl.BlockSpec((width, width // 2), lambda i, *_: (i, 0))] * 2,
-        [jax.ShapeDtypeStruct((rows, width // 2), jnp.bfloat16)] * 2,
-        flops=2 * count * width * rows,
+        functools.partial(grad_kernel, n_first, True, by_z),
+        (steps,),
+        specs + [spec],
+        [split] * 2,
+        [jax.ShapeDtypeStruct((n_z, 2, block, width), jnp.bfloat16)] * 2,
+        [pltpu.VMEM(shape, jnp.bfloat16)],
+        flops=flops,
         prefetch=1,
-        name="down_grad",
-    )(at, left, right)
-
-
-def in_grad_kernel(at_ref, a_ref, b_ref, give_ref, keep_ref):
-    grad = dot_rows(a_ref[...], b_ref[...]).astype(jnp.bfloat16)
-
-    @pl.when(pl.program_id(0) < 2)
-    def _():
-        give_ref[...] = grad
-
-    @pl.when(pl.program_id(0) >= 2)
-    def _():
-        keep_ref[...] = grad
-
-
-def in_grad(at, left, right):
-    count, width = left.shape
-    cols = right.shape[1] // 4
-    return call(
-        in_grad_kernel,
-        (4,),
-        [
-            whole((count, width)),
-            pl.BlockSpec((count, cols), lambda i, at_ref: (0, jnp.where(i < 2, 1 - at_ref[1], at_ref[1]) * 2 + i % 2)),
-        ],
-        [
-            pl.BlockSpec((width, cols), lambda i, at_ref: (0, jnp.minimum(i, 1))),
-            pl.BlockSpec((width, cols), lambda i, at_ref: (0, jnp.maximum(i - 2, 0))),
-        ],
-        [jax.ShapeDtypeStruct((width, 2 * cols), jnp.bfloat16)] * 2,
-        flops=8 * count * width * cols,
-        prefetch=1,
-        name="in_grad",
-    )(at, left, right)
+        name=name,
+    )(at, *arrays, got)
 
 
 def attend_back_kernel(n_pair, half_ref, q_ref, k_ref, v_ref, ctx_ref, inv_ref, p_ref, dctx_ref, out_ref):
@@ -539,40 +598,14 @@
     )(half, qkv, qkv, qkv, ctx, inv, expo, dctx)
 
 
-def attn_grad_kernel(half_ref, ctx_ref, dattn_ref, low_ref, dqkv_ref, out_ref):
-    cols = dattn_ref.shape[1]
-    out_ref[:, :cols] = dot_rows(ctx_ref[...], dattn_ref[...]).astype(jnp.bfloat16)
-    out_ref[:, cols:] = dot_rows(low_ref[...], dqkv_ref[...]).astype(jnp.bfloat16)
-
-
-def attn_grad(half, ctx, dattn, low, dqkv):
-    count, width = ctx.shape
-    cols = width // 2 + dqkv.shape[1]
-    return call(
-        attn_grad_kernel,
-        (1,),
-        [
-            whole((count, width)),
-            pl.BlockSpec((count, width // 2), lambda i, h: (0, h[0])),
-            whole((count, width)),
-            whole(dqkv.shape),
-        ],
-        whole((width, cols)),
-        jax.ShapeDtypeStruct((width, cols), jnp.bfloat16),
-        flops=2 * count * width * cols,
-        prefetch=1,
-        name="attn_grad",
-    )(half, ctx, dattn, low, dqkv)
-
-
-def embed_grad_kernel(n_z, at_ref, flag_ref, dresid_ref, mine_ref, theirs_ref, own_ref, other_ref, grad_ref, sums_ref, bias_ref, w_ref, sem):
-    cols = own_ref.shape[1]
+def embed_grad_kernel(n_z, at_ref, flag_ref, dresid_ref, mine_ref, theirs_ref, *refs):
+    pieces, (grad_ref, sums_ref, bias_ref, w_ref, sem) = refs[:-5], refs[-5:]
+    cols = mine_ref.shape[1]
+    start_sums(sums_ref, bias_ref)
 
     @pl.when(pl.program_id(0) == 0)
     def _():
-        sums_ref[...] = jnp.zeros_like(sums_ref)
-        bias_ref[...] = jnp.zeros_like(bias_ref)
-        load(at_ref, (own_ref, other_ref), n_z, [(0, cols, w_ref, sem)], relative=True)
+        load(at_ref, pieces, n_z, [(0, cols, w_ref, sem)], relative=True)
         loaded(w_ref, sem)
 
     mine, theirs = mine_ref[...], theirs_ref[...]
@@ -585,13 +618,13 @@
     bias_ref[1:2] += sum_rows(theirs.astype(jnp.float32))
 
 
-def embed_grad(at, flags, dresid, mine, theirs, sides, n_z):
+def embed_grad(at, flags, dresid, mine, theirs, pieces, n_z):
     count, width = dresid.shape
     cols = mine.shape[1]
     return call(
         functools.partial(embed_grad_kernel, n_z),
         (count // TILE,),
-        [pl.BlockSpec((16, TILE), lambda i, *_: (0, i)), tiles(width), tiles(cols), tiles(cols), ANY, ANY],
+        [FLAGS, tiles(width), tiles(cols), tiles(cols)] + [ANY] * len(pieces),
         [tiles(width), whole((16, width)), whole((8, cols))],
         [
             jax.ShapeDtypeStruct((count, width), jnp.bfloat16),
@@ -602,7 +635,37 @@
         4 * count * width * cols,
         1,
         name="embed_grad",
-    )(at, flags, dresid, mine, theirs, *sides)
+    )(at, flags, dresid, mine, theirs, *pieces)
+
+
+def pack_kernel(at_ref, sums_ref, in_ref, flag_ref, bias_ref, out_ref):
+    core = at_ref[1]
+    width = sums_ref.shape[1]
+    split = width // 2
+    bias = bias_ref[...]
+    mine, theirs = bias[0:1], bias[1:2]
+    low, high = jnp.where(core == 0, mine, theirs), jnp.where(core == 0, theirs, mine)
+    for row, cols in ((0, slice(0, split)), (1, slice(2 * split, 3 * split))):
+        out_ref[row : row + 1, :split] = low[:, cols]
+        out_ref[row : row + 1, split:] = high[:, cols]
+    for row, (ref, source) in enumerate(
+        ((sums_ref, 5), (sums_ref, 3), (sums_ref, 4), (flag_ref, 0), (flag_ref, 1), (sums_ref, 2), (sums_ref, 0), (sums_ref, 1)), 2
+    ):
+        out_ref[row : row + 1, :] = ref[source : source + 1, :]
+    out_ref[10:11, :] = jnp.zeros((1, width), jnp.float32)
+    for i in range(4):
+        out_ref[11 + i : 12 + i, :] = in_ref[0:1, i * width : (i + 1) * width]
+    out_ref[15:16, :] = jnp.zeros((1, width), jnp.float32)
+
+
+def pack(at, sums, in_sums, flag_sums, bias_sums):
+    return pl.pallas_call(
+        pack_kernel,
+        in_specs=[pl.BlockSpec(memory_space=pltpu.SMEM)] + [pl.BlockSpec(memory_space=pltpu.VMEM)] * 4,
+        out_specs=pl.BlockSpec(memory_space=pltpu.VMEM),
+        out_shape=jax.ShapeDtypeStruct((16, sums.shape[1]), jnp.float32),
+        name="pack",
+    )(at, sums, in_sums, flag_sums, bias_sums)
 
 
 def body(
@@ -643,136 +706,148 @@
         rows, cols = weight.shape[0] // 2, weight.shape[1] // 2
         return lax.dynamic_slice(weight, (y * rows, c * cols), (rows, cols))
 
-    vectors = (mask_vec, repl_vec, b_out, gain1, shift1, b_down, gain2, shift2, b_q, b_v, b_in)
-    packed = jnp.concatenate(vectors)[None]
-    for pairs in wires["fsdp_bits"]:
-        packed = jnp.concatenate([packed, send(packed, pairs)])
-    packed = flip_by(packed, 0, own)
-    rows = packed[:, : 10 * step].reshape(n_fsdp, 10, step).transpose(1, 0, 2).reshape(10, width)
-    b_in = packed[:, 10 * step :].reshape(1, ff_width).astype(jnp.float32)
-    b_qv = rows[8:].astype(jnp.float32)
-    bias = jnp.concatenate(
-        [piece for h in (0, split) for piece in (b_qv[0, h : h + split], jnp.zeros((split,)), b_qv[1, h : h + split])]
-    )[None]
-    scale = jnp.where(jnp.arange(6 * split) // split % 3 == 0, (width // HEADS) ** -0.5, 1.0).astype(jnp.float32)[None]
-    rows = jnp.concatenate([rows, jnp.zeros((6, width), rows.dtype)])
+    vectors = jnp.stack((mask_vec, repl_vec, b_out, gain1, shift1, b_down, gain2, shift2, b_q, b_v))
+    packed = jnp.concatenate([vectors, b_in.reshape(-1, step), jnp.zeros((2, step), b_in.dtype)])
+    packed = packed.astype(jnp.float32)[None]
     first_attn = jnp.concatenate([quarter(w_qkv[:, i * width : (i + 1) * width]) for i in range(3)], axis=1)
-    first_mid = jnp.concatenate([quarter(w_out), quarter(w_in)], axis=1)
+    first_mid = jnp.concatenate([quarter(w_in), quarter(w_out)], axis=1)
     first_down = quarter(w_down)
 
+    attn = gather_z(first_attn, wires)
+    attn, packed = tie(attn, packed)
+    got_attn = send(attn, wires["first"])
+    packed = gather_z(grow(packed, send(packed, wires["x"])), wires)
+    got_attn, first_mid, packed = tie(got_attn, first_mid, packed)
+    rows, bias, b_in = unpack(at, packed, own)
     flags = jnp.stack([masked.reshape(tok_count), replaced.reshape(tok_count)]).astype(jnp.bfloat16)
     flags = jnp.concatenate([flags, jnp.zeros((14, tok_count), jnp.bfloat16)])
     x = layer_input.reshape(tok_count, width)
     cot = cotangent.reshape(tok_count, width)
-    attn = gather_z(first_attn, wires)
-    first_mid, attn = tie(first_mid, attn)
-    attn = grow(attn, send(attn, wires["first"]))
+    attn = grow(attn, got_attn)
+    got_attn = send(attn, wires["second"])
     mid = gather_z(first_mid, wires)
-    first_down, mid = tie(first_down, mid)
+    mid, got_attn, first_down, rows = tie(mid, got_attn, first_down, rows)
     got_mid = send(mid, wires["first"])
+    pieces = (attn, got_attn, send(attn, wires["core"]), send(got_attn, wires["core"]))
     got_down = send_all([first_down] * (n_z - 1), wires["z"])
-    attn = grow(attn, send(attn, wires["second"]))
-    w_attn = sides_of(attn, send(attn, wires["core"]), at, n_z)
-
-    qkv, embed_low = project(at, flags, x, rows, bias, scale, w_attn, n_z)
-    qkv, got_mid, got_down = tie(qkv, got_mid, got_down)
+    got_mid, rows = tie(got_mid, rows)
     mid = grow(mid, got_mid)
+    rows, mid = tie(rows, mid)
+    got_mid = send(mid, wires["second"])
+    w_attn = sum(pieces_of(*pieces, at, n_z), ())
+
+    qkv, embed_low = project(at, flags, x, rows, bias, w_attn, n_z)
+    qkv, got_down = tie(qkv, got_down)
     down = jnp.concatenate([first_down] + got_down)
-    qkv, mid, down = tie(qkv, mid, down)
-    got_mid = send(mid, wires["second"])
+    qkv, down = tie(qkv, down)
     got_down = send(down, wires["first"])
+    other_mid = send(mid, wires["core"])
     part = attend(0, lengths, qkv, ())
-    part, got_mid, got_down = tie(part, got_mid, got_down)
-    mid = grow(mid, got_mid)
+    part, got_mid, got_down, other_mid = tie(part, got_mid, got_down, other_mid)
     down = grow(down, got_down)
-    part, mid, down = tie(part, mid, down)
-    got_mid = send(mid, wires["core"])
+    part, down = tie(part, down)
     got_down = send(down, wires["second"])
+    other_down = send(down, wires["core"])
+    w_mid = (mid, got_mid, other_mid, send(got_mid, wires["core"]))
     ctx, inv, expo = attend(1, lengths, qkv, part)
-    ctx, got_down = tie(ctx, got_down)
-    down = grow(down, got_down)
-    w_mid = sides_of(mid, got_mid, at, n_z)
-    w_back = sides_of(down, send(down, wires["core"]), at, n_z)
+    ctx, w_mid, got_down, other_down = tie(ctx, w_mid, got_down, other_down)
+    w_mid = sum(pieces_of(*w_mid, at, n_z), ())
+    w_back = sum(pieces_of(down, got_down, other_down, send(got_down, wires["core"]), at, n_z), ())
     out, normed_low, activated, dbranch, dhidden, dattn, dresid1, dctx, sums, in_sums = ffn(
         at, flags, x, ctx, cot, rows, b_in, w_mid, w_back, n_z
     )
 
     mine, theirs = c[None], 1 - c[None]
-    keep_d, give_d = down_grad(at, activated, dbranch)
-    dhidden, give_d = tie(dhidden, give_d)
+    part_d = [(activated, dbranch, split)]
+    part_m = [(normed_low, dhidden, ff_width // 2), (ctx, dattn, split)]
+    give_d = grads(at, theirs, part_d, None, n_z, width, "down_give")
+    dattn, give_d = tie(dattn, give_d)
+    part_m[1] = (ctx, dattn, split)
     got_d = send(give_d, wires["core"])
-    give_i, keep_i = in_grad(at, normed_low, dhidden)
-    got_d, give_i = tie(got_d, give_i)
-    keep_d, give_d = sum_core(keep_d, got_d, at, n_z)
-    dctx, give_d, give_i = tie(dctx, give_d, give_i)
+    give_m = grads(at, theirs, part_m, None, n_z, width, "mid_give")
+    got_d, give_m = tie(got_d, give_m)
+    got_m = send(give_m, wires["core"])
+    give_d, keep_d = grads(at, mine, part_d, got_d, n_z, width, "down_keep")
+    give_d, dctx = tie(give_d, dctx)
     got_d = send(give_d, wires["second"])
-    got_i = send(give_i, wires["core"])
     dqkv_theirs = attend_back(theirs, doc_count, qkv, ctx, inv, expo, dctx)
-    got_d, got_i, dqkv_theirs = tie(got_d, got_i, dqkv_theirs)
+    got_d, got_m, dqkv_theirs = tie(got_d, got_m, dqkv_theirs)
     keep_d, give_d = sum_second(keep_d, got_d, at)
-    keep_i, give_i = sum_core(keep_i, got_i, at, n_z)
-    dqkv_theirs, give_d, give_i = tie(dqkv_theirs, give_d, give_i)
+    give_d, got_m = tie(give_d, got_m)
     got_d = send(give_d, wires["first"])
-    got_i = send(give_i, wires["second"])
-    give_a = attn_grad(theirs, ctx, dattn, embed_low, dqkv_theirs)
-    dctx, give_a = tie(dctx, give_a)
+    give_m, keep_m = grads(at, mine, part_m, got_m, n_z, width, "mid_keep")
+    got_d, give_m, dqkv_theirs = tie(got_d, give_m, dqkv_theirs)
+    got_m = send(give_m, wires["second"])
+    keep_d, give_d = sum_first(keep_d, got_d, at)
+    give_d, dqkv_theirs = tie(give_d, dqkv_theirs)
+    got_d = send_all(give_d, wires["z"])
+    give_a = grads(at, theirs, [(embed_low, dqkv_theirs, 3 * split)], None, n_z, 3 * split, "attn_give")
+    give_a, dctx = tie(give_a, dctx)
     got_a = send(give_a, wires["core"])
     dqkv_mine = attend_back(mine, doc_count, qkv, ctx, inv, expo, dctx)
-    got_d, got_i, dqkv_mine = tie(got_d, got_i, dqkv_mine)
-    keep_d, give_d = sum_first(keep_d, got_d, at)
-    keep_i, give_i = sum_second(keep_i, got_i, at)
-    dqkv_mine, give_d, give_i = tie(dqkv_mine, give_d, give_i)
-    got_d = send_all(give_d, wires["z"])
-    got_i = send(give_i, wires["first"])
-    keep_a = attn_grad(mine, ctx, dattn, embed_low, dqkv_mine)
-    got_a, keep_a = tie(got_a, keep_a)
-    keep_a, give_a = sum_core(keep_a, got_a, at, n_z)
-    dqkv_mine, give_a = tie(dqkv_mine, give_a)
+    got_d, got_m, got_a, dqkv_mine = tie(got_d, got_m, got_a, dqkv_mine)
+    keep_m, give_m = sum_second(keep_m, got_m, at)
+    owned_d = sum_z(keep_d, got_d)
+    give_m, owned_d, got_a = tie(give_m, owned_d, got_a)
+    got_m = send(give_m, wires["first"])
+    give_a, keep_a = grads(at, mine, [(embed_low, dqkv_mine, 3 * split)], got_a, n_z, 3 * split, "attn_keep")
+    give_a, got_m = tie(give_a, got_m)
     got_a = send(give_a, wires["second"])
+    keep_m, give_m = sum_first(keep_m, got_m, at)
+    give_m, dqkv_mine, owned_d = tie(give_m, dqkv_mine, owned_d)
+    got_m = send_all(give_m, wires["z"])
+    got_d = send(owned_d, wires["rep"][1])
     grad_input, flag_sums, bias_sums = embed_grad(at, flags, dresid1, dqkv_mine, dqkv_theirs, w_attn, n_z)
-    got_d, got_i, got_a, flag_sums = tie(got_d, got_i, got_a, flag_sums)
-    keep_i, give_i = sum_first(keep_i, got_i, at)
+    got_d, got_a, flag_sums = tie(got_d, got_a, flag_sums)
     keep_a, give_a = sum_second(keep_a, got_a, at)
+    packed = pack(at, sums, in_sums, flag_sums, bias_sums)
+    give_a, packed, got_m = tie(give_a, packed, got_m)
     got_a = send(give_a, wires["first"])
-    got_i = send_all(give_i, wires["z"])
-    owned_d = sum_z(keep_d, got_d)
-    got_d = send_all([owned_d] * 3, wires["rep"])
+    got = send(packed, wires["x"])
+    pair_d = jnp.stack([owned_d, got_d])
+    owned_m = sum_z(keep_m, got_m)
+    got_a, got, pair_d, owned_m = tie(got_a, got, pair_d, owned_m)
+    packed = packed + got
     keep_a, give_a = sum_first(keep_a, got_a, at)
+    give_a, packed, pair_d, owned_m = tie(give_a, packed, pair_d, owned_m)
     got_a = send_all(give_a, wires["z"])
-    owned_i = sum_z(keep_i, got_i)
-    got_i = send_all([owned_i] * 3, wires["rep"])
+    got = send_all([packed] * (n_z - 1), wires["z"])
+    got_d = send(pair_d, wires["core"])
+    got_m = send(owned_m, wires["rep"][1])
+    got_a, got, got_d, got_m = tie(got_a, got, got_d, got_m)
     owned_a = sum_z(keep_a, got_a)
+    terms = jnp.stack([packed] + got)
+    packed = sum((pick(terms, 0, own // 2 ^ z) for z in range(1, n_z)), pick(terms, 0, own // 2))
+    pair_m = jnp.stack([owned_m, got_m])
+    owned_a, packed, pair_m = tie(owned_a, packed, pair_m)
     got_a = send_all([owned_a] * 3, wires["rep"])
-    o_down, o_in, o_attn = blocks_of(owned_d, got_d, at), blocks_of(owned_i, got_i, at), blocks_of(owned_a, got_a, at)
-
-    halves = [jnp.where(c == h, bias_sums[0], bias_sums[1]) for h in (0, 1)]
-    grad_b_q = jnp.concatenate([half[:split] for half in halves])
-    grad_b_v = jnp.concatenate([half[2 * split :] for half in halves])
-    small = (grad_b_q, grad_b_v, sums[5], sums[3], sums[4], flag_sums[0], flag_sums[1], sums[2], sums[0], sums[1], in_sums[0])
-    packed = jnp.concatenate([value.reshape(n_fsdp, -1) for value in small], axis=1)
-    for pairs in wires["rep_bits"] + wires["fsdp_bits"]:
-        packed = packed + send(packed, pairs)
-    packed = pick(packed, 0, own)
-    o_small = [packed[i * step : (i + 1) * step] for i in range(10)]
+    got = send_all([packed] * 3, wires["rep"])
+    got_m = send(pair_m, wires["core"])
+    terms = jnp.stack([packed] + got)
+    packed = sum((pick(terms, 0, rep ^ r) for r in range(1, 4)), pick(terms, 0, rep))
+    o_small = lax.dynamic_slice(packed, (0, own * step), (16, step))
+    o_b_in = lax.dynamic_slice(packed[11:15].reshape(ff_width), (own * (ff_width // n_fsdp),), (ff_width // n_fsdp,))
+    o_down, o_mid = blocks_of_pairs(pair_d, got_d, at), blocks_of_pairs(pair_m, got_m, at)
+    o_attn = blocks_of(owned_a, got_a, at)
 
     def join(blocks, cut=slice(None)):
         return jnp.concatenate([jnp.concatenate([block[:, cut] for block in row], axis=1) for row in blocks])
 
-    o_qkv = jnp.concatenate([join(o_attn, slice(i * split, (i + 1) * split)) for i in (1, 2, 3)], axis=1)
+    o_qkv = jnp.concatenate([join(o_attn, slice(i * split, (i + 1) * split)) for i in (0, 1, 2)], axis=1)
     return (
         out.reshape(layer_input.shape),
         grad_input.reshape(layer_input.shape),
         o_qkv,
         o_small[0],
         o_small[1],
-        join(o_attn, slice(0, split)),
+        join(o_mid, slice(ff_width // 2, None)),
         o_small[2],
         o_small[3],
         o_small[4],
         o_small[5],
         o_small[6],
-        join(o_in),
-        packed[10 * step :],
+        join(o_mid, slice(0, ff_width // 2)),
+        o_b_in,
         join(o_down),
         o_small[7],
         o_small[8],

time: 372 us -> 317 us (0.85); the launches traced: 365 us -> 316 us
  local copies, waits for them, and re-layouts: 44.4 us -> 10.8 us
  other arithmetic: 36.3 us -> 17.3 us
  Pallas kernels: 148 us -> 163 us
  waiting for transfers between devices: 74.5 us -> 62.1 us
    pallas_call x7 -> x11, Pallas kernels: 102 us -> 117 us  [the longest x1 45.4 us: ffn(): call(functools.partial(ffn_kernel, n_z, len(mid)), (count // TILE,), [FLA...]
    ppermute x53 -> x57, waiting for transfers between devices: 74.5 us -> 62.1 us  [send(): return lax.ppermute(value, AXES, pairs)]
    slice x12 -> x1, local copies, waits for them, and re-layouts: 9.68 us -> 0.01 us  [body(): packed[11:15].reshape(ff_width)]
    unnamed x47 -> x76, local copies, waits for them, and re-layouts: 9.22 us -> 1.58 us
    concatenate x4 -> x5, local copies, waits for them, and re-layouts: 8.88 us -> 1.52 us  [the longest x2 1.36 us: grads(): at = jnp.concatenate([at, half])]
    convert_element_type x9 -> x7, other arithmetic: 15.5 us -> 8.56 us  [add_low(): (left.astype(jnp.float32) + right.astype(jnp.float32)).astype(jnp.bfloat16)]
    select_n x8 -> x0, other arithmetic: 5.1 us -> none  [the longest x3 3.55 us: sum_core(): away = jnp.where(c == 0, pick(summed, 1, 1 - x), pick(summed, 2, 1 - y))]
    ppermute x53 -> x57, starting transfers between devices: 59.1 us -> 61.1 us  [send(): return lax.ppermute(value, AXES, pairs)]
  transfers between devices with their start and end apart: 53 -> 57, of which waited for: 23 -> 21; matrix products, arithmetic and copies ran while one was open for 13% -> 5% of each run, Pallas kernels for 26% -> 33%
where the time goes in v2:
time: 317 us; the launch traced here: 316 us
  Pallas kernels  163 us (51%)
  waiting for transfers between devices  62.1 us (20%)
  starting transfers between devices  61.1 us (19%)
  other arithmetic  17.3 us (5%)
  local copies, waits for them, and re-layouts  10.8 us (3%)
    ppermute x57, waiting for transfers between devices, send(): return lax.ppermute(value, AXES, pairs)  62.1 us
    ppermute x57, starting transfers between devices, send(): return lax.ppermute(value, AXES, pairs)  61.1 us
    pallas_call x1, Pallas kernels, ffn(): call(functools.partial(ffn_kernel, n_z, len(mid)), (count // TILE,), [FLA...  45.4 us
    pallas_call x2, Pallas kernels, attend_back(): call(functools.partial(attend_back_kernel, n_pair), (docs * n_pair,), [pa...  24.7 us
    pallas_call x3, Pallas kernels, grads(): call(functools.partial(grad_kernel, n_first, True, by_z), (steps,), specs...  24.3 us
    pallas_call x3, Pallas kernels, grads(): call(plain, (steps,), specs, spec, jax.ShapeDtypeStruct((rows, width), jn...  22.3 us
    pallas_call x2, Pallas kernels, attend(): call(functools.partial(attend_kernel, n_pair), (docs * n_pair,), [part(0)...  21.4 us
    pallas_call x1, Pallas kernels, embed_grad(): call(functools.partial(embed_grad_kernel, n_z), (count // TILE,), [FLAGS,...  11.5 us
  transfers between devices with their start and end apart: 57, of which 21 were waited for; matrix products, arithmetic and copies ran while one was open for 5% of the time, Pallas kernels for 33%

profile of v2, /device:TPU:0, one launch (start us, length us, event | category | flops | bytes accessed | tf_op | source)
XLA Modules:
  0.0 315.6 jit_solution(10274107121781520149)
XLA Ops:
  2.0 3.1 collective-permute-start
  5.1 2.6 collective-permute-start.1
  9.7 6.8 %collective-permute-done.1 = bf16[48,1152]{1,0:T(8,128)(2,1)S(1)} collective-permute-done((bf16[48,1152]{1,0:T(8,128)(2,1)S(1)}, bf16[48,1152]{1,0:T(8,128)(2,1)S(1)}, u32[]{:S(2)}, u32[]{:S(2)}) %collective-permute-start.1) | collective-permute-done | bytes 110624 | tf_op jit(solution)/shard_map/ppermute | solution.py:41
  16.5 1.6 collective-permute-start.4
  20.4 1.7 collective-permute-start.5
  24.9 1.9 collective-permute-done.6
  26.8 2.3 collective-permute-done.7
  29.2 1.7 collective-permute-start.11
  32.1 3.1 collective-permute-start.9
  38.6 1.7 collective-permute-done.8
  40.4 4.5 %collective-permute-done.9 = bf16[48,1920]{1,0:T(8,128)(2,1)S(1)} collective-permute-done((bf16[48,1920]{1,0:T(8,128)(2,1)S(1)}, bf16[48,1920]{1,0:T(8,128)(2,1)S(1)}, u32[]{:S(2)}, u32[]{:S(2)}) %collective-permute-start.9) | collective-permute-done | bytes 184352 | tf_op jit(solution)/shard_map/ppermute | solution.py:41
  46.5 13.0 %collective-permute-done.12 = bf16[192,1920]{1,0:T(8,128)(2,1)S(1)} collective-permute-done((bf16[192,1920]{1,0:T(8,128)(2,1)S(1)}, bf16[192,1920]{1,0:T(8,128)(2,1)S(1)}, u32[]{:S(2)}, u32[]{:S(2)}) %collective-permute-start.12) | collective-permute-done | bytes 737312 | tf_op jit(solution)/shard_map/ppermute | solution.py:41
  61.6 3.5 %collective-permute-start.17 = (bf16[192,384]{1,0:T(8,128)(2,1)S(1)}, bf16[192,384]{1,0:T(8,128)(2,1)S(1)}, u32[]{:S(2)}, u32[]{:S(2)}) collective-permute-start(bf16[192,384]{1,0:T(8,128)(2,1)S(1)} %dynamic_slice.216), channel_id=1, source_target_pairs={{0,6},{1,7},{2,4},{3,5},{4,2},{5,3},{6,0},{7,1},{8,14},{9,15},{10,... | collective-permute-start | bytes 442376 | tf_op jit(solution)/shard_map/ppermute | solution.py:41
  65.2 10.1 %project.1 = (bf16[2,1024,1152]{2,1,0:T(8,128)(2,1)}, bf16[1024,768]{1,0:T(8,128)(2,1)}) custom-call(s32[4]{0:T(128)} %pad_add_fusion.at_ref, bf16[16,1024]{1,0:T(8,128)(2,1)} %fusion.59.flag_ref, bf16[1024,768]{1,0:T(8,128)(2,1)} %bitcast.218, bf16[16,768]{1,0:T(8,128)(2,1)} %get-tuple-element.158.row_ref, f32[1,2304]{1,0:T(1,128)} %get-tuple-element.159.bias_ref, ...), custom_call_target="tpu_custom_call" | custom-call | flops 3623878656 | bytes 12582912 | tf_op jit(solution)/shard_map/project/pallas_call | solution.py:227
  76.1 10.7 %attend.2 = (bf16[1024,768]{1,0:T(8,128)(2,1)}, f32[1024,768]{1,0:T(8,128)}, bf16[2,6,2,512,512]{4,3,2,1,0:T(8,128)(2,1)}) custom-call(s32[2]{0:T(128)} %len_ref.3, bf16[2,1024,1152]{2,1,0:T(8,128)(2,1)} %get-tuple-element.167.q_ref.k_ref.v_ref, bf16[2,1024,1152]{2,1,0:T(8,128)(2,1)} %get-tuple-element.167.q_ref.k_ref.v_ref, ...), custom_call_target="tpu_custom_call" | custom-call | flops 3221225472 | bytes 34603008 | tf_op jit(solution)/shard_map/attend/pallas_call | solution.py:311
  88.7 10.7 %attend.3 = (bf16[1024,768]{1,0:T(8,128)(2,1)}, f32[1024,768]{1,0:T(8,128)}, bf16[2,6,2,512,512]{4,3,2,1,0:T(8,128)(2,1)}) custom-call(s32[2]{0:T(128)} %len_ref.3, bf16[2,1024,1152]{2,1,0:T(8,128)(2,1)} %get-tuple-element.167.q_ref.k_ref.v_ref, ...), custom_call_target="tpu_custom_call", output_to_operand_aliasing={{0}: (4, {}), {1}: (5, {}), {2}: (6, {})} | custom-call | flops 3221225472 | bytes 34603008 | tf_op jit(solution)/shard_map/attend/pallas_call | solution.py:311
  99.4 4.3 %collective-permute-done.22.refs_5_ = bf16[1536,384]{1,0:T(8,128)(2,1)S(1)} collective-permute-done((bf16[1536,384]{1,0:T(8,128)(2,1)S(1)}, bf16[1536,384]{1,0:T(8,128)(2,1)S(1)}, u32[]{:S(2)}, u32[]{:S(2)}) %collective-permute-start.22) | collective-permute-done | bytes 1179680 | tf_op jit(solution)/shard_map/ppermute | solution.py:41
  104.6 2.2 collective-permute-done.24.refs_7_
  106.8 45.4 %ffn.1 = (bf16[1024,768]{1,0:T(8,128)(2,1)}, bf16[1024,768]{1,0:T(8,128)(2,1)}, bf16[1024,3072]{1,0:T(8,128)(2,1)}, bf16[1024,768]{1,0:T(8,128)(2,1)}, bf16[1024...) custom-call(s32[4]{0:T(128)} %pad_add_fusion.at_ref, ...), custom_call_target="tpu_custom_call" | custom-call | flops 21743271936 | bytes 47431680 | tf_op jit(solution)/shard_map/ffn/pallas_call | solution.py:447
  152.2 7.9 %down_give.1 = bf16[3072,384]{1,0:T(8,128)(2,1)} custom-call(s32[5]{0:T(128)} %concatenate.168.at_ref, bf16[1024,3072]{1,0:T(8,128)(2,1)} %get-tuple-element.197.refs_0_, bf16[1024,768]{1,0:T(8,128)(2,1)} %get-tuple-element.198.refs_1_), custom_call_target="tpu_custom_call" | custom-call | flops 2415919104 | bytes 4718592 | tf_op jit(solution)/shard_map/down_give/pallas_call | solution.py:529
  160.2 8.1 %mid_give.1 = bf16[768,1920]{1,0:T(8,128)(2,1)} custom-call(s32[5]{0:T(128)} %concatenate.168.at_ref, bf16[1024,768]{1,0:T(8,128)(2,1)} %get-tuple-element.194.refs_0_, bf16[1024,3072]{1,0:T(8,128)(2,1)} %get-tuple-element.195.refs_1_, bf16[1024,768]{1,0:T(8,128)(2,1)} %get-tuple-element.184.ctx_ref.refs_2_, bf16[1024,768]{1,0:T(8,128)(2,1)} %get-tuple-element.199.refs_3_), custom_call_target="tpu_custom_call" | custom-call | flops 3019898880 | bytes 5898240 | tf_op jit(solution)/shard_map/mid_give/pallas_call | solution.py:529
  169.4 8.6 %down_keep.1 = (bf16[4,2,192,384]{3,2,1,0:T(8,128)(2,1)}, bf16[4,2,192,384]{3,2,1,0:T(8,128)(2,1)}) custom-call(s32[5]{0:T(128)} %concatenate.167.at_ref, bf16[1024,3072]{1,0:T(8,128)(2,1)} %get-tuple-element.197.refs_0_, bf16[1024,768]{1,0:T(8,128)(2,1)} %get-tuple-element.198.refs_1_, bf16[3072,384]{1,0:T(8,128)(2,1)} %collective-permute-done.25.refs_2_), custom_call_target="tpu_custom_call" | custom-call | flops 2415919104 | bytes 4718592 | tf_op jit(solution)/shard_map/down_keep/pallas_call | solution.py:540
  178.0 2.4 copy.41
  181.5 12.4 %attend_back.2.refs_1_.theirs_ref = bf16[1024,1152]{1,0:T(8,128)(2,1)} custom-call(s32[1]{0:T(128)S(6)} %sub.21.half_ref, bf16[2,1024,1152]{2,1,0:T(8,128)(2,1)} %get-tuple-element.167.q_ref.k_ref.v_ref, bf16[2,1024,1152]{2,1,0:T(8,128)(2,1)} %get-tuple-element.167.q_ref.k_ref.v_ref, bf16[2,1024,1152]{2,1,0:T(8,128)(2,1)} %get-tuple-element.167.q_ref.k_ref.v_ref, ...), custom_call_target="tpu_custom_call" | custom-call | flops 8053063680 | bytes 4718592 | tf_op jit(solution)/shard_map/attend_back/pallas_call | solution.py:588
  193.9 3.0 collective-permute-done.26
  196.9 3.1 fusion.2
  202.3 8.8 %mid_keep.1 = (bf16[4,2,48,1920]{3,2,1,0:T(8,128)(2,1)}, bf16[4,2,48,1920]{3,2,1,0:T(8,128)(2,1)}) custom-call(s32[5]{0:T(128)} %concatenate.167.at_ref, bf16[1024,768]{1,0:T(8,128)(2,1)} %get-tuple-element.194.refs_0_, bf16[1024,3072]{1,0:T(8,128)(2,1)} %get-tuple-element.195.refs_1_, bf16[1024,768]{1,0:T(8,128)(2,1)} %get-tuple-element.184.ctx_ref.refs_2_, ...), custom_call_target="tpu_custom_call" | custom-call | flops 3019898880 | bytes 5898240 | tf_op jit(solution)/shard_map/mid_keep/pallas_call | solution.py:540
  212.4 6.2 %attn_give.1 = bf16[768,1152]{1,0:T(8,128)(2,1)} custom-call(s32[5]{0:T(128)} %concatenate.168.at_ref, bf16[1024,768]{1,0:T(8,128)(2,1)} %get-tuple-element.223.refs_0_, bf16[1024,1152]{1,0:T(8,128)(2,1)} %attend_back.2.refs_1_.theirs_ref), custom_call_target="tpu_custom_call" | custom-call | flops 1811939328 | bytes 3538944 | tf_op jit(solution)/shard_map/attn_give/pallas_call | solution.py:529
  218.6 1.7 collective-permute-start.32
  220.3 2.7 collective-permute-start.29
  223.0 2.4 collective-permute-start.31
  225.4 12.3 %attend_back.3.refs_1_.mine_ref = bf16[1024,1152]{1,0:T(8,128)(2,1)} custom-call(s32[1]{0:T(128)} %bitcast.1.half_ref, bf16[2,1024,1152]{2,1,0:T(8,128)(2,1)} %get-tuple-element.167.q_ref.k_ref.v_ref, bf16[2,1024,1152]{2,1,0:T(8,128)(2,1)} %get-tuple-element.167.q_ref.k_ref.v_ref, bf16[2,1024,1152]{2,1,0:T(8,128)(2,1)} %get-tuple-element.167.q_ref.k_ref.v_ref, ...), custom_call_target="tpu_custom_call" | custom-call | flops 8053063680 | bytes 4718592 | tf_op jit(solution)/shard_map/attend_back/pallas_call | solution.py:588
  238.5 1.7 add_convert_fusion.1
  242.3 6.8 %attn_keep.1 = (bf16[4,2,48,1152]{3,2,1,0:T(8,128)(2,1)}, bf16[4,2,48,1152]{3,2,1,0:T(8,128)(2,1)}) custom-call(s32[5]{0:T(128)} %concatenate.167.at_ref, bf16[1024,768]{1,0:T(8,128)(2,1)} %get-tuple-element.223.refs_0_, bf16[1024,1152]{1,0:T(8,128)(2,1)} %attend_back.3.refs_1_.mine_ref, bf16[768,1152]{1,0:T(8,128)(2,1)} %collective-permute-done.33.refs_2_), custom_call_target="tpu_custom_call" | custom-call | flops 1811939328 | bytes 3538944 | tf_op jit(solution)/shard_map/attn_keep/pallas_call | solution.py:540
  249.1 3.7 %collective-permute-done.34 = bf16[4,48,1920]{2,1,0:T(8,128)(2,1)S(1)} collective-permute-done((bf16[4,48,1920]{2,1,0:T(8,128)(2,1)S(1)}, bf16[4,48,1920]{2,1,0:T(8,128)(2,1)S(1)}, u32[]{:S(2)}, u32[]{:S(2)}) %collective-permute-start.34) | collective-permute-done | bytes 737312 | tf_op jit(solution)/shard_map/ppermute | solution.py:41
  252.8 1.6 collective-permute-start.36
  255.7 2.7 collective-permute-start.37
  258.4 2.4 collective-permute-start.39
  260.8 11.5 %embed_grad.1 = (bf16[1024,768]{1,0:T(8,128)(2,1)}, f32[16,768]{1,0:T(8,128)}, f32[8,1152]{1,0:T(8,128)}) custom-call(s32[4]{0:T(128)} %pad_add_fusion.at_ref, bf16[16,1024]{1,0:T(8,128)(2,1)} %fusion.59.flag_ref, f32[1024,768]{1,0:T(8,128)} %get-tuple-element.193.dresid_ref, bf16[1024,1152]{1,0:T(8,128)(2,1)} %attend_back.3.refs_1_.mine_ref, ...), custom_call_target="tpu_custom_call" | custom-call | flops 3623878656 | bytes 3317760 | tf_op jit(solution)/shard_map/embed_grad/pallas_call | solution.py:624
  274.8 1.6 collective-permute-start.40
  278.0 2.8 collective-permute-done.41
  280.8 2.4 collective-permute-done.40
  283.4 1.6 collective-permute-start.49
  287.0 2.4 collective-permute-start.47
  290.5 2.3 collective-permute-done.46
  293.5 2.4 collective-permute-start.44
  296.1 6.1 %collective-permute-done.43 = bf16[48,1152]{1,0:T(8,128)(2,1)S(1)} collective-permute-done((bf16[48,1152]{1,0:T(8,128)(2,1)S(1)}, bf16[48,1152]{1,0:T(8,128)(2,1)S(1)}, u32[]{:S(2)}, u32[]{:S(2)}) %collective-permute-start.43) | collective-permute-done | bytes 110624 | tf_op jit(solution)/shard_map/ppermute | solution.py:41
  310.4 1.6 collective-permute-done.52
  (224 shorter events, 49.7 us)
Async XLA Ops:
  2.0 7.7 %collective-permute-start = (bf16[48,1152]{1,0:T(8,128)(2,1)S(1)}, bf16[48,1152]{1,0:T(8,128)(2,1)S(1)}, u32[]{:S(2)}, u32[]{:S(2)}) collective-permute-start(bf16[48,1152]{1,0:T(8,128)(2,1)S(1)} %pad_maximum_fusion.11), channel_id=1, source_target_pairs={{0,2},{1,3},{2,0},{3,1},{4,6},{5,7},{6,4},{7,5},{8,10},{9,11},{10,... | collective-permute-start | bytes 331784 | tf_op jit(solution)/shard_map/ppermute | solution.py:41
  5.1 11.3 %collective-permute-start.1 = (bf16[48,1152]{1,0:T(8,128)(2,1)S(1)}, bf16[48,1152]{1,0:T(8,128)(2,1)S(1)}, u32[]{:S(2)}, u32[]{:S(2)}) collective-permute-start(bf16[48,1152]{1,0:T(8,128)(2,1)S(1)} %pad_maximum_fusion.11), channel_id=1, source_target_pairs={{0,4},{1,5},{2,6},{3,7},{4,0},{5,1},{6,2},{7,3},{8,12},{9,13},{10,... | collective-permute-start | bytes 331784 | tf_op jit(solution)/shard_map/ppermute | solution.py:41
  7.7 8.8 %collective-permute-start.2 = (bf16[48,1152]{1,0:T(8,128)(2,1)S(1)}, bf16[48,1152]{1,0:T(8,128)(2,1)S(1)}, u32[]{:S(2)}, u32[]{:S(2)}) collective-permute-start(bf16[48,1152]{1,0:T(8,128)(2,1)S(1)} %pad_maximum_fusion.11), channel_id=1, source_target_pairs={{0,6},{1,7},{2,4},{3,5},{4,2},{5,3},{6,0},{7,1},{8,14},{9,15},{10,... | collective-permute-start | bytes 331784 | tf_op jit(solution)/shard_map/ppermute | solution.py:41
  18.1 11.0 %collective-permute-start.3 = (bf16[192,1152]{1,0:T(8,128)(2,1)S(1)}, bf16[192,1152]{1,0:T(8,128)(2,1)S(1)}, u32[]{:S(2)}, u32[]{:S(2)}) collective-permute-start(bf16[192,1152]{1,0:T(8,128)(2,1)S(1)} %pad_maximum_fusion.4), channel_id=1, source_target_pairs={{0,16},{1,17},{2,18},{3,19},{4,20},{5,21},{6,22},{7,23},{8,9},{9,8... | collective-permute-start | bytes 1327112 | tf_op jit(solution)/shard_map/ppermute | solution.py:41
  23.6 5.5 %collective-permute-start.7 = (f32[2,16,96]{2,1,0:T(8,128)S(1)}, f32[2,16,96]{2,1,0:T(8,128)S(1)}, u32[]{:S(2)}, u32[]{:S(2)}) collective-permute-start(f32[2,16,96]{2,1,0:T(8,128)S(1)} %get-tuple-element.329), channel_id=1, source_target_pairs={{0,6},{1,7},{2,4},{3,5},{4,2},{5,3},{6,0},{7,1},{8,14},{9,15},{10,... | collective-permute-start | bytes 36872 | tf_op jit(solution)/shard_map/ppermute | solution.py:41
  29.2 15.8 %collective-permute-start.11 = (bf16[384,1152]{1,0:T(8,128)(2,1)S(1)}, bf16[384,1152]{1,0:T(8,128)(2,1)S(1)}, u32[]{:S(2)}, u32[]{:S(2)}) collective-permute-start(bf16[384,1152]{1,0:T(8,128)(2,1)S(1)} %constant_dynamic-update-slice_fusion.7.refs_0_), channel_id=1, source_target_pairs={{0,1},{1,0},{2,3},{3,2},{4,5},{5,4},{6,7},{7,6},{8,24},{9,25},{10,... | collective-permute-start | bytes 2654216 | tf_op jit(solution)/shard_map/ppermute | solution.py:41
  30.8 7.8 %collective-permute-start.10 = (bf16[48,1920]{1,0:T(8,128)(2,1)S(1)}, bf16[48,1920]{1,0:T(8,128)(2,1)S(1)}, u32[]{:S(2)}, u32[]{:S(2)}) collective-permute-start(bf16[48,1920]{1,0:T(8,128)(2,1)S(1)} %pad_maximum_fusion.10), channel_id=1, source_target_pairs={{0,6},{1,7},{2,4},{3,5},{4,2},{5,3},{6,0},{7,1},{8,14},{9,15},{10,... | collective-permute-start | bytes 552968 | tf_op jit(solution)/shard_map/ppermute | solution.py:41
  32.1 8.3 %collective-permute-start.8 = (bf16[48,1920]{1,0:T(8,128)(2,1)S(1)}, bf16[48,1920]{1,0:T(8,128)(2,1)S(1)}, u32[]{:S(2)}, u32[]{:S(2)}) collective-permute-start(bf16[48,1920]{1,0:T(8,128)(2,1)S(1)} %pad_maximum_fusion.10), channel_id=1, source_target_pairs={{0,2},{1,3},{2,0},{3,1},{4,6},{5,7},{6,4},{7,5},{8,10},{9,11},{10,... | collective-permute-start | bytes 552968 | tf_op jit(solution)/shard_map/ppermute | solution.py:41
  32.1 12.8 %collective-permute-start.9 = (bf16[48,1920]{1,0:T(8,128)(2,1)S(1)}, bf16[48,1920]{1,0:T(8,128)(2,1)S(1)}, u32[]{:S(2)}, u32[]{:S(2)}) collective-permute-start(bf16[48,1920]{1,0:T(8,128)(2,1)S(1)} %pad_maximum_fusion.10), channel_id=1, source_target_pairs={{0,4},{1,5},{2,6},{3,7},{4,0},{5,1},{6,2},{7,3},{8,12},{9,13},{10,... | collective-permute-start | bytes 552968 | tf_op jit(solution)/shard_map/ppermute | solution.py:41
  45.0 14.5 %collective-permute-start.12 = (bf16[192,1920]{1,0:T(8,128)(2,1)S(1)}, bf16[192,1920]{1,0:T(8,128)(2,1)S(1)}, u32[]{:S(2)}, u32[]{:S(2)}) collective-permute-start(bf16[192,1920]{1,0:T(8,128)(2,1)S(1)} %pad_maximum_fusion.2), channel_id=1, source_target_pairs={{0,16},{1,17},{2,18},{3,19},{4,20},{5,21},{6,22},{7,23},{8,9},{9,8... | collective-permute-start | bytes 2211848 | tf_op jit(solution)/shard_map/ppermute | solution.py:41
  46.0 14.8 %collective-permute-start.13 = (bf16[384,1152]{1,0:T(8,128)(2,1)S(1)}, bf16[384,1152]{1,0:T(8,128)(2,1)S(1)}, u32[]{:S(2)}, u32[]{:S(2)}) collective-permute-start(bf16[384,1152]{1,0:T(8,128)(2,1)S(1)} %constant_dynamic-update-slice_fusion.7.refs_0_), channel_id=1, source_target_pairs={{0,8},{1,9},{2,10},{3,11},{4,12},{5,13},{6,14},{7,15},{8,0},{9,1},... | collective-permute-start | bytes 2654216 | tf_op jit(solution)/shard_map/ppermute | solution.py:41
  46.0 15.1 %collective-permute-start.14 = (bf16[384,1152]{1,0:T(8,128)(2,1)S(1)}, bf16[384,1152]{1,0:T(8,128)(2,1)S(1)}, u32[]{:S(2)}, u32[]{:S(2)}) collective-permute-start(bf16[384,1152]{1,0:T(8,128)(2,1)S(1)} %collective-permute-done.11.refs_1_), channel_id=1, source_target_pairs={{0,8},{1,9},{2,10},{3,11},{4,12},{5,13},{6,14},{7,15},{8,0},{9,1},... | collective-permute-start | bytes 2654216 | tf_op jit(solution)/shard_map/ppermute | solution.py:41
  59.6 27.2 %collective-permute-start.18 = (bf16[384,1920]{1,0:T(8,128)(2,1)S(1)}, bf16[384,1920]{1,0:T(8,128)(2,1)}, u32[]{:S(2)}, u32[]{:S(2)}) collective-permute-start(bf16[384,1920]{1,0:T(8,128)(2,1)S(1)} %pad_maximum_fusion.refs_0_), channel_id=1, source_target_pairs={{0,1},{1,0},{2,3},{3,2},{4,5},{5,4},{6,7},{7,6},{8,24},{9,25},{10,... | collective-permute-start | bytes 4423688 | tf_op jit(solution)/shard_map/ppermute | solution.py:41
  60.0 26.8 %collective-permute-start.20 = (bf16[384,1920]{1,0:T(8,128)(2,1)S(1)}, bf16[384,1920]{1,0:T(8,128)(2,1)}, u32[]{:S(2)}, u32[]{:S(2)}) collective-permute-start(bf16[384,1920]{1,0:T(8,128)(2,1)S(1)} %pad_maximum_fusion.refs_0_), channel_id=1, source_target_pairs={{0,8},{1,9},{2,10},{3,11},{4,12},{5,13},{6,14},{7,15},{8,0},{9,1},... | collective-permute-start | bytes 4423688 | tf_op jit(solution)/shard_map/ppermute | solution.py:41
  60.7 14.6 %collective-permute-start.15 = (bf16[192,384]{1,0:T(8,128)(2,1)S(1)}, bf16[192,384]{1,0:T(8,128)(2,1)S(1)}, u32[]{:S(2)}, u32[]{:S(2)}) collective-permute-start(bf16[192,384]{1,0:T(8,128)(2,1)S(1)} %dynamic_slice.216), channel_id=1, source_target_pairs={{0,2},{1,3},{2,0},{3,1},{4,6},{5,7},{6,4},{7,5},{8,10},{9,11},{10,... | collective-permute-start | bytes 442376 | tf_op jit(solution)/shard_map/ppermute | solution.py:41
  60.7 14.6 %collective-permute-start.16 = (bf16[192,384]{1,0:T(8,128)(2,1)S(1)}, bf16[192,384]{1,0:T(8,128)(2,1)S(1)}, u32[]{:S(2)}, u32[]{:S(2)}) collective-permute-start(bf16[192,384]{1,0:T(8,128)(2,1)S(1)} %dynamic_slice.216), channel_id=1, source_target_pairs={{0,4},{1,5},{2,6},{3,7},{4,0},{5,1},{6,2},{7,3},{8,12},{9,13},{10,... | collective-permute-start | bytes 442376 | tf_op jit(solution)/shard_map/ppermute | solution.py:41
  61.6 13.7 %collective-permute-start.17 = (bf16[192,384]{1,0:T(8,128)(2,1)S(1)}, bf16[192,384]{1,0:T(8,128)(2,1)S(1)}, u32[]{:S(2)}, u32[]{:S(2)}) collective-permute-start(bf16[192,384]{1,0:T(8,128)(2,1)S(1)} %dynamic_slice.216), channel_id=1, source_target_pairs={{0,6},{1,7},{2,4},{3,5},{4,2},{5,3},{6,0},{7,1},{8,14},{9,15},{10,... | collective-permute-start | bytes 442376 | tf_op jit(solution)/shard_map/ppermute | solution.py:41
  75.4 11.4 %collective-permute-start.19 = (bf16[768,384]{1,0:T(8,128)(2,1)S(1)}, bf16[768,384]{1,0:T(8,128)(2,1)S(1)}, u32[]{:S(2)}, u32[]{:S(2)}) collective-permute-start(bf16[768,384]{1,0:T(8,128)(2,1)S(1)} %pad_maximum_fusion.3), channel_id=1, source_target_pairs={{0,16},{1,17},{2,18},{3,19},{4,20},{5,21},{6,22},{7,23},{8,9},{9,8... | collective-permute-start | bytes 1769480 | tf_op jit(solution)/shard_map/ppermute | solution.py:41
  86.8 16.9 %collective-permute-start.21 = (bf16[384,1920]{1,0:T(8,128)(2,1)}, bf16[384,1920]{1,0:T(8,128)(2,1)S(1)}, u32[]{:S(2)}, u32[]{:S(2)}) collective-permute-start(bf16[384,1920]{1,0:T(8,128)(2,1)} %collective-permute-done.18.refs_1_), channel_id=1, source_target_pairs={{0,8},{1,9},{2,10},{3,11},{4,12},{5,13},{6,14},{7,15},{8,0},{9,1},... | collective-permute-start | bytes 4423688 | tf_op jit(solution)/shard_map/ppermute | solution.py:41
  87.5 16.3 %collective-permute-start.22 = (bf16[1536,384]{1,0:T(8,128)(2,1)S(1)}, bf16[1536,384]{1,0:T(8,128)(2,1)S(1)}, u32[]{:S(2)}, u32[]{:S(2)}) collective-permute-start(bf16[1536,384]{1,0:T(8,128)(2,1)S(1)} %pad_maximum_fusion.1.refs_4_), channel_id=1, source_target_pairs={{0,1},{1,0},{2,3},{3,2},{4,5},{5,4},{6,7},{7,6},{8,24},{9,25},{10,... | collective-permute-start | bytes 3538952 | tf_op jit(solution)/shard_map/ppermute | solution.py:41
  88.6 15.1 %collective-permute-start.23 = (bf16[1536,384]{1,0:T(8,128)(2,1)S(1)}, bf16[1536,384]{1,0:T(8,128)(2,1)}, u32[]{:S(2)}, u32[]{:S(2)}) collective-permute-start(bf16[1536,384]{1,0:T(8,128)(2,1)S(1)} %pad_maximum_fusion.1.refs_4_), channel_id=1, source_target_pairs={{0,8},{1,9},{2,10},{3,11},{4,12},{5,13},{6,14},{7,15},{8,0},{9,1},... | collective-permute-start | bytes 3538952 | tf_op jit(solution)/shard_map/ppermute | solution.py:41
  160.1 8.3 %collective-permute-start.25 = (bf16[3072,384]{1,0:T(8,128)(2,1)}, bf16[3072,384]{1,0:T(8,128)(2,1)}, u32[]{:S(2)}, u32[]{:S(2)}) collective-permute-start(bf16[3072,384]{1,0:T(8,128)(2,1)} %down_give.1), channel_id=1, source_target_pairs={{0,8},{1,9},{2,10},{3,11},{4,12},{5,13},{6,14},{7,15},{8,0},{9,1},... | collective-permute-start | bytes 7077896 | tf_op jit(solution)/shard_map/ppermute | solution.py:41
  168.4 28.5 %collective-permute-start.27 = (bf16[768,1920]{1,0:T(8,128)(2,1)}, bf16[768,1920]{1,0:T(8,128)(2,1)S(1)}, u32[]{:S(2)}, u32[]{:S(2)}) collective-permute-start(bf16[768,1920]{1,0:T(8,128)(2,1)} %mid_give.1), channel_id=1, source_target_pairs={{0,8},{1,9},{2,10},{3,11},{4,12},{5,13},{6,14},{7,15},{8,0},{9,1},... | collective-permute-start | bytes 8847368 | tf_op jit(solution)/shard_map/ppermute | solution.py:41
  180.4 16.5 %collective-permute-start.26 = (bf16[4,2,192,384]{3,2,0,1:T(8,128)(2,1)}, bf16[4,2,192,384]{3,2,0,1:T(8,128)(2,1)}, u32[]{:S(2)}, u32[]{:S(2)}) collective-permute-start(bf16[4,2,192,384]{3,2,0,1:T(8,128)(2,1)} %copy.41), channel_id=1, source_target_pairs={{0,1},{1,0},{2,3},{3,2},{4,5},{5,4},{6,7},{7,6},{8,24},{9,25},{10,... | collective-permute-start | bytes 3538952 | tf_op jit(solution)/shard_map/ppermute | solution.py:41
  200.0 11.2 %collective-permute-start.28 = (bf16[4,192,384]{2,1,0:T(8,128)(2,1)}, bf16[4,192,384]{2,1,0:T(8,128)(2,1)}, u32[]{:S(2)}, u32[]{:S(2)}) collective-permute-start(bf16[4,192,384]{2,1,0:T(8,128)(2,1)} %fusion.2), channel_id=1, source_target_pairs={{0,16},{1,17},{2,18},{3,19},{4,20},{5,21},{6,22},{7,23},{8,9},{9,8... | collective-permute-start | bytes 1769480 | tf_op jit(solution)/shard_map/ppermute | solution.py:41
  218.6 19.7 %collective-permute-start.33 = (bf16[768,1152]{1,0:T(8,128)(2,1)}, bf16[768,1152]{1,0:T(8,128)(2,1)}, u32[]{:S(2)}, u32[]{:S(2)}) collective-permute-start(bf16[768,1152]{1,0:T(8,128)(2,1)} %attn_give.1), channel_id=1, source_target_pairs={{0,8},{1,9},{2,10},{3,11},{4,12},{5,13},{6,14},{7,15},{8,0},{9,1},... | collective-permute-start | bytes 5308424 | tf_op jit(solution)/shard_map/ppermute | solution.py:41
  218.6 19.7 %collective-permute-start.32 = (bf16[4,2,48,1920]{3,2,1,0:T(8,128)(2,1)}, bf16[4,2,48,1920]{3,2,1,0:T(8,128)(2,1)}, u32[]{:S(2)}, u32[]{:S(2)}) collective-permute-start(bf16[4,2,48,1920]{3,2,1,0:T(8,128)(2,1)} %get-tuple-element.222), channel_id=1, source_target_pairs={{0,1},{1,0},{2,3},{3,2},{4,5},{5,4},{6,7},{7,6},{8,24},{9,25},{10,... | collective-permute-start | bytes 4423688 | tf_op jit(solution)/shard_map/ppermute | solution.py:41
  220.3 17.4 %collective-permute-start.29 = (bf16[192,384]{1,0:T(8,128)(2,1)S(1)}, bf16[192,384]{1,0:T(8,128)(2,1)S(1)}, u32[]{:S(2)}, u32[]{:S(2)}) collective-permute-start(bf16[192,384]{1,0:T(8,128)(2,1)S(1)} %get-tuple-element.219), channel_id=1, source_target_pairs={{0,2},{1,3},{2,0},{3,1},{4,6},{5,7},{6,4},{7,5},{8,10},{9,11},{10,... | collective-permute-start | bytes 442376 | tf_op jit(solution)/shard_map/ppermute | solution.py:41
  223.0 14.7 %collective-permute-start.30 = (bf16[192,384]{1,0:T(8,128)(2,1)S(1)}, bf16[192,384]{1,0:T(8,128)(2,1)S(1)}, u32[]{:S(2)}, u32[]{:S(2)}) collective-permute-start(bf16[192,384]{1,0:T(8,128)(2,1)S(1)} %get-tuple-element.220), channel_id=1, source_target_pairs={{0,4},{1,5},{2,6},{3,7},{4,0},{5,1},{6,2},{7,3},{8,12},{9,13},{10,... | collective-permute-start | bytes 442376 | tf_op jit(solution)/shard_map/ppermute | solution.py:41
  223.0 14.7 %collective-permute-start.31 = (bf16[192,384]{1,0:T(8,128)(2,1)S(1)}, bf16[192,384]{1,0:T(8,128)(2,1)S(1)}, u32[]{:S(2)}, u32[]{:S(2)}) collective-permute-start(bf16[192,384]{1,0:T(8,128)(2,1)S(1)} %get-tuple-element.221), channel_id=1, source_target_pairs={{0,6},{1,7},{2,4},{3,5},{4,2},{5,3},{6,0},{7,1},{8,14},{9,15},{10,... | collective-permute-start | bytes 442376 | tf_op jit(solution)/shard_map/ppermute | solution.py:41
  241.2 11.5 %collective-permute-start.34 = (bf16[4,48,1920]{2,1,0:T(8,128)(2,1)S(1)}, bf16[4,48,1920]{2,1,0:T(8,128)(2,1)S(1)}, u32[]{:S(2)}, u32[]{:S(2)}) collective-permute-start(bf16[4,48,1920]{2,1,0:T(8,128)(2,1)S(1)} %get-tuple-element.235), channel_id=1, source_target_pairs={{0,16},{1,17},{2,18},{3,19},{4,20},{5,21},{6,22},{7,23},{8,9},{9,8... | collective-permute-start | bytes 2211848 | tf_op jit(solution)/shard_map/ppermute | solution.py:41
  252.8 19.6 %collective-permute-start.36 = (bf16[4,2,48,1152]{3,2,1,0:T(8,128)(2,1)}, bf16[4,2,48,1152]{3,2,1,0:T(8,128)(2,1)S(1)}, u32[]{:S(2)}, u32[]{:S(2)}) collective-permute-start(bf16[4,2,48,1152]{3,2,1,0:T(8,128)(2,1)} %get-tuple-element.242), channel_id=1, source_target_pairs={{0,1},{1,0},{2,3},{3,2},{4,5},{5,4},{6,7},{7,6},{8,24},{9,25},{10,... | collective-permute-start | bytes 2654216 | tf_op jit(solution)/shard_map/ppermute | solution.py:41
  255.2 17.1 %collective-permute-start.35 = (bf16[192,384]{1,0:T(8,128)(2,1)S(1)}, bf16[192,384]{1,0:T(8,128)(2,1)S(1)}, u32[]{:S(2)}, u32[]{:S(2)}) collective-permute-start(bf16[192,384]{1,0:T(8,128)(2,1)S(1)} %fusion.13), channel_id=1, source_target_pairs={{0,16},{1,17},{2,18},{3,19},{4,20},{5,21},{6,22},{7,23},{8,24},{9,... | collective-permute-start | bytes 442376 | tf_op jit(solution)/shard_map/ppermute | solution.py:41
  255.7 19.1 %collective-permute-start.37 = (bf16[48,1920]{1,0:T(8,128)(2,1)}, bf16[48,1920]{1,0:T(8,128)(2,1)S(1)}, u32[]{:S(2)}, u32[]{:S(2)}) collective-permute-start(bf16[48,1920]{1,0:T(8,128)(2,1)} %get-tuple-element.249), channel_id=1, source_target_pairs={{0,2},{1,3},{2,0},{3,1},{4,6},{5,7},{6,4},{7,5},{8,10},{9,11},{10,... | collective-permute-start | bytes 552968 | tf_op jit(solution)/shard_map/ppermute | solution.py:41
  258.4 16.4 %collective-permute-start.38 = (bf16[48,1920]{1,0:T(8,128)(2,1)}, bf16[48,1920]{1,0:T(8,128)(2,1)S(1)}, u32[]{:S(2)}, u32[]{:S(2)}) collective-permute-start(bf16[48,1920]{1,0:T(8,128)(2,1)} %get-tuple-element.250), channel_id=1, source_target_pairs={{0,4},{1,5},{2,6},{3,7},{4,0},{5,1},{6,2},{7,3},{8,12},{9,13},{10,... | collective-permute-start | bytes 552968 | tf_op jit(solution)/shard_map/ppermute | solution.py:41
  258.4 16.4 %collective-permute-start.39 = (bf16[48,1920]{1,0:T(8,128)(2,1)S(1)}, bf16[48,1920]{1,0:T(8,128)(2,1)}, u32[]{:S(2)}, u32[]{:S(2)}) collective-permute-start(bf16[48,1920]{1,0:T(8,128)(2,1)S(1)} %get-tuple-element.251), channel_id=1, source_target_pairs={{0,6},{1,7},{2,4},{3,5},{4,2},{5,3},{6,0},{7,1},{8,14},{9,15},{10,... | collective-permute-start | bytes 552968 | tf_op jit(solution)/shard_map/ppermute | solution.py:41
  274.8 8.4 %collective-permute-start.40 = (bf16[4,48,1152]{2,1,0:T(8,128)(2,1)S(1)}, bf16[4,48,1152]{2,1,0:T(8,128)(2,1)S(1)}, u32[]{:S(2)}, u32[]{:S(2)}) collective-permute-start(bf16[4,48,1152]{2,1,0:T(8,128)(2,1)S(1)} %get-tuple-element.252), channel_id=1, source_target_pairs={{0,16},{1,17},{2,18},{3,19},{4,20},{5,21},{6,22},{7,23},{8,9},{9,8... | collective-permute-start | bytes 1327112 | tf_op jit(solution)/shard_map/ppermute | solution.py:41
  283.3 18.9 %collective-permute-start.48 = (bf16[2,192,384]{2,1,0:T(8,128)(2,1)S(1)}, bf16[2,192,384]{2,1,0:T(8,128)(2,1)S(1)}, u32[]{:S(2)}, u32[]{:S(2)}) collective-permute-start(bf16[2,192,384]{2,1,0:T(8,128)(2,1)S(1)} %pad_maximum_fusion.7), channel_id=1, source_target_pairs={{0,8},{1,9},{2,10},{3,11},{4,12},{5,13},{6,14},{7,15},{8,0},{9,1},... | collective-permute-start | bytes 884744 | tf_op jit(solution)/shard_map/ppermute | solution.py:41
  283.4 18.8 %collective-permute-start.49 = (bf16[48,1920]{1,0:T(8,128)(2,1)S(1)}, bf16[48,1920]{1,0:T(8,128)(2,1)S(1)}, u32[]{:S(2)}, u32[]{:S(2)}) collective-permute-start(bf16[48,1920]{1,0:T(8,128)(2,1)S(1)} %fusion.6), channel_id=1, source_target_pairs={{0,16},{1,17},{2,18},{3,19},{4,20},{5,21},{6,22},{7,23},{8,24},{9,... | collective-permute-start | bytes 552968 | tf_op jit(solution)/shard_map/ppermute | solution.py:41
  286.1 6.8 %collective-permute-start.46 = (f32[16,768]{1,0:T(8,128)S(1)}, f32[16,768]{1,0:T(8,128)S(1)}, u32[]{:S(2)}, u32[]{:S(2)}) collective-permute-start(f32[16,768]{1,0:T(8,128)S(1)} %add.357), channel_id=1, source_target_pairs={{0,4},{1,5},{2,6},{3,7},{4,0},{5,1},{6,2},{7,3},{8,12},{9,13},{10,... | collective-permute-start | bytes 147464 | tf_op jit(solution)/shard_map/ppermute | solution.py:41
  287.0 6.5 %collective-permute-start.47 = (f32[16,768]{1,0:T(8,128)S(1)}, f32[16,768]{1,0:T(8,128)S(1)}, u32[]{:S(2)}, u32[]{:S(2)}) collective-permute-start(f32[16,768]{1,0:T(8,128)S(1)} %add.357), channel_id=1, source_target_pairs={{0,6},{1,7},{2,4},{3,5},{4,2},{5,3},{6,0},{7,1},{8,14},{9,15},{10,... | collective-permute-start | bytes 147464 | tf_op jit(solution)/shard_map/ppermute | solution.py:41
  289.4 6.7 %collective-permute-start.42 = (bf16[48,1152]{1,0:T(8,128)(2,1)S(1)}, bf16[48,1152]{1,0:T(8,128)(2,1)S(1)}, u32[]{:S(2)}, u32[]{:S(2)}) collective-permute-start(bf16[48,1152]{1,0:T(8,128)(2,1)S(1)} %get-tuple-element.262), channel_id=1, source_target_pairs={{0,2},{1,3},{2,0},{3,1},{4,6},{5,7},{6,4},{7,5},{8,10},{9,11},{10,... | collective-permute-start | bytes 331784 | tf_op jit(solution)/shard_map/ppermute | solution.py:41
  292.9 9.3 %collective-permute-start.43 = (bf16[48,1152]{1,0:T(8,128)(2,1)S(1)}, bf16[48,1152]{1,0:T(8,128)(2,1)S(1)}, u32[]{:S(2)}, u32[]{:S(2)}) collective-permute-start(bf16[48,1152]{1,0:T(8,128)(2,1)S(1)} %get-tuple-element.263), channel_id=1, source_target_pairs={{0,4},{1,5},{2,6},{3,7},{4,0},{5,1},{6,2},{7,3},{8,12},{9,13},{10,... | collective-permute-start | bytes 331784 | tf_op jit(solution)/shard_map/ppermute | solution.py:41
  293.5 8.7 %collective-permute-start.44 = (bf16[48,1152]{1,0:T(8,128)(2,1)S(1)}, bf16[48,1152]{1,0:T(8,128)(2,1)S(1)}, u32[]{:S(2)}, u32[]{:S(2)}) collective-permute-start(bf16[48,1152]{1,0:T(8,128)(2,1)S(1)} %get-tuple-element.264), channel_id=1, source_target_pairs={{0,6},{1,7},{2,4},{3,5},{4,2},{5,3},{6,0},{7,1},{8,14},{9,15},{10,... | collective-permute-start | bytes 331784 | tf_op jit(solution)/shard_map/ppermute | solution.py:41
  304.3 5.2 %collective-permute-start.50 = (bf16[48,1152]{1,0:T(8,128)(2,1)S(1)}, bf16[48,1152]{1,0:T(8,128)(2,1)S(1)}, u32[]{:S(2)}, u32[]{:S(2)}) collective-permute-start(bf16[48,1152]{1,0:T(8,128)(2,1)S(1)} %fusion.23), channel_id=1, source_target_pairs={{0,8},{1,9},{2,10},{3,11},{4,12},{5,13},{6,14},{7,15},{8,0},{9,1},... | collective-permute-start | bytes 331784 | tf_op jit(solution)/shard_map/ppermute | solution.py:41
  304.6 5.7 %collective-permute-start.51 = (bf16[48,1152]{1,0:T(8,128)(2,1)S(1)}, bf16[48,1152]{1,0:T(8,128)(2,1)S(1)}, u32[]{:S(2)}, u32[]{:S(2)}) collective-permute-start(bf16[48,1152]{1,0:T(8,128)(2,1)S(1)} %fusion.23), channel_id=1, source_target_pairs={{0,16},{1,17},{2,18},{3,19},{4,20},{5,21},{6,22},{7,23},{8,24},{9,... | collective-permute-start | bytes 331784 | tf_op jit(solution)/shard_map/ppermute | solution.py:41
  306.6 5.4 %collective-permute-start.52 = (bf16[48,1152]{1,0:T(8,128)(2,1)S(1)}, bf16[48,1152]{1,0:T(8,128)(2,1)S(1)}, u32[]{:S(2)}, u32[]{:S(2)}) collective-permute-start(bf16[48,1152]{1,0:T(8,128)(2,1)S(1)} %fusion.23), channel_id=1, source_target_pairs={{0,24},{1,25},{2,26},{3,27},{4,28},{5,29},{6,30},{7,31},{8,16},{9,... | collective-permute-start | bytes 331784 | tf_op jit(solution)/shard_map/ppermute | solution.py:41
  307.5 5.7 %collective-permute-start.56 = (bf16[2,48,1920]{2,1,0:T(8,128)(2,1)S(1)}, bf16[2,48,1920]{2,1,0:T(8,128)(2,1)S(1)}, u32[]{:S(2)}, u32[]{:S(2)}) collective-permute-start(bf16[2,48,1920]{2,1,0:T(8,128)(2,1)S(1)} %pad_maximum_fusion.6), channel_id=1, source_target_pairs={{0,8},{1,9},{2,10},{3,11},{4,12},{5,13},{6,14},{7,15},{8,0},{9,1},... | collective-permute-start | bytes 1105928 | tf_op jit(solution)/shard_map/ppermute | solution.py:41
  (44 other events, 331.0 us)

commit v3 on v2

--- a/solution.py
+++ b/solution.py
@@ -11,6 +11,9 @@
 AXES = ("rep", "fsdp")
 EPSILON = 1e-05
 TILE = 256
+FFN_TILE = 512
+PART = 256
+OFFSET = 1
 VMEM_BYTES = 60 * 1024 * 1024
 STEEP = 0.28
 TAIL = (0.11652066258099363, 0.06749752053058514, 0.2689081593014359, -0.23699088133158833, 0.38987234732742354, -0.10580781763400933)
@@ -34,6 +37,7 @@
         "z": [pairs(lambda y, c, z, x, m=m: (y, c, z ^ m, x)) for m in range(1, n_z)],
         "rep": [pairs(lambda y, c, z, x, m=m: (y ^ (m // 2), c ^ (m % 2), z, x)) for m in (1, 2, 3)],
         "x": pairs(lambda y, c, z, x: (y, c, z, 1 - x)),
+        "z_bits": [pairs(lambda y, c, z, x, b=b: (y, c, z ^ (1 << b), x)) for b in range(n_z.bit_length() - 1)],
     }
 
 
@@ -170,16 +174,16 @@
 ANY = pl.BlockSpec(memory_space=pl.ANY)
 
 
-def load(at_ref, refs, n_z, targets, relative=False):
+def load(at_ref, refs, n_z, targets, sides=(0, 1)):
     y, c, z, x = at_ref[0], at_ref[1], at_ref[2], at_ref[3]
-    per_side = len(refs) // 2
-    for side in (0, 1):
+    per_side = len(refs) // len(sides)
+    for number, side in enumerate(sides):
         core = jnp.bitwise_xor(c, side)
-        half = side if relative else core
-        pieces = refs[side * per_side : (side + 1) * per_side]
+        half = core if len(sides) > 1 else 0
+        pieces = refs[number * per_side : (number + 1) * per_side]
         rows = pieces[0].shape[0] // (2 * n_z)
         for first, cols, into, sem in targets:
-            lanes = pl.ds(pl.multiple_of(half * cols, 128), cols)
+            lanes = pl.ds(pl.multiple_of(half * cols, 128) if len(sides) > 1 else 0, cols)
             if per_side == 1:
                 pltpu.make_async_copy(pieces[0].at[:, pl.ds(first, cols)], into.at[:, lanes], sem).start()
                 continue
@@ -273,56 +277,62 @@
     )(at, packed)
 
 
-def attend_kernel(n_pair, len_ref, q_ref, k_ref, v_ref, *refs):
-    ctx_ref, inv_ref, p_ref = refs[-3:]
-    length = len_ref[pl.program_id(0) // n_pair]
-    query, keys, values = q_ref[...], k_ref[...], v_ref[...]
-    lane = lax.broadcasted_iota(jnp.int32, query.shape, 1)
-    row = lax.broadcasted_iota(jnp.int32, query.shape, 0)
-    unused = jnp.where(row >= length, -1e30, 0.0).astype(jnp.bfloat16)
-    zero, one = jnp.zeros_like(query), jnp.ones_like(query)
+def attend_kernel(docs, len_ref, q_ref, k_ref, v_ref, ctx_ref, inv_ref, p_ref):
+    seq = q_ref.shape[0] // docs
+    lane = lax.broadcasted_iota(jnp.int32, (seq, 128), 1)
+    row = lax.broadcasted_iota(jnp.int32, (seq, 128), 0)
     low = lane < 64
+    zero, one = jnp.zeros((seq, 128), jnp.bfloat16), jnp.ones((seq, 128), jnp.bfloat16)
+    heads = []
+    for doc in range(docs):
+        here = slice(doc * seq, (doc + 1) * seq)
+        query, keys, values = q_ref[here], k_ref[here], v_ref[here]
+        unused = jnp.where(row >= len_ref[doc], -1e30, 0.0).astype(jnp.bfloat16)
+        for head in (0, 1):
+            mine = low if head == 0 else ~low
+            spare = lane == 64 - 64 * head
+            left = jnp.where(mine, query, jnp.where(spare, one, zero))
+            heads.append((left, jnp.where(mine, keys, jnp.where(spare, unused, zero)), jnp.where(mine, values, one)))
+    later = dot_cols(*heads[0][:2])
     parts = []
-    for head in (0, 1):
-        mine = low if head == 0 else ~low
-        spare = lane == 64 - 64 * head
-        scores = dot_cols(
-            jnp.where(mine, query, jnp.where(spare, one, zero)), jnp.where(mine, keys, jnp.where(spare, unused, zero))
-        )
+    for i, (_, _, values) in enumerate(heads):
+        scores = later
+        if i + 1 < len(heads):
+            later = dot_cols(*heads[i + 1][:2])
+        doc, head = i // 2, i % 2
         expo = jnp.exp(scores - jnp.max(scores, axis=1, keepdims=True)).astype(jnp.bfloat16)
-        p_ref[head] = expo
-        parts.append(dot(expo, jnp.where(mine, values, one)))
-    inv = 1.0 / pltpu.roll(jnp.where(low, parts[1], parts[0]), 64, axis=1)
-    inv_ref[...] = inv
-    ctx_ref[...] = (jnp.where(low, parts[0], parts[1]) * inv).astype(jnp.bfloat16)
-
-
-def attend(half, lengths, qkv, before):
+        p_ref[doc, head] = expo
+        parts.append(dot(expo, values))
+        if head == 1:
+            here = slice(doc * seq, (doc + 1) * seq)
+            inv = 1.0 / pltpu.roll(jnp.where(low, parts[i], parts[i - 1]), 64, axis=1)
+            inv_ref[here] = inv
+            ctx_ref[here] = (jnp.where(low, parts[i - 1], parts[i]) * inv).astype(jnp.bfloat16)
+
+
+def attend(lengths, qkv):
     docs = lengths.shape[0]
     count, cols = qkv.shape[1:]
     seq, n_pair = count // docs, cols // 384
 
     def part(which):
-        return pl.BlockSpec((None, seq, 128), lambda i, *_: (half, i // n_pair, which * n_pair + i % n_pair))
-
-    def out():
-        return pl.BlockSpec((seq, 128), lambda i, *_: (i // n_pair, half * n_pair + i % n_pair))
-
+        return pl.BlockSpec((None, count, 128), lambda i, *_: (i // n_pair, 0, which * n_pair + i % n_pair))
+
+    out = pl.BlockSpec((count, 128), lambda i, *_: (0, i))
     return call(
-        functools.partial(attend_kernel, n_pair),
-        (docs * n_pair,),
-        [part(0), part(1), part(2)] + [ANY] * len(before),
-        [out(), out(), pl.BlockSpec((None, None, 2, seq, seq), lambda i, *_: (half, i, 0, 0, 0))],
+        functools.partial(attend_kernel, docs),
+        (2 * n_pair,),
+        [part(0), part(1), part(2)],
+        [out, out, pl.BlockSpec((None, None, docs, 2, seq, seq), lambda i, *_: (i // n_pair, i % n_pair, 0, 0, 0, 0))],
         [
             jax.ShapeDtypeStruct((count, 2 * cols // 3), jnp.bfloat16),
             jax.ShapeDtypeStruct((count, 2 * cols // 3), jnp.float32),
-            jax.ShapeDtypeStruct((2, docs * n_pair, 2, seq, seq), jnp.bfloat16),
+            jax.ShapeDtypeStruct((2, n_pair, docs, 2, seq, seq), jnp.bfloat16),
         ],
-        flops=docs * n_pair * 2 * seq * seq * 256 * 4,
+        flops=2 * docs * n_pair * 2 * seq * seq * 256 * 4,
         prefetch=1,
-        aliases={4 + i: i for i in range(len(before))},
         name="attend",
-    )(lengths, qkv, qkv, qkv, *before)
+    )(lengths, qkv, qkv, qkv)
 
 
 def norm(resid):
@@ -399,69 +409,98 @@
         loaded(wd_ref, sems.at[2])
 
     b_out, gain1, shift1, b_down, gain2, shift2 = wide_of(row_ref[...], 2, 3, 4, 5, 6, 7)
-    embed = x_ref[...].astype(jnp.float32) + dot_rows(flag_ref[...], row_ref[...])
-    normal1, inv1 = norm(embed + dot(ctx_ref[...], wo_ref[...]) + b_out)
-    normed = normal1 * gain1 + shift1
-    normed_low = normed.astype(jnp.bfloat16)
-    low_ref[...] = normed_low
-    branch = normed + b_down
-    for at in chunks:
-        cols = slice(at, at + width)
-        hidden = dot(normed_low, wi_ref[:, cols]) + b_in_ref[:, cols]
-        phi, slope = gelu_parts(hidden)
-        slope_ref[:, cols] = slope
-        activated = (hidden * phi).astype(jnp.bfloat16)
-        act_ref[:, cols] = activated
-        branch = branch + dot(activated, wd_ref[cols, :])
-    normal2, inv2 = norm(branch)
-    out_ref[...] = (normal2 * gain2 + shift2).astype(jnp.bfloat16)
-    grad = cot_ref[...].astype(jnp.float32)
-    dresid2 = norm_back(grad, normal2, inv2, gain2)
-    dbranch = dresid2.astype(jnp.bfloat16)
-    dbranch_ref[...] = dbranch
-    sums_ref[0:1] += sum_rows(grad * normal2)
-    sums_ref[1:2] += sum_rows(grad)
-    sums_ref[2:3] += sum_rows(dbranch.astype(jnp.float32))
-    dnormed = dresid2
-    for at in chunks:
-        cols = slice(at, at + width)
-        dhidden = (dot_cols(dbranch, wd_ref[cols, :]) * slope_ref[:, cols]).astype(jnp.bfloat16)
-        dhidden_ref[:, cols] = dhidden
-        in_sums_ref[0:1, cols] += sum_rows(dhidden.astype(jnp.float32))
-        dnormed = dnormed + dot_cols(dhidden, wi_ref[:, cols])
-    dresid1 = norm_back(dnormed, normal1, inv1, gain1)
-    dattn = dresid1.astype(jnp.bfloat16)
-    dresid_ref[...] = dresid1
-    dattn_ref[...] = dattn
-    sums_ref[3:4] += sum_rows(dnormed * normal1)
-    sums_ref[4:5] += sum_rows(dnormed)
-    sums_ref[5:6] += sum_rows(dattn.astype(jnp.float32))
-    dctx_ref[...] = dot_cols(dattn, wo_ref[...]).astype(jnp.bfloat16)
+
+    def chain(here):
+        flags = flag_ref[:, here]
+        embed = x_ref[here].astype(jnp.float32) + dot_rows(flags, row_ref[...])
+        resid1 = embed + dot(ctx_ref[here], wo_ref[...]) + b_out
+        yield
+        normal1, inv1 = norm(resid1)
+        normed = normal1 * gain1 + shift1
+        normed_low = normed.astype(jnp.bfloat16)
+        low_ref[here] = normed_low
+        branch = normed + b_down
+        yield
+        for at in chunks:
+            cols = slice(at, at + width)
+            hidden = dot(normed_low, wi_ref[:, cols]) + b_in_ref[:, cols]
+            phi, slope = gelu_parts(hidden)
+            slope_ref[here, cols] = slope
+            activated = (hidden * phi).astype(jnp.bfloat16)
+            act_ref[here, cols] = activated
+            branch = branch + dot(activated, wd_ref[cols, :])
+            yield
+        normal2, inv2 = norm(branch)
+        out_ref[here] = (normal2 * gain2 + shift2).astype(jnp.bfloat16)
+        grad = cot_ref[here].astype(jnp.float32)
+        dresid2 = norm_back(grad, normal2, inv2, gain2)
+        dbranch = dresid2.astype(jnp.bfloat16)
+        dbranch_ref[here] = dbranch
+        sums_ref[0:1] += sum_rows(grad * normal2)
+        sums_ref[1:2] += sum_rows(grad)
+        sums_ref[2:3] += sum_rows(dbranch.astype(jnp.float32))
+        dnormed = dresid2
+        yield
+        for at in chunks:
+            cols = slice(at, at + width)
+            dhidden = (dot_cols(dbranch, wd_ref[cols, :]) * slope_ref[here, cols]).astype(jnp.bfloat16)
+            dhidden_ref[here, cols] = dhidden
+            in_sums_ref[0:1, cols] += sum_rows(dhidden.astype(jnp.float32))
+            dnormed = dnormed + dot_cols(dhidden, wi_ref[:, cols])
+            yield
+        dresid1 = norm_back(dnormed, normal1, inv1, gain1)
+        dattn = dresid1.astype(jnp.bfloat16)
+        dresid_ref[here] = dresid1
+        dattn_ref[here] = dattn
+        sums_ref[3:4] += sum_rows(dnormed * normal1)
+        sums_ref[4:5] += sum_rows(dnormed)
+        sums_ref[5:6] += sum_rows(dattn.astype(jnp.float32))
+        rest = (dresid1 - dattn.astype(jnp.float32)).astype(jnp.bfloat16)
+        sums_ref[8:24] += dot(flags, dattn) + dot(flags, rest)
+        yield
+        dctx_ref[here] = dot_cols(dattn, wo_ref[...]).astype(jnp.bfloat16)
+
+    count = x_ref.shape[0] // PART
+    running = [chain(slice(i * PART, (i + 1) * PART)) for i in range(count)]
+    offset = OFFSET
+    step = 0
+    while running:
+        alive = []
+        for number, one in enumerate(running):
+            if step >= number * offset and next(one, "end") == "end":
+                continue
+            alive.append(one)
+        running = alive
+        step += 1
 
 
 def ffn(at, flags, x, ctx, cot, rows, b_in, mid, down, n_z):
     count, width = x.shape
     ff_width = b_in.shape[1]
     low = jax.ShapeDtypeStruct((count, width), jnp.bfloat16)
+
+    def rows_of(cols):
+        return pl.BlockSpec((FFN_TILE, cols), lambda i, *_: (i, 0))
+
     wide = jax.ShapeDtypeStruct((count, ff_width), jnp.bfloat16)
     return call(
         functools.partial(ffn_kernel, n_z, len(mid)),
-        (count // TILE,),
-        [FLAGS]
-        + [tiles(width)] * 3
+        (count // FFN_TILE,),
+        [pl.BlockSpec((16, FFN_TILE), lambda i, *_: (0, i))]
+        + [rows_of(width)] * 3
         + [whole((16, width)), whole((1, ff_width))]
         + [ANY] * (len(mid) + len(down)),
-        [tiles(width)] * 2
-        + [tiles(ff_width), tiles(width), tiles(ff_width)]
-        + [tiles(width)] * 3
-        + [whole((8, width)), whole((8, ff_width))],
+        [rows_of(width)] * 2
+        + [rows_of(ff_width), rows_of(width), rows_of(ff_width)]
+        + [rows_of(width)] * 3
+        + [whole((24, width)), whole((8, ff_width))],
         [low, low, wide, low, wide, low, jax.ShapeDtypeStruct((count, width), jnp.float32), low]
-        + [jax.ShapeDtypeStruct((8, width), jnp.float32), jax.ShapeDtypeStruct((8, ff_width), jnp.float32)],
+        + [jax.ShapeDtypeStruct((24, width), jnp.float32), jax.ShapeDtypeStruct((8, ff_width), jnp.float32)],
         [
             pltpu.VMEM((width, width), jnp.bfloat16),
             pltpu.VMEM((width, ff_width), jnp.bfloat16),
             pltpu.VMEM((ff_width, width), jnp.bfloat16),
-            pltpu.VMEM((TILE, ff_width), jnp.float32),
+            pltpu.VMEM((FFN_TILE, ff_width), jnp.float32),
             pltpu.SemaphoreType.DMA((3,)),
         ],
         4 * count * width * (width + 2 * ff_width),
@@ -470,7 +509,18 @@
     )(at, flags, x, ctx, cot, rows, b_in, *mid, *down)
 
 
-def grad_kernel(n_first, first_z, by_z, at_ref, *refs):
+def split_sum(at_ref, grad, got_ref, away_ref, stay_ref, sum_ref, lanes):
+    sum_ref[:, lanes] = (grad + got_ref[:, lanes].astype(jnp.float32)).astype(jnp.bfloat16)
+    y, c, x = at_ref[0], at_ref[1], at_ref[3]
+    rows = away_ref.shape[2]
+    for z in range(away_ref.shape[0]):
+        for b in (0, 1):
+            for ref, this_x, this_y in ((away_ref, 1 - x, 1 - y), (stay_ref, x, y)):
+                block = jnp.where(c == 0, this_x * 2 + b, b * 2 + this_y) + z * 4
+                ref[z, b, :, lanes] = sum_ref[pl.ds(pl.multiple_of(block * rows, rows), rows), lanes]
+
+
+def grad_kernel(n_first, first_z, at_ref, *refs):
     *lefts, got_ref, away_ref, stay_ref, sum_ref = refs if first_z else (*refs[:-1], None, None, refs[-1], None)
     step = pl.program_id(0)
 
@@ -480,14 +530,7 @@
         if not first_z:
             stay_ref[:, lanes] = grad.astype(jnp.bfloat16)
             return
-        sum_ref[:, lanes] = (grad + got_ref[:, lanes].astype(jnp.float32)).astype(jnp.bfloat16)
-        y, c, x = at_ref[0], at_ref[1], at_ref[3]
-        rows = away_ref.shape[2]
-        for z in range(by_z):
-            for b in (0, 1):
-                for ref, this_x, this_y in ((away_ref, 1 - x, 1 - y), (stay_ref, x, y)):
-                    block = jnp.where(c == 0, this_x * 2 + b, b * 2 + this_y) + z * 4
-                    ref[z, b, :, lanes] = sum_ref[pl.ds(pl.multiple_of(block * rows, rows), rows), lanes]
+        split_sum(at_ref, grad, got_ref, away_ref, stay_ref, sum_ref, lanes)
 
     if len(lefts) == 2:
         put(*lefts)
@@ -523,7 +566,7 @@
     shape = (tile, width) if tall else (rows, tile)
     spec = pl.BlockSpec(shape, (lambda i, *_: (i, 0)) if tall else (lambda i, *_: (0, i)))
     flops = 2 * count * rows * width
-    plain = functools.partial(grad_kernel, n_first, False, 0)
+    plain = functools.partial(grad_kernel, n_first, False)
     fused = got is not None and block % 16 == 0
     if not fused:
         grad = call(
@@ -538,7 +581,7 @@
         (by_z, 2, block, shape[1]), (lambda i, *_: (i, 0, 0, 0)) if tall else (lambda i, *_: (0, 0, 0, i))
     )
     return call(
-        functools.partial(grad_kernel, n_first, True, by_z),
+        functools.partial(grad_kernel, n_first, True),
         (steps,),
         specs + [spec],
         [split] * 2,
@@ -550,122 +593,135 @@
     )(at, *arrays, got)
 
 
-def attend_back_kernel(n_pair, half_ref, q_ref, k_ref, v_ref, ctx_ref, inv_ref, p_ref, dctx_ref, out_ref):
-    pair = pl.program_id(0) % n_pair
-    query, keys, values = q_ref[...], k_ref[...], v_ref[...]
-    lane = lax.broadcasted_iota(jnp.int32, query.shape, 1)
+def attend_back_kernel(
+    docs, fused, at_ref, q_ref, k_ref, v_ref, ctx_ref, inv_ref, p_ref, dctx_ref, low_ref, flag_ref, *refs
+):
+    got_ref, out_ref, sums_ref, *grads_ref = refs if fused else (None, *refs)
+    pair = pl.program_id(0)
+    seq = q_ref.shape[0] // docs
+    third = out_ref.shape[1] // 3
+    lane = lax.broadcasted_iota(jnp.int32, (seq, 128), 1)
     low = lane < 64
-    zero, one = jnp.zeros_like(query), jnp.ones_like(query)
-    dctx = (dctx_ref[...].astype(jnp.float32) * inv_ref[...]).astype(jnp.bfloat16)
-    product = dctx.astype(jnp.float32) * ctx_ref[...].astype(jnp.float32)
-    grads = []
-    for head in (0, 1):
-        mine = low if head == 0 else ~low
-        spare = lane == 64 - 64 * head
-        fine = lane == 65 - 64 * head
-        delta = jnp.sum(jnp.where(mine, product, 0.0), axis=1, keepdims=True)
-        coarse = delta.astype(jnp.bfloat16)
-        rest = (delta - coarse.astype(jnp.float32)).astype(jnp.bfloat16)
-        left = jnp.where(mine, dctx, jnp.where(spare, -coarse, jnp.where(fine, -rest, zero)))
-        expo = p_ref[head]
-        dprobs = dot_cols(left, jnp.where(mine, values, jnp.where(spare | fine, one, zero)))
-        dscores = (expo.astype(jnp.float32) * dprobs).astype(jnp.bfloat16)
-        grads.append((dot(dscores, keys) * 0.125, dot_rows(dscores, query), dot_rows(expo, dctx)))
-    third = out_ref.shape[1] // 3
-    for which in range(3):
-        grad = jnp.where(low, grads[0][which], grads[1][which]).astype(jnp.bfloat16)
-        out_ref[:, pl.ds(pl.multiple_of(which * third + pair * 128, 128), 128)] = grad
-
-
-def attend_back(half, docs, qkv, ctx, inv, expo, dctx):
+    zero, one = jnp.zeros((seq, 128), jnp.bfloat16), jnp.ones((seq, 128), jnp.bfloat16)
+    for doc in range(docs):
+        here = slice(doc * seq, (doc + 1) * seq)
+        query, keys, values = q_ref[here], k_ref[here], v_ref[here]
+        dctx = (dctx_ref[here].astype(jnp.float32) * inv_ref[here]).astype(jnp.bfloat16)
+        product = dctx.astype(jnp.float32) * ctx_ref[here].astype(jnp.float32)
+        grads = []
+        for head in (0, 1):
+            mine = low if head == 0 else ~low
+            spare = lane == 64 - 64 * head
+            fine = lane == 65 - 64 * head
+            delta = jnp.sum(jnp.where(mine, product, 0.0), axis=1, keepdims=True)
+            coarse = delta.astype(jnp.bfloat16)
+            rest = (delta - coarse.astype(jnp.float32)).astype(jnp.bfloat16)
+            left = jnp.where(mine, dctx, jnp.where(spare, -coarse, jnp.where(fine, -rest, zero)))
+            expo = p_ref[doc, head]
+            dprobs = dot_cols(left, jnp.where(mine, values, jnp.where(spare | fine, one, zero)))
+            dscores = (expo.astype(jnp.float32) * dprobs).astype(jnp.bfloat16)
+            grads.append((dot(dscores, keys) * 0.125, dot_rows(dscores, query), dot_rows(expo, dctx)))
+        for which in range(3):
+            grad = jnp.where(low, grads[0][which], grads[1][which]).astype(jnp.bfloat16)
+            out_ref[here, pl.ds(pl.multiple_of(which * third + pair * 128, 128), 128)] = grad
+
+    @pl.when(pair == pl.num_programs(0) - 1)
+    def _():
+        sums_ref[...] = dot(flag_ref[...], out_ref[...])
+        grad = dot_rows(low_ref[...], out_ref[...])
+        if fused:
+            split_sum(at_ref, grad, got_ref, *grads_ref, slice(0, 3 * third))
+        else:
+            grads_ref[0][...] = grad.astype(jnp.bfloat16)
+
+
+def attend_back(at, half, docs, qkv, ctx, inv, expo, dctx, low, flags, got, n_z):
     count, cols = qkv.shape[1:]
     seq, n_pair = count // docs, cols // 384
+    rows = low.shape[1]
 
     def part(which):
-        return pl.BlockSpec((None, seq, 128), lambda i, h: (h[0], i // n_pair, which * n_pair + i % n_pair))
-
-    one = pl.BlockSpec((seq, 128), lambda i, h: (i // n_pair, h[0] * n_pair + i % n_pair))
-    return call(
-        functools.partial(attend_back_kernel, n_pair),
-        (docs * n_pair,),
+        return pl.BlockSpec((None, count, 128), lambda i, at_ref: (at_ref[4], 0, which * n_pair + i))
+
+    one = pl.BlockSpec((count, 128), lambda i, at_ref: (0, at_ref[4] * n_pair + i))
+    block = rows // (4 * n_z)
+    fused = got is not None and block % 16 == 0
+    shape = (n_z, 2, block, cols) if fused else (rows, cols)
+    more = [whole((rows, cols))] if fused else []
+    dqkv, sums, *out = call(
+        functools.partial(attend_back_kernel, docs, fused),
+        (n_pair,),
         [part(0), part(1), part(2), one, one]
-        + [pl.BlockSpec((None, None, 2, seq, seq), lambda i, h: (h[0], i, 0, 0, 0)), one],
-        pl.BlockSpec((seq, cols), lambda i, h: (i // n_pair, 0)),
-        jax.ShapeDtypeStruct((count, cols), jnp.bfloat16),
-        flops=docs * n_pair * 2 * seq * seq * 256 * 10,
+        + [pl.BlockSpec((None, None, docs, 2, seq, seq), lambda i, at_ref: (at_ref[4], i, 0, 0, 0, 0)), one]
+        + [whole((count, rows)), whole((16, count))]
+        + more,
+        [whole((count, cols)), whole((16, cols))] + [whole(shape)] * (2 if fused else 1),
+        [jax.ShapeDtypeStruct((count, cols), jnp.bfloat16), jax.ShapeDtypeStruct((16, cols), jnp.float32)]
+        + [jax.ShapeDtypeStruct(shape, jnp.bfloat16)] * (2 if fused else 1),
+        [pltpu.VMEM((rows, cols), jnp.bfloat16)] if fused else (),
+        flops=docs * n_pair * 2 * seq * seq * 256 * 10 + 2 * count * rows * cols,
         prefetch=1,
         name="attend_back",
-    )(half, qkv, qkv, qkv, ctx, inv, expo, dctx)
-
-
-def embed_grad_kernel(n_z, at_ref, flag_ref, dresid_ref, mine_ref, theirs_ref, *refs):
-    pieces, (grad_ref, sums_ref, bias_ref, w_ref, sem) = refs[:-5], refs[-5:]
-    cols = mine_ref.shape[1]
-    start_sums(sums_ref, bias_ref)
+    )(jnp.concatenate([at, half]), qkv, qkv, qkv, ctx, inv, expo, dctx, low, flags, *([got] if fused else []))
+    if got is None or fused:
+        return dqkv, sums, *out
+    stay, away = sum_core(out[0], got, at, n_z)
+    return dqkv, sums, away, stay
+
+
+def embed_grad_kernel(n_z, side, at_ref, before_ref, dqkv_ref, *refs):
+    pieces, (out_ref, w_ref, sem) = refs[:-3], refs[-3:]
 
     @pl.when(pl.program_id(0) == 0)
     def _():
-        load(at_ref, pieces, n_z, [(0, cols, w_ref, sem)], relative=True)
+        load(at_ref, pieces, n_z, [(0, w_ref.shape[1], w_ref, sem)], (side,))
         loaded(w_ref, sem)
 
-    mine, theirs = mine_ref[...], theirs_ref[...]
-    dembed = dresid_ref[...] + dot_cols(mine, w_ref[:, :cols]) + dot_cols(theirs, w_ref[:, cols:])
-    coarse = dembed.astype(jnp.bfloat16)
-    grad_ref[...] = coarse
-    rest = (dembed - coarse.astype(jnp.float32)).astype(jnp.bfloat16)
-    sums_ref[...] += dot(flag_ref[...], coarse) + dot(flag_ref[...], rest)
-    bias_ref[0:1] += sum_rows(mine.astype(jnp.float32))
-    bias_ref[1:2] += sum_rows(theirs.astype(jnp.float32))
-
-
-def embed_grad(at, flags, dresid, mine, theirs, pieces, n_z):
-    count, width = dresid.shape
-    cols = mine.shape[1]
+    out_ref[...] = (before_ref[...] + dot_cols(dqkv_ref[...], w_ref[...])).astype(out_ref.dtype)
+
+
+def embed_grad(at, before, dqkv, side, pieces, n_z, dtype):
+    count, width = before.shape
+    cols = dqkv.shape[1]
     return call(
-        functools.partial(embed_grad_kernel, n_z),
+        functools.partial(embed_grad_kernel, n_z, side),
         (count // TILE,),
-        [FLAGS, tiles(width), tiles(cols), tiles(cols)] + [ANY] * len(pieces),
-        [tiles(width), whole((16, width)), whole((8, cols))],
-        [
-            jax.ShapeDtypeStruct((count, width), jnp.bfloat16),
-            jax.ShapeDtypeStruct((16, width), jnp.float32),
-            jax.ShapeDtypeStruct((8, cols), jnp.float32),
-        ],
-        [pltpu.VMEM((width, 2 * cols), jnp.bfloat16), pltpu.SemaphoreType.DMA],
-        4 * count * width * cols,
+        [tiles(width), tiles(cols)] + [ANY] * len(pieces),
+        tiles(width),
+        jax.ShapeDtypeStruct((count, width), dtype),
+        [pltpu.VMEM((width, cols), jnp.bfloat16), pltpu.SemaphoreType.DMA],
+        2 * count * width * cols,
         1,
         name="embed_grad",
-    )(at, flags, dresid, mine, theirs, *pieces)
-
-
-def pack_kernel(at_ref, sums_ref, in_ref, flag_ref, bias_ref, out_ref):
+    )(at, before, dqkv, *pieces)
+
+
+def pack_kernel(at_ref, sums_ref, in_ref, mine_ref, theirs_ref, out_ref):
     core = at_ref[1]
     width = sums_ref.shape[1]
     split = width // 2
-    bias = bias_ref[...]
-    mine, theirs = bias[0:1], bias[1:2]
+    mine, theirs = mine_ref[...], theirs_ref[...]
     low, high = jnp.where(core == 0, mine, theirs), jnp.where(core == 0, theirs, mine)
-    for row, cols in ((0, slice(0, split)), (1, slice(2 * split, 3 * split))):
-        out_ref[row : row + 1, :split] = low[:, cols]
-        out_ref[row : row + 1, split:] = high[:, cols]
-    for row, (ref, source) in enumerate(
-        ((sums_ref, 5), (sums_ref, 3), (sums_ref, 4), (flag_ref, 0), (flag_ref, 1), (sums_ref, 2), (sums_ref, 0), (sums_ref, 1)), 2
-    ):
-        out_ref[row : row + 1, :] = ref[source : source + 1, :]
-    out_ref[10:11, :] = jnp.zeros((1, width), jnp.float32)
+    out_ref[...] = jnp.zeros_like(out_ref)
+    places = [(0, 15, 0), (1, 15, 2)] + [(16 + 3 * flag + part, flag, part) for flag in (0, 1) for part in range(3)]
+    for row, flag, part in places:
+        cols = slice(part * split, (part + 1) * split)
+        out_ref[row : row + 1, :split] = low[flag : flag + 1, cols]
+        out_ref[row : row + 1, split:] = high[flag : flag + 1, cols]
+    for row, source in enumerate((5, 3, 4, 8, 9, 2, 0, 1), 2):
+        out_ref[row : row + 1, :] = sums_ref[source : source + 1, :]
     for i in range(4):
         out_ref[11 + i : 12 + i, :] = in_ref[0:1, i * width : (i + 1) * width]
-    out_ref[15:16, :] = jnp.zeros((1, width), jnp.float32)
-
-
-def pack(at, sums, in_sums, flag_sums, bias_sums):
+
+
+def pack(at, sums, in_sums, mine, theirs):
     return pl.pallas_call(
         pack_kernel,
         in_specs=[pl.BlockSpec(memory_space=pltpu.SMEM)] + [pl.BlockSpec(memory_space=pltpu.VMEM)] * 4,
         out_specs=pl.BlockSpec(memory_space=pltpu.VMEM),
-        out_shape=jax.ShapeDtypeStruct((16, sums.shape[1]), jnp.float32),
+        out_shape=jax.ShapeDtypeStruct((24, sums.shape[1]), jnp.float32),
         name="pack",
-    )(at, sums, in_sums, flag_sums, bias_sums)
+    )(at, sums, in_sums, mine, theirs)
 
 
 def body(
@@ -720,7 +776,7 @@
     got_attn, first_mid, packed = tie(got_attn, first_mid, packed)
     rows, bias, b_in = unpack(at, packed, own)
     flags = jnp.stack([masked.reshape(tok_count), replaced.reshape(tok_count)]).astype(jnp.bfloat16)
-    flags = jnp.concatenate([flags, jnp.zeros((14, tok_count), jnp.bfloat16)])
+    flags = jnp.concatenate([flags, jnp.zeros((13, tok_count), jnp.bfloat16), jnp.ones((1, tok_count), jnp.bfloat16)])
     x = layer_input.reshape(tok_count, width)
     cot = cotangent.reshape(tok_count, width)
     attn = grow(attn, got_attn)
@@ -730,28 +786,25 @@
     got_mid = send(mid, wires["first"])
     pieces = (attn, got_attn, send(attn, wires["core"]), send(got_attn, wires["core"]))
     got_down = send_all([first_down] * (n_z - 1), wires["z"])
-    got_mid, rows = tie(got_mid, rows)
+    got_mid, got_down, rows = tie(got_mid, got_down, rows)
     mid = grow(mid, got_mid)
-    rows, mid = tie(rows, mid)
+    down = jnp.concatenate([first_down] + got_down)
+    rows, mid, down = tie(rows, mid, down)
     got_mid = send(mid, wires["second"])
-    w_attn = sum(pieces_of(*pieces, at, n_z), ())
+    got_down = send(down, wires["first"])
+    own_attn, other_attn = pieces_of(*pieces, at, n_z)
+    w_attn = own_attn + other_attn
 
     qkv, embed_low = project(at, flags, x, rows, bias, w_attn, n_z)
     qkv, got_down = tie(qkv, got_down)
-    down = jnp.concatenate([first_down] + got_down)
+    down = grow(down, got_down)
     qkv, down = tie(qkv, down)
-    got_down = send(down, wires["first"])
+    got_down = send(down, wires["second"])
     other_mid = send(mid, wires["core"])
-    part = attend(0, lengths, qkv, ())
-    part, got_mid, got_down, other_mid = tie(part, got_mid, got_down, other_mid)
-    down = grow(down, got_down)
-    part, down = tie(part, down)
-    got_down = send(down, wires["second"])
     other_down = send(down, wires["core"])
-    w_mid = (mid, got_mid, other_mid, send(got_mid, wires["core"]))
-    ctx, inv, expo = attend(1, lengths, qkv, part)
-    ctx, w_mid, got_down, other_down = tie(ctx, w_mid, got_down, other_down)
-    w_mid = sum(pieces_of(*w_mid, at, n_z), ())
+    ctx, inv, expo = attend(lengths, qkv)
+    ctx, got_mid, got_down, other_mid, other_down = tie(ctx, got_mid, got_down, other_mid, other_down)
+    w_mid = sum(pieces_of(mid, got_mid, other_mid, send(got_mid, wires["core"]), at, n_z), ())
     w_back = sum(pieces_of(down, got_down, other_down, send(got_down, wires["core"]), at, n_z), ())
     out, normed_low, activated, dbranch, dhidden, dattn, dresid1, dctx, sums, in_sums = ffn(
         at, flags, x, ctx, cot, rows, b_in, w_mid, w_back, n_z
@@ -760,74 +813,78 @@
     mine, theirs = c[None], 1 - c[None]
     part_d = [(activated, dbranch, split)]
     part_m = [(normed_low, dhidden, ff_width // 2), (ctx, dattn, split)]
+    give_m = grads(at, theirs, part_m, None, n_z, width, "mid_give")
+    activated, give_m = tie(activated, give_m)
+    part_d = [(activated, dbranch, split)]
+    got_m = send(give_m, wires["core"])
     give_d = grads(at, theirs, part_d, None, n_z, width, "down_give")
-    dattn, give_d = tie(dattn, give_d)
-    part_m[1] = (ctx, dattn, split)
+    got_m, give_d = tie(got_m, give_d)
     got_d = send(give_d, wires["core"])
-    give_m = grads(at, theirs, part_m, None, n_z, width, "mid_give")
-    got_d, give_m = tie(got_d, give_m)
-    got_m = send(give_m, wires["core"])
+    give_m, keep_m = grads(at, mine, part_m, got_m, n_z, width, "mid_keep")
+    give_m, got_d = tie(give_m, got_d)
+    got_m = send(give_m, wires["second"])
     give_d, keep_d = grads(at, mine, part_d, got_d, n_z, width, "down_keep")
     give_d, dctx = tie(give_d, dctx)
     got_d = send(give_d, wires["second"])
-    dqkv_theirs = attend_back(theirs, doc_count, qkv, ctx, inv, expo, dctx)
-    got_d, got_m, dqkv_theirs = tie(got_d, got_m, dqkv_theirs)
+    dqkv_theirs, sums_theirs, give_a = attend_back(
+        at, theirs, doc_count, qkv, ctx, inv, expo, dctx, embed_low, flags, None, n_z
+    )
+    got_d, got_m, give_a = tie(got_d, got_m, give_a)
+    keep_m, give_m = sum_second(keep_m, got_m, at)
     keep_d, give_d = sum_second(keep_d, got_d, at)
-    give_d, got_m = tie(give_d, got_m)
+    give_m, give_d, give_a, dqkv_theirs = tie(give_m, give_d, give_a, dqkv_theirs)
+    got_m = send(give_m, wires["first"])
+    got_a = send(give_a, wires["core"])
+    dembed = embed_grad(at, dresid1, dqkv_theirs, 1, other_attn, n_z, jnp.float32)
+    got_m, got_a, dembed = tie(got_m, got_a, dembed)
+    keep_m, give_m = sum_first(keep_m, got_m, at)
+    give_m, give_d, got_a = tie(give_m, give_d, got_a)
+    got_m = send_all(give_m, wires["z"])
     got_d = send(give_d, wires["first"])
-    give_m, keep_m = grads(at, mine, part_m, got_m, n_z, width, "mid_keep")
-    got_d, give_m, dqkv_theirs = tie(got_d, give_m, dqkv_theirs)
-    got_m = send(give_m, wires["second"])
+    dqkv_mine, sums_mine, give_a, keep_a = attend_back(
+        at, mine, doc_count, qkv, ctx, inv, expo, dctx, embed_low, flags, got_a, n_z
+    )
+    got_d, got_m, give_a = tie(got_d, got_m, give_a)
+    got_a = send(give_a, wires["second"])
     keep_d, give_d = sum_first(keep_d, got_d, at)
-    give_d, dqkv_theirs = tie(give_d, dqkv_theirs)
+    packed = pack(at, sums, in_sums, sums_mine, sums_theirs)
+    give_d, packed, dqkv_mine = tie(give_d, packed, dqkv_mine)
     got_d = send_all(give_d, wires["z"])
-    give_a = grads(at, theirs, [(embed_low, dqkv_theirs, 3 * split)], None, n_z, 3 * split, "attn_give")
-    give_a, dctx = tie(give_a, dctx)
-    got_a = send(give_a, wires["core"])
-    dqkv_mine = attend_back(mine, doc_count, qkv, ctx, inv, expo, dctx)
-    got_d, got_m, got_a, dqkv_mine = tie(got_d, got_m, got_a, dqkv_mine)
-    keep_m, give_m = sum_second(keep_m, got_m, at)
+    got = send(packed, wires["x"])
+    grad_input = embed_grad(at, dembed, dqkv_mine, 0, own_attn, n_z, jnp.bfloat16)
+    owned_m = sum_z(keep_m, got_m)
+    got_a, got_d, got, grad_input, owned_m = tie(got_a, got_d, got, grad_input, owned_m)
+    keep_a, give_a = sum_second(keep_a, got_a, at)
+    packed = packed + got
+    give_a, packed, got_d = tie(give_a, packed, got_d)
+    got_a = send(give_a, wires["first"])
+    got_m = send(owned_m, wires["rep"][1])
+    for pairs in wires["z_bits"]:
+        packed = packed + send(packed, pairs)
     owned_d = sum_z(keep_d, got_d)
-    give_m, owned_d, got_a = tie(give_m, owned_d, got_a)
-    got_m = send(give_m, wires["first"])
-    give_a, keep_a = grads(at, mine, [(embed_low, dqkv_mine, 3 * split)], got_a, n_z, 3 * split, "attn_keep")
-    give_a, got_m = tie(give_a, got_m)
-    got_a = send(give_a, wires["second"])
-    keep_m, give_m = sum_first(keep_m, got_m, at)
-    give_m, dqkv_mine, owned_d = tie(give_m, dqkv_mine, owned_d)
-    got_m = send_all(give_m, wires["z"])
+    got_a, got_m, packed, owned_d = tie(got_a, got_m, packed, owned_d)
+    keep_a, give_a = sum_first(keep_a, got_a, at)
+    give_a, packed, owned_d = tie(give_a, packed, owned_d)
+    got_a = send_all(give_a, wires["z"])
     got_d = send(owned_d, wires["rep"][1])
-    grad_input, flag_sums, bias_sums = embed_grad(at, flags, dresid1, dqkv_mine, dqkv_theirs, w_attn, n_z)
-    got_d, got_a, flag_sums = tie(got_d, got_a, flag_sums)
-    keep_a, give_a = sum_second(keep_a, got_a, at)
-    packed = pack(at, sums, in_sums, flag_sums, bias_sums)
-    give_a, packed, got_m = tie(give_a, packed, got_m)
-    got_a = send(give_a, wires["first"])
-    got = send(packed, wires["x"])
+    pair_m = jnp.stack([owned_m, got_m])
+    for pairs in (wires["rep"][1], wires["core"]):
+        packed = packed + send(packed, pairs)
+    got_a, got_d, packed, pair_m = tie(got_a, got_d, packed, pair_m)
+    owned_a = sum_z(keep_a, got_a)
+    owned_a, packed, got_d, pair_m = tie(owned_a, packed, got_d, pair_m)
+    got_a = send_all([owned_a] * 3, wires["rep"])
     pair_d = jnp.stack([owned_d, got_d])
-    owned_m = sum_z(keep_m, got_m)
-    got_a, got, pair_d, owned_m = tie(got_a, got, pair_d, owned_m)
-    packed = packed + got
-    keep_a, give_a = sum_first(keep_a, got_a, at)
-    give_a, packed, pair_d, owned_m = tie(give_a, packed, pair_d, owned_m)
-    got_a = send_all(give_a, wires["z"])
-    got = send_all([packed] * (n_z - 1), wires["z"])
+    got_m = send(pair_m, wires["core"])
     got_d = send(pair_d, wires["core"])
-    got_m = send(owned_m, wires["rep"][1])
-    got_a, got, got_d, got_m = tie(got_a, got, got_d, got_m)
-    owned_a = sum_z(keep_a, got_a)
-    terms = jnp.stack([packed] + got)
-    packed = sum((pick(terms, 0, own // 2 ^ z) for z in range(1, n_z)), pick(terms, 0, own // 2))
-    pair_m = jnp.stack([owned_m, got_m])
-    owned_a, packed, pair_m = tie(owned_a, packed, pair_m)
-    got_a = send_all([owned_a] * 3, wires["rep"])
-    got = send_all([packed] * 3, wires["rep"])
-    got_m = send(pair_m, wires["core"])
-    terms = jnp.stack([packed] + got)
-    packed = sum((pick(terms, 0, rep ^ r) for r in range(1, 4)), pick(terms, 0, rep))
     o_small = lax.dynamic_slice(packed, (0, own * step), (16, step))
     o_b_in = lax.dynamic_slice(packed[11:15].reshape(ff_width), (own * (ff_width // n_fsdp),), (ff_width // n_fsdp,))
-    o_down, o_mid = blocks_of_pairs(pair_d, got_d, at), blocks_of_pairs(pair_m, got_m, at)
+    through = packed[16:22].reshape(2, 3 * width)
+    coarse = through.astype(jnp.bfloat16)
+    rest = (through - coarse.astype(jnp.float32)).astype(jnp.bfloat16)
+    through = dot_cols(coarse, w_qkv) + dot_cols(rest, w_qkv)
+    o_mask, o_repl = o_small[5] + through[0], o_small[6] + through[1]
+    o_mid, o_down = blocks_of_pairs(pair_m, got_m, at), blocks_of_pairs(pair_d, got_d, at)
     o_attn = blocks_of(owned_a, got_a, at)
 
     def join(blocks, cut=slice(None)):
@@ -844,8 +901,8 @@
         o_small[2],
         o_small[3],
         o_small[4],
-        o_small[5],
-        o_small[6],
+        o_mask,
+        o_repl,
         join(o_mid, slice(0, ff_width // 2)),
         o_b_in,
         join(o_down),

time: 317 us -> 316 us (level); the launches traced: 316 us -> 309 us
  Pallas kernels: 163 us -> 157 us
  waiting for transfers between devices: 62.1 us -> 58.4 us
  local copies, waits for them, and re-layouts: 10.8 us -> 14.2 us
    pallas_call x3 -> x2, Pallas kernels: 22.3 us -> 16.1 us  [grads(): call(plain, (steps,), specs, spec, jax.ShapeDtypeStruct((rows, width), jn...]
    unnamed x76 -> x84, local copies, waits for them, and re-layouts: 1.58 us -> 6.39 us
    ppermute x57 -> x55, waiting for transfers between devices: 62.1 us -> 58.4 us  [send(): return lax.ppermute(value, AXES, pairs)]
    pallas_call x9 -> x8, Pallas kernels: 127 us -> 128 us  [the longest x1 45.3 us: ffn(): call(functools.partial(ffn_kernel, n_z, len(mid)), (count // FFN_TILE,),...]
    ppermute x57 -> x55, starting transfers between devices: 61.1 us -> 60.8 us  [send(): return lax.ppermute(value, AXES, pairs)]
  transfers between devices with their start and end apart: 57 -> 55, of which waited for: 21 -> 22; matrix products, arithmetic and copies ran while one was open for 5% -> 6% of each run, Pallas kernels for 33% -> 34%
where the time goes in v3:
time: 316 us; the launch traced here: 309 us
  Pallas kernels  157 us (50%)
  starting transfers between devices  60.8 us (19%)
  waiting for transfers between devices  58.4 us (18%)
  other arithmetic  16.4 us (5%)
  local copies, waits for them, and re-layouts  14.2 us (4%)
    ppermute x55, starting transfers between devices, send(): return lax.ppermute(value, AXES, pairs)  60.8 us
    ppermute x55, waiting for transfers between devices, send(): return lax.ppermute(value, AXES, pairs)  58.4 us
    pallas_call x1, Pallas kernels, ffn(): call(functools.partial(ffn_kernel, n_z, len(mid)), (count // FFN_TILE,),...  45.3 us
    pallas_call x2, Pallas kernels, attend_back(): call(functools.partial(attend_back_kernel, docs, fused), (n_pair,), [part...  34.8 us
    pallas_call x2, Pallas kernels, grads(): call(functools.partial(grad_kernel, n_first, True), (steps,), specs + [sp...  17.2 us
    pallas_call x2, Pallas kernels, embed_grad(): call(functools.partial(embed_grad_kernel, n_z, side), (count // TILE,), [...  16.5 us
    pallas_call x2, Pallas kernels, grads(): call(plain, (steps,), specs, spec, jax.ShapeDtypeStruct((rows, width), jn...  16.1 us
    pallas_call x1, Pallas kernels, attend(): call(functools.partial(attend_kernel, docs), (2 * n_pair,), [part(0), par...  14.2 us
  transfers between devices with their start and end apart: 55, of which 22 were waited for; matrix products, arithmetic and copies ran while one was open for 6% of the time, Pallas kernels for 34%

profile of v3, /device:TPU:0, one launch (start us, length us, event | category | flops | bytes accessed | tf_op | source)
XLA Modules:
  0.0 309.4 jit_solution(5235885164802595049)
XLA Ops:
  2.0 3.1 collective-permute-start
  5.1 2.6 collective-permute-start.1
  9.7 6.8 %collective-permute-done.1 = bf16[48,1152]{1,0:T(8,128)(2,1)S(1)} collective-permute-done((bf16[48,1152]{1,0:T(8,128)(2,1)S(1)}, bf16[48,1152]{1,0:T(8,128)(2,1)S(1)}, u32[]{:S(2)}, u32[]{:S(2)}) %collective-permute-start.1) | collective-permute-done | bytes 110624 | tf_op jit(solution)/shard_map/ppermute | solution.py:45
  16.5 1.6 collective-permute-start.4
  18.1 1.5 collective-permute-start.3
  20.4 1.7 collective-permute-start.5
  22.1 1.4 collective-permute-start.6
  24.9 1.9 collective-permute-done.6
  26.8 2.3 collective-permute-done.7
  29.2 1.7 collective-permute-start.11
  32.1 3.1 %collective-permute-start.9 = (bf16[48,1920]{1,0:T(8,128)(2,1)S(1)}, bf16[48,1920]{1,0:T(8,128)(2,1)S(1)}, u32[]{:S(2)}, u32[]{:S(2)}) collective-permute-start(bf16[48,1920]{1,0:T(8,128)(2,1)S(1)} %pad_maximum_fusion.8), channel_id=1, source_target_pairs={{0,4},{1,5},{2,6},{3,7},{4,0},{5,1},{6,2},{7,3},{8,12},{9,13},{10,... | collective-permute-start | bytes 552968 | tf_op jit(solution)/shard_map/ppermute | solution.py:45
  36.7 1.6 unpack.1
  38.7 1.7 collective-permute-done.8
  40.4 4.6 %collective-permute-done.9 = bf16[48,1920]{1,0:T(8,128)(2,1)S(1)} collective-permute-done((bf16[48,1920]{1,0:T(8,128)(2,1)S(1)}, bf16[48,1920]{1,0:T(8,128)(2,1)S(1)}, u32[]{:S(2)}, u32[]{:S(2)}) %collective-permute-start.9) | collective-permute-done | bytes 184352 | tf_op jit(solution)/shard_map/ppermute | solution.py:45
  46.0 2.6 collective-permute-start.14
  48.6 1.8 collective-permute-start.15
  50.4 2.3 collective-permute-done.13
  52.7 7.2 %collective-permute-done.14 = bf16[192,384]{1,0:T(8,128)(2,1)S(1)} collective-permute-done((bf16[192,384]{1,0:T(8,128)(2,1)S(1)}, bf16[192,384]{1,0:T(8,128)(2,1)S(1)}, u32[]{:S(2)}, u32[]{:S(2)}) %collective-permute-start.14) | collective-permute-done | bytes 147488 | tf_op jit(solution)/shard_map/ppermute | solution.py:45
  65.1 10.1 %project.1 = (bf16[2,1024,1152]{2,1,0:T(8,128)(2,1)}, bf16[1024,768]{1,0:T(8,128)(2,1)}) custom-call(s32[4]{0:T(128)} %pad_add_fusion.at_ref, bf16[16,1024]{1,0:T(8,128)(2,1)} %maximum_maximum_fusion.3.flag_ref, bf16[1024,768]{1,0:T(8,128)(2,1)} %bitcast.204, bf16[16,768]{1,0:T(8,128)(2,1)} %get-tuple-element.150.row_ref, ...), custom_call_target="tpu_custom_call" | custom-call | flops 3623878656 | bytes 12582912 | tf_op jit(solution)/shard_map/project/pallas_call | solution.py:231
  78.7 14.2 %attend.1 = (bf16[1024,768]{1,0:T(8,128)(2,1)}, f32[1024,768]{1,0:T(8,128)}, bf16[2,3,2,2,512,512]{5,4,3,2,1,0:T(8,128)(2,1)}) custom-call(s32[2]{0:T(128)} %len_ref.1, bf16[2,1024,1152]{2,1,0:T(8,128)(2,1)} %get-tuple-element.157.q_ref.k_ref.v_ref, bf16[2,1024,1152]{2,1,0:T(8,128)(2,1)} %get-tuple-element.157.q_ref.k_ref.v_ref, ...), custom_call_target="tpu_custom_call" | custom-call | flops 6442450944 | bytes 34603008 | tf_op jit(solution)/shard_map/attend/pallas_call | solution.py:322
  92.9 4.0 %collective-permute-done.20.refs_5_ = bf16[1536,384]{1,0:T(8,128)(2,1)S(1)} collective-permute-done((bf16[1536,384]{1,0:T(8,128)(2,1)S(1)}, bf16[1536,384]{1,0:T(8,128)(2,1)S(1)}, u32[]{:S(2)}, u32[]{:S(2)}) %collective-permute-start.20) | collective-permute-done | bytes 1179680 | tf_op jit(solution)/shard_map/ppermute | solution.py:45
  99.9 4.2 %collective-permute-done.24.refs_7_ = bf16[1536,384]{1,0:T(8,128)(2,1)S(1)} collective-permute-done((bf16[1536,384]{1,0:T(8,128)(2,1)}, bf16[1536,384]{1,0:T(8,128)(2,1)S(1)}, u32[]{:S(2)}, u32[]{:S(2)}) %collective-permute-start.24) | collective-permute-done | bytes 1179680 | tf_op jit(solution)/shard_map/ppermute | solution.py:45
  105.7 45.3 %ffn.1 = (bf16[1024,768]{1,0:T(8,128)(2,1)}, bf16[1024,768]{1,0:T(8,128)(2,1)}, bf16[1024,3072]{1,0:T(8,128)(2,1)}, bf16[1024,768]{1,0:T(8,128)(2,1)}, bf16[1024...) custom-call(s32[4]{0:T(128)} %pad_add_fusion.at_ref, ...), custom_call_target="tpu_custom_call" | custom-call | flops 21743271936 | bytes 47529984 | tf_op jit(solution)/shard_map/ffn/pallas_call | solution.py:486
  151.0 8.2 %mid_give.1 = bf16[768,1920]{1,0:T(8,128)(2,1)} custom-call(s32[5]{0:T(128)} %concatenate.169.at_ref, bf16[1024,768]{1,0:T(8,128)(2,1)} %get-tuple-element.168.refs_0_, bf16[1024,3072]{1,0:T(8,128)(2,1)} %get-tuple-element.169.refs_1_, bf16[1024,768]{1,0:T(8,128)(2,1)} %get-tuple-element.161.ctx_ref.refs_2_, bf16[1024,768]{1,0:T(8,128)(2,1)} %get-tuple-element.170.refs_3_), custom_call_target="tpu_custom_call" | custom-call | flops 3019898880 | bytes 5898240 | tf_op jit(solution)/shard_map/mid_give/pallas_call | solution.py:572
  159.5 7.9 %down_give.1 = bf16[3072,384]{1,0:T(8,128)(2,1)} custom-call(s32[5]{0:T(128)} %concatenate.169.at_ref, bf16[1024,3072]{1,0:T(8,128)(2,1)} %get-tuple-element.173.refs_0_, bf16[1024,768]{1,0:T(8,128)(2,1)} %get-tuple-element.174.refs_1_), custom_call_target="tpu_custom_call" | custom-call | flops 2415919104 | bytes 4718592 | tf_op jit(solution)/shard_map/down_give/pallas_call | solution.py:572
  169.0 8.9 %mid_keep.1 = (bf16[4,2,48,1920]{3,2,1,0:T(8,128)(2,1)}, bf16[4,2,48,1920]{3,2,1,0:T(8,128)(2,1)}) custom-call(s32[5]{0:T(128)} %concatenate.168.at_ref, bf16[1024,768]{1,0:T(8,128)(2,1)} %get-tuple-element.168.refs_0_, bf16[1024,3072]{1,0:T(8,128)(2,1)} %get-tuple-element.169.refs_1_, bf16[1024,768]{1,0:T(8,128)(2,1)} %get-tuple-element.161.ctx_ref.refs_2_, ...), custom_call_target="tpu_custom_call" | custom-call | flops 3019898880 | bytes 5898240 | tf_op jit(solution)/shard_map/mid_keep/pallas_call | solution.py:583
  179.0 8.4 %down_keep.1 = (bf16[4,2,192,384]{3,2,1,0:T(8,128)(2,1)}, bf16[4,2,192,384]{3,2,1,0:T(8,128)(2,1)}) custom-call(s32[5]{0:T(128)} %concatenate.168.at_ref, bf16[1024,3072]{1,0:T(8,128)(2,1)} %get-tuple-element.173.refs_0_, bf16[1024,768]{1,0:T(8,128)(2,1)} %get-tuple-element.174.refs_1_, bf16[3072,384]{1,0:T(8,128)(2,1)} %collective-permute-done.26.refs_2_), custom_call_target="tpu_custom_call" | custom-call | flops 2415919104 | bytes 4718592 | tf_op jit(solution)/shard_map/down_keep/pallas_call | solution.py:583
  189.8 17.1 %attend_back.2 = (bf16[1024,1152]{1,0:T(8,128)(2,1)}, f32[16,1152]{1,0:T(8,128)}, bf16[768,1152]{1,0:T(8,128)(2,1)}) custom-call(s32[5]{0:T(128)} %concatenate.169.at_ref, bf16[2,1024,1152]{2,1,0:T(8,128)(2,1)} %get-tuple-element.157.q_ref.k_ref.v_ref, bf16[2,1024,1152]{2,1,0:T(8,128)(2,1)} %get-tuple-element.157.q_ref.k_ref.v_ref, ...), custom_call_target="tpu_custom_call" | custom-call | flops 9865003008 | bytes 8404992 | tf_op jit(solution)/shard_map/attend_back/pallas_call | solution.py:651
  206.9 3.3 %collective-permute-done.27 = bf16[4,2,192,384]{3,2,0,1:T(8,128)(2,1)} collective-permute-done((bf16[4,2,192,384]{3,2,0,1:T(8,128)(2,1)S(1)}, bf16[4,2,192,384]{3,2,0,1:T(8,128)(2,1)}, u32[]{:S(2)}, u32[]{:S(2)}) %collective-permute-start.27) | collective-permute-done | bytes 1179680 | tf_op jit(solution)/shard_map/ppermute | solution.py:45
  213.4 8.4 %embed_grad.2.before_ref = f32[1024,768]{1,0:T(8,128)} custom-call(s32[4]{0:T(128)} %pad_add_fusion.at_ref, f32[1024,768]{1,0:T(8,128)} %get-tuple-element.196.before_ref, bf16[1024,1152]{1,0:T(8,128)(2,1)} %get-tuple-element.197.dqkv_ref, bf16[384,1152]{1,0:T(8,128)(2,1)} %copy-done.10, bf16[384,1152]{1,0:T(8,128)(2,1)} %copy-done.11), custom_call_target="tpu_custom_call" | custom-call | flops 1811939328 | bytes 6291456 | tf_op jit(solution)/shard_map/embed_grad/pallas_call | solution.py:686
  221.8 1.7 collective-permute-done.29
  225.8 3.5 %collective-permute-start.32 = (bf16[48,1920]{1,0:T(8,128)(2,1)}, bf16[48,1920]{1,0:T(8,128)(2,1)S(1)}, u32[]{:S(2)}, u32[]{:S(2)}) collective-permute-start(bf16[48,1920]{1,0:T(8,128)(2,1)} %get-tuple-element.202), channel_id=1, source_target_pairs={{0,2},{1,3},{2,0},{3,1},{4,6},{5,7},{6,4},{7,5},{8,10},{9,11},{10,... | collective-permute-start | bytes 552968 | tf_op jit(solution)/shard_map/ppermute | solution.py:45
  229.9 1.8 collective-permute-start.34
  231.7 17.7 %attend_back.3 = (bf16[1024,1152]{1,0:T(8,128)(2,1)}, f32[16,1152]{1,0:T(8,128)}, bf16[4,2,48,1152]{3,2,1,0:T(8,128)(2,1)}, bf16[4,2,48,1152]{3,2,1,0:T(8,128)(2,1)}) custom-call(s32[5]{0:T(128)} %concatenate.168.at_ref, bf16[2,1024,1152]{2,1,0:T(8,128)(2,1)} %get-tuple-element.157.q_ref.k_ref.v_ref, ...), custom_call_target="tpu_custom_call" | custom-call | flops 9865003008 | bytes 8404992 | tf_op jit(solution)/shard_map/attend_back/pallas_call | solution.py:651
  252.0 1.7 pack.1
  253.7 1.9 fusion.43
  258.1 1.8 collective-permute-start.38
  262.5 8.1 %embed_grad.3 = bf16[1024,768]{1,0:T(8,128)(2,1)} custom-call(s32[4]{0:T(128)} %pad_add_fusion.at_ref, f32[1024,768]{1,0:T(8,128)} %embed_grad.2.before_ref, bf16[1024,1152]{1,0:T(8,128)(2,1)} %get-tuple-element.219.dqkv_ref, bf16[384,1152]{1,0:T(8,128)(2,1)} %copy-done.2, bf16[384,1152]{1,0:T(8,128)(2,1)} %copy-done.8), custom_call_target="tpu_custom_call" | custom-call | flops 1811939328 | bytes 3145728 | tf_op jit(solution)/shard_map/embed_grad/pallas_call | solution.py:686
  274.2 2.0 collective-permute-done.42
  276.2 1.9 collective-permute-start.43
  279.2 3.2 %collective-permute-done.43 = f32[24,768]{1,0:T(8,128)S(1)} collective-permute-done((f32[24,768]{1,0:T(8,128)S(1)}, f32[24,768]{1,0:T(8,128)S(1)}, u32[]{:S(2)}, u32[]{:S(2)}) %collective-permute-start.43) | collective-permute-done | bytes 73760 | tf_op jit(solution)/shard_map/ppermute | solution.py:45
  282.4 2.8 collective-permute-done.41
  286.0 1.5 collective-permute-start.47
  287.5 2.6 collective-permute-start.45
  290.1 1.8 collective-permute-start.46
  293.4 3.3 %collective-permute-done.46 = bf16[48,1152]{1,0:T(8,128)(2,1)S(1)} collective-permute-done((bf16[48,1152]{1,0:T(8,128)(2,1)S(1)}, bf16[48,1152]{1,0:T(8,128)(2,1)S(1)}, u32[]{:S(2)}, u32[]{:S(2)}) %collective-permute-start.46) | collective-permute-done | bytes 110624 | tf_op jit(solution)/shard_map/ppermute | solution.py:45
  301.2 1.6 collective-permute-done.51
  302.8 1.5 collective-permute-done.52
  (233 shorter events, 57.8 us)
Async XLA Ops:
  2.0 7.7 %collective-permute-start = (bf16[48,1152]{1,0:T(8,128)(2,1)S(1)}, bf16[48,1152]{1,0:T(8,128)(2,1)S(1)}, u32[]{:S(2)}, u32[]{:S(2)}) collective-permute-start(bf16[48,1152]{1,0:T(8,128)(2,1)S(1)} %pad_maximum_fusion.9), channel_id=1, source_target_pairs={{0,2},{1,3},{2,0},{3,1},{4,6},{5,7},{6,4},{7,5},{8,10},{9,11},{10,... | collective-permute-start | bytes 331784 | tf_op jit(solution)/shard_map/ppermute | solution.py:45
  5.1 11.3 %collective-permute-start.1 = (bf16[48,1152]{1,0:T(8,128)(2,1)S(1)}, bf16[48,1152]{1,0:T(8,128)(2,1)S(1)}, u32[]{:S(2)}, u32[]{:S(2)}) collective-permute-start(bf16[48,1152]{1,0:T(8,128)(2,1)S(1)} %pad_maximum_fusion.9), channel_id=1, source_target_pairs={{0,4},{1,5},{2,6},{3,7},{4,0},{5,1},{6,2},{7,3},{8,12},{9,13},{10,... | collective-permute-start | bytes 331784 | tf_op jit(solution)/shard_map/ppermute | solution.py:45
  7.7 8.8 %collective-permute-start.2 = (bf16[48,1152]{1,0:T(8,128)(2,1)S(1)}, bf16[48,1152]{1,0:T(8,128)(2,1)S(1)}, u32[]{:S(2)}, u32[]{:S(2)}) collective-permute-start(bf16[48,1152]{1,0:T(8,128)(2,1)S(1)} %pad_maximum_fusion.9), channel_id=1, source_target_pairs={{0,6},{1,7},{2,4},{3,5},{4,2},{5,3},{6,0},{7,1},{8,14},{9,15},{10,... | collective-permute-start | bytes 331784 | tf_op jit(solution)/shard_map/ppermute | solution.py:45
  18.1 11.0 %collective-permute-start.3 = (bf16[192,1152]{1,0:T(8,128)(2,1)S(1)}, bf16[192,1152]{1,0:T(8,128)(2,1)S(1)}, u32[]{:S(2)}, u32[]{:S(2)}) collective-permute-start(bf16[192,1152]{1,0:T(8,128)(2,1)S(1)} %pad_maximum_fusion.4), channel_id=1, source_target_pairs={{0,16},{1,17},{2,18},{3,19},{4,20},{5,21},{6,22},{7,23},{8,9},{9,8... | collective-permute-start | bytes 1327112 | tf_op jit(solution)/shard_map/ppermute | solution.py:45
  23.6 5.5 %collective-permute-start.7 = (f32[2,16,96]{2,1,0:T(8,128)S(1)}, f32[2,16,96]{2,1,0:T(8,128)S(1)}, u32[]{:S(2)}, u32[]{:S(2)}) collective-permute-start(f32[2,16,96]{2,1,0:T(8,128)S(1)} %get-tuple-element.309), channel_id=1, source_target_pairs={{0,6},{1,7},{2,4},{3,5},{4,2},{5,3},{6,0},{7,1},{8,14},{9,15},{10,... | collective-permute-start | bytes 36872 | tf_op jit(solution)/shard_map/ppermute | solution.py:45
  29.2 15.9 %collective-permute-start.11 = (bf16[384,1152]{1,0:T(8,128)(2,1)S(1)}, bf16[384,1152]{1,0:T(8,128)(2,1)S(1)}, u32[]{:S(2)}, u32[]{:S(2)}) collective-permute-start(bf16[384,1152]{1,0:T(8,128)(2,1)S(1)} %constant_dynamic-update-slice_fusion.7.refs_0_), channel_id=1, source_target_pairs={{0,1},{1,0},{2,3},{3,2},{4,5},{5,4},{6,7},{7,6},{8,24},{9,25},{10,... | collective-permute-start | bytes 2654216 | tf_op jit(solution)/shard_map/ppermute | solution.py:45
  30.8 7.8 %collective-permute-start.10 = (bf16[48,1920]{1,0:T(8,128)(2,1)S(1)}, bf16[48,1920]{1,0:T(8,128)(2,1)S(1)}, u32[]{:S(2)}, u32[]{:S(2)}) collective-permute-start(bf16[48,1920]{1,0:T(8,128)(2,1)S(1)} %pad_maximum_fusion.8), channel_id=1, source_target_pairs={{0,6},{1,7},{2,4},{3,5},{4,2},{5,3},{6,0},{7,1},{8,14},{9,15},{10,... | collective-permute-start | bytes 552968 | tf_op jit(solution)/shard_map/ppermute | solution.py:45
  32.1 8.3 %collective-permute-start.8 = (bf16[48,1920]{1,0:T(8,128)(2,1)S(1)}, bf16[48,1920]{1,0:T(8,128)(2,1)S(1)}, u32[]{:S(2)}, u32[]{:S(2)}) collective-permute-start(bf16[48,1920]{1,0:T(8,128)(2,1)S(1)} %pad_maximum_fusion.8), channel_id=1, source_target_pairs={{0,2},{1,3},{2,0},{3,1},{4,6},{5,7},{6,4},{7,5},{8,10},{9,11},{10,... | collective-permute-start | bytes 552968 | tf_op jit(solution)/shard_map/ppermute | solution.py:45
  32.1 12.9 %collective-permute-start.9 = (bf16[48,1920]{1,0:T(8,128)(2,1)S(1)}, bf16[48,1920]{1,0:T(8,128)(2,1)S(1)}, u32[]{:S(2)}, u32[]{:S(2)}) collective-permute-start(bf16[48,1920]{1,0:T(8,128)(2,1)S(1)} %pad_maximum_fusion.8), channel_id=1, source_target_pairs={{0,4},{1,5},{2,6},{3,7},{4,0},{5,1},{6,2},{7,3},{8,12},{9,13},{10,... | collective-permute-start | bytes 552968 | tf_op jit(solution)/shard_map/ppermute | solution.py:45
  45.1 14.9 %collective-permute-start.12 = (bf16[192,1920]{1,0:T(8,128)(2,1)S(1)}, bf16[192,1920]{1,0:T(8,128)(2,1)S(1)}, u32[]{:S(2)}, u32[]{:S(2)}) collective-permute-start(bf16[192,1920]{1,0:T(8,128)(2,1)S(1)} %pad_maximum_fusion.2), channel_id=1, source_target_pairs={{0,16},{1,17},{2,18},{3,19},{4,20},{5,21},{6,22},{7,23},{8,9},{9,8... | collective-permute-start | bytes 2211848 | tf_op jit(solution)/shard_map/ppermute | solution.py:45
  46.0 6.7 %collective-permute-start.13 = (bf16[192,384]{1,0:T(8,128)(2,1)S(1)}, bf16[192,384]{1,0:T(8,128)(2,1)S(1)}, u32[]{:S(2)}, u32[]{:S(2)}) collective-permute-start(bf16[192,384]{1,0:T(8,128)(2,1)S(1)} %dynamic_slice.191), channel_id=1, source_target_pairs={{0,2},{1,3},{2,0},{3,1},{4,6},{5,7},{6,4},{7,5},{8,10},{9,11},{10,... | collective-permute-start | bytes 442376 | tf_op jit(solution)/shard_map/ppermute | solution.py:45
  46.0 17.2 %collective-permute-start.16 = (bf16[384,1152]{1,0:T(8,128)(2,1)S(1)}, bf16[384,1152]{1,0:T(8,128)(2,1)S(1)}, u32[]{:S(2)}, u32[]{:S(2)}) collective-permute-start(bf16[384,1152]{1,0:T(8,128)(2,1)S(1)} %constant_dynamic-update-slice_fusion.7.refs_0_), channel_id=1, source_target_pairs={{0,8},{1,9},{2,10},{3,11},{4,12},{5,13},{6,14},{7,15},{8,0},{9,1},... | collective-permute-start | bytes 2654216 | tf_op jit(solution)/shard_map/ppermute | solution.py:45
  46.0 13.9 %collective-permute-start.14 = (bf16[192,384]{1,0:T(8,128)(2,1)S(1)}, bf16[192,384]{1,0:T(8,128)(2,1)S(1)}, u32[]{:S(2)}, u32[]{:S(2)}) collective-permute-start(bf16[192,384]{1,0:T(8,128)(2,1)S(1)} %dynamic_slice.191), channel_id=1, source_target_pairs={{0,4},{1,5},{2,6},{3,7},{4,0},{5,1},{6,2},{7,3},{8,12},{9,13},{10,... | collective-permute-start | bytes 442376 | tf_op jit(solution)/shard_map/ppermute | solution.py:45
  48.6 11.3 %collective-permute-start.15 = (bf16[192,384]{1,0:T(8,128)(2,1)S(1)}, bf16[192,384]{1,0:T(8,128)(2,1)S(1)}, u32[]{:S(2)}, u32[]{:S(2)}) collective-permute-start(bf16[192,384]{1,0:T(8,128)(2,1)S(1)} %dynamic_slice.191), channel_id=1, source_target_pairs={{0,6},{1,7},{2,4},{3,5},{4,2},{5,3},{6,0},{7,1},{8,14},{9,15},{10,... | collective-permute-start | bytes 442376 | tf_op jit(solution)/shard_map/ppermute | solution.py:45
  52.7 10.5 %collective-permute-start.17 = (bf16[384,1152]{1,0:T(8,128)(2,1)S(1)}, bf16[384,1152]{1,0:T(8,128)(2,1)S(1)}, u32[]{:S(2)}, u32[]{:S(2)}) collective-permute-start(bf16[384,1152]{1,0:T(8,128)(2,1)S(1)} %collective-permute-done.11.refs_1_), channel_id=1, source_target_pairs={{0,8},{1,9},{2,10},{3,11},{4,12},{5,13},{6,14},{7,15},{8,0},{9,1},... | collective-permute-start | bytes 2654216 | tf_op jit(solution)/shard_map/ppermute | solution.py:45
  60.2 16.4 %collective-permute-start.18 = (bf16[768,384]{1,0:T(8,128)(2,1)S(1)}, bf16[768,384]{1,0:T(8,128)(2,1)}, u32[]{:S(2)}, u32[]{:S(2)}) collective-permute-start(bf16[768,384]{1,0:T(8,128)(2,1)S(1)} %pad_maximum_fusion.3), channel_id=1, source_target_pairs={{0,16},{1,17},{2,18},{3,19},{4,20},{5,21},{6,22},{7,23},{8,9},{9,8... | collective-permute-start | bytes 1769480 | tf_op jit(solution)/shard_map/ppermute | solution.py:45
  62.4 30.5 %collective-permute-start.19 = (bf16[384,1920]{1,0:T(8,128)(2,1)S(1)}, bf16[384,1920]{1,0:T(8,128)(2,1)}, u32[]{:S(2)}, u32[]{:S(2)}) collective-permute-start(bf16[384,1920]{1,0:T(8,128)(2,1)S(1)} %pad_maximum_fusion.refs_0_), channel_id=1, source_target_pairs={{0,1},{1,0},{2,3},{3,2},{4,5},{5,4},{6,7},{7,6},{8,24},{9,25},{10,... | collective-permute-start | bytes 4423688 | tf_op jit(solution)/shard_map/ppermute | solution.py:45
  63.2 29.7 %collective-permute-start.21 = (bf16[384,1920]{1,0:T(8,128)(2,1)S(1)}, bf16[384,1920]{1,0:T(8,128)(2,1)}, u32[]{:S(2)}, u32[]{:S(2)}) collective-permute-start(bf16[384,1920]{1,0:T(8,128)(2,1)S(1)} %pad_maximum_fusion.refs_0_), channel_id=1, source_target_pairs={{0,8},{1,9},{2,10},{3,11},{4,12},{5,13},{6,14},{7,15},{8,0},{9,1},... | collective-permute-start | bytes 4423688 | tf_op jit(solution)/shard_map/ppermute | solution.py:45
  77.8 19.2 %collective-permute-start.20 = (bf16[1536,384]{1,0:T(8,128)(2,1)S(1)}, bf16[1536,384]{1,0:T(8,128)(2,1)S(1)}, u32[]{:S(2)}, u32[]{:S(2)}) collective-permute-start(bf16[1536,384]{1,0:T(8,128)(2,1)S(1)} %pad_maximum_fusion.1.refs_4_), channel_id=1, source_target_pairs={{0,1},{1,0},{2,3},{3,2},{4,5},{5,4},{6,7},{7,6},{8,24},{9,25},{10,... | collective-permute-start | bytes 3538952 | tf_op jit(solution)/shard_map/ppermute | solution.py:45
  78.7 18.2 %collective-permute-start.22 = (bf16[1536,384]{1,0:T(8,128)(2,1)S(1)}, bf16[1536,384]{1,0:T(8,128)(2,1)}, u32[]{:S(2)}, u32[]{:S(2)}) collective-permute-start(bf16[1536,384]{1,0:T(8,128)(2,1)S(1)} %pad_maximum_fusion.1.refs_4_), channel_id=1, source_target_pairs={{0,8},{1,9},{2,10},{3,11},{4,12},{5,13},{6,14},{7,15},{8,0},{9,1},... | collective-permute-start | bytes 3538952 | tf_op jit(solution)/shard_map/ppermute | solution.py:45
  98.0 6.2 %collective-permute-start.23 = (bf16[384,1920]{1,0:T(8,128)(2,1)}, bf16[384,1920]{1,0:T(8,128)(2,1)S(1)}, u32[]{:S(2)}, u32[]{:S(2)}) collective-permute-start(bf16[384,1920]{1,0:T(8,128)(2,1)} %collective-permute-done.19.refs_1_), channel_id=1, source_target_pairs={{0,8},{1,9},{2,10},{3,11},{4,12},{5,13},{6,14},{7,15},{8,0},{9,1},... | collective-permute-start | bytes 4423688 | tf_op jit(solution)/shard_map/ppermute | solution.py:45
  159.1 8.3 %collective-permute-start.25 = (bf16[768,1920]{1,0:T(8,128)(2,1)}, bf16[768,1920]{1,0:T(8,128)(2,1)S(1)}, u32[]{:S(2)}, u32[]{:S(2)}) collective-permute-start(bf16[768,1920]{1,0:T(8,128)(2,1)} %mid_give.1), channel_id=1, source_target_pairs={{0,8},{1,9},{2,10},{3,11},{4,12},{5,13},{6,14},{7,15},{8,0},{9,1},... | collective-permute-start | bytes 8847368 | tf_op jit(solution)/shard_map/ppermute | solution.py:45
  167.4 10.4 %collective-permute-start.26 = (bf16[3072,384]{1,0:T(8,128)(2,1)}, bf16[3072,384]{1,0:T(8,128)(2,1)}, u32[]{:S(2)}, u32[]{:S(2)}) collective-permute-start(bf16[3072,384]{1,0:T(8,128)(2,1)} %down_give.1), channel_id=1, source_target_pairs={{0,8},{1,9},{2,10},{3,11},{4,12},{5,13},{6,14},{7,15},{8,0},{9,1},... | collective-permute-start | bytes 7077896 | tf_op jit(solution)/shard_map/ppermute | solution.py:45
  177.9 32.4 %collective-permute-start.28 = (bf16[4,2,48,1920]{3,2,1,0:T(8,128)(2,1)}, bf16[4,2,48,1920]{3,2,1,0:T(8,128)(2,1)S(1)}, u32[]{:S(2)}, u32[]{:S(2)}) collective-permute-start(bf16[4,2,48,1920]{3,2,1,0:T(8,128)(2,1)} %get-tuple-element.183), channel_id=1, source_target_pairs={{0,1},{1,0},{2,3},{3,2},{4,5},{5,4},{6,7},{7,6},{8,24},{9,25},{10,... | collective-permute-start | bytes 4423688 | tf_op jit(solution)/shard_map/ppermute | solution.py:45
  188.7 21.5 %collective-permute-start.27 = (bf16[4,2,192,384]{3,2,0,1:T(8,128)(2,1)S(1)}, bf16[4,2,192,384]{3,2,0,1:T(8,128)(2,1)}, u32[]{:S(2)}, u32[]{:S(2)}) collective-permute-start(bf16[4,2,192,384]{3,2,0,1:T(8,128)(2,1)S(1)} %copy.37), channel_id=1, source_target_pairs={{0,1},{1,0},{2,3},{3,2},{4,5},{5,4},{6,7},{7,6},{8,24},{9,25},{10,... | collective-permute-start | bytes 3538952 | tf_op jit(solution)/shard_map/ppermute | solution.py:45
  211.9 11.6 %collective-permute-start.30 = (bf16[768,1152]{1,0:T(8,128)(2,1)}, bf16[768,1152]{1,0:T(8,128)(2,1)}, u32[]{:S(2)}, u32[]{:S(2)}) collective-permute-start(bf16[768,1152]{1,0:T(8,128)(2,1)} %get-tuple-element.195), channel_id=1, source_target_pairs={{0,8},{1,9},{2,10},{3,11},{4,12},{5,13},{6,14},{7,15},{8,0},{9,1},... | collective-permute-start | bytes 5308424 | tf_op jit(solution)/shard_map/ppermute | solution.py:45
  211.9 11.5 %collective-permute-start.29 = (bf16[4,48,1920]{2,1,0:T(8,128)(2,1)S(1)}, bf16[4,48,1920]{2,1,0:T(8,128)(2,1)S(1)}, u32[]{:S(2)}, u32[]{:S(2)}) collective-permute-start(bf16[4,48,1920]{2,1,0:T(8,128)(2,1)S(1)} %get-tuple-element.194), channel_id=1, source_target_pairs={{0,16},{1,17},{2,18},{3,19},{4,20},{5,21},{6,22},{7,23},{8,9},{9,8... | collective-permute-start | bytes 2211848 | tf_op jit(solution)/shard_map/ppermute | solution.py:45
  224.4 25.0 %collective-permute-start.31 = (bf16[4,192,384]{2,1,0:T(8,128)(2,1)S(1)}, bf16[4,192,384]{2,1,0:T(8,128)(2,1)}, u32[]{:S(2)}, u32[]{:S(2)}) collective-permute-start(bf16[4,192,384]{2,1,0:T(8,128)(2,1)S(1)} %fusion.2), channel_id=1, source_target_pairs={{0,16},{1,17},{2,18},{3,19},{4,20},{5,21},{6,22},{7,23},{8,9},{9,8... | collective-permute-start | bytes 1769480 | tf_op jit(solution)/shard_map/ppermute | solution.py:45
  225.8 23.6 %collective-permute-start.32 = (bf16[48,1920]{1,0:T(8,128)(2,1)}, bf16[48,1920]{1,0:T(8,128)(2,1)S(1)}, u32[]{:S(2)}, u32[]{:S(2)}) collective-permute-start(bf16[48,1920]{1,0:T(8,128)(2,1)} %get-tuple-element.202), channel_id=1, source_target_pairs={{0,2},{1,3},{2,0},{3,1},{4,6},{5,7},{6,4},{7,5},{8,10},{9,11},{10,... | collective-permute-start | bytes 552968 | tf_op jit(solution)/shard_map/ppermute | solution.py:45
  229.3 20.1 %collective-permute-start.33 = (bf16[48,1920]{1,0:T(8,128)(2,1)S(1)}, bf16[48,1920]{1,0:T(8,128)(2,1)S(1)}, u32[]{:S(2)}, u32[]{:S(2)}) collective-permute-start(bf16[48,1920]{1,0:T(8,128)(2,1)S(1)} %get-tuple-element.203), channel_id=1, source_target_pairs={{0,4},{1,5},{2,6},{3,7},{4,0},{5,1},{6,2},{7,3},{8,12},{9,13},{10,... | collective-permute-start | bytes 552968 | tf_op jit(solution)/shard_map/ppermute | solution.py:45
  229.9 19.5 %collective-permute-start.34 = (bf16[48,1920]{1,0:T(8,128)(2,1)S(1)}, bf16[48,1920]{1,0:T(8,128)(2,1)S(1)}, u32[]{:S(2)}, u32[]{:S(2)}) collective-permute-start(bf16[48,1920]{1,0:T(8,128)(2,1)S(1)} %get-tuple-element.204), channel_id=1, source_target_pairs={{0,6},{1,7},{2,4},{3,5},{4,2},{5,3},{6,0},{7,1},{8,14},{9,15},{10,... | collective-permute-start | bytes 552968 | tf_op jit(solution)/shard_map/ppermute | solution.py:45
  250.1 20.5 %collective-permute-start.35 = (bf16[4,2,48,1152]{3,2,1,0:T(8,128)(2,1)}, bf16[4,2,48,1152]{3,2,1,0:T(8,128)(2,1)S(1)}, u32[]{:S(2)}, u32[]{:S(2)}) collective-permute-start(bf16[4,2,48,1152]{3,2,1,0:T(8,128)(2,1)} %get-tuple-element.207), channel_id=1, source_target_pairs={{0,1},{1,0},{2,3},{3,2},{4,5},{5,4},{6,7},{7,6},{8,24},{9,25},{10,... | collective-permute-start | bytes 2654216 | tf_op jit(solution)/shard_map/ppermute | solution.py:45
  255.5 15.0 %collective-permute-start.36 = (bf16[192,384]{1,0:T(8,128)(2,1)}, bf16[192,384]{1,0:T(8,128)(2,1)S(1)}, u32[]{:S(2)}, u32[]{:S(2)}) collective-permute-start(bf16[192,384]{1,0:T(8,128)(2,1)} %get-tuple-element.214), channel_id=1, source_target_pairs={{0,2},{1,3},{2,0},{3,1},{4,6},{5,7},{6,4},{7,5},{8,10},{9,11},{10,... | collective-permute-start | bytes 442376 | tf_op jit(solution)/shard_map/ppermute | solution.py:45
  256.7 13.9 %collective-permute-start.37 = (bf16[192,384]{1,0:T(8,128)(2,1)}, bf16[192,384]{1,0:T(8,128)(2,1)S(1)}, u32[]{:S(2)}, u32[]{:S(2)}) collective-permute-start(bf16[192,384]{1,0:T(8,128)(2,1)} %get-tuple-element.215), channel_id=1, source_target_pairs={{0,4},{1,5},{2,6},{3,7},{4,0},{5,1},{6,2},{7,3},{8,12},{9,13},{10,... | collective-permute-start | bytes 442376 | tf_op jit(solution)/shard_map/ppermute | solution.py:45
  258.1 12.5 %collective-permute-start.38 = (bf16[192,384]{1,0:T(8,128)(2,1)}, bf16[192,384]{1,0:T(8,128)(2,1)S(1)}, u32[]{:S(2)}, u32[]{:S(2)}) collective-permute-start(bf16[192,384]{1,0:T(8,128)(2,1)} %get-tuple-element.216), channel_id=1, source_target_pairs={{0,6},{1,7},{2,4},{3,5},{4,2},{5,3},{6,0},{7,1},{8,14},{9,15},{10,... | collective-permute-start | bytes 442376 | tf_op jit(solution)/shard_map/ppermute | solution.py:45
  259.9 10.6 %collective-permute-start.39 = (f32[24,768]{1,0:T(8,128)}, f32[24,768]{1,0:T(8,128)S(1)}, u32[]{:S(2)}, u32[]{:S(2)}) collective-permute-start(f32[24,768]{1,0:T(8,128)} %pack.1), channel_id=1, source_target_pairs={{0,1},{1,0},{2,3},{3,2},{4,5},{5,4},{6,7},{7,6},{8,9},{9,8},{10,11... | collective-permute-start | bytes 221192 | tf_op jit(solution)/shard_map/ppermute | solution.py:45
  271.3 14.0 %collective-permute-start.40 = (bf16[4,48,1152]{2,1,0:T(8,128)(2,1)S(1)}, bf16[4,48,1152]{2,1,0:T(8,128)(2,1)S(1)}, u32[]{:S(2)}, u32[]{:S(2)}) collective-permute-start(bf16[4,48,1152]{2,1,0:T(8,128)(2,1)S(1)} %get-tuple-element.230), channel_id=1, source_target_pairs={{0,16},{1,17},{2,18},{3,19},{4,20},{5,21},{6,22},{7,23},{8,9},{9,8... | collective-permute-start | bytes 1327112 | tf_op jit(solution)/shard_map/ppermute | solution.py:45
  273.0 12.3 %collective-permute-start.41 = (bf16[48,1920]{1,0:T(8,128)(2,1)S(1)}, bf16[48,1920]{1,0:T(8,128)(2,1)S(1)}, u32[]{:S(2)}, u32[]{:S(2)}) collective-permute-start(bf16[48,1920]{1,0:T(8,128)(2,1)S(1)} %fusion.6), channel_id=1, source_target_pairs={{0,16},{1,17},{2,18},{3,19},{4,20},{5,21},{6,22},{7,23},{8,24},{9,... | collective-permute-start | bytes 552968 | tf_op jit(solution)/shard_map/ppermute | solution.py:45
  276.2 6.2 %collective-permute-start.43 = (f32[24,768]{1,0:T(8,128)S(1)}, f32[24,768]{1,0:T(8,128)S(1)}, u32[]{:S(2)}, u32[]{:S(2)}) collective-permute-start(f32[24,768]{1,0:T(8,128)S(1)} %add.332), channel_id=1, source_target_pairs={{0,4},{1,5},{2,6},{3,7},{4,0},{5,1},{6,2},{7,3},{8,12},{9,13},{10,... | collective-permute-start | bytes 221192 | tf_op jit(solution)/shard_map/ppermute | solution.py:45
  285.4 6.5 %collective-permute-start.48 = (f32[24,768]{1,0:T(8,128)S(1)}, f32[24,768]{1,0:T(8,128)S(1)}, u32[]{:S(2)}, u32[]{:S(2)}) collective-permute-start(f32[24,768]{1,0:T(8,128)S(1)} %add.333), channel_id=1, source_target_pairs={{0,16},{1,17},{2,18},{3,19},{4,20},{5,21},{6,22},{7,23},{8,24},{9,... | collective-permute-start | bytes 221192 | tf_op jit(solution)/shard_map/ppermute | solution.py:45
  286.0 10.7 %collective-permute-start.47 = (bf16[192,384]{1,0:T(8,128)(2,1)S(1)}, bf16[192,384]{1,0:T(8,128)(2,1)S(1)}, u32[]{:S(2)}, u32[]{:S(2)}) collective-permute-start(bf16[192,384]{1,0:T(8,128)(2,1)S(1)} %fusion.13), channel_id=1, source_target_pairs={{0,16},{1,17},{2,18},{3,19},{4,20},{5,21},{6,22},{7,23},{8,24},{9,... | collective-permute-start | bytes 442376 | tf_op jit(solution)/shard_map/ppermute | solution.py:45
  287.5 5.9 %collective-permute-start.44 = (bf16[48,1152]{1,0:T(8,128)(2,1)S(1)}, bf16[48,1152]{1,0:T(8,128)(2,1)S(1)}, u32[]{:S(2)}, u32[]{:S(2)}) collective-permute-start(bf16[48,1152]{1,0:T(8,128)(2,1)S(1)} %get-tuple-element.239), channel_id=1, source_target_pairs={{0,2},{1,3},{2,0},{3,1},{4,6},{5,7},{6,4},{7,5},{8,10},{9,11},{10,... | collective-permute-start | bytes 331784 | tf_op jit(solution)/shard_map/ppermute | solution.py:45
  287.5 5.9 %collective-permute-start.45 = (bf16[48,1152]{1,0:T(8,128)(2,1)S(1)}, bf16[48,1152]{1,0:T(8,128)(2,1)S(1)}, u32[]{:S(2)}, u32[]{:S(2)}) collective-permute-start(bf16[48,1152]{1,0:T(8,128)(2,1)S(1)} %get-tuple-element.240), channel_id=1, source_target_pairs={{0,4},{1,5},{2,6},{3,7},{4,0},{5,1},{6,2},{7,3},{8,12},{9,13},{10,... | collective-permute-start | bytes 331784 | tf_op jit(solution)/shard_map/ppermute | solution.py:45
  290.1 6.6 %collective-permute-start.46 = (bf16[48,1152]{1,0:T(8,128)(2,1)S(1)}, bf16[48,1152]{1,0:T(8,128)(2,1)S(1)}, u32[]{:S(2)}, u32[]{:S(2)}) collective-permute-start(bf16[48,1152]{1,0:T(8,128)(2,1)S(1)} %get-tuple-element.241), channel_id=1, source_target_pairs={{0,6},{1,7},{2,4},{3,5},{4,2},{5,3},{6,0},{7,1},{8,14},{9,15},{10,... | collective-permute-start | bytes 331784 | tf_op jit(solution)/shard_map/ppermute | solution.py:45
  296.9 5.9 %collective-permute-start.51 = (bf16[48,1152]{1,0:T(8,128)(2,1)S(1)}, bf16[48,1152]{1,0:T(8,128)(2,1)S(1)}, u32[]{:S(2)}, u32[]{:S(2)}) collective-permute-start(bf16[48,1152]{1,0:T(8,128)(2,1)S(1)} %fusion.23), channel_id=1, source_target_pairs={{0,16},{1,17},{2,18},{3,19},{4,20},{5,21},{6,22},{7,23},{8,24},{9,... | collective-permute-start | bytes 331784 | tf_op jit(solution)/shard_map/ppermute | solution.py:45
  297.5 6.8 %collective-permute-start.52 = (bf16[48,1152]{1,0:T(8,128)(2,1)S(1)}, bf16[48,1152]{1,0:T(8,128)(2,1)S(1)}, u32[]{:S(2)}, u32[]{:S(2)}) collective-permute-start(bf16[48,1152]{1,0:T(8,128)(2,1)S(1)} %fusion.23), channel_id=1, source_target_pairs={{0,24},{1,25},{2,26},{3,27},{4,28},{5,29},{6,30},{7,31},{8,16},{9,... | collective-permute-start | bytes 331784 | tf_op jit(solution)/shard_map/ppermute | solution.py:45
  298.8 6.7 %collective-permute-start.54 = (bf16[2,192,384]{2,1,0:T(8,128)(2,1)S(1)}, bf16[2,192,384]{2,1,0:T(8,128)(2,1)S(1)}, u32[]{:S(2)}, u32[]{:S(2)}) collective-permute-start(bf16[2,192,384]{2,1,0:T(8,128)(2,1)S(1)} %get-tuple-element.283), channel_id=1, source_target_pairs={{0,8},{1,9},{2,10},{3,11},{4,12},{5,13},{6,14},{7,15},{8,0},{9,1},... | collective-permute-start | bytes 884744 | tf_op jit(solution)/shard_map/ppermute | solution.py:45
  299.2 7.6 %collective-permute-start.53 = (bf16[2,48,1920]{2,1,0:T(8,128)(2,1)S(1)}, bf16[2,48,1920]{2,1,0:T(8,128)(2,1)S(1)}, u32[]{:S(2)}, u32[]{:S(2)}) collective-permute-start(bf16[2,48,1920]{2,1,0:T(8,128)(2,1)S(1)} %pad_maximum_fusion.6), channel_id=1, source_target_pairs={{0,8},{1,9},{2,10},{3,11},{4,12},{5,13},{6,14},{7,15},{8,0},{9,1},... | collective-permute-start | bytes 1105928 | tf_op jit(solution)/shard_map/ppermute | solution.py:45
  (46 other events, 363.8 us)

commit v4 on v3

--- a/solution.py
+++ b/solution.py
@@ -1,4 +1,5 @@
 import functools
+import math
 
 import jax
 import jax.numpy as jnp
@@ -146,8 +147,9 @@
     return lax.dot_general(left, right, (((0,), (0,)), ((), ())), preferred_element_type=jnp.float32)
 
 
-def call(kernel, grid, in_specs, out_specs, out_shape, scratch=(), flops=0, prefetch=0, aliases=None, name=None):
-    sizes = [s.size * s.dtype.itemsize for s in jax.tree.leaves(out_shape)]
+def call(kernel, grid, in_specs, out_specs, out_shape, scratch=(), flops=0, prefetch=0, aliases=None, name=None, grant=VMEM_BYTES):
+    shapes = out_shape if isinstance(out_shape, list) else [out_shape]
+    sizes = [math.prod(s.shape) * jnp.dtype(s.dtype).itemsize for s in shapes]
     return pl.pallas_call(
         kernel,
         grid_spec=pltpu.PrefetchScalarGridSpec(
@@ -155,7 +157,7 @@
         ),
         out_shape=out_shape,
         compiler_params=pltpu.CompilerParams(
-            dimension_semantics=("arbitrary",) * len(grid), vmem_limit_bytes=VMEM_BYTES
+            dimension_semantics=("arbitrary",) * len(grid), vmem_limit_bytes=grant
         ),
         cost_estimate=pl.CostEstimate(flops=flops, bytes_accessed=2 * sum(sizes), transcendentals=0),
         input_output_aliases=aliases or {},
@@ -233,11 +235,12 @@
         (count // TILE,),
         [FLAGS, tiles(width), whole((16, width)), whole((1, 2 * cols))] + [ANY] * len(pieces),
         [pl.BlockSpec((2, TILE, cols), lambda i, *_: (0, i, 0)), tiles(width)],
-        [jax.ShapeDtypeStruct((2, count, cols), jnp.bfloat16), jax.ShapeDtypeStruct((count, width), jnp.bfloat16)],
+        [pltpu.HBM((2, count, cols), jnp.bfloat16), pltpu.HBM((count, width), jnp.bfloat16)],
         [pltpu.VMEM((width, 2 * cols), jnp.bfloat16), pltpu.SemaphoreType.DMA],
         4 * count * width * cols,
         1,
         name="project",
+        grant=24 << 20,
     )(at, flags, x, rows, bias, *pieces)
 
 
@@ -539,7 +542,7 @@
     pl.when(step >= n_first)(lambda: put(lefts[2], lefts[3]))
 
 
-def grads(at, half, parts, got, n_z, tile, name):
+def grads(at, parts, got, n_z, tile, name):
     count, rows = parts[0][0].shape
     width = sum(cols for _, _, cols in parts)
     tall = rows > 2 * width
@@ -561,7 +564,6 @@
                 ),
             ]
         arrays += [left, right]
-    at = jnp.concatenate([at, half])
     block = rows // (4 * n_z)
     shape = (tile, width) if tall else (rows, tile)
     spec = pl.BlockSpec(shape, (lambda i, *_: (i, 0)) if tall else (lambda i, *_: (0, i)))
@@ -635,7 +637,7 @@
             grads_ref[0][...] = grad.astype(jnp.bfloat16)
 
 
-def attend_back(at, half, docs, qkv, ctx, inv, expo, dctx, low, flags, got, n_z):
+def attend_back(at, docs, qkv, ctx, inv, expo, dctx, low, flags, got, n_z):
     count, cols = qkv.shape[1:]
     seq, n_pair = count // docs, cols // 384
     rows = low.shape[1]
@@ -662,7 +664,7 @@
         flops=docs * n_pair * 2 * seq * seq * 256 * 10 + 2 * count * rows * cols,
         prefetch=1,
         name="attend_back",
-    )(jnp.concatenate([at, half]), qkv, qkv, qkv, ctx, inv, expo, dctx, low, flags, *([got] if fused else []))
+    )(at, qkv, qkv, qkv, ctx, inv, expo, dctx, low, flags, *([got] if fused else []))
     if got is None or fused:
         return dqkv, sums, *out
     stay, away = sum_core(out[0], got, at, n_z)
@@ -683,11 +685,15 @@
 def embed_grad(at, before, dqkv, side, pieces, n_z, dtype):
     count, width = before.shape
     cols = dqkv.shape[1]
+
+    def rows_of(cols):
+        return pl.BlockSpec((FFN_TILE, cols), lambda i, *_: (i, 0))
+
     return call(
         functools.partial(embed_grad_kernel, n_z, side),
-        (count // TILE,),
-        [tiles(width), tiles(cols)] + [ANY] * len(pieces),
-        tiles(width),
+        (count // FFN_TILE,),
+        [rows_of(width), rows_of(cols)] + [ANY] * len(pieces),
+        rows_of(width),
         jax.ShapeDtypeStruct((count, width), dtype),
         [pltpu.VMEM((width, cols), jnp.bfloat16), pltpu.SemaphoreType.DMA],
         2 * count * width * cols,
@@ -769,14 +775,15 @@
     first_mid = jnp.concatenate([quarter(w_in), quarter(w_out)], axis=1)
     first_down = quarter(w_down)
 
+    flags = jnp.stack([masked.reshape(tok_count), replaced.reshape(tok_count)]).astype(jnp.bfloat16)
+    flags = jnp.concatenate([flags, jnp.zeros((13, tok_count), jnp.bfloat16), jnp.ones((1, tok_count), jnp.bfloat16)])
     attn = gather_z(first_attn, wires)
-    attn, packed = tie(attn, packed)
+    mine, theirs = jnp.concatenate([at, c[None]]), jnp.concatenate([at, 1 - c[None]])
+    attn, packed, flags, mine, theirs = tie(attn, packed, flags, mine, theirs)
     got_attn = send(attn, wires["first"])
     packed = gather_z(grow(packed, send(packed, wires["x"])), wires)
     got_attn, first_mid, packed = tie(got_attn, first_mid, packed)
     rows, bias, b_in = unpack(at, packed, own)
-    flags = jnp.stack([masked.reshape(tok_count), replaced.reshape(tok_count)]).astype(jnp.bfloat16)
-    flags = jnp.concatenate([flags, jnp.zeros((13, tok_count), jnp.bfloat16), jnp.ones((1, tok_count), jnp.bfloat16)])
     x = layer_input.reshape(tok_count, width)
     cot = cotangent.reshape(tok_count, width)
     attn = grow(attn, got_attn)
@@ -810,24 +817,23 @@
         at, flags, x, ctx, cot, rows, b_in, w_mid, w_back, n_z
     )
 
-    mine, theirs = c[None], 1 - c[None]
     part_d = [(activated, dbranch, split)]
     part_m = [(normed_low, dhidden, ff_width // 2), (ctx, dattn, split)]
-    give_m = grads(at, theirs, part_m, None, n_z, width, "mid_give")
+    give_m = grads(theirs, part_m, None, n_z, width, "mid_give")
     activated, give_m = tie(activated, give_m)
     part_d = [(activated, dbranch, split)]
     got_m = send(give_m, wires["core"])
-    give_d = grads(at, theirs, part_d, None, n_z, width, "down_give")
+    give_d = grads(theirs, part_d, None, n_z, 2 * width, "down_give")
     got_m, give_d = tie(got_m, give_d)
     got_d = send(give_d, wires["core"])
-    give_m, keep_m = grads(at, mine, part_m, got_m, n_z, width, "mid_keep")
+    give_m, keep_m = grads(mine, part_m, got_m, n_z, width, "mid_keep")
     give_m, got_d = tie(give_m, got_d)
     got_m = send(give_m, wires["second"])
-    give_d, keep_d = grads(at, mine, part_d, got_d, n_z, width, "down_keep")
+    give_d, keep_d = grads(mine, part_d, got_d, n_z, 2 * width, "down_keep")
     give_d, dctx = tie(give_d, dctx)
     got_d = send(give_d, wires["second"])
     dqkv_theirs, sums_theirs, give_a = attend_back(
-        at, theirs, doc_count, qkv, ctx, inv, expo, dctx, embed_low, flags, None, n_z
+        theirs, doc_count, qkv, ctx, inv, expo, dctx, embed_low, flags, None, n_z
     )
     got_d, got_m, give_a = tie(got_d, got_m, give_a)
     keep_m, give_m = sum_second(keep_m, got_m, at)
@@ -842,7 +848,7 @@
     got_m = send_all(give_m, wires["z"])
     got_d = send(give_d, wires["first"])
     dqkv_mine, sums_mine, give_a, keep_a = attend_back(
-        at, mine, doc_count, qkv, ctx, inv, expo, dctx, embed_low, flags, got_a, n_z
+        mine, doc_count, qkv, ctx, inv, expo, dctx, embed_low, flags, got_a, n_z
     )
     got_d, got_m, give_a = tie(got_d, got_m, give_a)
     got_a = send(give_a, wires["second"])
@@ -858,25 +864,24 @@
     packed = packed + got
     give_a, packed, got_d = tie(give_a, packed, got_d)
     got_a = send(give_a, wires["first"])
-    got_m = send(owned_m, wires["rep"][1])
     for pairs in wires["z_bits"]:
         packed = packed + send(packed, pairs)
     owned_d = sum_z(keep_d, got_d)
-    got_a, got_m, packed, owned_d = tie(got_a, got_m, packed, owned_d)
+    got_a, packed, owned_d, owned_m = tie(got_a, packed, owned_d, owned_m)
     keep_a, give_a = sum_first(keep_a, got_a, at)
-    give_a, packed, owned_d = tie(give_a, packed, owned_d)
+    give_a, packed, owned_d, owned_m = tie(give_a, packed, owned_d, owned_m)
     got_a = send_all(give_a, wires["z"])
+    got_m = send(owned_m, wires["rep"][1])
     got_d = send(owned_d, wires["rep"][1])
-    pair_m = jnp.stack([owned_m, got_m])
-    for pairs in (wires["rep"][1], wires["core"]):
-        packed = packed + send(packed, pairs)
-    got_a, got_d, packed, pair_m = tie(got_a, got_d, packed, pair_m)
+    got_a, got_d, got_m, packed = tie(got_a, got_d, got_m, packed)
     owned_a = sum_z(keep_a, got_a)
-    owned_a, packed, got_d, pair_m = tie(owned_a, packed, got_d, pair_m)
+    pair_m, pair_d = jnp.stack([owned_m, got_m]), jnp.stack([owned_d, got_d])
+    owned_a, packed, pair_d, pair_m = tie(owned_a, packed, pair_d, pair_m)
     got_a = send_all([owned_a] * 3, wires["rep"])
-    pair_d = jnp.stack([owned_d, got_d])
     got_m = send(pair_m, wires["core"])
     got_d = send(pair_d, wires["core"])
+    for pairs in (wires["core"], wires["rep"][1]):
+        packed = packed + send(packed, pairs)
     o_small = lax.dynamic_slice(packed, (0, own * step), (16, step))
     o_b_in = lax.dynamic_slice(packed[11:15].reshape(ff_width), (own * (ff_width // n_fsdp),), (ff_width // n_fsdp,))
     through = packed[16:22].reshape(2, 3 * width)

time: 316 us -> 315 us (level)
  starting transfers between devices: 60.8 us -> 65.4 us
  Pallas kernels: 157 us -> 153 us
    ppermute x55, starting transfers between devices: 60.8 us -> 65.4 us  [send(): return lax.ppermute(value, AXES, pairs)]
    unnamed x84 -> x88, local copies, waits for them, and re-layouts: 6.39 us -> 5.03 us
  transfers between devices with their start and end apart: 55 -> 55, of which waited for: 22 -> 22; matrix products, arithmetic and copies ran while one was open for 6% -> 6% of each run, Pallas kernels for 34% -> 32%
where the time goes in v4:
time: 315 us; the launch traced here: 309 us
  Pallas kernels  153 us (49%)
  starting transfers between devices  65.4 us (21%)
  waiting for transfers between devices  57.1 us (18%)
  other arithmetic  18.4 us (6%)
  local copies, waits for them, and re-layouts  12.6 us (4%)
    ppermute x55, starting transfers between devices, send(): return lax.ppermute(value, AXES, pairs)  65.4 us
    ppermute x55, waiting for transfers between devices, send(): return lax.ppermute(value, AXES, pairs)  57.1 us
    pallas_call x1, Pallas kernels, ffn(): call(functools.partial(ffn_kernel, n_z, len(mid)), (count // FFN_TILE,),...  45.3 us
    pallas_call x2, Pallas kernels, attend_back(): call(functools.partial(attend_back_kernel, docs, fused), (n_pair,), [part...  34.9 us
    pallas_call x2, Pallas kernels, grads(): call(functools.partial(grad_kernel, n_first, True), (steps,), specs + [sp...  17 us
    pallas_call x2, Pallas kernels, grads(): call(plain, (steps,), specs, spec, jax.ShapeDtypeStruct((rows, width), jn...  15.6 us
    pallas_call x2, Pallas kernels, embed_grad(): call(functools.partial(embed_grad_kernel, n_z, side), (count // FFN_TILE,...  15.2 us
    pallas_call x1, Pallas kernels, attend(): call(functools.partial(attend_kernel, docs), (2 * n_pair,), [part(0), par...  14.1 us
  transfers between devices with their start and end apart: 55, of which 22 were waited for; matrix products, arithmetic and copies ran while one was open for 6% of the time, Pallas kernels for 32%

profile of v4, /device:TPU:0, one launch (start us, length us, event | category | flops | bytes accessed | tf_op | source)
XLA Modules:
  0.0 309.1 jit_solution(16770382905496644789)
XLA Ops:
  2.0 3.1 collective-permute-start
  5.1 2.6 collective-permute-start.1
  13.1 3.3 %collective-permute-done.1 = bf16[48,1152]{1,0:T(8,128)(2,1)S(1)} collective-permute-done((bf16[48,1152]{1,0:T(8,128)(2,1)S(1)}, bf16[48,1152]{1,0:T(8,128)(2,1)S(1)}, u32[]{:S(2)}, u32[]{:S(2)}) %collective-permute-start.1) | collective-permute-done | bytes 110624 | tf_op jit(solution)/shard_map/ppermute | solution.py:46
  16.5 1.6 collective-permute-start.4
  20.4 1.7 collective-permute-start.5
  24.9 1.9 collective-permute-done.6
  26.8 2.3 collective-permute-done.7
  29.2 1.7 collective-permute-start.11
  32.1 3.1 %collective-permute-start.9 = (bf16[48,1920]{1,0:T(8,128)(2,1)S(1)}, bf16[48,1920]{1,0:T(8,128)(2,1)S(1)}, u32[]{:S(2)}, u32[]{:S(2)}) collective-permute-start(bf16[48,1920]{1,0:T(8,128)(2,1)S(1)} %pad_maximum_fusion.8), channel_id=1, source_target_pairs={{0,4},{1,5},{2,6},{3,7},{4,0},{5,1},{6,2},{7,3},{8,12},{9,13},{10,... | collective-permute-start | bytes 552968 | tf_op jit(solution)/shard_map/ppermute | solution.py:46
  38.6 1.7 collective-permute-done.8
  40.4 4.6 %collective-permute-done.9 = bf16[48,1920]{1,0:T(8,128)(2,1)S(1)} collective-permute-done((bf16[48,1920]{1,0:T(8,128)(2,1)S(1)}, bf16[48,1920]{1,0:T(8,128)(2,1)S(1)}, u32[]{:S(2)}, u32[]{:S(2)}) %collective-permute-start.9) | collective-permute-done | bytes 184352 | tf_op jit(solution)/shard_map/ppermute | solution.py:46
  46.6 2.6 collective-permute-start.14
  49.1 3.6 %collective-permute-done.13 = bf16[192,384]{1,0:T(8,128)(2,1)S(1)} collective-permute-done((bf16[192,384]{1,0:T(8,128)(2,1)S(1)}, bf16[192,384]{1,0:T(8,128)(2,1)S(1)}, u32[]{:S(2)}, u32[]{:S(2)}) %collective-permute-start.13) | collective-permute-done | bytes 147488 | tf_op jit(solution)/shard_map/ppermute | solution.py:46
  52.7 2.0 collective-permute-start.15
  54.7 5.8 %collective-permute-done.14 = bf16[192,384]{1,0:T(8,128)(2,1)S(1)} collective-permute-done((bf16[192,384]{1,0:T(8,128)(2,1)S(1)}, bf16[192,384]{1,0:T(8,128)(2,1)S(1)}, u32[]{:S(2)}, u32[]{:S(2)}) %collective-permute-start.14) | collective-permute-done | bytes 147488 | tf_op jit(solution)/shard_map/ppermute | solution.py:46
  63.0 7.9 %project.1 = (bf16[2,1024,1152]{2,1,0:T(8,128)(2,1)}, bf16[1024,768]{1,0:T(8,128)(2,1)}) custom-call(s32[4]{0:T(128)S(1)} %copy-done.5, bf16[16,1024]{1,0:T(8,128)(2,1)S(1)} %copy-done.4, bf16[1024,768]{1,0:T(8,128)(2,1)S(1)} %bitcast.180, bf16[16,768]{1,0:T(8,128)(2,1)S(1)} %copy-done.7, f32[1,2304]{1,0:T(1,128)S(1)} %copy-done.8, ...), custom_call_target="tpu_custom_call" | custom-call | flops 3623878656 | bytes 12582912 | tf_op jit(solution)/shard_map/project/pallas_call | solution.py:233
  71.0 6.1 %collective-permute-done.18 = bf16[768,384]{1,0:T(8,128)(2,1)S(1)} collective-permute-done((bf16[768,384]{1,0:T(8,128)(2,1)S(1)}, bf16[768,384]{1,0:T(8,128)(2,1)S(1)}, u32[]{:S(2)}, u32[]{:S(2)}) %collective-permute-start.18) | collective-permute-done | bytes 589856 | tf_op jit(solution)/shard_map/ppermute | solution.py:46
  78.3 14.1 %attend.1 = (bf16[1024,768]{1,0:T(8,128)(2,1)}, f32[1024,768]{1,0:T(8,128)}, bf16[2,3,2,2,512,512]{5,4,3,2,1,0:T(8,128)(2,1)}) custom-call(s32[2]{0:T(128)} %len_ref.1, bf16[2,1024,1152]{2,1,0:T(8,128)(2,1)} %get-tuple-element.162.q_ref.k_ref.v_ref, bf16[2,1024,1152]{2,1,0:T(8,128)(2,1)} %get-tuple-element.162.q_ref.k_ref.v_ref, ...), custom_call_target="tpu_custom_call" | custom-call | flops 6442450944 | bytes 34603008 | tf_op jit(solution)/shard_map/attend/pallas_call | solution.py:325
  92.4 2.4 collective-permute-done.20.refs_5_
  96.3 4.8 %collective-permute-done.24.refs_7_ = bf16[1536,384]{1,0:T(8,128)(2,1)S(1)} collective-permute-done((bf16[1536,384]{1,0:T(8,128)(2,1)}, bf16[1536,384]{1,0:T(8,128)(2,1)S(1)}, u32[]{:S(2)}, u32[]{:S(2)}) %collective-permute-start.24) | collective-permute-done | bytes 1179680 | tf_op jit(solution)/shard_map/ppermute | solution.py:46
  102.6 45.3 %ffn.1 = (bf16[1024,768]{1,0:T(8,128)(2,1)}, bf16[1024,768]{1,0:T(8,128)(2,1)}, bf16[1024,3072]{1,0:T(8,128)(2,1)}, bf16[1024,768]{1,0:T(8,128)(2,1)}, bf16[1024...) custom-call(s32[4]{0:T(128)} %pad_add_fusion.at_ref, ...), custom_call_target="tpu_custom_call" | custom-call | flops 21743271936 | bytes 47529984 | tf_op jit(solution)/shard_map/ffn/pallas_call | solution.py:489
  148.0 8.2 %mid_give.1 = bf16[768,1920]{1,0:T(8,128)(2,1)} custom-call(s32[5]{0:T(128)} %concatenate.153.at_ref, bf16[1024,768]{1,0:T(8,128)(2,1)} %get-tuple-element.174.refs_0_, bf16[1024,3072]{1,0:T(8,128)(2,1)} %get-tuple-element.175.refs_1_, bf16[1024,768]{1,0:T(8,128)(2,1)} %get-tuple-element.166.ctx_ref.refs_2_, bf16[1024,768]{1,0:T(8,128)(2,1)} %get-tuple-element.176.refs_3_), custom_call_target="tpu_custom_call" | custom-call | flops 3019898880 | bytes 5898240 | tf_op jit(solution)/shard_map/mid_give/pallas_call | solution.py:574
  156.5 7.5 %down_give.1 = bf16[3072,384]{1,0:T(8,128)(2,1)} custom-call(s32[5]{0:T(128)} %concatenate.153.at_ref, bf16[1024,3072]{1,0:T(8,128)(2,1)} %get-tuple-element.180.refs_0_, bf16[1024,768]{1,0:T(8,128)(2,1)} %get-tuple-element.181.refs_1_), custom_call_target="tpu_custom_call" | custom-call | flops 2415919104 | bytes 4718592 | tf_op jit(solution)/shard_map/down_give/pallas_call | solution.py:574
  165.5 8.9 %mid_keep.1 = (bf16[4,2,48,1920]{3,2,1,0:T(8,128)(2,1)}, bf16[4,2,48,1920]{3,2,1,0:T(8,128)(2,1)}) custom-call(s32[5]{0:T(128)} %concatenate.152.at_ref, bf16[1024,768]{1,0:T(8,128)(2,1)} %get-tuple-element.174.refs_0_, bf16[1024,3072]{1,0:T(8,128)(2,1)} %get-tuple-element.175.refs_1_, bf16[1024,768]{1,0:T(8,128)(2,1)} %get-tuple-element.166.ctx_ref.refs_2_, ...), custom_call_target="tpu_custom_call" | custom-call | flops 3019898880 | bytes 5898240 | tf_op jit(solution)/shard_map/mid_keep/pallas_call | solution.py:585
  175.6 8.1 %down_keep.1 = (bf16[4,2,192,384]{3,2,1,0:T(8,128)(2,1)}, bf16[4,2,192,384]{3,2,1,0:T(8,128)(2,1)}) custom-call(s32[5]{0:T(128)} %concatenate.152.at_ref, bf16[1024,3072]{1,0:T(8,128)(2,1)} %get-tuple-element.180.refs_0_, bf16[1024,768]{1,0:T(8,128)(2,1)} %get-tuple-element.181.refs_1_, bf16[3072,384]{1,0:T(8,128)(2,1)} %collective-permute-done.26.refs_2_), custom_call_target="tpu_custom_call" | custom-call | flops 2415919104 | bytes 4718592 | tf_op jit(solution)/shard_map/down_keep/pallas_call | solution.py:585
  186.0 17.3 %attend_back.2 = (bf16[1024,1152]{1,0:T(8,128)(2,1)}, f32[16,1152]{1,0:T(8,128)}, bf16[768,1152]{1,0:T(8,128)(2,1)}) custom-call(s32[5]{0:T(128)} %concatenate.153.at_ref, bf16[2,1024,1152]{2,1,0:T(8,128)(2,1)} %get-tuple-element.162.q_ref.k_ref.v_ref, bf16[2,1024,1152]{2,1,0:T(8,128)(2,1)} %get-tuple-element.162.q_ref.k_ref.v_ref, ...), custom_call_target="tpu_custom_call" | custom-call | flops 9865003008 | bytes 8404992 | tf_op jit(solution)/shard_map/attend_back/pallas_call | solution.py:653
  203.3 3.5 %collective-permute-done.27 = bf16[4,2,192,384]{3,2,0,1:T(8,128)(2,1)} collective-permute-done((bf16[4,2,192,384]{3,2,0,1:T(8,128)(2,1)S(1)}, bf16[4,2,192,384]{3,2,0,1:T(8,128)(2,1)}, u32[]{:S(2)}, u32[]{:S(2)}) %collective-permute-start.27) | collective-permute-done | bytes 1179680 | tf_op jit(solution)/shard_map/ppermute | solution.py:46
  206.8 2.0 fusion.2
  210.8 7.6 %embed_grad.2.before_ref = f32[1024,768]{1,0:T(8,128)} custom-call(s32[4]{0:T(128)} %pad_add_fusion.at_ref, f32[1024,768]{1,0:T(8,128)} %get-tuple-element.203.before_ref, bf16[1024,1152]{1,0:T(8,128)(2,1)} %get-tuple-element.204.dqkv_ref, bf16[384,1152]{1,0:T(8,128)(2,1)} %copy-done.2, bf16[384,1152]{1,0:T(8,128)(2,1)} %copy-done.3), custom_call_target="tpu_custom_call" | custom-call | flops 1811939328 | bytes 6291456 | tf_op jit(solution)/shard_map/embed_grad/pallas_call | solution.py:692
  218.5 2.3 collective-permute-done.29
  223.3 5.3 %collective-permute-start.32 = (bf16[48,1920]{1,0:T(8,128)(2,1)}, bf16[48,1920]{1,0:T(8,128)(2,1)S(1)}, u32[]{:S(2)}, u32[]{:S(2)}) collective-permute-start(bf16[48,1920]{1,0:T(8,128)(2,1)} %get-tuple-element.209), channel_id=1, source_target_pairs={{0,2},{1,3},{2,0},{3,1},{4,6},{5,7},{6,4},{7,5},{8,10},{9,11},{10,... | collective-permute-start | bytes 552968 | tf_op jit(solution)/shard_map/ppermute | solution.py:46
  229.0 2.1 collective-permute-start.34
  231.0 17.7 %attend_back.3 = (bf16[1024,1152]{1,0:T(8,128)(2,1)}, f32[16,1152]{1,0:T(8,128)}, bf16[4,2,48,1152]{3,2,1,0:T(8,128)(2,1)}, bf16[4,2,48,1152]{3,2,1,0:T(8,128)(2,1)}) custom-call(s32[5]{0:T(128)} %concatenate.152.at_ref, bf16[2,1024,1152]{2,1,0:T(8,128)(2,1)} %get-tuple-element.162.q_ref.k_ref.v_ref, ...), custom_call_target="tpu_custom_call" | custom-call | flops 9865003008 | bytes 8404992 | tf_op jit(solution)/shard_map/attend_back/pallas_call | solution.py:653
  252.4 1.7 pack.1
  254.1 1.8 fusion.43
  258.3 2.0 collective-permute-start.38
  262.0 7.5 %embed_grad.3 = bf16[1024,768]{1,0:T(8,128)(2,1)} custom-call(s32[4]{0:T(128)} %pad_add_fusion.at_ref, f32[1024,768]{1,0:T(8,128)} %embed_grad.2.before_ref, bf16[1024,1152]{1,0:T(8,128)(2,1)} %get-tuple-element.226.dqkv_ref, bf16[384,1152]{1,0:T(8,128)(2,1)} %copy-done, bf16[384,1152]{1,0:T(8,128)(2,1)} %copy-done.1), custom_call_target="tpu_custom_call" | custom-call | flops 1811939328 | bytes 3145728 | tf_op jit(solution)/shard_map/embed_grad/pallas_call | solution.py:692
  271.3 1.9 collective-permute-start.41
  273.2 2.5 collective-permute-done.41
  275.7 2.4 collective-permute-start.42
  279.1 1.9 collective-permute-done.42
  281.1 1.7 collective-permute-start.47
  283.2 2.3 collective-permute-start.43
  285.8 2.0 collective-permute-start.45
  288.8 4.7 %collective-permute-done.44 = bf16[48,1152]{1,0:T(8,128)(2,1)S(1)} collective-permute-done((bf16[48,1152]{1,0:T(8,128)(2,1)S(1)}, bf16[48,1152]{1,0:T(8,128)(2,1)S(1)}, u32[]{:S(2)}, u32[]{:S(2)}) %collective-permute-start.44) | collective-permute-done | bytes 110624 | tf_op jit(solution)/shard_map/ppermute | solution.py:46
  293.8 2.0 collective-permute-start.49
  297.3 2.0 collective-permute-start.52
  299.8 1.8 collective-permute-done.50
  (237 shorter events, 56.4 us)
Async XLA Ops:
  2.0 11.1 %collective-permute-start = (bf16[48,1152]{1,0:T(8,128)(2,1)S(1)}, bf16[48,1152]{1,0:T(8,128)(2,1)S(1)}, u32[]{:S(2)}, u32[]{:S(2)}) collective-permute-start(bf16[48,1152]{1,0:T(8,128)(2,1)S(1)} %pad_maximum_fusion.9), channel_id=1, source_target_pairs={{0,2},{1,3},{2,0},{3,1},{4,6},{5,7},{6,4},{7,5},{8,10},{9,11},{10,... | collective-permute-start | bytes 331784 | tf_op jit(solution)/shard_map/ppermute | solution.py:46
  5.1 11.3 %collective-permute-start.1 = (bf16[48,1152]{1,0:T(8,128)(2,1)S(1)}, bf16[48,1152]{1,0:T(8,128)(2,1)S(1)}, u32[]{:S(2)}, u32[]{:S(2)}) collective-permute-start(bf16[48,1152]{1,0:T(8,128)(2,1)S(1)} %pad_maximum_fusion.9), channel_id=1, source_target_pairs={{0,4},{1,5},{2,6},{3,7},{4,0},{5,1},{6,2},{7,3},{8,12},{9,13},{10,... | collective-permute-start | bytes 331784 | tf_op jit(solution)/shard_map/ppermute | solution.py:46
  7.7 8.8 %collective-permute-start.2 = (bf16[48,1152]{1,0:T(8,128)(2,1)S(1)}, bf16[48,1152]{1,0:T(8,128)(2,1)S(1)}, u32[]{:S(2)}, u32[]{:S(2)}) collective-permute-start(bf16[48,1152]{1,0:T(8,128)(2,1)S(1)} %pad_maximum_fusion.9), channel_id=1, source_target_pairs={{0,6},{1,7},{2,4},{3,5},{4,2},{5,3},{6,0},{7,1},{8,14},{9,15},{10,... | collective-permute-start | bytes 331784 | tf_op jit(solution)/shard_map/ppermute | solution.py:46
  18.1 11.0 %collective-permute-start.3 = (bf16[192,1152]{1,0:T(8,128)(2,1)S(1)}, bf16[192,1152]{1,0:T(8,128)(2,1)S(1)}, u32[]{:S(2)}, u32[]{:S(2)}) collective-permute-start(bf16[192,1152]{1,0:T(8,128)(2,1)S(1)} %pad_maximum_fusion.4), channel_id=1, source_target_pairs={{0,16},{1,17},{2,18},{3,19},{4,20},{5,21},{6,22},{7,23},{8,9},{9,8... | collective-permute-start | bytes 1327112 | tf_op jit(solution)/shard_map/ppermute | solution.py:46
  23.5 5.5 %collective-permute-start.7 = (f32[2,16,96]{2,1,0:T(8,128)S(1)}, f32[2,16,96]{2,1,0:T(8,128)S(1)}, u32[]{:S(2)}, u32[]{:S(2)}) collective-permute-start(f32[2,16,96]{2,1,0:T(8,128)S(1)} %get-tuple-element.315), channel_id=1, source_target_pairs={{0,6},{1,7},{2,4},{3,5},{4,2},{5,3},{6,0},{7,1},{8,14},{9,15},{10,... | collective-permute-start | bytes 36872 | tf_op jit(solution)/shard_map/ppermute | solution.py:46
  29.2 15.9 %collective-permute-start.11 = (bf16[384,1152]{1,0:T(8,128)(2,1)S(1)}, bf16[384,1152]{1,0:T(8,128)(2,1)S(1)}, u32[]{:S(2)}, u32[]{:S(2)}) collective-permute-start(bf16[384,1152]{1,0:T(8,128)(2,1)S(1)} %constant_dynamic-update-slice_fusion.7.refs_0_), channel_id=1, source_target_pairs={{0,1},{1,0},{2,3},{3,2},{4,5},{5,4},{6,7},{7,6},{8,24},{9,25},{10,... | collective-permute-start | bytes 2654216 | tf_op jit(solution)/shard_map/ppermute | solution.py:46
  30.8 7.8 %collective-permute-start.10 = (bf16[48,1920]{1,0:T(8,128)(2,1)S(1)}, bf16[48,1920]{1,0:T(8,128)(2,1)S(1)}, u32[]{:S(2)}, u32[]{:S(2)}) collective-permute-start(bf16[48,1920]{1,0:T(8,128)(2,1)S(1)} %pad_maximum_fusion.8), channel_id=1, source_target_pairs={{0,6},{1,7},{2,4},{3,5},{4,2},{5,3},{6,0},{7,1},{8,14},{9,15},{10,... | collective-permute-start | bytes 552968 | tf_op jit(solution)/shard_map/ppermute | solution.py:46
  32.1 8.3 %collective-permute-start.8 = (bf16[48,1920]{1,0:T(8,128)(2,1)S(1)}, bf16[48,1920]{1,0:T(8,128)(2,1)S(1)}, u32[]{:S(2)}, u32[]{:S(2)}) collective-permute-start(bf16[48,1920]{1,0:T(8,128)(2,1)S(1)} %pad_maximum_fusion.8), channel_id=1, source_target_pairs={{0,2},{1,3},{2,0},{3,1},{4,6},{5,7},{6,4},{7,5},{8,10},{9,11},{10,... | collective-permute-start | bytes 552968 | tf_op jit(solution)/shard_map/ppermute | solution.py:46
  32.1 12.9 %collective-permute-start.9 = (bf16[48,1920]{1,0:T(8,128)(2,1)S(1)}, bf16[48,1920]{1,0:T(8,128)(2,1)S(1)}, u32[]{:S(2)}, u32[]{:S(2)}) collective-permute-start(bf16[48,1920]{1,0:T(8,128)(2,1)S(1)} %pad_maximum_fusion.8), channel_id=1, source_target_pairs={{0,4},{1,5},{2,6},{3,7},{4,0},{5,1},{6,2},{7,3},{8,12},{9,13},{10,... | collective-permute-start | bytes 552968 | tf_op jit(solution)/shard_map/ppermute | solution.py:46
  45.1 15.5 %collective-permute-start.12 = (bf16[192,1920]{1,0:T(8,128)(2,1)S(1)}, bf16[192,1920]{1,0:T(8,128)(2,1)S(1)}, u32[]{:S(2)}, u32[]{:S(2)}) collective-permute-start(bf16[192,1920]{1,0:T(8,128)(2,1)S(1)} %pad_maximum_fusion.2), channel_id=1, source_target_pairs={{0,16},{1,17},{2,18},{3,19},{4,20},{5,21},{6,22},{7,23},{8,9},{9,8... | collective-permute-start | bytes 2211848 | tf_op jit(solution)/shard_map/ppermute | solution.py:46
  46.0 6.7 %collective-permute-start.13 = (bf16[192,384]{1,0:T(8,128)(2,1)S(1)}, bf16[192,384]{1,0:T(8,128)(2,1)S(1)}, u32[]{:S(2)}, u32[]{:S(2)}) collective-permute-start(bf16[192,384]{1,0:T(8,128)(2,1)S(1)} %dynamic_slice.191), channel_id=1, source_target_pairs={{0,2},{1,3},{2,0},{3,1},{4,6},{5,7},{6,4},{7,5},{8,10},{9,11},{10,... | collective-permute-start | bytes 442376 | tf_op jit(solution)/shard_map/ppermute | solution.py:46
  46.0 16.9 %collective-permute-start.16 = (bf16[384,1152]{1,0:T(8,128)(2,1)S(1)}, bf16[384,1152]{1,0:T(8,128)(2,1)S(1)}, u32[]{:S(2)}, u32[]{:S(2)}) collective-permute-start(bf16[384,1152]{1,0:T(8,128)(2,1)S(1)} %constant_dynamic-update-slice_fusion.7.refs_0_), channel_id=1, source_target_pairs={{0,8},{1,9},{2,10},{3,11},{4,12},{5,13},{6,14},{7,15},{8,0},{9,1},... | collective-permute-start | bytes 2654216 | tf_op jit(solution)/shard_map/ppermute | solution.py:46
  46.0 16.9 %collective-permute-start.17 = (bf16[384,1152]{1,0:T(8,128)(2,1)S(1)}, bf16[384,1152]{1,0:T(8,128)(2,1)S(1)}, u32[]{:S(2)}, u32[]{:S(2)}) collective-permute-start(bf16[384,1152]{1,0:T(8,128)(2,1)S(1)} %collective-permute-done.11.refs_1_), channel_id=1, source_target_pairs={{0,8},{1,9},{2,10},{3,11},{4,12},{5,13},{6,14},{7,15},{8,0},{9,1},... | collective-permute-start | bytes 2654216 | tf_op jit(solution)/shard_map/ppermute | solution.py:46
  46.6 14.0 %collective-permute-start.14 = (bf16[192,384]{1,0:T(8,128)(2,1)S(1)}, bf16[192,384]{1,0:T(8,128)(2,1)S(1)}, u32[]{:S(2)}, u32[]{:S(2)}) collective-permute-start(bf16[192,384]{1,0:T(8,128)(2,1)S(1)} %dynamic_slice.191), channel_id=1, source_target_pairs={{0,4},{1,5},{2,6},{3,7},{4,0},{5,1},{6,2},{7,3},{8,12},{9,13},{10,... | collective-permute-start | bytes 442376 | tf_op jit(solution)/shard_map/ppermute | solution.py:46
  52.7 7.8 %collective-permute-start.15 = (bf16[192,384]{1,0:T(8,128)(2,1)S(1)}, bf16[192,384]{1,0:T(8,128)(2,1)S(1)}, u32[]{:S(2)}, u32[]{:S(2)}) collective-permute-start(bf16[192,384]{1,0:T(8,128)(2,1)S(1)} %dynamic_slice.191), channel_id=1, source_target_pairs={{0,6},{1,7},{2,4},{3,5},{4,2},{5,3},{6,0},{7,1},{8,14},{9,15},{10,... | collective-permute-start | bytes 442376 | tf_op jit(solution)/shard_map/ppermute | solution.py:46
  60.8 16.3 %collective-permute-start.18 = (bf16[768,384]{1,0:T(8,128)(2,1)S(1)}, bf16[768,384]{1,0:T(8,128)(2,1)S(1)}, u32[]{:S(2)}, u32[]{:S(2)}) collective-permute-start(bf16[768,384]{1,0:T(8,128)(2,1)S(1)} %pad_maximum_fusion.3), channel_id=1, source_target_pairs={{0,16},{1,17},{2,18},{3,19},{4,20},{5,21},{6,22},{7,23},{8,9},{9,8... | collective-permute-start | bytes 1769480 | tf_op jit(solution)/shard_map/ppermute | solution.py:46
  62.0 30.4 %collective-permute-start.19 = (bf16[384,1920]{1,0:T(8,128)(2,1)S(1)}, bf16[384,1920]{1,0:T(8,128)(2,1)}, u32[]{:S(2)}, u32[]{:S(2)}) collective-permute-start(bf16[384,1920]{1,0:T(8,128)(2,1)S(1)} %pad_maximum_fusion.refs_0_), channel_id=1, source_target_pairs={{0,1},{1,0},{2,3},{3,2},{4,5},{5,4},{6,7},{7,6},{8,24},{9,25},{10,... | collective-permute-start | bytes 4423688 | tf_op jit(solution)/shard_map/ppermute | solution.py:46
  62.9 29.5 %collective-permute-start.21 = (bf16[384,1920]{1,0:T(8,128)(2,1)S(1)}, bf16[384,1920]{1,0:T(8,128)(2,1)}, u32[]{:S(2)}, u32[]{:S(2)}) collective-permute-start(bf16[384,1920]{1,0:T(8,128)(2,1)S(1)} %pad_maximum_fusion.refs_0_), channel_id=1, source_target_pairs={{0,8},{1,9},{2,10},{3,11},{4,12},{5,13},{6,14},{7,15},{8,0},{9,1},... | collective-permute-start | bytes 4423688 | tf_op jit(solution)/shard_map/ppermute | solution.py:46
  77.3 17.6 %collective-permute-start.20 = (bf16[1536,384]{1,0:T(8,128)(2,1)S(1)}, bf16[1536,384]{1,0:T(8,128)(2,1)S(1)}, u32[]{:S(2)}, u32[]{:S(2)}) collective-permute-start(bf16[1536,384]{1,0:T(8,128)(2,1)S(1)} %pad_maximum_fusion.1.refs_4_), channel_id=1, source_target_pairs={{0,1},{1,0},{2,3},{3,2},{4,5},{5,4},{6,7},{7,6},{8,24},{9,25},{10,... | collective-permute-start | bytes 3538952 | tf_op jit(solution)/shard_map/ppermute | solution.py:46
  78.3 16.6 %collective-permute-start.22 = (bf16[1536,384]{1,0:T(8,128)(2,1)S(1)}, bf16[1536,384]{1,0:T(8,128)(2,1)}, u32[]{:S(2)}, u32[]{:S(2)}) collective-permute-start(bf16[1536,384]{1,0:T(8,128)(2,1)S(1)} %pad_maximum_fusion.1.refs_4_), channel_id=1, source_target_pairs={{0,8},{1,9},{2,10},{3,11},{4,12},{5,13},{6,14},{7,15},{8,0},{9,1},... | collective-permute-start | bytes 3538952 | tf_op jit(solution)/shard_map/ppermute | solution.py:46
  95.8 5.3 %collective-permute-start.23 = (bf16[384,1920]{1,0:T(8,128)(2,1)}, bf16[384,1920]{1,0:T(8,128)(2,1)S(1)}, u32[]{:S(2)}, u32[]{:S(2)}) collective-permute-start(bf16[384,1920]{1,0:T(8,128)(2,1)} %collective-permute-done.19.refs_1_), channel_id=1, source_target_pairs={{0,8},{1,9},{2,10},{3,11},{4,12},{5,13},{6,14},{7,15},{8,0},{9,1},... | collective-permute-start | bytes 4423688 | tf_op jit(solution)/shard_map/ppermute | solution.py:46
  156.1 7.8 %collective-permute-start.25 = (bf16[768,1920]{1,0:T(8,128)(2,1)}, bf16[768,1920]{1,0:T(8,128)(2,1)S(1)}, u32[]{:S(2)}, u32[]{:S(2)}) collective-permute-start(bf16[768,1920]{1,0:T(8,128)(2,1)} %mid_give.1), channel_id=1, source_target_pairs={{0,8},{1,9},{2,10},{3,11},{4,12},{5,13},{6,14},{7,15},{8,0},{9,1},... | collective-permute-start | bytes 8847368 | tf_op jit(solution)/shard_map/ppermute | solution.py:46
  164.0 10.4 %collective-permute-start.26 = (bf16[3072,384]{1,0:T(8,128)(2,1)}, bf16[3072,384]{1,0:T(8,128)(2,1)}, u32[]{:S(2)}, u32[]{:S(2)}) collective-permute-start(bf16[3072,384]{1,0:T(8,128)(2,1)} %down_give.1), channel_id=1, source_target_pairs={{0,8},{1,9},{2,10},{3,11},{4,12},{5,13},{6,14},{7,15},{8,0},{9,1},... | collective-permute-start | bytes 7077896 | tf_op jit(solution)/shard_map/ppermute | solution.py:46
  174.4 32.4 %collective-permute-start.28 = (bf16[4,2,48,1920]{3,2,1,0:T(8,128)(2,1)}, bf16[4,2,48,1920]{3,2,1,0:T(8,128)(2,1)S(1)}, u32[]{:S(2)}, u32[]{:S(2)}) collective-permute-start(bf16[4,2,48,1920]{3,2,1,0:T(8,128)(2,1)} %get-tuple-element.190), channel_id=1, source_target_pairs={{0,1},{1,0},{2,3},{3,2},{4,5},{5,4},{6,7},{7,6},{8,24},{9,25},{10,... | collective-permute-start | bytes 4423688 | tf_op jit(solution)/shard_map/ppermute | solution.py:46
  185.1 21.6 %collective-permute-start.27 = (bf16[4,2,192,384]{3,2,0,1:T(8,128)(2,1)S(1)}, bf16[4,2,192,384]{3,2,0,1:T(8,128)(2,1)}, u32[]{:S(2)}, u32[]{:S(2)}) collective-permute-start(bf16[4,2,192,384]{3,2,0,1:T(8,128)(2,1)S(1)} %copy.37), channel_id=1, source_target_pairs={{0,1},{1,0},{2,3},{3,2},{4,5},{5,4},{6,7},{7,6},{8,24},{9,25},{10,... | collective-permute-start | bytes 3538952 | tf_op jit(solution)/shard_map/ppermute | solution.py:46
  209.2 11.6 %collective-permute-start.30 = (bf16[768,1152]{1,0:T(8,128)(2,1)}, bf16[768,1152]{1,0:T(8,128)(2,1)}, u32[]{:S(2)}, u32[]{:S(2)}) collective-permute-start(bf16[768,1152]{1,0:T(8,128)(2,1)} %get-tuple-element.202), channel_id=1, source_target_pairs={{0,8},{1,9},{2,10},{3,11},{4,12},{5,13},{6,14},{7,15},{8,0},{9,1},... | collective-permute-start | bytes 5308424 | tf_op jit(solution)/shard_map/ppermute | solution.py:46
  209.3 11.5 %collective-permute-start.29 = (bf16[4,48,1920]{2,1,0:T(8,128)(2,1)S(1)}, bf16[4,48,1920]{2,1,0:T(8,128)(2,1)S(1)}, u32[]{:S(2)}, u32[]{:S(2)}) collective-permute-start(bf16[4,48,1920]{2,1,0:T(8,128)(2,1)S(1)} %get-tuple-element.201), channel_id=1, source_target_pairs={{0,16},{1,17},{2,18},{3,19},{4,20},{5,21},{6,22},{7,23},{8,9},{9,8... | collective-permute-start | bytes 2211848 | tf_op jit(solution)/shard_map/ppermute | solution.py:46
  221.9 26.9 %collective-permute-start.31 = (bf16[4,192,384]{2,1,0:T(8,128)(2,1)}, bf16[4,192,384]{2,1,0:T(8,128)(2,1)S(1)}, u32[]{:S(2)}, u32[]{:S(2)}) collective-permute-start(bf16[4,192,384]{2,1,0:T(8,128)(2,1)} %fusion.2), channel_id=1, source_target_pairs={{0,16},{1,17},{2,18},{3,19},{4,20},{5,21},{6,22},{7,23},{8,9},{9,8... | collective-permute-start | bytes 1769480 | tf_op jit(solution)/shard_map/ppermute | solution.py:46
  223.3 25.3 %collective-permute-start.32 = (bf16[48,1920]{1,0:T(8,128)(2,1)}, bf16[48,1920]{1,0:T(8,128)(2,1)S(1)}, u32[]{:S(2)}, u32[]{:S(2)}) collective-permute-start(bf16[48,1920]{1,0:T(8,128)(2,1)} %get-tuple-element.209), channel_id=1, source_target_pairs={{0,2},{1,3},{2,0},{3,1},{4,6},{5,7},{6,4},{7,5},{8,10},{9,11},{10,... | collective-permute-start | bytes 552968 | tf_op jit(solution)/shard_map/ppermute | solution.py:46
  228.6 20.0 %collective-permute-start.33 = (bf16[48,1920]{1,0:T(8,128)(2,1)}, bf16[48,1920]{1,0:T(8,128)(2,1)S(1)}, u32[]{:S(2)}, u32[]{:S(2)}) collective-permute-start(bf16[48,1920]{1,0:T(8,128)(2,1)} %get-tuple-element.210), channel_id=1, source_target_pairs={{0,4},{1,5},{2,6},{3,7},{4,0},{5,1},{6,2},{7,3},{8,12},{9,13},{10,... | collective-permute-start | bytes 552968 | tf_op jit(solution)/shard_map/ppermute | solution.py:46
  229.0 19.8 %collective-permute-start.34 = (bf16[48,1920]{1,0:T(8,128)(2,1)}, bf16[48,1920]{1,0:T(8,128)(2,1)S(1)}, u32[]{:S(2)}, u32[]{:S(2)}) collective-permute-start(bf16[48,1920]{1,0:T(8,128)(2,1)} %get-tuple-element.211), channel_id=1, source_target_pairs={{0,6},{1,7},{2,4},{3,5},{4,2},{5,3},{6,0},{7,1},{8,14},{9,15},{10,... | collective-permute-start | bytes 552968 | tf_op jit(solution)/shard_map/ppermute | solution.py:46
  249.6 19.9 %collective-permute-start.35 = (bf16[4,2,48,1152]{3,2,1,0:T(8,128)(2,1)}, bf16[4,2,48,1152]{3,2,1,0:T(8,128)(2,1)S(1)}, u32[]{:S(2)}, u32[]{:S(2)}) collective-permute-start(bf16[4,2,48,1152]{3,2,1,0:T(8,128)(2,1)} %get-tuple-element.214), channel_id=1, source_target_pairs={{0,1},{1,0},{2,3},{3,2},{4,5},{5,4},{6,7},{7,6},{8,24},{9,25},{10,... | collective-permute-start | bytes 2654216 | tf_op jit(solution)/shard_map/ppermute | solution.py:46
  255.9 13.6 %collective-permute-start.36 = (bf16[192,384]{1,0:T(8,128)(2,1)}, bf16[192,384]{1,0:T(8,128)(2,1)S(1)}, u32[]{:S(2)}, u32[]{:S(2)}) collective-permute-start(bf16[192,384]{1,0:T(8,128)(2,1)} %get-tuple-element.221), channel_id=1, source_target_pairs={{0,2},{1,3},{2,0},{3,1},{4,6},{5,7},{6,4},{7,5},{8,10},{9,11},{10,... | collective-permute-start | bytes 442376 | tf_op jit(solution)/shard_map/ppermute | solution.py:46
  257.0 12.5 %collective-permute-start.37 = (bf16[192,384]{1,0:T(8,128)(2,1)S(1)}, bf16[192,384]{1,0:T(8,128)(2,1)S(1)}, u32[]{:S(2)}, u32[]{:S(2)}) collective-permute-start(bf16[192,384]{1,0:T(8,128)(2,1)S(1)} %get-tuple-element.222), channel_id=1, source_target_pairs={{0,4},{1,5},{2,6},{3,7},{4,0},{5,1},{6,2},{7,3},{8,12},{9,13},{10,... | collective-permute-start | bytes 442376 | tf_op jit(solution)/shard_map/ppermute | solution.py:46
  258.3 11.3 %collective-permute-start.38 = (bf16[192,384]{1,0:T(8,128)(2,1)S(1)}, bf16[192,384]{1,0:T(8,128)(2,1)S(1)}, u32[]{:S(2)}, u32[]{:S(2)}) collective-permute-start(bf16[192,384]{1,0:T(8,128)(2,1)S(1)} %get-tuple-element.223), channel_id=1, source_target_pairs={{0,6},{1,7},{2,4},{3,5},{4,2},{5,3},{6,0},{7,1},{8,14},{9,15},{10,... | collective-permute-start | bytes 442376 | tf_op jit(solution)/shard_map/ppermute | solution.py:46
  260.3 9.2 %collective-permute-start.39 = (f32[24,768]{1,0:T(8,128)}, f32[24,768]{1,0:T(8,128)}, u32[]{:S(2)}, u32[]{:S(2)}) collective-permute-start(f32[24,768]{1,0:T(8,128)} %pack.1), channel_id=1, source_target_pairs={{0,1},{1,0},{2,3},{3,2},{4,5},{5,4},{6,7},{7,6},{8,9},{9,8},{10,11... | collective-permute-start | bytes 221192 | tf_op jit(solution)/shard_map/ppermute | solution.py:46
  270.7 10.3 %collective-permute-start.40 = (bf16[4,48,1152]{2,1,0:T(8,128)(2,1)S(1)}, bf16[4,48,1152]{2,1,0:T(8,128)(2,1)S(1)}, u32[]{:S(2)}, u32[]{:S(2)}) collective-permute-start(bf16[4,48,1152]{2,1,0:T(8,128)(2,1)S(1)} %get-tuple-element.237), channel_id=1, source_target_pairs={{0,16},{1,17},{2,18},{3,19},{4,20},{5,21},{6,22},{7,23},{8,9},{9,8... | collective-permute-start | bytes 1327112 | tf_op jit(solution)/shard_map/ppermute | solution.py:46
  275.7 5.3 %collective-permute-start.42 = (f32[24,768]{1,0:T(8,128)S(1)}, f32[24,768]{1,0:T(8,128)S(1)}, u32[]{:S(2)}, u32[]{:S(2)}) collective-permute-start(f32[24,768]{1,0:T(8,128)S(1)} %add.332), channel_id=1, source_target_pairs={{0,4},{1,5},{2,6},{3,7},{4,0},{5,1},{6,2},{7,3},{8,12},{9,13},{10,... | collective-permute-start | bytes 221192 | tf_op jit(solution)/shard_map/ppermute | solution.py:46
  281.1 12.4 %collective-permute-start.47 = (bf16[48,1920]{1,0:T(8,128)(2,1)S(1)}, bf16[48,1920]{1,0:T(8,128)(2,1)S(1)}, u32[]{:S(2)}, u32[]{:S(2)}) collective-permute-start(bf16[48,1920]{1,0:T(8,128)(2,1)S(1)} %fusion.6), channel_id=1, source_target_pairs={{0,16},{1,17},{2,18},{3,19},{4,20},{5,21},{6,22},{7,23},{8,24},{9,... | collective-permute-start | bytes 552968 | tf_op jit(solution)/shard_map/ppermute | solution.py:46
  282.8 10.7 %collective-permute-start.46 = (bf16[192,384]{1,0:T(8,128)(2,1)S(1)}, bf16[192,384]{1,0:T(8,128)(2,1)S(1)}, u32[]{:S(2)}, u32[]{:S(2)}) collective-permute-start(bf16[192,384]{1,0:T(8,128)(2,1)S(1)} %fusion.13), channel_id=1, source_target_pairs={{0,16},{1,17},{2,18},{3,19},{4,20},{5,21},{6,22},{7,23},{8,24},{9,... | collective-permute-start | bytes 442376 | tf_op jit(solution)/shard_map/ppermute | solution.py:46
  283.2 5.6 %collective-permute-start.43 = (bf16[48,1152]{1,0:T(8,128)(2,1)S(1)}, bf16[48,1152]{1,0:T(8,128)(2,1)S(1)}, u32[]{:S(2)}, u32[]{:S(2)}) collective-permute-start(bf16[48,1152]{1,0:T(8,128)(2,1)S(1)} %get-tuple-element.247), channel_id=1, source_target_pairs={{0,2},{1,3},{2,0},{3,1},{4,6},{5,7},{6,4},{7,5},{8,10},{9,11},{10,... | collective-permute-start | bytes 331784 | tf_op jit(solution)/shard_map/ppermute | solution.py:46
  285.5 8.0 %collective-permute-start.44 = (bf16[48,1152]{1,0:T(8,128)(2,1)S(1)}, bf16[48,1152]{1,0:T(8,128)(2,1)S(1)}, u32[]{:S(2)}, u32[]{:S(2)}) collective-permute-start(bf16[48,1152]{1,0:T(8,128)(2,1)S(1)} %get-tuple-element.248), channel_id=1, source_target_pairs={{0,4},{1,5},{2,6},{3,7},{4,0},{5,1},{6,2},{7,3},{8,12},{9,13},{10,... | collective-permute-start | bytes 331784 | tf_op jit(solution)/shard_map/ppermute | solution.py:46
  285.8 7.7 %collective-permute-start.45 = (bf16[48,1152]{1,0:T(8,128)(2,1)S(1)}, bf16[48,1152]{1,0:T(8,128)(2,1)S(1)}, u32[]{:S(2)}, u32[]{:S(2)}) collective-permute-start(bf16[48,1152]{1,0:T(8,128)(2,1)S(1)} %get-tuple-element.249), channel_id=1, source_target_pairs={{0,6},{1,7},{2,4},{3,5},{4,2},{5,3},{6,0},{7,1},{8,14},{9,15},{10,... | collective-permute-start | bytes 331784 | tf_op jit(solution)/shard_map/ppermute | solution.py:46
  293.8 6.0 %collective-permute-start.49 = (bf16[48,1152]{1,0:T(8,128)(2,1)S(1)}, bf16[48,1152]{1,0:T(8,128)(2,1)S(1)}, u32[]{:S(2)}, u32[]{:S(2)}) collective-permute-start(bf16[48,1152]{1,0:T(8,128)(2,1)S(1)} %fusion.23), channel_id=1, source_target_pairs={{0,16},{1,17},{2,18},{3,19},{4,20},{5,21},{6,22},{7,23},{8,24},{9,... | collective-permute-start | bytes 331784 | tf_op jit(solution)/shard_map/ppermute | solution.py:46
  295.8 5.7 %collective-permute-start.50 = (bf16[48,1152]{1,0:T(8,128)(2,1)S(1)}, bf16[48,1152]{1,0:T(8,128)(2,1)S(1)}, u32[]{:S(2)}, u32[]{:S(2)}) collective-permute-start(bf16[48,1152]{1,0:T(8,128)(2,1)S(1)} %fusion.23), channel_id=1, source_target_pairs={{0,24},{1,25},{2,26},{3,27},{4,28},{5,29},{6,30},{7,31},{8,16},{9,... | collective-permute-start | bytes 331784 | tf_op jit(solution)/shard_map/ppermute | solution.py:46
  296.0 9.2 %collective-permute-start.54 = (bf16[2,192,384]{2,1,0:T(8,128)(2,1)S(1)}, bf16[2,192,384]{2,1,0:T(8,128)(2,1)S(1)}, u32[]{:S(2)}, u32[]{:S(2)}) collective-permute-start(bf16[2,192,384]{2,1,0:T(8,128)(2,1)S(1)} %pad_maximum_fusion.7), channel_id=1, source_target_pairs={{0,8},{1,9},{2,10},{3,11},{4,12},{5,13},{6,14},{7,15},{8,0},{9,1},... | collective-permute-start | bytes 884744 | tf_op jit(solution)/shard_map/ppermute | solution.py:46
  297.1 9.5 %collective-permute-start.53 = (bf16[2,48,1920]{2,1,0:T(8,128)(2,1)S(1)}, bf16[2,48,1920]{2,1,0:T(8,128)(2,1)S(1)}, u32[]{:S(2)}, u32[]{:S(2)}) collective-permute-start(bf16[2,48,1920]{2,1,0:T(8,128)(2,1)S(1)} %pad_maximum_fusion.6), channel_id=1, source_target_pairs={{0,8},{1,9},{2,10},{3,11},{4,12},{5,13},{6,14},{7,15},{8,0},{9,1},... | collective-permute-start | bytes 1105928 | tf_op jit(solution)/shard_map/ppermute | solution.py:46
  297.3 6.1 %collective-permute-start.52 = (f32[24,768]{1,0:T(8,128)S(1)}, f32[24,768]{1,0:T(8,128)S(1)}, u32[]{:S(2)}, u32[]{:S(2)}) collective-permute-start(f32[24,768]{1,0:T(8,128)S(1)} %add.353), channel_id=1, source_target_pairs={{0,16},{1,17},{2,18},{3,19},{4,20},{5,21},{6,22},{7,23},{8,24},{9,... | collective-permute-start | bytes 221192 | tf_op jit(solution)/shard_map/ppermute | solution.py:46
  (48 other events, 418.6 us)

commit v5 on v3

--- a/solution.py
+++ b/solution.py
@@ -32,8 +32,8 @@
 
     return {
         "core": pairs(lambda y, c, z, x: (y, 1 - c, z, x)),
-        "first": pairs(lambda y, c, z, x: (1 - y, c, z, x) if c == 0 else (y, c, z, 1 - x)),
-        "second": pairs(lambda y, c, z, x: (y, c, z, 1 - x) if c == 0 else (1 - y, c, z, x)),
+        "first": pairs(lambda y, c, z, x: (1 - y, c, z, x) if c == z % 2 else (y, c, z, 1 - x)),
+        "second": pairs(lambda y, c, z, x: (y, c, z, 1 - x) if c == z % 2 else (1 - y, c, z, x)),
         "z": [pairs(lambda y, c, z, x, m=m: (y, c, z ^ m, x)) for m in range(1, n_z)],
         "rep": [pairs(lambda y, c, z, x, m=m: (y ^ (m // 2), c ^ (m % 2), z, x)) for m in (1, 2, 3)],
         "x": pairs(lambda y, c, z, x: (y, c, z, 1 - x)),
@@ -81,7 +81,7 @@
     out = []
     for side, source in ((0, grow(eight, got)), (1, grow(other_eight, other_got))):
         blocks = source.reshape(2, 2, n_z, rows, -1)
-        blocks = jnp.where(at[1] ^ side == 0, blocks, blocks.swapaxes(0, 1))
+        blocks = jnp.where(at[1] ^ side == z % 2, blocks, blocks.swapaxes(0, 1))
         blocks = flip_by(flip_by(flip_by(blocks, 0, x), 1, y), 2, z)
         out.append((blocks.transpose(2, 0, 1, 3, 4).reshape(source.shape),))
     return tuple(out)
@@ -92,14 +92,14 @@
 
 
 def sum_core(keep, got, at, n_z):
-    y, c, x = at[0], at[1], at[3]
+    y, c, x = at[0], at[1] ^ at[2] % 2, at[3]
     summed = add_low(keep, got).reshape(n_z, 2, 2, -1, keep.shape[1])
     away = jnp.where(c == 0, pick(summed, 1, 1 - x), pick(summed, 2, 1 - y))
     return jnp.where(c == 0, pick(summed, 1, x), pick(summed, 2, y)), away
 
 
 def sum_second(keep, got, at):
-    spot = jnp.where(at[1] == 0, at[0], at[3])
+    spot = jnp.where(at[1] == at[2] % 2, at[0], at[3])
     return tuple(add_low(pick(keep, 1, which), pick(got, 1, which)) for which in (spot, 1 - spot))
 
 
@@ -189,8 +189,8 @@
                 continue
             for late, ref in enumerate(pieces):
                 for b in (0, 1):
-                    by_x = jnp.bitwise_xor(x, jnp.where(core == 0, late, b))
-                    by_y = jnp.bitwise_xor(y, jnp.where(core == 0, b, late))
+                    by_x = jnp.bitwise_xor(x, jnp.where(core == z % 2, late, b))
+                    by_y = jnp.bitwise_xor(y, jnp.where(core == z % 2, b, late))
                     for m in range(n_z):
                         slot = (jnp.bitwise_xor(z, m) * 2 + by_x) * 2 + by_y
                         pltpu.make_async_copy(
@@ -511,7 +511,7 @@
 
 def split_sum(at_ref, grad, got_ref, away_ref, stay_ref, sum_ref, lanes):
     sum_ref[:, lanes] = (grad + got_ref[:, lanes].astype(jnp.float32)).astype(jnp.bfloat16)
-    y, c, x = at_ref[0], at_ref[1], at_ref[3]
+    y, c, x = at_ref[0], jnp.bitwise_xor(at_ref[1], at_ref[2] % 2), at_ref[3]
     rows = away_ref.shape[2]
     for z in range(away_ref.shape[0]):
         for b in (0, 1):

time: 316 us -> 315 us (level)
  no operation moved by 1% of the time
where the time goes in v5:
time: 315 us; the launch traced here: 308 us
  Pallas kernels  157 us (50%)
  starting transfers between devices  61.7 us (20%)
  waiting for transfers between devices  56.6 us (18%)
  other arithmetic  16.4 us (5%)
  local copies, waits for them, and re-layouts  14.2 us (5%)
    ppermute x55, starting transfers between devices, send(): return lax.ppermute(value, AXES, pairs)  61.7 us
    ppermute x55, waiting for transfers between devices, send(): return lax.ppermute(value, AXES, pairs)  56.6 us
    pallas_call x1, Pallas kernels, ffn(): call(functools.partial(ffn_kernel, n_z, len(mid)), (count // FFN_TILE,),...  45.3 us
    pallas_call x2, Pallas kernels, attend_back(): call(functools.partial(attend_back_kernel, docs, fused), (n_pair,), [part...  34.8 us
    pallas_call x2, Pallas kernels, grads(): call(functools.partial(grad_kernel, n_first, True), (steps,), specs + [sp...  17.2 us
    pallas_call x2, Pallas kernels, embed_grad(): call(functools.partial(embed_grad_kernel, n_z, side), (count // TILE,), [...  16.5 us
    pallas_call x2, Pallas kernels, grads(): call(plain, (steps,), specs, spec, jax.ShapeDtypeStruct((rows, width), jn...  16.1 us
    pallas_call x1, Pallas kernels, attend(): call(functools.partial(attend_kernel, docs), (2 * n_pair,), [part(0), par...  14.2 us
  transfers between devices with their start and end apart: 55, of which 22 were waited for; matrix products, arithmetic and copies ran while one was open for 6% of the time, Pallas kernels for 34%

profile of v5, /device:TPU:0, one launch (start us, length us, event | category | flops | bytes accessed | tf_op | source)
XLA Modules:
  0.0 308.5 jit_solution(13415012700619212244)
XLA Ops:
  2.0 3.1 %collective-permute-start = (bf16[48,1152]{1,0:T(8,128)(2,1)S(1)}, bf16[48,1152]{1,0:T(8,128)(2,1)S(1)}, u32[]{:S(2)}, u32[]{:S(2)}) collective-permute-start(bf16[48,1152]{1,0:T(8,128)(2,1)S(1)} %pad_maximum_fusion.9), channel_id=1, source_target_pairs={{0,2},{1,3},{2,0},{3,1},{4,6},{5,7},{6,4},{7,5},{8,10},{9,11},{10,... | collective-permute-start | bytes 331784 | tf_op jit(solution)/shard_map/ppermute | solution.py:45
  5.1 2.6 collective-permute-start.1
  9.7 6.8 %collective-permute-done.1 = bf16[48,1152]{1,0:T(8,128)(2,1)S(1)} collective-permute-done((bf16[48,1152]{1,0:T(8,128)(2,1)S(1)}, bf16[48,1152]{1,0:T(8,128)(2,1)S(1)}, u32[]{:S(2)}, u32[]{:S(2)}) %collective-permute-start.1) | collective-permute-done | bytes 110624 | tf_op jit(solution)/shard_map/ppermute | solution.py:45
  16.5 1.6 collective-permute-start.4
  18.1 1.5 collective-permute-start.3
  20.4 1.6 collective-permute-start.5
  23.4 1.5 collective-permute-start.7
  24.9 1.9 collective-permute-done.6
  26.8 2.2 collective-permute-done.7
  29.0 1.7 collective-permute-start.11
  32.1 3.0 collective-permute-start.9
  36.6 1.6 unpack.1
  38.7 1.7 collective-permute-done.8
  40.3 4.5 %collective-permute-done.9 = bf16[48,1920]{1,0:T(8,128)(2,1)S(1)} collective-permute-done((bf16[48,1920]{1,0:T(8,128)(2,1)S(1)}, bf16[48,1920]{1,0:T(8,128)(2,1)S(1)}, u32[]{:S(2)}, u32[]{:S(2)}) %collective-permute-start.9) | collective-permute-done | bytes 184352 | tf_op jit(solution)/shard_map/ppermute | solution.py:45
  46.1 2.6 collective-permute-start.14
  48.7 1.8 collective-permute-start.15
  50.5 2.3 collective-permute-done.13
  52.8 7.2 %collective-permute-done.14 = bf16[192,384]{1,0:T(8,128)(2,1)S(1)} collective-permute-done((bf16[192,384]{1,0:T(8,128)(2,1)S(1)}, bf16[192,384]{1,0:T(8,128)(2,1)S(1)}, u32[]{:S(2)}, u32[]{:S(2)}) %collective-permute-start.14) | collective-permute-done | bytes 147488 | tf_op jit(solution)/shard_map/ppermute | solution.py:45
  65.1 10.1 %project.1 = (bf16[2,1024,1152]{2,1,0:T(8,128)(2,1)}, bf16[1024,768]{1,0:T(8,128)(2,1)}) custom-call(s32[4]{0:T(128)} %pad_add_fusion.at_ref, bf16[16,1024]{1,0:T(8,128)(2,1)} %maximum_maximum_fusion.3.flag_ref, bf16[1024,768]{1,0:T(8,128)(2,1)} %bitcast.204, bf16[16,768]{1,0:T(8,128)(2,1)} %get-tuple-element.150.row_ref, ...), custom_call_target="tpu_custom_call" | custom-call | flops 3623878656 | bytes 12582912 | tf_op jit(solution)/shard_map/project/pallas_call | solution.py:231
  77.4 1.8 collective-permute-start.20
  79.2 14.2 %attend.1 = (bf16[1024,768]{1,0:T(8,128)(2,1)}, f32[1024,768]{1,0:T(8,128)}, bf16[2,3,2,2,512,512]{5,4,3,2,1,0:T(8,128)(2,1)}) custom-call(s32[2]{0:T(128)} %len_ref.1, bf16[2,1024,1152]{2,1,0:T(8,128)(2,1)} %get-tuple-element.157.q_ref.k_ref.v_ref, bf16[2,1024,1152]{2,1,0:T(8,128)(2,1)} %get-tuple-element.157.q_ref.k_ref.v_ref, ...), custom_call_target="tpu_custom_call" | custom-call | flops 6442450944 | bytes 34603008 | tf_op jit(solution)/shard_map/attend/pallas_call | solution.py:322
  93.5 3.5 %collective-permute-done.20.refs_5_ = bf16[1536,384]{1,0:T(8,128)(2,1)S(1)} collective-permute-done((bf16[1536,384]{1,0:T(8,128)(2,1)S(1)}, bf16[1536,384]{1,0:T(8,128)(2,1)S(1)}, u32[]{:S(2)}, u32[]{:S(2)}) %collective-permute-start.20) | collective-permute-done | bytes 1179680 | tf_op jit(solution)/shard_map/ppermute | solution.py:45
  98.0 1.4 collective-permute-start.23
  100.1 4.2 %collective-permute-done.24.refs_7_ = bf16[1536,384]{1,0:T(8,128)(2,1)S(1)} collective-permute-done((bf16[1536,384]{1,0:T(8,128)(2,1)}, bf16[1536,384]{1,0:T(8,128)(2,1)S(1)}, u32[]{:S(2)}, u32[]{:S(2)}) %collective-permute-start.24) | collective-permute-done | bytes 1179680 | tf_op jit(solution)/shard_map/ppermute | solution.py:45
  105.8 45.3 %ffn.1 = (bf16[1024,768]{1,0:T(8,128)(2,1)}, bf16[1024,768]{1,0:T(8,128)(2,1)}, bf16[1024,3072]{1,0:T(8,128)(2,1)}, bf16[1024,768]{1,0:T(8,128)(2,1)}, bf16[1024...) custom-call(s32[4]{0:T(128)} %pad_add_fusion.at_ref, ...), custom_call_target="tpu_custom_call" | custom-call | flops 21743271936 | bytes 47529984 | tf_op jit(solution)/shard_map/ffn/pallas_call | solution.py:486
  151.1 8.2 %mid_give.1 = bf16[768,1920]{1,0:T(8,128)(2,1)} custom-call(s32[5]{0:T(128)} %concatenate.169.at_ref, bf16[1024,768]{1,0:T(8,128)(2,1)} %get-tuple-element.168.refs_0_, bf16[1024,3072]{1,0:T(8,128)(2,1)} %get-tuple-element.169.refs_1_, bf16[1024,768]{1,0:T(8,128)(2,1)} %get-tuple-element.161.ctx_ref.refs_2_, bf16[1024,768]{1,0:T(8,128)(2,1)} %get-tuple-element.170.refs_3_), custom_call_target="tpu_custom_call" | custom-call | flops 3019898880 | bytes 5898240 | tf_op jit(solution)/shard_map/mid_give/pallas_call | solution.py:572
  159.7 7.9 %down_give.1 = bf16[3072,384]{1,0:T(8,128)(2,1)} custom-call(s32[5]{0:T(128)} %concatenate.169.at_ref, bf16[1024,3072]{1,0:T(8,128)(2,1)} %get-tuple-element.173.refs_0_, bf16[1024,768]{1,0:T(8,128)(2,1)} %get-tuple-element.174.refs_1_), custom_call_target="tpu_custom_call" | custom-call | flops 2415919104 | bytes 4718592 | tf_op jit(solution)/shard_map/down_give/pallas_call | solution.py:572
  169.1 8.9 %mid_keep.1 = (bf16[4,2,48,1920]{3,2,1,0:T(8,128)(2,1)}, bf16[4,2,48,1920]{3,2,1,0:T(8,128)(2,1)}) custom-call(s32[5]{0:T(128)} %concatenate.168.at_ref, bf16[1024,768]{1,0:T(8,128)(2,1)} %get-tuple-element.168.refs_0_, bf16[1024,3072]{1,0:T(8,128)(2,1)} %get-tuple-element.169.refs_1_, bf16[1024,768]{1,0:T(8,128)(2,1)} %get-tuple-element.161.ctx_ref.refs_2_, ...), custom_call_target="tpu_custom_call" | custom-call | flops 3019898880 | bytes 5898240 | tf_op jit(solution)/shard_map/mid_keep/pallas_call | solution.py:583
  179.3 8.4 %down_keep.1 = (bf16[4,2,192,384]{3,2,1,0:T(8,128)(2,1)}, bf16[4,2,192,384]{3,2,1,0:T(8,128)(2,1)}) custom-call(s32[5]{0:T(128)} %concatenate.168.at_ref, bf16[1024,3072]{1,0:T(8,128)(2,1)} %get-tuple-element.173.refs_0_, bf16[1024,768]{1,0:T(8,128)(2,1)} %get-tuple-element.174.refs_1_, bf16[3072,384]{1,0:T(8,128)(2,1)} %collective-permute-done.26.refs_2_), custom_call_target="tpu_custom_call" | custom-call | flops 2415919104 | bytes 4718592 | tf_op jit(solution)/shard_map/down_keep/pallas_call | solution.py:583
  189.9 17.1 %attend_back.2 = (bf16[1024,1152]{1,0:T(8,128)(2,1)}, f32[16,1152]{1,0:T(8,128)}, bf16[768,1152]{1,0:T(8,128)(2,1)}) custom-call(s32[5]{0:T(128)} %concatenate.169.at_ref, bf16[2,1024,1152]{2,1,0:T(8,128)(2,1)} %get-tuple-element.157.q_ref.k_ref.v_ref, bf16[2,1024,1152]{2,1,0:T(8,128)(2,1)} %get-tuple-element.157.q_ref.k_ref.v_ref, ...), custom_call_target="tpu_custom_call" | custom-call | flops 9865003008 | bytes 8404992 | tf_op jit(solution)/shard_map/attend_back/pallas_call | solution.py:651
  207.0 3.3 %collective-permute-done.27 = bf16[4,2,192,384]{3,2,0,1:T(8,128)(2,1)} collective-permute-done((bf16[4,2,192,384]{3,2,0,1:T(8,128)(2,1)S(1)}, bf16[4,2,192,384]{3,2,0,1:T(8,128)(2,1)}, u32[]{:S(2)}, u32[]{:S(2)}) %collective-permute-start.27) | collective-permute-done | bytes 1179680 | tf_op jit(solution)/shard_map/ppermute | solution.py:45
  213.1 8.4 %embed_grad.2.before_ref = f32[1024,768]{1,0:T(8,128)} custom-call(s32[4]{0:T(128)} %pad_add_fusion.at_ref, f32[1024,768]{1,0:T(8,128)} %get-tuple-element.196.before_ref, bf16[1024,1152]{1,0:T(8,128)(2,1)} %get-tuple-element.197.dqkv_ref, bf16[384,1152]{1,0:T(8,128)(2,1)} %copy-done.10, bf16[384,1152]{1,0:T(8,128)(2,1)} %copy-done.11), custom_call_target="tpu_custom_call" | custom-call | flops 1811939328 | bytes 6291456 | tf_op jit(solution)/shard_map/embed_grad/pallas_call | solution.py:686
  221.5 2.1 collective-permute-done.29
  225.5 3.8 %collective-permute-start.32 = (bf16[48,1920]{1,0:T(8,128)(2,1)}, bf16[48,1920]{1,0:T(8,128)(2,1)S(1)}, u32[]{:S(2)}, u32[]{:S(2)}) collective-permute-start(bf16[48,1920]{1,0:T(8,128)(2,1)} %get-tuple-element.202), channel_id=1, source_target_pairs={{0,2},{1,3},{2,0},{3,1},{4,6},{5,7},{6,4},{7,5},{8,10},{9,11},{10,... | collective-permute-start | bytes 552968 | tf_op jit(solution)/shard_map/ppermute | solution.py:45
  229.3 2.4 collective-permute-start.34
  231.7 17.7 %attend_back.3 = (bf16[1024,1152]{1,0:T(8,128)(2,1)}, f32[16,1152]{1,0:T(8,128)}, bf16[4,2,48,1152]{3,2,1,0:T(8,128)(2,1)}, bf16[4,2,48,1152]{3,2,1,0:T(8,128)(2,1)}) custom-call(s32[5]{0:T(128)} %concatenate.168.at_ref, bf16[2,1024,1152]{2,1,0:T(8,128)(2,1)} %get-tuple-element.157.q_ref.k_ref.v_ref, ...), custom_call_target="tpu_custom_call" | custom-call | flops 9865003008 | bytes 8404992 | tf_op jit(solution)/shard_map/attend_back/pallas_call | solution.py:651
  252.0 1.7 pack.1
  253.7 1.9 fusion.43
  258.1 1.8 collective-permute-start.38
  262.4 8.1 %embed_grad.3 = bf16[1024,768]{1,0:T(8,128)(2,1)} custom-call(s32[4]{0:T(128)} %pad_add_fusion.at_ref, f32[1024,768]{1,0:T(8,128)} %embed_grad.2.before_ref, bf16[1024,1152]{1,0:T(8,128)(2,1)} %get-tuple-element.219.dqkv_ref, bf16[384,1152]{1,0:T(8,128)(2,1)} %copy-done.2, bf16[384,1152]{1,0:T(8,128)(2,1)} %copy-done.8), custom_call_target="tpu_custom_call" | custom-call | flops 1811939328 | bytes 3145728 | tf_op jit(solution)/shard_map/embed_grad/pallas_call | solution.py:686
  274.2 2.1 collective-permute-done.42
  276.3 2.3 collective-permute-start.43
  279.7 1.9 collective-permute-done.43
  281.7 3.6 %collective-permute-done.41 = bf16[48,1920]{1,0:T(8,128)(2,1)S(1)} collective-permute-done((bf16[48,1920]{1,0:T(8,128)(2,1)S(1)}, bf16[48,1920]{1,0:T(8,128)(2,1)S(1)}, u32[]{:S(2)}, u32[]{:S(2)}) %collective-permute-start.41) | collective-permute-done | bytes 184352 | tf_op jit(solution)/shard_map/ppermute | solution.py:45
  287.4 4.4 %collective-permute-start.46 = (bf16[48,1152]{1,0:T(8,128)(2,1)S(1)}, bf16[48,1152]{1,0:T(8,128)(2,1)S(1)}, u32[]{:S(2)}, u32[]{:S(2)}) collective-permute-start(bf16[48,1152]{1,0:T(8,128)(2,1)S(1)} %get-tuple-element.241), channel_id=1, source_target_pairs={{0,6},{1,7},{2,4},{3,5},{4,2},{5,3},{6,0},{7,1},{8,14},{9,15},{10,... | collective-permute-start | bytes 331784 | tf_op jit(solution)/shard_map/ppermute | solution.py:45
  293.4 2.5 collective-permute-done.46
  300.3 1.6 collective-permute-done.51
  301.9 1.5 collective-permute-done.52
  (233 shorter events, 55.8 us)
Async XLA Ops:
  2.0 7.7 %collective-permute-start = (bf16[48,1152]{1,0:T(8,128)(2,1)S(1)}, bf16[48,1152]{1,0:T(8,128)(2,1)S(1)}, u32[]{:S(2)}, u32[]{:S(2)}) collective-permute-start(bf16[48,1152]{1,0:T(8,128)(2,1)S(1)} %pad_maximum_fusion.9), channel_id=1, source_target_pairs={{0,2},{1,3},{2,0},{3,1},{4,6},{5,7},{6,4},{7,5},{8,10},{9,11},{10,... | collective-permute-start | bytes 331784 | tf_op jit(solution)/shard_map/ppermute | solution.py:45
  5.1 11.3 %collective-permute-start.1 = (bf16[48,1152]{1,0:T(8,128)(2,1)S(1)}, bf16[48,1152]{1,0:T(8,128)(2,1)S(1)}, u32[]{:S(2)}, u32[]{:S(2)}) collective-permute-start(bf16[48,1152]{1,0:T(8,128)(2,1)S(1)} %pad_maximum_fusion.9), channel_id=1, source_target_pairs={{0,4},{1,5},{2,6},{3,7},{4,0},{5,1},{6,2},{7,3},{8,12},{9,13},{10,... | collective-permute-start | bytes 331784 | tf_op jit(solution)/shard_map/ppermute | solution.py:45
  7.7 8.8 %collective-permute-start.2 = (bf16[48,1152]{1,0:T(8,128)(2,1)S(1)}, bf16[48,1152]{1,0:T(8,128)(2,1)S(1)}, u32[]{:S(2)}, u32[]{:S(2)}) collective-permute-start(bf16[48,1152]{1,0:T(8,128)(2,1)S(1)} %pad_maximum_fusion.9), channel_id=1, source_target_pairs={{0,6},{1,7},{2,4},{3,5},{4,2},{5,3},{6,0},{7,1},{8,14},{9,15},{10,... | collective-permute-start | bytes 331784 | tf_op jit(solution)/shard_map/ppermute | solution.py:45
  18.1 10.9 %collective-permute-start.3 = (bf16[192,1152]{1,0:T(8,128)(2,1)S(1)}, bf16[192,1152]{1,0:T(8,128)(2,1)S(1)}, u32[]{:S(2)}, u32[]{:S(2)}) collective-permute-start(bf16[192,1152]{1,0:T(8,128)(2,1)S(1)} %pad_maximum_fusion.4), channel_id=1, source_target_pairs={{0,16},{1,17},{2,3},{3,2},{4,20},{5,21},{6,7},{7,6},{8,9},{9,8},{1... | collective-permute-start | bytes 1327112 | tf_op jit(solution)/shard_map/ppermute | solution.py:45
  23.4 5.5 %collective-permute-start.7 = (f32[2,16,96]{2,1,0:T(8,128)S(1)}, f32[2,16,96]{2,1,0:T(8,128)S(1)}, u32[]{:S(2)}, u32[]{:S(2)}) collective-permute-start(f32[2,16,96]{2,1,0:T(8,128)S(1)} %get-tuple-element.309), channel_id=1, source_target_pairs={{0,6},{1,7},{2,4},{3,5},{4,2},{5,3},{6,0},{7,1},{8,14},{9,15},{10,... | collective-permute-start | bytes 36872 | tf_op jit(solution)/shard_map/ppermute | solution.py:45
  29.0 15.9 %collective-permute-start.11 = (bf16[384,1152]{1,0:T(8,128)(2,1)S(1)}, bf16[384,1152]{1,0:T(8,128)(2,1)S(1)}, u32[]{:S(2)}, u32[]{:S(2)}) collective-permute-start(bf16[384,1152]{1,0:T(8,128)(2,1)S(1)} %constant_dynamic-update-slice_fusion.7.refs_0_), channel_id=1, source_target_pairs={{0,1},{1,0},{2,18},{3,19},{4,5},{5,4},{6,22},{7,23},{8,24},{9,25},... | collective-permute-start | bytes 2654216 | tf_op jit(solution)/shard_map/ppermute | solution.py:45
  30.7 8.0 %collective-permute-start.10 = (bf16[48,1920]{1,0:T(8,128)(2,1)S(1)}, bf16[48,1920]{1,0:T(8,128)(2,1)S(1)}, u32[]{:S(2)}, u32[]{:S(2)}) collective-permute-start(bf16[48,1920]{1,0:T(8,128)(2,1)S(1)} %pad_maximum_fusion.8), channel_id=1, source_target_pairs={{0,6},{1,7},{2,4},{3,5},{4,2},{5,3},{6,0},{7,1},{8,14},{9,15},{10,... | collective-permute-start | bytes 552968 | tf_op jit(solution)/shard_map/ppermute | solution.py:45
  32.1 8.2 %collective-permute-start.8 = (bf16[48,1920]{1,0:T(8,128)(2,1)S(1)}, bf16[48,1920]{1,0:T(8,128)(2,1)S(1)}, u32[]{:S(2)}, u32[]{:S(2)}) collective-permute-start(bf16[48,1920]{1,0:T(8,128)(2,1)S(1)} %pad_maximum_fusion.8), channel_id=1, source_target_pairs={{0,2},{1,3},{2,0},{3,1},{4,6},{5,7},{6,4},{7,5},{8,10},{9,11},{10,... | collective-permute-start | bytes 552968 | tf_op jit(solution)/shard_map/ppermute | solution.py:45
  32.1 12.7 %collective-permute-start.9 = (bf16[48,1920]{1,0:T(8,128)(2,1)S(1)}, bf16[48,1920]{1,0:T(8,128)(2,1)S(1)}, u32[]{:S(2)}, u32[]{:S(2)}) collective-permute-start(bf16[48,1920]{1,0:T(8,128)(2,1)S(1)} %pad_maximum_fusion.8), channel_id=1, source_target_pairs={{0,4},{1,5},{2,6},{3,7},{4,0},{5,1},{6,2},{7,3},{8,12},{9,13},{10,... | collective-permute-start | bytes 552968 | tf_op jit(solution)/shard_map/ppermute | solution.py:45
  44.9 15.1 %collective-permute-start.12 = (bf16[192,1920]{1,0:T(8,128)(2,1)S(1)}, bf16[192,1920]{1,0:T(8,128)(2,1)S(1)}, u32[]{:S(2)}, u32[]{:S(2)}) collective-permute-start(bf16[192,1920]{1,0:T(8,128)(2,1)S(1)} %pad_maximum_fusion.2), channel_id=1, source_target_pairs={{0,16},{1,17},{2,3},{3,2},{4,20},{5,21},{6,7},{7,6},{8,9},{9,8},{1... | collective-permute-start | bytes 2211848 | tf_op jit(solution)/shard_map/ppermute | solution.py:45
  46.1 6.7 %collective-permute-start.13 = (bf16[192,384]{1,0:T(8,128)(2,1)S(1)}, bf16[192,384]{1,0:T(8,128)(2,1)S(1)}, u32[]{:S(2)}, u32[]{:S(2)}) collective-permute-start(bf16[192,384]{1,0:T(8,128)(2,1)S(1)} %dynamic_slice.191), channel_id=1, source_target_pairs={{0,2},{1,3},{2,0},{3,1},{4,6},{5,7},{6,4},{7,5},{8,10},{9,11},{10,... | collective-permute-start | bytes 442376 | tf_op jit(solution)/shard_map/ppermute | solution.py:45
  46.1 17.1 %collective-permute-start.16 = (bf16[384,1152]{1,0:T(8,128)(2,1)S(1)}, bf16[384,1152]{1,0:T(8,128)(2,1)S(1)}, u32[]{:S(2)}, u32[]{:S(2)}) collective-permute-start(bf16[384,1152]{1,0:T(8,128)(2,1)S(1)} %constant_dynamic-update-slice_fusion.7.refs_0_), channel_id=1, source_target_pairs={{0,8},{1,9},{2,10},{3,11},{4,12},{5,13},{6,14},{7,15},{8,0},{9,1},... | collective-permute-start | bytes 2654216 | tf_op jit(solution)/shard_map/ppermute | solution.py:45
  46.1 13.9 %collective-permute-start.14 = (bf16[192,384]{1,0:T(8,128)(2,1)S(1)}, bf16[192,384]{1,0:T(8,128)(2,1)S(1)}, u32[]{:S(2)}, u32[]{:S(2)}) collective-permute-start(bf16[192,384]{1,0:T(8,128)(2,1)S(1)} %dynamic_slice.191), channel_id=1, source_target_pairs={{0,4},{1,5},{2,6},{3,7},{4,0},{5,1},{6,2},{7,3},{8,12},{9,13},{10,... | collective-permute-start | bytes 442376 | tf_op jit(solution)/shard_map/ppermute | solution.py:45
  48.7 11.3 %collective-permute-start.15 = (bf16[192,384]{1,0:T(8,128)(2,1)S(1)}, bf16[192,384]{1,0:T(8,128)(2,1)S(1)}, u32[]{:S(2)}, u32[]{:S(2)}) collective-permute-start(bf16[192,384]{1,0:T(8,128)(2,1)S(1)} %dynamic_slice.191), channel_id=1, source_target_pairs={{0,6},{1,7},{2,4},{3,5},{4,2},{5,3},{6,0},{7,1},{8,14},{9,15},{10,... | collective-permute-start | bytes 442376 | tf_op jit(solution)/shard_map/ppermute | solution.py:45
  52.7 10.5 %collective-permute-start.17 = (bf16[384,1152]{1,0:T(8,128)(2,1)S(1)}, bf16[384,1152]{1,0:T(8,128)(2,1)S(1)}, u32[]{:S(2)}, u32[]{:S(2)}) collective-permute-start(bf16[384,1152]{1,0:T(8,128)(2,1)S(1)} %collective-permute-done.11.refs_1_), channel_id=1, source_target_pairs={{0,8},{1,9},{2,10},{3,11},{4,12},{5,13},{6,14},{7,15},{8,0},{9,1},... | collective-permute-start | bytes 2654216 | tf_op jit(solution)/shard_map/ppermute | solution.py:45
  60.2 16.0 %collective-permute-start.18 = (bf16[768,384]{1,0:T(8,128)(2,1)S(1)}, bf16[768,384]{1,0:T(8,128)(2,1)}, u32[]{:S(2)}, u32[]{:S(2)}) collective-permute-start(bf16[768,384]{1,0:T(8,128)(2,1)S(1)} %pad_maximum_fusion.3), channel_id=1, source_target_pairs={{0,16},{1,17},{2,3},{3,2},{4,20},{5,21},{6,7},{7,6},{8,9},{9,8},{1... | collective-permute-start | bytes 1769480 | tf_op jit(solution)/shard_map/ppermute | solution.py:45
  62.1 31.3 %collective-permute-start.19 = (bf16[384,1920]{1,0:T(8,128)(2,1)S(1)}, bf16[384,1920]{1,0:T(8,128)(2,1)}, u32[]{:S(2)}, u32[]{:S(2)}) collective-permute-start(bf16[384,1920]{1,0:T(8,128)(2,1)S(1)} %pad_maximum_fusion.refs_0_), channel_id=1, source_target_pairs={{0,1},{1,0},{2,18},{3,19},{4,5},{5,4},{6,22},{7,23},{8,24},{9,25},... | collective-permute-start | bytes 4423688 | tf_op jit(solution)/shard_map/ppermute | solution.py:45
  63.2 30.2 %collective-permute-start.21 = (bf16[384,1920]{1,0:T(8,128)(2,1)S(1)}, bf16[384,1920]{1,0:T(8,128)(2,1)}, u32[]{:S(2)}, u32[]{:S(2)}) collective-permute-start(bf16[384,1920]{1,0:T(8,128)(2,1)S(1)} %pad_maximum_fusion.refs_0_), channel_id=1, source_target_pairs={{0,8},{1,9},{2,10},{3,11},{4,12},{5,13},{6,14},{7,15},{8,0},{9,1},... | collective-permute-start | bytes 4423688 | tf_op jit(solution)/shard_map/ppermute | solution.py:45
  77.4 19.6 %collective-permute-start.20 = (bf16[1536,384]{1,0:T(8,128)(2,1)S(1)}, bf16[1536,384]{1,0:T(8,128)(2,1)S(1)}, u32[]{:S(2)}, u32[]{:S(2)}) collective-permute-start(bf16[1536,384]{1,0:T(8,128)(2,1)S(1)} %pad_maximum_fusion.1.refs_4_), channel_id=1, source_target_pairs={{0,1},{1,0},{2,18},{3,19},{4,5},{5,4},{6,22},{7,23},{8,24},{9,25},... | collective-permute-start | bytes 3538952 | tf_op jit(solution)/shard_map/ppermute | solution.py:45
  79.2 17.8 %collective-permute-start.22 = (bf16[1536,384]{1,0:T(8,128)(2,1)S(1)}, bf16[1536,384]{1,0:T(8,128)(2,1)}, u32[]{:S(2)}, u32[]{:S(2)}) collective-permute-start(bf16[1536,384]{1,0:T(8,128)(2,1)S(1)} %pad_maximum_fusion.1.refs_4_), channel_id=1, source_target_pairs={{0,8},{1,9},{2,10},{3,11},{4,12},{5,13},{6,14},{7,15},{8,0},{9,1},... | collective-permute-start | bytes 3538952 | tf_op jit(solution)/shard_map/ppermute | solution.py:45
  98.0 6.2 %collective-permute-start.23 = (bf16[384,1920]{1,0:T(8,128)(2,1)}, bf16[384,1920]{1,0:T(8,128)(2,1)S(1)}, u32[]{:S(2)}, u32[]{:S(2)}) collective-permute-start(bf16[384,1920]{1,0:T(8,128)(2,1)} %collective-permute-done.19.refs_1_), channel_id=1, source_target_pairs={{0,8},{1,9},{2,10},{3,11},{4,12},{5,13},{6,14},{7,15},{8,0},{9,1},... | collective-permute-start | bytes 4423688 | tf_op jit(solution)/shard_map/ppermute | solution.py:45
  159.3 8.3 %collective-permute-start.25 = (bf16[768,1920]{1,0:T(8,128)(2,1)}, bf16[768,1920]{1,0:T(8,128)(2,1)S(1)}, u32[]{:S(2)}, u32[]{:S(2)}) collective-permute-start(bf16[768,1920]{1,0:T(8,128)(2,1)} %mid_give.1), channel_id=1, source_target_pairs={{0,8},{1,9},{2,10},{3,11},{4,12},{5,13},{6,14},{7,15},{8,0},{9,1},... | collective-permute-start | bytes 8847368 | tf_op jit(solution)/shard_map/ppermute | solution.py:45
  167.6 10.4 %collective-permute-start.26 = (bf16[3072,384]{1,0:T(8,128)(2,1)}, bf16[3072,384]{1,0:T(8,128)(2,1)}, u32[]{:S(2)}, u32[]{:S(2)}) collective-permute-start(bf16[3072,384]{1,0:T(8,128)(2,1)} %down_give.1), channel_id=1, source_target_pairs={{0,8},{1,9},{2,10},{3,11},{4,12},{5,13},{6,14},{7,15},{8,0},{9,1},... | collective-permute-start | bytes 7077896 | tf_op jit(solution)/shard_map/ppermute | solution.py:45
  178.0 32.4 %collective-permute-start.28 = (bf16[4,2,48,1920]{3,2,1,0:T(8,128)(2,1)}, bf16[4,2,48,1920]{3,2,1,0:T(8,128)(2,1)S(1)}, u32[]{:S(2)}, u32[]{:S(2)}) collective-permute-start(bf16[4,2,48,1920]{3,2,1,0:T(8,128)(2,1)} %get-tuple-element.183), channel_id=1, source_target_pairs={{0,1},{1,0},{2,18},{3,19},{4,5},{5,4},{6,22},{7,23},{8,24},{9,25},... | collective-permute-start | bytes 4423688 | tf_op jit(solution)/shard_map/ppermute | solution.py:45
  189.0 21.4 %collective-permute-start.27 = (bf16[4,2,192,384]{3,2,0,1:T(8,128)(2,1)S(1)}, bf16[4,2,192,384]{3,2,0,1:T(8,128)(2,1)}, u32[]{:S(2)}, u32[]{:S(2)}) collective-permute-start(bf16[4,2,192,384]{3,2,0,1:T(8,128)(2,1)S(1)} %copy.37), channel_id=1, source_target_pairs={{0,1},{1,0},{2,18},{3,19},{4,5},{5,4},{6,22},{7,23},{8,24},{9,25},... | collective-permute-start | bytes 3538952 | tf_op jit(solution)/shard_map/ppermute | solution.py:45
  212.0 11.6 %collective-permute-start.30 = (bf16[768,1152]{1,0:T(8,128)(2,1)}, bf16[768,1152]{1,0:T(8,128)(2,1)}, u32[]{:S(2)}, u32[]{:S(2)}) collective-permute-start(bf16[768,1152]{1,0:T(8,128)(2,1)} %get-tuple-element.195), channel_id=1, source_target_pairs={{0,8},{1,9},{2,10},{3,11},{4,12},{5,13},{6,14},{7,15},{8,0},{9,1},... | collective-permute-start | bytes 5308424 | tf_op jit(solution)/shard_map/ppermute | solution.py:45
  212.1 11.5 %collective-permute-start.29 = (bf16[4,48,1920]{2,1,0:T(8,128)(2,1)S(1)}, bf16[4,48,1920]{2,1,0:T(8,128)(2,1)S(1)}, u32[]{:S(2)}, u32[]{:S(2)}) collective-permute-start(bf16[4,48,1920]{2,1,0:T(8,128)(2,1)S(1)} %get-tuple-element.194), channel_id=1, source_target_pairs={{0,16},{1,17},{2,3},{3,2},{4,20},{5,21},{6,7},{7,6},{8,9},{9,8},{1... | collective-permute-start | bytes 2211848 | tf_op jit(solution)/shard_map/ppermute | solution.py:45
  224.6 24.9 %collective-permute-start.31 = (bf16[4,192,384]{2,1,0:T(8,128)(2,1)S(1)}, bf16[4,192,384]{2,1,0:T(8,128)(2,1)}, u32[]{:S(2)}, u32[]{:S(2)}) collective-permute-start(bf16[4,192,384]{2,1,0:T(8,128)(2,1)S(1)} %fusion.2), channel_id=1, source_target_pairs={{0,16},{1,17},{2,3},{3,2},{4,20},{5,21},{6,7},{7,6},{8,9},{9,8},{1... | collective-permute-start | bytes 1769480 | tf_op jit(solution)/shard_map/ppermute | solution.py:45
  225.5 23.9 %collective-permute-start.32 = (bf16[48,1920]{1,0:T(8,128)(2,1)}, bf16[48,1920]{1,0:T(8,128)(2,1)S(1)}, u32[]{:S(2)}, u32[]{:S(2)}) collective-permute-start(bf16[48,1920]{1,0:T(8,128)(2,1)} %get-tuple-element.202), channel_id=1, source_target_pairs={{0,2},{1,3},{2,0},{3,1},{4,6},{5,7},{6,4},{7,5},{8,10},{9,11},{10,... | collective-permute-start | bytes 552968 | tf_op jit(solution)/shard_map/ppermute | solution.py:45
  229.3 20.1 %collective-permute-start.33 = (bf16[48,1920]{1,0:T(8,128)(2,1)S(1)}, bf16[48,1920]{1,0:T(8,128)(2,1)S(1)}, u32[]{:S(2)}, u32[]{:S(2)}) collective-permute-start(bf16[48,1920]{1,0:T(8,128)(2,1)S(1)} %get-tuple-element.203), channel_id=1, source_target_pairs={{0,4},{1,5},{2,6},{3,7},{4,0},{5,1},{6,2},{7,3},{8,12},{9,13},{10,... | collective-permute-start | bytes 552968 | tf_op jit(solution)/shard_map/ppermute | solution.py:45
  229.3 20.1 %collective-permute-start.34 = (bf16[48,1920]{1,0:T(8,128)(2,1)S(1)}, bf16[48,1920]{1,0:T(8,128)(2,1)S(1)}, u32[]{:S(2)}, u32[]{:S(2)}) collective-permute-start(bf16[48,1920]{1,0:T(8,128)(2,1)S(1)} %get-tuple-element.204), channel_id=1, source_target_pairs={{0,6},{1,7},{2,4},{3,5},{4,2},{5,3},{6,0},{7,1},{8,14},{9,15},{10,... | collective-permute-start | bytes 552968 | tf_op jit(solution)/shard_map/ppermute | solution.py:45
  250.1 20.5 %collective-permute-start.35 = (bf16[4,2,48,1152]{3,2,1,0:T(8,128)(2,1)}, bf16[4,2,48,1152]{3,2,1,0:T(8,128)(2,1)S(1)}, u32[]{:S(2)}, u32[]{:S(2)}) collective-permute-start(bf16[4,2,48,1152]{3,2,1,0:T(8,128)(2,1)} %get-tuple-element.207), channel_id=1, source_target_pairs={{0,1},{1,0},{2,18},{3,19},{4,5},{5,4},{6,22},{7,23},{8,24},{9,25},... | collective-permute-start | bytes 2654216 | tf_op jit(solution)/shard_map/ppermute | solution.py:45
  255.6 15.0 %collective-permute-start.36 = (bf16[192,384]{1,0:T(8,128)(2,1)}, bf16[192,384]{1,0:T(8,128)(2,1)S(1)}, u32[]{:S(2)}, u32[]{:S(2)}) collective-permute-start(bf16[192,384]{1,0:T(8,128)(2,1)} %get-tuple-element.214), channel_id=1, source_target_pairs={{0,2},{1,3},{2,0},{3,1},{4,6},{5,7},{6,4},{7,5},{8,10},{9,11},{10,... | collective-permute-start | bytes 442376 | tf_op jit(solution)/shard_map/ppermute | solution.py:45
  256.7 13.9 %collective-permute-start.37 = (bf16[192,384]{1,0:T(8,128)(2,1)}, bf16[192,384]{1,0:T(8,128)(2,1)S(1)}, u32[]{:S(2)}, u32[]{:S(2)}) collective-permute-start(bf16[192,384]{1,0:T(8,128)(2,1)} %get-tuple-element.215), channel_id=1, source_target_pairs={{0,4},{1,5},{2,6},{3,7},{4,0},{5,1},{6,2},{7,3},{8,12},{9,13},{10,... | collective-permute-start | bytes 442376 | tf_op jit(solution)/shard_map/ppermute | solution.py:45
  258.1 12.5 %collective-permute-start.38 = (bf16[192,384]{1,0:T(8,128)(2,1)}, bf16[192,384]{1,0:T(8,128)(2,1)S(1)}, u32[]{:S(2)}, u32[]{:S(2)}) collective-permute-start(bf16[192,384]{1,0:T(8,128)(2,1)} %get-tuple-element.216), channel_id=1, source_target_pairs={{0,6},{1,7},{2,4},{3,5},{4,2},{5,3},{6,0},{7,1},{8,14},{9,15},{10,... | collective-permute-start | bytes 442376 | tf_op jit(solution)/shard_map/ppermute | solution.py:45
  259.9 10.6 %collective-permute-start.39 = (f32[24,768]{1,0:T(8,128)}, f32[24,768]{1,0:T(8,128)S(1)}, u32[]{:S(2)}, u32[]{:S(2)}) collective-permute-start(f32[24,768]{1,0:T(8,128)} %pack.1), channel_id=1, source_target_pairs={{0,1},{1,0},{2,3},{3,2},{4,5},{5,4},{6,7},{7,6},{8,9},{9,8},{10,11... | collective-permute-start | bytes 221192 | tf_op jit(solution)/shard_map/ppermute | solution.py:45
  271.3 14.0 %collective-permute-start.40 = (bf16[4,48,1152]{2,1,0:T(8,128)(2,1)S(1)}, bf16[4,48,1152]{2,1,0:T(8,128)(2,1)S(1)}, u32[]{:S(2)}, u32[]{:S(2)}) collective-permute-start(bf16[4,48,1152]{2,1,0:T(8,128)(2,1)S(1)} %get-tuple-element.230), channel_id=1, source_target_pairs={{0,16},{1,17},{2,3},{3,2},{4,20},{5,21},{6,7},{7,6},{8,9},{9,8},{1... | collective-permute-start | bytes 1327112 | tf_op jit(solution)/shard_map/ppermute | solution.py:45
  273.1 12.1 %collective-permute-start.41 = (bf16[48,1920]{1,0:T(8,128)(2,1)S(1)}, bf16[48,1920]{1,0:T(8,128)(2,1)S(1)}, u32[]{:S(2)}, u32[]{:S(2)}) collective-permute-start(bf16[48,1920]{1,0:T(8,128)(2,1)S(1)} %fusion.6), channel_id=1, source_target_pairs={{0,16},{1,17},{2,18},{3,19},{4,20},{5,21},{6,22},{7,23},{8,24},{9,... | collective-permute-start | bytes 552968 | tf_op jit(solution)/shard_map/ppermute | solution.py:45
  276.3 5.3 %collective-permute-start.43 = (f32[24,768]{1,0:T(8,128)S(1)}, f32[24,768]{1,0:T(8,128)S(1)}, u32[]{:S(2)}, u32[]{:S(2)}) collective-permute-start(f32[24,768]{1,0:T(8,128)S(1)} %add.338), channel_id=1, source_target_pairs={{0,4},{1,5},{2,6},{3,7},{4,0},{5,1},{6,2},{7,3},{8,12},{9,13},{10,... | collective-permute-start | bytes 221192 | tf_op jit(solution)/shard_map/ppermute | solution.py:45
  285.3 6.5 %collective-permute-start.48 = (f32[24,768]{1,0:T(8,128)S(1)}, f32[24,768]{1,0:T(8,128)S(1)}, u32[]{:S(2)}, u32[]{:S(2)}) collective-permute-start(f32[24,768]{1,0:T(8,128)S(1)} %add.339), channel_id=1, source_target_pairs={{0,16},{1,17},{2,18},{3,19},{4,20},{5,21},{6,22},{7,23},{8,24},{9,... | collective-permute-start | bytes 221192 | tf_op jit(solution)/shard_map/ppermute | solution.py:45
  286.1 9.7 %collective-permute-start.47 = (bf16[192,384]{1,0:T(8,128)(2,1)S(1)}, bf16[192,384]{1,0:T(8,128)(2,1)S(1)}, u32[]{:S(2)}, u32[]{:S(2)}) collective-permute-start(bf16[192,384]{1,0:T(8,128)(2,1)S(1)} %fusion.13), channel_id=1, source_target_pairs={{0,16},{1,17},{2,18},{3,19},{4,20},{5,21},{6,22},{7,23},{8,24},{9,... | collective-permute-start | bytes 442376 | tf_op jit(solution)/shard_map/ppermute | solution.py:45
  287.4 5.9 %collective-permute-start.44 = (bf16[48,1152]{1,0:T(8,128)(2,1)S(1)}, bf16[48,1152]{1,0:T(8,128)(2,1)S(1)}, u32[]{:S(2)}, u32[]{:S(2)}) collective-permute-start(bf16[48,1152]{1,0:T(8,128)(2,1)S(1)} %get-tuple-element.239), channel_id=1, source_target_pairs={{0,2},{1,3},{2,0},{3,1},{4,6},{5,7},{6,4},{7,5},{8,10},{9,11},{10,... | collective-permute-start | bytes 331784 | tf_op jit(solution)/shard_map/ppermute | solution.py:45
  287.4 5.9 %collective-permute-start.45 = (bf16[48,1152]{1,0:T(8,128)(2,1)S(1)}, bf16[48,1152]{1,0:T(8,128)(2,1)S(1)}, u32[]{:S(2)}, u32[]{:S(2)}) collective-permute-start(bf16[48,1152]{1,0:T(8,128)(2,1)S(1)} %get-tuple-element.240), channel_id=1, source_target_pairs={{0,4},{1,5},{2,6},{3,7},{4,0},{5,1},{6,2},{7,3},{8,12},{9,13},{10,... | collective-permute-start | bytes 331784 | tf_op jit(solution)/shard_map/ppermute | solution.py:45
  287.4 8.4 %collective-permute-start.46 = (bf16[48,1152]{1,0:T(8,128)(2,1)S(1)}, bf16[48,1152]{1,0:T(8,128)(2,1)S(1)}, u32[]{:S(2)}, u32[]{:S(2)}) collective-permute-start(bf16[48,1152]{1,0:T(8,128)(2,1)S(1)} %get-tuple-element.241), channel_id=1, source_target_pairs={{0,6},{1,7},{2,4},{3,5},{4,2},{5,3},{6,0},{7,1},{8,14},{9,15},{10,... | collective-permute-start | bytes 331784 | tf_op jit(solution)/shard_map/ppermute | solution.py:45
  296.0 5.9 %collective-permute-start.51 = (bf16[48,1152]{1,0:T(8,128)(2,1)S(1)}, bf16[48,1152]{1,0:T(8,128)(2,1)S(1)}, u32[]{:S(2)}, u32[]{:S(2)}) collective-permute-start(bf16[48,1152]{1,0:T(8,128)(2,1)S(1)} %fusion.23), channel_id=1, source_target_pairs={{0,16},{1,17},{2,18},{3,19},{4,20},{5,21},{6,22},{7,23},{8,24},{9,... | collective-permute-start | bytes 331784 | tf_op jit(solution)/shard_map/ppermute | solution.py:45
  296.8 6.6 %collective-permute-start.52 = (bf16[48,1152]{1,0:T(8,128)(2,1)S(1)}, bf16[48,1152]{1,0:T(8,128)(2,1)S(1)}, u32[]{:S(2)}, u32[]{:S(2)}) collective-permute-start(bf16[48,1152]{1,0:T(8,128)(2,1)S(1)} %fusion.23), channel_id=1, source_target_pairs={{0,24},{1,25},{2,26},{3,27},{4,28},{5,29},{6,30},{7,31},{8,16},{9,... | collective-permute-start | bytes 331784 | tf_op jit(solution)/shard_map/ppermute | solution.py:45
  297.9 6.7 %collective-permute-start.54 = (bf16[2,192,384]{2,1,0:T(8,128)(2,1)S(1)}, bf16[2,192,384]{2,1,0:T(8,128)(2,1)S(1)}, u32[]{:S(2)}, u32[]{:S(2)}) collective-permute-start(bf16[2,192,384]{2,1,0:T(8,128)(2,1)S(1)} %get-tuple-element.283), channel_id=1, source_target_pairs={{0,8},{1,9},{2,10},{3,11},{4,12},{5,13},{6,14},{7,15},{8,0},{9,1},... | collective-permute-start | bytes 884744 | tf_op jit(solution)/shard_map/ppermute | solution.py:45
  298.3 7.6 %collective-permute-start.53 = (bf16[2,48,1920]{2,1,0:T(8,128)(2,1)S(1)}, bf16[2,48,1920]{2,1,0:T(8,128)(2,1)S(1)}, u32[]{:S(2)}, u32[]{:S(2)}) collective-permute-start(bf16[2,48,1920]{2,1,0:T(8,128)(2,1)S(1)} %pad_maximum_fusion.6), channel_id=1, source_target_pairs={{0,8},{1,9},{2,10},{3,11},{4,12},{5,13},{6,14},{7,15},{8,0},{9,1},... | collective-permute-start | bytes 1105928 | tf_op jit(solution)/shard_map/ppermute | solution.py:45
  (46 other events, 363.7 us)
